TPU v7x, 32 devices: a whole 2x2x4 slice. The times are simulated.
32 devices in a mesh: shot: 4 (over x, core), tm: 8 (over z, y).
Axes of the slice: x: 2, y: 2, z: 4, core: 2. Of those that a mesh axis runs over, the one named last changes fastest.
Arguments:
- features: bfloat16 [8, 2048, 1024], P('shot', 'tm'), may hold values from -6 to 6
- weight_pool: bfloat16 [64, 128, 128], replicated, may hold values from -0.25 to 0.25
- pattern_in: int32 [24, 4], replicated, may hold values from 0 to 7
- pattern_pool: int32 [24, 4], replicated, may hold values from 0 to 63, as said below
- gate_weight: bfloat16 [1024, 16], replicated, may hold values from -0.1875 to 0.1875
- decay_rate: float32 [8], replicated, may hold values from 5e-05 to 0.04
- beta_bias: float32 [8], replicated, may hold values from -8 to -4
- norm_gain: float32 [128], replicated, may hold values from 0.25 to 1.75
- out_weight: bfloat16 [1024, 1024], replicated, may hold values from -0.1875 to 0.1875
- cotangent: bfloat16 [8, 2048, 1024], P('shot', 'tm'), may hold values from -6 to 6
Outputs:
- output: bfloat16 [8, 2048, 1024], P('shot', 'tm')
- weight_grad: bfloat16 [1024, 1024], replicated
- gain_grad: float32 [128], replicated
Inputs may be any that keep to these rules, and one draw needn't show every extreme that they name: `pattern_pool`: every weight block is used by some member.
All inputs are finite; a program needn't handle non-finite values.
Results may differ from a plain program's by a relative error of at most 0.0077.
Values sent between devices are 32-bit elements; how exact they have to be, the bound alone decides.
No kernel may reach another device: no remote copies, remote signals or barrier semaphores. Data moves between devices by JAX's collectives and lax.ppermute only.
A program may use at most 128 MiB of HBM per device.

v0:
```python
import math

import jax
import jax.numpy as jnp
from jax import lax
from jax.sharding import PartitionSpec as P

BLOCK = 64


FULL_PRECISION = lax.Precision.HIGHEST


def passed_along(block, axis, distance):
    devices = range(lax.axis_size(axis))
    route = [(i - distance, i) for i in devices if i - distance in devices]
    return lax.ppermute(block, axis, route)


def split_blocks(array, span):
    seqs, length = (array.shape[0], array.shape[1])
    shaped = array.reshape((seqs, length // span, span) + array.shape[2:])
    return jnp.moveaxis(shaped, 3, 2)


def multiply(left, right):
    return jnp.einsum("shcd,shde->shce", left, right, precision=FULL_PRECISION)


def chain_maps(earlier, later):
    return (multiply(later[0], earlier[0]), multiply(later[0], earlier[1]) + later[1])


def block_terms(queries, keys, values, logdecay, betas, span):
    query_h = split_blocks(queries, span)
    key_h = split_blocks(keys, span)
    value_h = split_blocks(values, span)
    beta_h = split_blocks(betas, span)
    cumulative = jnp.cumsum(split_blocks(logdecay, span), axis=-1)
    position = jnp.arange(span)
    strict = position[:, None] > position[None, :]
    inclusive = position[:, None] >= position[None, :]
    spread = cumulative[..., :, None] - cumulative[..., None, :]
    ratio_strict = jnp.where(strict, jnp.exp(jnp.where(strict, spread, 0.0)), 0.0)
    ratio_incl = jnp.where(inclusive, jnp.exp(jnp.where(inclusive, spread, 0.0)), 0.0)
    key_inner = jnp.einsum("snhtc,snhuc->snhtu", key_h, key_h, precision=FULL_PRECISION)
    system = jnp.eye(span, dtype=jnp.float32) + beta_h[..., :, None] * ratio_strict * key_inner
    growth = jnp.exp(cumulative)
    right_side = jnp.concatenate(
        [beta_h[..., None] * value_h, (beta_h * growth)[..., None] * key_h], axis=-1
    )
    solved = lax.linalg.triangular_solve(
        system, right_side, left_side=True, lower=True, unit_diagonal=True
    )
    value_width = value_h.shape[-1]
    pseudo = solved[..., :value_width]
    mixing = solved[..., value_width:]
    tail = jnp.exp(cumulative[..., -1:] - cumulative)
    weighted = key_h * tail[..., None]
    final = jnp.exp(cumulative[..., -1])
    identity = jnp.eye(key_h.shape[-1], dtype=jnp.float32)
    transit = final[..., None, None] * identity - jnp.einsum(
        "snhtc,snhtd->snhcd", weighted, mixing, precision=FULL_PRECISION
    )
    pushed = jnp.einsum("snhtc,snhtd->snhcd", weighted, pseudo, precision=FULL_PRECISION)
    attend = jnp.einsum("snhtc,snhuc->snhtu", query_h, key_h, precision=FULL_PRECISION) * ratio_incl
    return (query_h, growth, attend, pseudo, mixing, transit, pushed)


def shards(
    features,
    weight_pool,
    pattern_in,
    pattern_pool,
    gate_weight,
    decay_rate,
    beta_bias,
    norm_gain,
    out_weight,
    cotangent,
):
    seqs, length, width = features.shape
    heads = decay_rate.shape[0]
    dims = weight_pool.shape[1]
    count = seqs * length
    rows = features.reshape(count, width)
    blocks_in = rows.reshape(count, width // dims, dims)
    picked = jnp.take(blocks_in, pattern_in, axis=1)
    chosen = jnp.take(weight_pool, pattern_pool, axis=0)
    projected = jnp.einsum(
        "tojc,ojcd->tod", picked, chosen, preferred_element_type=jnp.float32
    ).astype(jnp.bfloat16)
    queries = projected[:, :heads].astype(jnp.float32)
    keys_raw = projected[:, heads : 2 * heads].astype(jnp.float32)
    keys = keys_raw * lax.rsqrt(jnp.sum(keys_raw * keys_raw, axis=-1, keepdims=True) + 1e-06)
    values = projected[:, 2 * heads :].astype(jnp.float32)
    gates = jnp.dot(rows, gate_weight, preferred_element_type=jnp.float32)
    logdecay = -decay_rate * jax.nn.softplus(gates[:, :heads])
    betas = jax.nn.sigmoid(gates[:, heads:] + beta_bias)
    terms = block_terms(
        queries.reshape(seqs, length, heads, dims),
        keys.reshape(seqs, length, heads, dims),
        values.reshape(seqs, length, heads, dims),
        logdecay.reshape(seqs, length, heads),
        betas.reshape(seqs, length, heads),
        BLOCK,
    )
    query_h, growth, attend, pseudo, mixing, transit, pushed = terms
    identity = jnp.broadcast_to(jnp.eye(dims, dtype=jnp.float32), (seqs, heads, dims, dims))
    empty = jnp.zeros((seqs, heads, dims, dims), jnp.float32)

    def compose(carry, item):
        return (chain_maps(carry, item), None)

    (total_map, total_push), _ = lax.scan(
        compose, (identity, empty), (jnp.moveaxis(transit, 1, 0), jnp.moveaxis(pushed, 1, 0))
    )

    def relay(turn, arriving):
        leaving = multiply(total_map, arriving) + total_push
        return passed_along(leaving, "tm", 1)

    incoming = lax.fori_loop(0, lax.axis_size("tm") - 1, relay, empty)

    def advance(state, item):
        query_n, growth_n, attend_n, pseudo_n, mixing_n, transit_n, pushed_n = item
        recalled = (
            jnp.einsum("shtc,shcd->shtd", query_n, state, precision=FULL_PRECISION)
            * growth_n[..., None]
        )
        corrected = pseudo_n - jnp.einsum(
            "shtc,shcd->shtd", mixing_n, state, precision=FULL_PRECISION
        )
        produced = recalled + jnp.einsum(
            "shtu,shud->shtd", attend_n, corrected, precision=FULL_PRECISION
        )
        return (multiply(transit_n, state) + pushed_n, produced)

    _, produced = lax.scan(advance, incoming, tuple((jnp.moveaxis(array, 1, 0) for array in terms)))
    core = jnp.transpose(produced, (1, 0, 3, 2, 4)).reshape(count, heads, dims)
    normal = core * lax.rsqrt(jnp.mean(core * core, axis=-1, keepdims=True) + 1e-05)
    mixed_in = (normal * norm_gain).astype(jnp.bfloat16).reshape(count, heads * dims)
    output = (
        jnp.dot(mixed_in, out_weight, preferred_element_type=jnp.float32)
        .astype(jnp.bfloat16)
        .reshape(seqs, length, width)
    )
    cot_rows = cotangent.reshape(count, width)
    back = lax.dot_general(
        cot_rows, out_weight, (((1,), (1,)), ((), ())), preferred_element_type=jnp.float32
    )
    gain_part = jnp.sum(back.reshape(count, heads, dims) * normal, axis=(0, 1))
    weight_part = lax.dot_general(
        mixed_in, cot_rows, (((0,), (0,)), ((), ())), preferred_element_type=jnp.float32
    )
    summed = lax.psum((weight_part, gain_part), ("shot", "tm"))
    scale = 1.0 / math.sqrt(count * lax.axis_size("shot") * lax.axis_size("tm"))
    weight_grad = (summed[0] * scale).astype(jnp.bfloat16)
    gain_grad = summed[1] * scale
    return (output, weight_grad, gain_grad)


def solution(mesh):
    placed = (P("shot", "tm", None), P(), P(), P(), P(), P(), P(), P(), P(), P("shot", "tm", None))
    return jax.shard_map(
        shards,
        mesh=mesh,
        in_specs=placed,
        out_specs=(P("shot", "tm", None), P(), P()),
        check_vma=False,
    )
```

profile of v0, /device:TPU:0, one launch (start us, length us, event | category | flops | bytes accessed | tf_op | source)
XLA Modules:
  0.0 863.4 jit_solution(17168145357962392265)
XLA Ops:
  21.3 6.8 gather_fusion.1
  28.2 11.5 %fusion.33 = bf16[512,24,128]{0,2,1:T(8,128)(2,1)} fusion(bf16[24,4,512,128]{3,2,1,0:T(8,128)(2,1)} %bitcast.199, pred[24,4]{1,0:T(8,128)(4,1)S(1)} %copy.69, bf16[24,4,128,128]{2,3,1,0:T(8,128)(2,1)} %copy.68, pred[24,4]{1,0:T(8,128)(4,1)S(1)} %copy.66), kind=kOutput, calls=%fused_computation.46 | convolution fusion | flops 1620049920 | bytes 18874560 | tf_op jit(solution)/shard_map/tojc,ojcd->tod/dot_general | solution.py:90
  56.5 7.6 add_bitcast_fusion
  64.1 316.0 %custom-call.3 = f32[2,4,8,1,64,64]{4,5,3,2,1,0:T(8,128)} custom-call(f32[2,4,8,1,64,64]{5,4,3,2,1,0:T(8,128)} %add_bitcast_fusion), custom_call_target="InvertDiagBlocksLowerTriangular" | custom-call | tf_op jit(solution)/shard_map/triangular_solve | solution.py:52
  390.4 7.4 convolution_bitcast_fusion
  397.7 8.1 bitcast_subtract_fusion
  410.8 29.6 %while.37 = (s32[]{:T(128)}, f32[2,8,128,128]{3,2,1,0:T(8,128)S(1)}, f32[2,8,128,128]{3,2,1,0:T(8,128)}, f32[4,2,8,128,128]{4,3,2,1,0:T(8,128)}, f32[4,2,8,128,128]{4,3,2,1,0:T(8,128)}, /*index=5*/s32[]{:T(128)}, s32[]{:T(128)}) while((s32[]{:T(128)}, f32[2,8,128,128]{3,2,1,0:T(8,128)S(1)}, f32[2,8,128,128]{3,2,1,0:T(8,128)}, ...), condition=%wide.region_3.4_spmd.clone, body=%wide.region_2.3_spmd.clone.sunk | while | flops 805830656 | bytes 11535959 | solution.py:115
  450.0 200.4 %while.35 = (s32[]{:T(128)}, f32[2,8,128,128]{3,2,1,0:T(8,128)}, f32[2,8,128,128]{3,2,1,0:T(8,128)S(1)}, f32[2,8,128,128]{3,2,1,0:T(8,128)}, s32[]{:T(128)}) while((s32[]{:T(128)}, f32[2,8,128,128]{3,2,1,0:T(8,128)}, f32[2,8,128,128]{3,2,1,0:T(8,128)S(1)}, f32[2,8,128,128]{3,2,1,0:T(8,128)}, s32[]{:T(128)}) %tuple.68), condition=%wide.region_5.6_spmd, body=%wide.region_4.5_spmd.sunk | while | flops 402915328 | bytes 8388709 | solution.py:123
  453.7 5.9 collective-permute-start
  459.6 21.7 %collective-permute-done = f32[2,8,128,128]{3,2,1,0:T(8,128)} collective-permute-done((f32[2,8,128,128]{3,2,1,0:T(8,128)}, f32[2,8,128,128]{3,2,1,0:T(8,128)}, u32[]{:S(2)}, u32[]{:S(2)}) %collective-permute-start) | collective-permute-done | bytes 1048608 | tf_op jit(solution)/shard_map/while/body/eval_jaxpr/ppermute | solution.py:17
  490.4 20.8 %collective-permute-done = f32[2,8,128,128]{3,2,1,0:T(8,128)} collective-permute-done((f32[2,8,128,128]{3,2,1,0:T(8,128)}, f32[2,8,128,128]{3,2,1,0:T(8,128)}, u32[]{:S(2)}, u32[]{:S(2)}) %collective-permute-start) | collective-permute-done | bytes 1048608 | tf_op jit(solution)/shard_map/while/body/eval_jaxpr/ppermute | solution.py:17
  514.9 5.4 collective-permute-start
  520.3 19.9 %collective-permute-done = f32[2,8,128,128]{3,2,1,0:T(8,128)} collective-permute-done((f32[2,8,128,128]{3,2,1,0:T(8,128)}, f32[2,8,128,128]{3,2,1,0:T(8,128)}, u32[]{:S(2)}, u32[]{:S(2)}) %collective-permute-start) | collective-permute-done | bytes 1048608 | tf_op jit(solution)/shard_map/while/body/eval_jaxpr/ppermute | solution.py:17
  543.9 6.2 collective-permute-start
  550.1 19.0 %collective-permute-done = f32[2,8,128,128]{3,2,1,0:T(8,128)} collective-permute-done((f32[2,8,128,128]{3,2,1,0:T(8,128)}, f32[2,8,128,128]{3,2,1,0:T(8,128)}, u32[]{:S(2)}, u32[]{:S(2)}) %collective-permute-start) | collective-permute-done | bytes 1048608 | tf_op jit(solution)/shard_map/while/body/eval_jaxpr/ppermute | solution.py:17
  572.7 6.3 collective-permute-start
  579.1 18.0 %collective-permute-done = f32[2,8,128,128]{3,2,1,0:T(8,128)} collective-permute-done((f32[2,8,128,128]{3,2,1,0:T(8,128)}, f32[2,8,128,128]{3,2,1,0:T(8,128)}, u32[]{:S(2)}, u32[]{:S(2)}) %collective-permute-start) | collective-permute-done | bytes 1048608 | tf_op jit(solution)/shard_map/while/body/eval_jaxpr/ppermute | solution.py:17
  600.8 6.3 collective-permute-start
  607.1 17.1 %collective-permute-done = f32[2,8,128,128]{3,2,1,0:T(8,128)} collective-permute-done((f32[2,8,128,128]{3,2,1,0:T(8,128)}, f32[2,8,128,128]{3,2,1,0:T(8,128)}, u32[]{:S(2)}, u32[]{:S(2)}) %collective-permute-start) | collective-permute-done | bytes 1048608 | tf_op jit(solution)/shard_map/while/body/eval_jaxpr/ppermute | solution.py:17
  627.9 6.3 collective-permute-start
  634.2 16.2 %collective-permute-done = f32[2,8,128,128]{3,2,1,0:T(8,128)} collective-permute-done((f32[2,8,128,128]{3,2,1,0:T(8,128)}, f32[2,8,128,128]{3,2,1,0:T(8,128)}, u32[]{:S(2)}, u32[]{:S(2)}) %collective-permute-start) | collective-permute-done | bytes 1048608 | tf_op jit(solution)/shard_map/while/body/eval_jaxpr/ppermute | solution.py:17
  650.4 48.3 %while.36 = (s32[]{:T(128)}, f32[2,8,128,128]{3,2,1,0:T(8,128)}, f32[4,2,8,64,128]{4,3,2,1,0:T(8,128)}, f32[4,2,8,128,128]{4,3,2,1,0:T(8,128)}, f32[4,2,8,128,12...) while((s32[]{:T(128)}, f32[2,8,128,128]{3,2,1,0:T(8,128)}, ...), condition=%wide.region_7.8_spmd, body=%wide.region_6.7_spmd.sunk | while | flops 906625024 | bytes 14171253 | solution.py:139
  719.6 43.4 %psum.15 = f32[128]{0:T(128)S(1)} all-reduce(f32[128]{0:T(128)S(1)} %fusion.44), channel_id=1, replica_groups=mesh['shot'=4,'tm'=8] {'shot','tm'}, use_global_device_ids=true, to_apply=%region_11.12 | all-reduce | flops 128 | bytes 1024 | tf_op jit(solution)/shard_map/psum | solution.py:156
  767.9 84.1 %all-reduce.2.cloned.1.call-done = f32[1024,1024]{1,0:T(8,128)} async-done(((f32[1024,1024]{1,0:T(8,128)}), f32[1024,1024]{1,0:T(8,128)}) %all-reduce.2.cloned.1.call-update) | async-done | bytes 4194320 | tf_op jit(solution)/shard_map/psum | solution.py:156
  (147 shorter events, 194.3 us)
Async XLA Ops:
  7.2 709.4 %copy-start = (bf16[1024,1024]{1,0:T(8,128)(2,1)S(1)}, bf16[1024,1024]{1,0:T(8,128)(2,1)}, u32[]{:S(2)}) copy-start(bf16[1024,1024]{1,0:T(8,128)(2,1)} %param.24) | copy-start | bytes 6291460
  7.2 844.8 %all-reduce.2.cloned.1.call-start = ((), (), s32[]{:S(2)}) async-start(), calls=%async_computation | async-start | bytes 8388608 | tf_op jit(solution)/shard_map/psum | solution.py:156
  41.1 3.8 copy-start.12
  41.1 3.8 copy-start.6
  41.1 3.8 copy-start.9
  41.1 4.2 copy-start.11
  380.1 3.9 copy-start.7
  387.8 2.6 copy-start.3
  442.8 2.8 copy-start.4
  442.8 2.8 copy-start.5
  453.7 27.6 %collective-permute-start = (f32[2,8,128,128]{3,2,1,0:T(8,128)}, f32[2,8,128,128]{3,2,1,0:T(8,128)}, u32[]{:S(2)}, u32[]{:S(2)}) collective-permute-start(f32[2,8,128,128]{3,2,1,0:T(8,128)} %convolution_add_fusion.6), channel_id=1, source_target_pairs={{0,1},{1,2},{2,3},{3,4},{4,5},{5,6},{6,7},{8,9},{9,10},{10,11},{11... | collective-permute-start | bytes 3145736 | tf_op jit(solution)/shard_map/while/body/eval_jaxpr/ppermute | solution.py:17
  485.0 26.2 %collective-permute-start = (f32[2,8,128,128]{3,2,1,0:T(8,128)}, f32[2,8,128,128]{3,2,1,0:T(8,128)}, u32[]{:S(2)}, u32[]{:S(2)}) collective-permute-start(f32[2,8,128,128]{3,2,1,0:T(8,128)} %convolution_add_fusion.6), channel_id=1, source_target_pairs={{0,1},{1,2},{2,3},{3,4},{4,5},{5,6},{6,7},{8,9},{9,10},{10,11},{11... | collective-permute-start | bytes 3145736 | tf_op jit(solution)/shard_map/while/body/eval_jaxpr/ppermute | solution.py:17
  514.9 25.3 %collective-permute-start = (f32[2,8,128,128]{3,2,1,0:T(8,128)}, f32[2,8,128,128]{3,2,1,0:T(8,128)}, u32[]{:S(2)}, u32[]{:S(2)}) collective-permute-start(f32[2,8,128,128]{3,2,1,0:T(8,128)} %convolution_add_fusion.6), channel_id=1, source_target_pairs={{0,1},{1,2},{2,3},{3,4},{4,5},{5,6},{6,7},{8,9},{9,10},{10,11},{11... | collective-permute-start | bytes 3145736 | tf_op jit(solution)/shard_map/while/body/eval_jaxpr/ppermute | solution.py:17
  543.9 25.2 %collective-permute-start = (f32[2,8,128,128]{3,2,1,0:T(8,128)}, f32[2,8,128,128]{3,2,1,0:T(8,128)}, u32[]{:S(2)}, u32[]{:S(2)}) collective-permute-start(f32[2,8,128,128]{3,2,1,0:T(8,128)} %convolution_add_fusion.6), channel_id=1, source_target_pairs={{0,1},{1,2},{2,3},{3,4},{4,5},{5,6},{6,7},{8,9},{9,10},{10,11},{11... | collective-permute-start | bytes 3145736 | tf_op jit(solution)/shard_map/while/body/eval_jaxpr/ppermute | solution.py:17
  572.7 24.4 %collective-permute-start = (f32[2,8,128,128]{3,2,1,0:T(8,128)}, f32[2,8,128,128]{3,2,1,0:T(8,128)}, u32[]{:S(2)}, u32[]{:S(2)}) collective-permute-start(f32[2,8,128,128]{3,2,1,0:T(8,128)} %convolution_add_fusion.6), channel_id=1, source_target_pairs={{0,1},{1,2},{2,3},{3,4},{4,5},{5,6},{6,7},{8,9},{9,10},{10,11},{11... | collective-permute-start | bytes 3145736 | tf_op jit(solution)/shard_map/while/body/eval_jaxpr/ppermute | solution.py:17
  600.8 23.4 %collective-permute-start = (f32[2,8,128,128]{3,2,1,0:T(8,128)}, f32[2,8,128,128]{3,2,1,0:T(8,128)}, u32[]{:S(2)}, u32[]{:S(2)}) collective-permute-start(f32[2,8,128,128]{3,2,1,0:T(8,128)} %convolution_add_fusion.6), channel_id=1, source_target_pairs={{0,1},{1,2},{2,3},{3,4},{4,5},{5,6},{6,7},{8,9},{9,10},{10,11},{11... | collective-permute-start | bytes 3145736 | tf_op jit(solution)/shard_map/while/body/eval_jaxpr/ppermute | solution.py:17
  627.9 22.5 %collective-permute-start = (f32[2,8,128,128]{3,2,1,0:T(8,128)}, f32[2,8,128,128]{3,2,1,0:T(8,128)}, u32[]{:S(2)}, u32[]{:S(2)}) collective-permute-start(f32[2,8,128,128]{3,2,1,0:T(8,128)} %convolution_add_fusion.6), channel_id=1, source_target_pairs={{0,1},{1,2},{2,3},{3,4},{4,5},{5,6},{6,7},{8,9},{9,10},{10,11},{11... | collective-permute-start | bytes 3145736 | tf_op jit(solution)/shard_map/while/body/eval_jaxpr/ppermute | solution.py:17
  698.7 2.4 copy-start.1
  698.7 2.4 copy-start.10
  701.1 1.4 copy-start.8
  705.8 3.4 copy-start.2
Sparse Core Ops, SparseCore 0:
  705.9 146.0 all-reduce.1
where the time goes:
time: 874 us; the launch traced here: 863 us
  other arithmetic  343 us (39%)
  waiting for transfers between devices  217 us (25%)
  matrix products  141 us (16%)
  local copies, waits for them, and re-layouts  61.4 us (7%)
  blocking collectives  43.4 us (5%)
  starting transfers between devices  42 us (5%)
  between operations  14.9 us (2%)
    another operation x2, other arithmetic, block_terms(): lax.linalg.triangular_solve(system, right_side, left_side=True, lower=Tru...  316 us
    ppermute x7, waiting for transfers between devices, passed_along(): return lax.ppermute(block, axis, route)  133 us
    psum x1, waiting for transfers between devices, shards(): summed = lax.psum((weight_part, gain_part), ('shot', 'tm'))  84.1 us
    dot_general x19, matrix products, multiply(): return jnp.einsum('shcd,shde->shce', left, right, precision=FULL_PRECISION)  65 us
    psum x1, blocking collectives, shards(): summed = lax.psum((weight_part, gain_part), ('shot', 'tm'))  43.4 us
    ppermute x7, starting transfers between devices, passed_along(): return lax.ppermute(block, axis, route)  41.9 us
  transfers between devices with their start and end apart: 8, of which 8 were waited for; matrix products, arithmetic and copies ran while one was open for 2% of the time, Pallas kernels for 0%

commit v1 on v0

v1 whole, which is shorter than its diff:
```python
import functools
import math

import jax
import jax.numpy as jnp
from jax import lax
from jax.experimental import pallas as pl
from jax.experimental.pallas import tpu as pltpu
from jax.sharding import PartitionSpec as P

GROUPS = 1
CORES = 2
PAIR = 2
F32 = jnp.float32
BF16 = jnp.bfloat16
VMEM_LIMIT = 40 * 1024 * 1024


def dot(a, b):
    return lax.dot_general(a, b, (((1,), (0,)), ((), ())), preferred_element_type=F32)


def dot_nt(a, b):
    return lax.dot_general(a, b, (((1,), (1,)), ((), ())), preferred_element_type=F32)


def dot_tn(a, b):
    return lax.dot_general(a, b, (((0,), (0,)), ((), ())), preferred_element_type=F32)


def halves(a):
    high = a.astype(BF16)
    return high, (a - high.astype(F32)).astype(BF16)


def dot3(a, b):
    ah, al = halves(a)
    bh, bl = halves(b)
    return dot(ah, bh) + (dot(ah, bl) + dot(al, bh))


def params(**more):
    return pltpu.CompilerParams(vmem_limit_bytes=VMEM_LIMIT, **more)


def whole(shape):
    return pl.BlockSpec(shape, lambda *_: (0,) * len(shape))


def cost(flops, size):
    return pl.CostEstimate(flops=flops, bytes_accessed=size, transcendentals=0)


def gates_kernel(span, x_ref, w_ref, rate_ref, bias_ref, out_ref):
    heads = rate_ref.shape[1]
    gates = dot(x_ref[...], w_ref[...])
    raw = gates[:, :heads]
    softplus = jnp.maximum(raw, 0.0) + jnp.log1p(jnp.exp(-jnp.abs(raw)))
    logdecay = -rate_ref[...] * softplus
    out_ref[:, heads : 2 * heads] = jax.nn.sigmoid(gates[:, heads:] + bias_ref[...])
    row = lax.broadcasted_iota(jnp.int32, (span, span), 0)
    col = lax.broadcasted_iota(jnp.int32, (span, span), 1)
    lower = jnp.where(row >= col, 1.0, 0.0).astype(F32)
    for first in range(0, x_ref.shape[0], span):
        piece = logdecay[first : first + span]
        out_ref[first : first + span, :heads] = lax.dot_general(
            lower, piece, (((1,), (0,)), ((), ())), precision=lax.Precision.HIGHEST, preferred_element_type=F32
        )


def gates_call(rows, gate_weight, decay_rate, beta_bias, span):
    count, width = rows.shape
    heads = decay_rate.shape[0]
    return pl.pallas_call(
        functools.partial(gates_kernel, span),
        out_shape=jax.ShapeDtypeStruct((count, 2 * heads), F32),
        compiler_params=params(),
        cost_estimate=cost(2 * count * width * 128, count * width * 2),
        name="gates",
    )(rows, gate_weight, decay_rate.reshape(1, heads), beta_bias.reshape(1, heads))


def inverse_times(system, right):
    span = system.shape[0]
    row = lax.broadcasted_iota(jnp.int32, (span, span), 0)
    col = lax.broadcasted_iota(jnp.int32, (span, span), 1)
    apart = row ^ col
    inv = jnp.where(row == col, 1.0, jnp.where(apart == 1, -system, 0.0)).astype(BF16)
    step = 2
    while step < span:
        band = jnp.where((apart >= step) & (apart < 2 * step), system, 0.0).astype(BF16)
        inner = dot(inv, band).astype(BF16)
        inv = inv - dot(inner, inv).astype(BF16)
        step *= 2
    rounded = right.astype(BF16)
    first = dot(inv, rounded) + (right - rounded.astype(F32))
    residual = (right - first) - dot3(system, first)
    return first + dot(inv, residual.astype(BF16))


def local_kernel(
    first_head, heads, span, info, pin, ppool, x_ref, pool_ref, gate_ref, own_ref, send_ref, core_ref, query_ref
):
    head = first_head + pl.program_id(0)
    members = pin.shape[0] // (3 * heads)
    dims = pool_ref.shape[1]
    lane = lax.broadcasted_iota(jnp.int32, (span, 2 * heads), 1)
    wide = lax.broadcasted_iota(jnp.int32, (span, dims), 1)
    row = lax.broadcasted_iota(jnp.int32, (span, span), 0)
    col = lax.broadcasted_iota(jnp.int32, (span, span), 1)
    eye = (
        lax.broadcasted_iota(jnp.int32, (dims, dims), 0) == lax.broadcasted_iota(jnp.int32, (dims, dims), 1)
    ).astype(F32)
    for part in range(2):
        seq = info[0] if part == 0 else 1 - info[0]
        rows = pl.ds(pl.multiple_of(seq * span, span), span)
        projected = []
        for kind in range(3):
            target = (kind * heads + head) * members
            picked = [
                x_ref[rows, pl.ds(pl.multiple_of(pin[target + j] * dims, dims), dims)] for j in range(members)
            ]
            chosen = [pool_ref[ppool[target + j]] for j in range(members)]
            projected.append(dot(jnp.concatenate(picked, 1), jnp.concatenate(chosen, 0)).astype(BF16))
        query, key, value = projected
        key_wide = key.astype(F32)
        gates = gate_ref[rows, :]
        cumulative = jnp.sum(jnp.where(lane == head, gates, 0.0), axis=1, keepdims=True)
        beta = jnp.sum(jnp.where(lane == heads + head, gates, 0.0), axis=1, keepdims=True)
        norm = lax.rsqrt(jnp.sum(key_wide * key_wide, axis=1, keepdims=True) + 1e-06)
        across = jnp.where(wide == 0, cumulative, norm).T
        cumulative_row, norm_row = across[0:1, :], across[1:2, :]
        ratio = jnp.where(row >= col, jnp.exp(jnp.minimum(cumulative - cumulative_row, 0.0)), 0.0) * norm_row
        attend = ratio * dot_nt(query, key)
        system = jnp.where(row > col, ratio * dot_nt(key, key), 0.0) * (beta * norm)
        growth = jnp.exp(cumulative)
        right = jnp.concatenate([(beta * growth * norm) * key_wide, beta * value.astype(F32)], axis=1)
        solved = inverse_times(system, right)
        last = cumulative[span - 1 : span, :]
        high, low = halves(solved * (norm * jnp.exp(last - cumulative)))
        pushed = dot_tn(key, high) + dot_tn(key, low)
        out = own_ref if part == 0 else send_ref
        out[0, :, :dims] = jnp.exp(last) * eye - pushed[:, :dims]
        out[0, :, dims:] = pushed[:, dims:]
        seen = dot3(attend, solved)
        query_ref[rows, :] = growth * query.astype(F32) - seen[:, :dims]
        core_ref[rows, :] = seen[:, dims:]


def local_call(info, pin, ppool, rows, pool, gates, first_head, count_heads, heads, span):
    count, width = rows.shape
    dims = pool.shape[1]
    maps = jax.ShapeDtypeStruct((count_heads, dims, 2 * dims), F32)
    wide = jax.ShapeDtypeStruct((count, count_heads * dims), F32)
    map_spec = pl.BlockSpec((1, dims, 2 * dims), lambda i, *_: (i, 0, 0))
    row_spec = pl.BlockSpec((count, dims), lambda i, *_: (0, i))
    return pl.pallas_call(
        functools.partial(local_kernel, first_head, heads, span),
        out_shape=(maps, maps, wide, wide),
        grid_spec=pltpu.PrefetchScalarGridSpec(
            num_scalar_prefetch=3,
            grid=(count_heads,),
            in_specs=[whole(rows.shape), whole(pool.shape), whole(gates.shape)],
            out_specs=(map_spec, map_spec, row_spec, row_spec),
        ),
        compiler_params=params(),
        cost_estimate=cost(count_heads * 2 * 2 * span * 256 * 256 * 24, 8 * 1024 * 1024),
        name="local",
    )(info, pin, ppool, rows, pool, gates)


def apply_map(maps, state):
    dims = maps.shape[0]
    return dot3(maps[:, :dims], state)


def combine_kernel(info, own_ref, got_ref, early_ref, both_ref):
    later_is_own = info[0] == 1
    for h in range(own_ref.shape[0]):
        own, got = own_ref[h], got_ref[h]
        early = jnp.where(later_is_own, got, own)
        late = jnp.where(later_is_own, own, got)
        dims = own.shape[0]
        early_ref[h] = early
        both = apply_map(late, early)
        both_ref[h, :, :dims] = both[:, :dims]
        both_ref[h, :, dims:] = both[:, dims:] + late[:, dims:]


def combine_call(info, own, got):
    shape = jax.ShapeDtypeStruct(own.shape, F32)
    return pl.pallas_call(
        combine_kernel,
        out_shape=(shape, shape),
        in_specs=[pl.BlockSpec(memory_space=pltpu.SMEM)] + [pl.BlockSpec(memory_space=pltpu.VMEM)] * 2,
        compiler_params=params(),
        cost_estimate=cost(own.shape[0] * 6 * 128 * 128 * 256, own.size * 16),
        name="combine",
    )(info, own, got)


def hop_kernel(maps_ref, state_ref, out_ref):
    for h in range(maps_ref.shape[0]):
        maps = maps_ref[h]
        dims = maps.shape[0]
        out_ref[h] = apply_map(maps, state_ref[h]) + maps[:, dims:]


def hop_call(maps, state):
    return pl.pallas_call(
        hop_kernel,
        out_shape=jax.ShapeDtypeStruct(state.shape, F32),
        compiler_params=params(),
        cost_estimate=cost(maps.shape[0] * 6 * 128 * 128 * 128, maps.size * 8),
        name="hop",
    )(maps, state)


def split_kernel(info, maps_ref, state_ref, keep_ref, send_ref):
    second = info[0] == 1
    for h in range(maps_ref.shape[0]):
        maps = maps_ref[h]
        state = state_ref[h]
        dims = maps.shape[0]
        middle = apply_map(maps, state) + maps[:, dims:]
        keep_ref[h] = jnp.where(second, middle, state)
        send_ref[h] = jnp.where(second, state, middle)


def split_call(info, maps, state):
    shape = jax.ShapeDtypeStruct(state.shape, F32)
    return pl.pallas_call(
        split_kernel,
        out_shape=(shape, shape),
        in_specs=[pl.BlockSpec(memory_space=pltpu.SMEM)] + [pl.BlockSpec(memory_space=pltpu.VMEM)] * 2,
        compiler_params=params(),
        cost_estimate=cost(maps.shape[0] * 6 * 128 * 128 * 128, maps.size * 8),
        name="split",
    )(info, maps, state)


def mix_kernel(span, info, core_ref, query_ref, keep_ref, got_ref, gain_ref, cot_ref, normal_ref, mixed_ref, wsend_ref, wkeep_ref):
    step = pl.program_id(0)
    half = wsend_ref.shape[0]
    for part in range(2):
        seq = info[0] if part == 0 else 1 - info[0]
        rows = pl.ds(pl.multiple_of(seq * span, span), span)
        state = (keep_ref if part == 0 else got_ref)[0]
        core = core_ref[rows, :] + dot3(query_ref[rows, :], state)
        normal = core * lax.rsqrt(jnp.mean(core * core, axis=1, keepdims=True) + 1e-05)
        normal_ref[rows, :] = normal
        mixed_ref[rows, :] = (normal * gain_ref[...]).astype(BF16)
    product = dot_tn(mixed_ref[...], cot_ref[...])

    @pl.when(step < half)
    def _():
        wsend_ref[step] = product

    @pl.when(step >= half)
    def _():
        wkeep_ref[step - half] = product


def mix_call(info, core, query, keep, got, gain, cot, span):
    count, width = cot.shape
    heads_here = keep.shape[0]
    dims = gain.shape[1]
    half = heads_here // 2

    def order(i, info):
        first = jnp.where(i < half, 1 - info[1], info[1])
        return first * half + lax.rem(i, half)

    row_spec = pl.BlockSpec((count, dims), lambda i, info: (0, order(i, info)))
    state_spec = pl.BlockSpec((1, dims, dims), lambda i, info: (order(i, info), 0, 0))
    weight = jax.ShapeDtypeStruct((half, dims, width), F32)
    return pl.pallas_call(
        functools.partial(mix_kernel, span),
        out_shape=(
            jax.ShapeDtypeStruct((count, heads_here * dims), F32),
            jax.ShapeDtypeStruct((count, heads_here * dims), BF16),
            weight,
            weight,
        ),
        grid_spec=pltpu.PrefetchScalarGridSpec(
            num_scalar_prefetch=1,
            grid=(heads_here,),
            in_specs=[row_spec, row_spec, state_spec, state_spec, whole(gain.shape), whole(cot.shape)],
            out_specs=(row_spec, row_spec, whole(weight.shape), whole(weight.shape)),
        ),
        compiler_params=params(),
        cost_estimate=cost(heads_here * 2 * 512 * 1024 * 128, 6 * 1024 * 1024),
        name="mix",
    )(info, core, query, keep, got, gain, cot)


def finish_kernel(groups, *refs):
    mixed, normal = refs[:groups], refs[groups : 2 * groups]
    weight_ref, cot_ref, out_ref, gain_ref = refs[2 * groups :]
    dims = gain_ref.shape[1]

    @pl.when(pl.program_id(0) == 0)
    def _():
        gain_ref[...] = jnp.zeros_like(gain_ref)

    stacked = jnp.concatenate([ref[...] for ref in mixed], axis=1)
    out_ref[...] = dot(stacked, weight_ref[...]).astype(BF16)
    back = dot_nt(cot_ref[...], weight_ref[...])
    total = jnp.zeros((out_ref.shape[0], dims), F32)
    first = 0
    for ref in normal:
        for lane in range(0, ref.shape[1], dims):
            total += back[:, first : first + dims] * ref[:, lane : lane + dims]
            first += dims
    gain_ref[...] += jnp.sum(total.reshape(-1, 8, dims), axis=0)


def finish_call(mixed, normal, weight, cot):
    count, width = cot.shape
    block = 128
    groups = len(mixed)
    part = mixed[0].shape[1]
    dims = 128
    part_spec = pl.BlockSpec((block, part), lambda i: (i, 0))
    row_spec = pl.BlockSpec((block, width), lambda i: (i, 0))
    return pl.pallas_call(
        functools.partial(finish_kernel, groups),
        out_shape=(jax.ShapeDtypeStruct((count, width), BF16), jax.ShapeDtypeStruct((8, dims), F32)),
        grid=(count // block,),
        in_specs=[part_spec] * (2 * groups) + [whole(weight.shape), row_spec],
        out_specs=(row_spec, whole((8, dims))),
        compiler_params=params(),
        cost_estimate=cost(4 * count * width * width, 7 * 1024 * 1024),
        name="finish",
    )(*mixed, *normal, weight, cot)


def shards(mesh, features, weight_pool, pattern_in, pattern_pool, gate_weight, decay_rate, beta_bias, norm_gain, out_weight, cotangent):
    n_shot, n_tm = mesh.shape["shot"], mesh.shape["tm"]
    n_x, n_z = n_shot // CORES, n_tm // PAIR
    seqs, span, width = features.shape
    heads = decay_rate.shape[0]
    dims = weight_pool.shape[1]
    count = seqs * span
    both = ("shot", "tm")
    shot, tm = lax.axis_index("shot"), lax.axis_index("tm")
    x, core, z, y = shot // CORES, shot % CORES, tm // PAIR, tm % PAIR

    def place(xi, ci, zi, yi):
        return (xi * CORES + ci) * n_tm + zi * PAIR + yi

    def moved(array, shift, wrap=True):
        dx, dc, dz, dy = shift
        route = []
        for xi in range(n_x):
            for ci in range(CORES):
                for zi in range(n_z):
                    for yi in range(PAIR):
                        if not wrap and zi + dz >= n_z:
                            continue
                        to = place((xi + dx) % n_x, (ci + dc) % CORES, (zi + dz) % n_z, (yi + dy) % PAIR)
                        route.append((place(xi, ci, zi, yi), to))
        return lax.ppermute(array, both, route)

    info = jnp.stack([y, core]).astype(jnp.int32)
    rows = features.reshape(count, width)
    cot = cotangent.reshape(count, width)
    gain = norm_gain.reshape(1, dims)
    pin, ppool = pattern_in.reshape(-1), pattern_pool.reshape(-1)
    gates = gates_call(rows, gate_weight, decay_rate, beta_bias, span)
    each = heads // GROUPS

    locals_ = [local_call(info, pin, ppool, rows, weight_pool, gates, g * each, each, heads, span) for g in range(GROUPS)]
    maps = []
    for own, send, _, _ in locals_:
        got = moved(send, (0, 0, 0, 1))
        maps.append(combine_call(info, own, got))
    states = [jnp.zeros((each, dims, dims), F32)] * GROUPS
    for _ in range(n_z - 1):
        states = [moved(hop_call(maps[g][1], states[g]), (0, 0, 1, 0), wrap=False) for g in range(GROUPS)]
    mixes = []
    for g in range(GROUPS):
        keep, send = split_call(info, maps[g][0], states[g])
        got = moved(send, (0, 0, 0, 1))
        mixes.append(mix_call(info, locals_[g][2], locals_[g][3], keep, got, gain, cot, span))
    output, gain_part = finish_call([m[1] for m in mixes], [m[0] for m in mixes], out_weight, cot)
    scale = 1.0 / math.sqrt(count * n_shot * n_tm)
    gain_grad = jnp.sum(lax.all_gather(gain_part, both, axis=0, tiled=True), axis=0) * scale

    plane = [(dx, dy) for dx in range(n_x) for dy in range(PAIR)]
    n_plane = len(plane)
    share = each * dims // (CORES * n_plane * n_z)

    def plane_index(dx, dy):
        return ((x + dx) % n_x) * PAIR + (y + dy) % PAIR

    def picked(array, index):
        return lax.dynamic_index_in_dim(array, index, 0, keepdims=False)

    grads = []
    for g in range(GROUPS):
        _, _, w_send, w_keep = mixes[g]
        summed = w_keep + moved(w_send, (0, 1, 0, 0))
        summed = summed.reshape(n_plane, n_z, share, width)
        total = picked(summed, plane_index(0, 0))
        for dx, dy in plane[1:]:
            total = total + moved(picked(summed, plane_index(dx, dy)), (dx, 0, 0, dy))
        final = picked(total, z)
        for dz in range(1, n_z):
            final = final + moved(picked(total, (z + dz) % n_z), (0, 0, dz, 0))
        grads.append(final)
    pieces = []
    for g in range(GROUPS):
        along = jnp.zeros((n_z, share, width), F32)
        for dz in range(n_z):
            piece = grads[g] if dz == 0 else moved(grads[g], (0, 0, dz, 0))
            along = lax.dynamic_update_index_in_dim(along, piece, (z - dz) % n_z, 0)
        wide = jnp.zeros((n_plane, n_z, share, width), F32)
        for dx, dy in plane:
            piece = along if (dx, dy) == (0, 0) else moved(along, (dx, 0, 0, dy))
            wide = lax.dynamic_update_index_in_dim(wide, piece, plane_index(-dx, -dy), 0)
        other = moved(wide, (0, 1, 0, 0))
        first = jnp.where(core == 0, wide, other)
        second = jnp.where(core == 0, other, wide)
        pieces += [first.reshape(-1, width), second.reshape(-1, width)]
    weight_grad = (jnp.concatenate(pieces, axis=0) * scale).astype(BF16)
    return (output.reshape(seqs, span, width), weight_grad, gain_grad)


def solution(mesh):
    placed = (P("shot", "tm", None), P(), P(), P(), P(), P(), P(), P(), P(), P("shot", "tm", None))
    return jax.shard_map(
        functools.partial(shards, mesh),
        mesh=mesh,
        in_specs=placed,
        out_specs=(P("shot", "tm", None), P(), P()),
        check_vma=False,
    )
```

time: 874 us -> 331 us (0.38); the launches traced: 863 us -> 330 us
  other arithmetic: 343 us -> 9.45 us
  matrix products: 141 us -> 0 us
  waiting for transfers between devices: 217 us -> 115 us
  Pallas kernels: 0 us -> 71.9 us
  local copies, waits for them, and re-layouts: 61.4 us -> 24.5 us
  blocking collectives: 43.4 us -> 71.7 us
  between operations: 14.9 us -> 0.85 us
    another operation x4 -> x1, other arithmetic: 321 us -> 0.08 us  [shards(): info = jnp.stack([y, core]).astype(jnp.int32)]
    dot_general x40 -> x0, matrix products: 138 us -> none  [the longest x19 65 us: multiply(): return jnp.einsum('shcd,shde->shce', left, right, precision=FULL_PRECISION)]
    psum x1 -> x0, waiting for transfers between devices: 84.1 us -> none  [shards(): summed = lax.psum((weight_part, gain_part), ('shot', 'tm'))]
    pallas_call x0 -> x9, Pallas kernels: none -> 71.9 us  [the longest x1 53.1 us: local_call(): pl.pallas_call(functools.partial(local_kernel, first_head, heads, span),...]
    all_gather x0 -> x1, blocking collectives: none -> 71.7 us  [shards(): lax.all_gather(gain_part, both, axis=0, tiled=True)]
    psum x1 -> x0, blocking collectives: 43.4 us -> none  [shards(): summed = lax.psum((weight_part, gain_part), ('shot', 'tm'))]
    ppermute x7 -> x19, waiting for transfers between devices: 133 us -> 115 us  [moved(): return lax.ppermute(array, both, route)]
    gather x3 -> x0, local copies, waits for them, and re-layouts: 15.8 us -> none  [the longest x2 8.97 us: shards(): chosen = jnp.take(weight_pool, pattern_pool, axis=0)]
  transfers between devices with their start and end apart: 8 -> 19, of which waited for: 8 -> 15; matrix products, arithmetic and copies ran while one was open for 2% -> 3% of each run, Pallas kernels for 0% -> 1%
where the time goes in v1:
time: 331 us; the launch traced here: 330 us
  waiting for transfers between devices  115 us (35%)
  Pallas kernels  71.9 us (22%)
  blocking collectives  71.7 us (22%)
  starting transfers between devices  37 us (11%)
  local copies, waits for them, and re-layouts  24.5 us (7%)
  other arithmetic  9.45 us (3%)
    ppermute x19, waiting for transfers between devices, moved(): return lax.ppermute(array, both, route)  115 us
    all_gather x1, blocking collectives, shards(): lax.all_gather(gain_part, both, axis=0, tiled=True)  71.7 us
    pallas_call x1, Pallas kernels, local_call(): pl.pallas_call(functools.partial(local_kernel, first_head, heads, span),...  53.1 us
    ppermute x19, starting transfers between devices, moved(): return lax.ppermute(array, both, route)  37 us
    unnamed x27, local copies, waits for them, and re-layouts  13 us
    pallas_call x1, Pallas kernels, mix_call(): pl.pallas_call(functools.partial(mix_kernel, span), out_shape=(jax.ShapeD...  9.28 us
    dynamic_update_slice x4, local copies, waits for them, and re-layouts, shards(): lax.dynamic_update_index_in_dim(wide, piece, plane_index(-dx, -dy), 0)  6.64 us
  transfers between devices with their start and end apart: 19, of which 15 were waited for; matrix products, arithmetic and copies ran while one was open for 3% of the time, Pallas kernels for 1%

profile of v1, /device:TPU:0, one launch (start us, length us, event | category | flops | bytes accessed | tf_op | source)
XLA Modules:
  0.0 330.4 jit_solution(8233455169731174793)
XLA Ops:
  9.0 53.1 %local.1 = (f32[8,128,256]{2,1,0:T(8,128)S(1)}, f32[8,128,256]{2,1,0:T(8,128)S(1)}, f32[512,1024]{1,0:T(8,128)S(1)}, f32[512,1024]{1,0:T(8,128)S(1)}) custom-call(s32[2]{0:T(128)S(1)} %pad_add_fusion.info, s32[96]{0:T(128)S(1)} %reshape.39.pin, s32[96]{0:T(128)S(1)} %reshape.40.ppool, bf16[512,1024]{1,0:T(8,128)(2,1)S(1)} %bitcast.53, ...), custom_call_target="tpu_custom_call" | custom-call | flops 12884901888 | bytes 8388608 | tf_op jit(solution)/shard_map/local/pallas_call | solution.py:157
  62.1 3.0 collective-permute-start
  65.1 23.2 %collective-permute-done.got_ref = f32[8,128,256]{2,1,0:T(8,128)S(1)} collective-permute-done((f32[8,128,256]{2,1,0:T(8,128)S(1)}, f32[8,128,256]{2,1,0:T(8,128)S(1)}, u32[]{:S(2)}, u32[]{:S(2)}) %collective-permute-start) | collective-permute-done | bytes 1048608 | tf_op jit(solution)/shard_map/ppermute | solution.py:363
  90.0 3.7 %collective-permute-start.1 = (f32[8,128,128]{2,1,0:T(8,128)S(1)}, f32[8,128,128]{2,1,0:T(8,128)S(1)}, u32[]{:S(2)}, u32[]{:S(2)}) collective-permute-start(f32[8,128,128]{2,1,0:T(8,128)S(1)} %hop.3), channel_id=1, source_target_pairs={{0,2},{1,3},{2,4},{3,5},{4,6},{5,7},{8,10},{9,11},{10,12},{11,13},... | collective-permute-start | bytes 1572872 | tf_op jit(solution)/shard_map/ppermute | solution.py:363
  93.7 10.3 %collective-permute-done.1.state_ref = f32[8,128,128]{2,1,0:T(8,128)S(1)} collective-permute-done((f32[8,128,128]{2,1,0:T(8,128)S(1)}, f32[8,128,128]{2,1,0:T(8,128)S(1)}, u32[]{:S(2)}, u32[]{:S(2)}) %collective-permute-start.1) | collective-permute-done | bytes 524320 | tf_op jit(solution)/shard_map/ppermute | solution.py:363
  104.4 4.6 %collective-permute-start.2 = (f32[8,128,128]{2,1,0:T(8,128)S(1)}, f32[8,128,128]{2,1,0:T(8,128)S(1)}, u32[]{:S(2)}, u32[]{:S(2)}) collective-permute-start(f32[8,128,128]{2,1,0:T(8,128)S(1)} %hop.4), channel_id=1, source_target_pairs={{0,2},{1,3},{2,4},{3,5},{4,6},{5,7},{8,10},{9,11},{10,12},{11,13},... | collective-permute-start | bytes 1572872 | tf_op jit(solution)/shard_map/ppermute | solution.py:363
  109.0 9.3 %collective-permute-done.2.state_ref = f32[8,128,128]{2,1,0:T(8,128)S(1)} collective-permute-done((f32[8,128,128]{2,1,0:T(8,128)S(1)}, f32[8,128,128]{2,1,0:T(8,128)S(1)}, u32[]{:S(2)}, u32[]{:S(2)}) %collective-permute-start.2) | collective-permute-done | bytes 524320 | tf_op jit(solution)/shard_map/ppermute | solution.py:363
  118.7 4.4 %collective-permute-start.3 = (f32[8,128,128]{2,1,0:T(8,128)S(1)}, f32[8,128,128]{2,1,0:T(8,128)S(1)}, u32[]{:S(2)}, u32[]{:S(2)}) collective-permute-start(f32[8,128,128]{2,1,0:T(8,128)S(1)} %hop.5), channel_id=1, source_target_pairs={{0,2},{1,3},{2,4},{3,5},{4,6},{5,7},{8,10},{9,11},{10,12},{11,13},... | collective-permute-start | bytes 1572872 | tf_op jit(solution)/shard_map/ppermute | solution.py:363
  123.1 8.4 %collective-permute-done.3.state_ref = f32[8,128,128]{2,1,0:T(8,128)S(1)} collective-permute-done((f32[8,128,128]{2,1,0:T(8,128)S(1)}, f32[8,128,128]{2,1,0:T(8,128)S(1)}, u32[]{:S(2)}, u32[]{:S(2)}) %collective-permute-start.3) | collective-permute-done | bytes 524320 | tf_op jit(solution)/shard_map/ppermute | solution.py:363
  134.0 8.5 %collective-permute-done.4.got_ref = f32[8,128,128]{2,1,0:T(8,128)S(1)} collective-permute-done((f32[8,128,128]{2,1,0:T(8,128)S(1)}, f32[8,128,128]{2,1,0:T(8,128)S(1)}, u32[]{:S(2)}, u32[]{:S(2)}) %collective-permute-start.4) | collective-permute-done | bytes 524320 | tf_op jit(solution)/shard_map/ppermute | solution.py:363
  142.6 9.3 %mix.1 = (f32[512,1024]{1,0:T(8,128)S(1)}, bf16[512,1024]{1,0:T(8,128)(2,1)S(1)}, f32[4,128,1024]{2,1,0:T(8,128)}, f32[4,128,1024]{2,1,0:T(8,128)S(1)}) custom-call(s32[2]{0:T(128)S(1)} %pad_add_fusion.info, f32[512,1024]{1,0:T(8,128)S(1)} %get-tuple-element.17.core_ref, f32[512,1024]{1,0:T(8,128)S(1)} %get-tuple-element.18.query_ref, ...), custom_call_target="tpu_custom_call" | custom-call | flops 1073741824 | bytes 6291456 | tf_op jit(solution)/shard_map/mix/pallas_call | solution.py:277
  154.2 4.5 %collective-permute-done.5 = f32[4,128,1024]{2,1,0:T(8,128)} collective-permute-done((f32[4,128,1024]{2,1,0:T(8,128)}, f32[4,128,1024]{2,1,0:T(8,128)}, u32[]{:S(2)}, u32[]{:S(2)}) %collective-permute-start.5) | collective-permute-done | bytes 2097184 | tf_op jit(solution)/shard_map/ppermute | solution.py:363
  165.7 10.5 %collective-permute-done.6 = f32[4,32,1024]{2,1,0:T(8,128)S(1)} collective-permute-done((f32[4,32,1024]{2,1,0:T(8,128)S(1)}, f32[4,32,1024]{2,1,0:T(8,128)S(1)}, u32[]{:S(2)}, u32[]{:S(2)}) %collective-permute-start.6) | collective-permute-done | bytes 524320 | tf_op jit(solution)/shard_map/ppermute | solution.py:363
  176.1 2.4 collective-permute-done.7
  178.6 10.1 %collective-permute-done.8 = f32[4,32,1024]{2,1,0:T(8,128)} collective-permute-done((f32[4,32,1024]{2,1,0:T(8,128)S(1)}, f32[4,32,1024]{2,1,0:T(8,128)}, u32[]{:S(2)}, u32[]{:S(2)}) %collective-permute-start.8) | collective-permute-done | bytes 524320 | tf_op jit(solution)/shard_map/ppermute | solution.py:363
  190.2 3.6 %collective-permute-start.10 = (f32[32,1024]{1,0:T(8,128)S(1)}, f32[32,1024]{1,0:T(8,128)S(1)}, u32[]{:S(2)}, u32[]{:S(2)}) collective-permute-start(f32[32,1024]{1,0:T(8,128)S(1)} %get-tuple-element.40), channel_id=1, source_target_pairs={{0,4},{1,5},{2,6},{3,7},{4,0},{5,1},{6,2},{7,3},{8,12},{9,13},{10,... | collective-permute-start | bytes 393224 | tf_op jit(solution)/shard_map/ppermute | solution.py:363
  195.8 6.1 %collective-permute-done.10 = f32[32,1024]{1,0:T(8,128)S(1)} collective-permute-done((f32[32,1024]{1,0:T(8,128)S(1)}, f32[32,1024]{1,0:T(8,128)S(1)}, u32[]{:S(2)}, u32[]{:S(2)}) %collective-permute-start.10) | collective-permute-done | bytes 131104 | tf_op jit(solution)/shard_map/ppermute | solution.py:363
  209.0 2.9 collective-permute-start.14
  212.6 4.7 %collective-permute-done.13 = f32[32,1024]{1,0:T(8,128)S(1)} collective-permute-done((f32[32,1024]{1,0:T(8,128)S(1)}, f32[32,1024]{1,0:T(8,128)S(1)}, u32[]{:S(2)}, u32[]{:S(2)}) %collective-permute-start.13) | collective-permute-done | bytes 131104 | tf_op jit(solution)/shard_map/ppermute | solution.py:363
  225.7 7.1 %collective-permute-done.15 = f32[4,32,1024]{2,1,0:T(8,128)} collective-permute-done((f32[4,32,1024]{2,1,0:T(8,128)}, f32[4,32,1024]{2,1,0:T(8,128)}, u32[]{:S(2)}, u32[]{:S(2)}) %collective-permute-start.15) | collective-permute-done | bytes 524320 | tf_op jit(solution)/shard_map/ppermute | solution.py:363
  237.1 7.9 %collective-permute-done.17 = f32[4,32,1024]{2,1,0:T(8,128)S(1)} collective-permute-done((f32[4,32,1024]{2,1,0:T(8,128)}, f32[4,32,1024]{2,1,0:T(8,128)S(1)}, u32[]{:S(2)}, u32[]{:S(2)}) %collective-permute-start.17) | collective-permute-done | bytes 524320 | tf_op jit(solution)/shard_map/ppermute | solution.py:363
  248.7 4.7 %finish.1 = (bf16[512,1024]{1,0:T(8,128)(2,1)}, f32[8,128]{1,0:T(8,128)S(1)}) custom-call(bf16[512,1024]{1,0:T(8,128)(2,1)S(1)} %copy-done.10, f32[512,1024]{1,0:T(8,128)S(1)} %copy-done.8, bf16[1024,1024]{1,0:T(8,128)(2,1)S(1)} %copy-done.6, bf16[512,1024]{1,0:T(8,128)(2,1)S(1)} %bitcast.55), custom_call_target="tpu_custom_call" | custom-call | flops 2147483648 | bytes 7340032 | tf_op jit(solution)/shard_map/finish/pallas_call | solution.py:326
  253.4 71.7 %all_gather.3 = f32[256,128]{1,0:T(8,128)S(1)} all-gather(f32[8,128]{1,0:T(8,128)S(1)} %get-tuple-element.30), channel_id=1, replica_groups=mesh['shot'=4,'tm'=8] {'shot','tm'}, dimensions={0}, use_global_device_ids=true | all-gather | bytes 135168 | tf_op jit(solution)/shard_map/all_gather | solution.py:388
  325.7 2.7 broadcast_select_fusion.1
  (73 shorter events, 52.8 us)
Async XLA Ops:
  7.4 1.6 copy-start.5
  62.1 26.2 %collective-permute-start = (f32[8,128,256]{2,1,0:T(8,128)S(1)}, f32[8,128,256]{2,1,0:T(8,128)S(1)}, u32[]{:S(2)}, u32[]{:S(2)}) collective-permute-start(f32[8,128,256]{2,1,0:T(8,128)S(1)} %get-tuple-element.20), channel_id=1, source_target_pairs={{0,1},{1,0},{2,3},{3,2},{4,5},{5,4},{6,7},{7,6},{8,9},{9,8},{10,11... | collective-permute-start | bytes 3145736 | tf_op jit(solution)/shard_map/ppermute | solution.py:363
  90.0 14.0 %collective-permute-start.1 = (f32[8,128,128]{2,1,0:T(8,128)S(1)}, f32[8,128,128]{2,1,0:T(8,128)S(1)}, u32[]{:S(2)}, u32[]{:S(2)}) collective-permute-start(f32[8,128,128]{2,1,0:T(8,128)S(1)} %hop.3), channel_id=1, source_target_pairs={{0,2},{1,3},{2,4},{3,5},{4,6},{5,7},{8,10},{9,11},{10,12},{11,13},... | collective-permute-start | bytes 1572872 | tf_op jit(solution)/shard_map/ppermute | solution.py:363
  104.4 38.2 %copy-start.1 = (bf16[2,256,1024]{2,1,0:T(8,128)(2,1)S(1)}, bf16[2,256,1024]{2,1,0:T(8,128)(2,1)}, u32[]{:S(2)}) copy-start(bf16[2,256,1024]{2,1,0:T(8,128)(2,1)} %param.19) | copy-start | bytes 3145732
  104.4 38.2 %copy-start.4 = (f32[128]{0:T(128)S(1)}, f32[128]{0:T(128)}, u32[]{:S(2)}) copy-start(f32[128]{0:T(128)} %param.17) | copy-start | bytes 1540
  104.4 13.9 %collective-permute-start.2 = (f32[8,128,128]{2,1,0:T(8,128)S(1)}, f32[8,128,128]{2,1,0:T(8,128)S(1)}, u32[]{:S(2)}, u32[]{:S(2)}) collective-permute-start(f32[8,128,128]{2,1,0:T(8,128)S(1)} %hop.4), channel_id=1, source_target_pairs={{0,2},{1,3},{2,4},{3,5},{4,6},{5,7},{8,10},{9,11},{10,12},{11,13},... | collective-permute-start | bytes 1572872 | tf_op jit(solution)/shard_map/ppermute | solution.py:363
  118.7 12.8 %collective-permute-start.3 = (f32[8,128,128]{2,1,0:T(8,128)S(1)}, f32[8,128,128]{2,1,0:T(8,128)S(1)}, u32[]{:S(2)}, u32[]{:S(2)}) collective-permute-start(f32[8,128,128]{2,1,0:T(8,128)S(1)} %hop.5), channel_id=1, source_target_pairs={{0,2},{1,3},{2,4},{3,5},{4,6},{5,7},{8,10},{9,11},{10,12},{11,13},... | collective-permute-start | bytes 1572872 | tf_op jit(solution)/shard_map/ppermute | solution.py:363
  132.5 10.1 %collective-permute-start.4 = (f32[8,128,128]{2,1,0:T(8,128)S(1)}, f32[8,128,128]{2,1,0:T(8,128)S(1)}, u32[]{:S(2)}, u32[]{:S(2)}) collective-permute-start(f32[8,128,128]{2,1,0:T(8,128)S(1)} %get-tuple-element.24), channel_id=1, source_target_pairs={{0,1},{1,0},{2,3},{3,2},{4,5},{5,4},{6,7},{7,6},{8,9},{9,8},{10,11... | collective-permute-start | bytes 1572872 | tf_op jit(solution)/shard_map/ppermute | solution.py:363
  154.2 4.5 %collective-permute-start.5 = (f32[4,128,1024]{2,1,0:T(8,128)}, f32[4,128,1024]{2,1,0:T(8,128)}, u32[]{:S(2)}, u32[]{:S(2)}) collective-permute-start(f32[4,128,1024]{2,1,0:T(8,128)} %get-tuple-element.29), channel_id=1, source_target_pairs={{0,8},{1,9},{2,10},{3,11},{4,12},{5,13},{6,14},{7,15},{8,0},{9,1},... | collective-permute-start | bytes 6291464 | tf_op jit(solution)/shard_map/ppermute | solution.py:363
  162.1 14.0 %collective-permute-start.6 = (f32[4,32,1024]{2,1,0:T(8,128)S(1)}, f32[4,32,1024]{2,1,0:T(8,128)S(1)}, u32[]{:S(2)}, u32[]{:S(2)}) collective-permute-start(f32[4,32,1024]{2,1,0:T(8,128)S(1)} %get-tuple-element.35), channel_id=1, source_target_pairs={{0,1},{1,0},{2,3},{3,2},{4,5},{5,4},{6,7},{7,6},{8,9},{9,8},{10,11... | collective-permute-start | bytes 1572872 | tf_op jit(solution)/shard_map/ppermute | solution.py:363
  163.7 14.9 %collective-permute-start.7 = (f32[4,32,1024]{2,1,0:T(8,128)S(1)}, f32[4,32,1024]{2,1,0:T(8,128)}, u32[]{:S(2)}, u32[]{:S(2)}) collective-permute-start(f32[4,32,1024]{2,1,0:T(8,128)S(1)} %get-tuple-element.37), channel_id=1, source_target_pairs={{0,16},{1,17},{2,18},{3,19},{4,20},{5,21},{6,22},{7,23},{8,24},{9,... | collective-permute-start | bytes 1572872 | tf_op jit(solution)/shard_map/ppermute | solution.py:363
  165.2 23.5 %collective-permute-start.8 = (f32[4,32,1024]{2,1,0:T(8,128)S(1)}, f32[4,32,1024]{2,1,0:T(8,128)}, u32[]{:S(2)}, u32[]{:S(2)}) collective-permute-start(f32[4,32,1024]{2,1,0:T(8,128)S(1)} %get-tuple-element.36), channel_id=1, source_target_pairs={{0,17},{1,16},{2,19},{3,18},{4,21},{5,20},{6,23},{7,22},{8,25},{9,... | collective-permute-start | bytes 1572872 | tf_op jit(solution)/shard_map/ppermute | solution.py:363
  190.2 11.7 %collective-permute-start.10 = (f32[32,1024]{1,0:T(8,128)S(1)}, f32[32,1024]{1,0:T(8,128)S(1)}, u32[]{:S(2)}, u32[]{:S(2)}) collective-permute-start(f32[32,1024]{1,0:T(8,128)S(1)} %get-tuple-element.40), channel_id=1, source_target_pairs={{0,4},{1,5},{2,6},{3,7},{4,0},{5,1},{6,2},{7,3},{8,12},{9,13},{10,... | collective-permute-start | bytes 393224 | tf_op jit(solution)/shard_map/ppermute | solution.py:363
  193.8 8.1 %collective-permute-start.11 = (f32[32,1024]{1,0:T(8,128)S(1)}, f32[32,1024]{1,0:T(8,128)S(1)}, u32[]{:S(2)}, u32[]{:S(2)}) collective-permute-start(f32[32,1024]{1,0:T(8,128)S(1)} %get-tuple-element.39), channel_id=1, source_target_pairs={{0,6},{1,7},{2,0},{3,1},{4,2},{5,3},{6,4},{7,5},{8,14},{9,15},{10,... | collective-permute-start | bytes 393224 | tf_op jit(solution)/shard_map/ppermute | solution.py:363
  195.1 8.2 %collective-permute-start.9 = (f32[32,1024]{1,0:T(8,128)S(1)}, f32[32,1024]{1,0:T(8,128)S(1)}, u32[]{:S(2)}, u32[]{:S(2)}) collective-permute-start(f32[32,1024]{1,0:T(8,128)S(1)} %get-tuple-element.38), channel_id=1, source_target_pairs={{0,2},{1,3},{2,4},{3,5},{4,6},{5,7},{6,0},{7,1},{8,10},{9,11},{10,... | collective-permute-start | bytes 393224 | tf_op jit(solution)/shard_map/ppermute | solution.py:363
  204.8 7.1 %collective-permute-start.12 = (f32[32,1024]{1,0:T(8,128)S(1)}, f32[32,1024]{1,0:T(8,128)S(1)}, u32[]{:S(2)}, u32[]{:S(2)}) collective-permute-start(f32[32,1024]{1,0:T(8,128)S(1)} %get-tuple-element.32), channel_id=1, source_target_pairs={{0,2},{1,3},{2,4},{3,5},{4,6},{5,7},{6,0},{7,1},{8,10},{9,11},{10,... | collective-permute-start | bytes 393224 | tf_op jit(solution)/shard_map/ppermute | solution.py:363
  207.1 10.2 %collective-permute-start.13 = (f32[32,1024]{1,0:T(8,128)S(1)}, f32[32,1024]{1,0:T(8,128)S(1)}, u32[]{:S(2)}, u32[]{:S(2)}) collective-permute-start(f32[32,1024]{1,0:T(8,128)S(1)} %get-tuple-element.32), channel_id=1, source_target_pairs={{0,4},{1,5},{2,6},{3,7},{4,0},{5,1},{6,2},{7,3},{8,12},{9,13},{10,... | collective-permute-start | bytes 393224 | tf_op jit(solution)/shard_map/ppermute | solution.py:363
  209.0 8.9 %collective-permute-start.14 = (f32[32,1024]{1,0:T(8,128)S(1)}, f32[32,1024]{1,0:T(8,128)S(1)}, u32[]{:S(2)}, u32[]{:S(2)}) collective-permute-start(f32[32,1024]{1,0:T(8,128)S(1)} %get-tuple-element.32), channel_id=1, source_target_pairs={{0,6},{1,7},{2,0},{3,1},{4,2},{5,3},{6,4},{7,5},{8,14},{9,15},{10,... | collective-permute-start | bytes 393224 | tf_op jit(solution)/shard_map/ppermute | solution.py:363
  218.6 14.2 %collective-permute-start.15 = (f32[4,32,1024]{2,1,0:T(8,128)}, f32[4,32,1024]{2,1,0:T(8,128)}, u32[]{:S(2)}, u32[]{:S(2)}) collective-permute-start(f32[4,32,1024]{2,1,0:T(8,128)} %bitcast_dynamic-update-slice_fusion.4), channel_id=1, source_target_pairs={{0,1},{1,0},{2,3},{3,2},{4,5},{5,4},{6,7},{7,6},{8,9},{9,8},{10,11... | collective-permute-start | bytes 1572872 | tf_op jit(solution)/shard_map/ppermute | solution.py:363
  220.1 15.2 %collective-permute-start.16 = (f32[4,32,1024]{2,1,0:T(8,128)}, f32[4,32,1024]{2,1,0:T(8,128)}, u32[]{:S(2)}, u32[]{:S(2)}) collective-permute-start(f32[4,32,1024]{2,1,0:T(8,128)} %bitcast_dynamic-update-slice_fusion.4), channel_id=1, source_target_pairs={{0,16},{1,17},{2,18},{3,19},{4,20},{5,21},{6,22},{7,23},{8,24},{9,... | collective-permute-start | bytes 1572872 | tf_op jit(solution)/shard_map/ppermute | solution.py:363
  221.7 23.4 %collective-permute-start.17 = (f32[4,32,1024]{2,1,0:T(8,128)}, f32[4,32,1024]{2,1,0:T(8,128)S(1)}, u32[]{:S(2)}, u32[]{:S(2)}) collective-permute-start(f32[4,32,1024]{2,1,0:T(8,128)} %bitcast_dynamic-update-slice_fusion.4), channel_id=1, source_target_pairs={{0,17},{1,16},{2,19},{3,18},{4,21},{5,20},{6,23},{7,22},{8,25},{9,... | collective-permute-start | bytes 1572872 | tf_op jit(solution)/shard_map/ppermute | solution.py:363
  223.7 22.2 %copy-start.6 = (bf16[1024,1024]{1,0:T(8,128)(2,1)S(1)}, bf16[1024,1024]{1,0:T(8,128)(2,1)}, u32[]{:S(2)}) copy-start(bf16[1024,1024]{1,0:T(8,128)(2,1)} %refs_2_.1) | copy-start | bytes 6291460
  245.8 79.9 %collective-permute-start.18 = (f32[4,4,32,1024]{3,2,1,0:T(8,128)}, f32[4,4,32,1024]{3,2,1,0:T(8,128)}, u32[]{:S(2)}, u32[]{:S(2)}) collective-permute-start(f32[4,4,32,1024]{3,2,1,0:T(8,128)} %bitcast_dynamic-update-slice_fusion), channel_id=1, source_target_pairs={{0,8},{1,9},{2,10},{3,11},{4,12},{5,13},{6,14},{7,15},{8,0},{9,1},... | collective-permute-start | bytes 6291464 | tf_op jit(solution)/shard_map/ppermute | solution.py:363
  245.9 1.6 copy-start.8
  (7 other events, 7.4 us)

commit v2 on v1

--- a/solution.py
+++ b/solution.py
@@ -8,9 +8,10 @@
 from jax.experimental.pallas import tpu as pltpu
 from jax.sharding import PartitionSpec as P
 
-GROUPS = 1
+GROUPS = 2
 CORES = 2
 PAIR = 2
+PER_STEP = 2
 F32 = jnp.float32
 BF16 = jnp.bfloat16
 VMEM_LIMIT = 40 * 1024 * 1024
@@ -80,28 +81,28 @@
     )(rows, gate_weight, decay_rate.reshape(1, heads), beta_bias.reshape(1, heads))
 
 
-def inverse_times(system, right):
-    span = system.shape[0]
+def solve_lower(systems, rights):
+    span = systems[0].shape[0]
     row = lax.broadcasted_iota(jnp.int32, (span, span), 0)
     col = lax.broadcasted_iota(jnp.int32, (span, span), 1)
     apart = row ^ col
-    inv = jnp.where(row == col, 1.0, jnp.where(apart == 1, -system, 0.0)).astype(BF16)
+    invs = [jnp.where(row == col, 1.0, jnp.where(apart == 1, -s, 0.0)).astype(BF16) for s in systems]
     step = 2
     while step < span:
-        band = jnp.where((apart >= step) & (apart < 2 * step), system, 0.0).astype(BF16)
-        inner = dot(inv, band).astype(BF16)
-        inv = inv - dot(inner, inv).astype(BF16)
+        keep = (apart >= step) & (apart < 2 * step)
+        bands = [jnp.where(keep, s, 0.0).astype(BF16) for s in systems]
+        inners = [dot(i, b).astype(BF16) for i, b in zip(invs, bands)]
+        invs = [i - dot(n, i).astype(BF16) for n, i in zip(inners, invs)]
         step *= 2
-    rounded = right.astype(BF16)
-    first = dot(inv, rounded) + (right - rounded.astype(F32))
-    residual = (right - first) - dot3(system, first)
-    return first + dot(inv, residual.astype(BF16))
+    rounded = [r.astype(BF16) for r in rights]
+    firsts = [dot(i, b) + (r - b.astype(F32)) for i, b, r in zip(invs, rounded, rights)]
+    residuals = [(r - f) - dot3(s, f) for r, f, s in zip(rights, firsts, systems)]
+    return [f + dot(i, r.astype(BF16)) for f, i, r in zip(firsts, invs, residuals)]
 
 
 def local_kernel(
-    first_head, heads, span, info, pin, ppool, x_ref, pool_ref, gate_ref, own_ref, send_ref, core_ref, query_ref
+    first_head, heads, span, per_step, info, pin, ppool, x_ref, pool_ref, gate_ref, own_ref, send_ref, core_ref, query_ref
 ):
-    head = first_head + pl.program_id(0)
     members = pin.shape[0] // (3 * heads)
     dims = pool_ref.shape[1]
     lane = lax.broadcasted_iota(jnp.int32, (span, 2 * heads), 1)
@@ -111,18 +112,28 @@
     eye = (
         lax.broadcasted_iota(jnp.int32, (dims, dims), 0) == lax.broadcasted_iota(jnp.int32, (dims, dims), 1)
     ).astype(F32)
-    for part in range(2):
-        seq = info[0] if part == 0 else 1 - info[0]
-        rows = pl.ds(pl.multiple_of(seq * span, span), span)
-        projected = []
+    where = []
+    heads_in = []
+    for local in range(per_step):
+        head = first_head + pl.program_id(0) * per_step + local
+        chosen = []
         for kind in range(3):
             target = (kind * heads + head) * members
-            picked = [
-                x_ref[rows, pl.ds(pl.multiple_of(pin[target + j] * dims, dims), dims)] for j in range(members)
-            ]
-            chosen = [pool_ref[ppool[target + j]] for j in range(members)]
-            projected.append(dot(jnp.concatenate(picked, 1), jnp.concatenate(chosen, 0)).astype(BF16))
-        query, key, value = projected
+            chosen.append(jnp.concatenate([pool_ref[ppool[target + j]] for j in range(members)], 0))
+        for part in range(2):
+            seq = info[0] if part == 0 else 1 - info[0]
+            where.append((local, part, pl.ds(pl.multiple_of(seq * span, span), span)))
+            projected = []
+            for kind in range(3):
+                target = (kind * heads + head) * members
+                picked = [
+                    x_ref[where[-1][2], pl.ds(pl.multiple_of(pin[target + j] * dims, dims), dims)]
+                    for j in range(members)
+                ]
+                projected.append(dot(jnp.concatenate(picked, 1), chosen[kind]).astype(BF16))
+            heads_in.append((head, projected))
+    kept, systems, rights = [], [], []
+    for (local, part, rows), (head, (query, key, value)) in zip(where, heads_in):
         key_wide = key.astype(F32)
         gates = gate_ref[rows, :]
         cumulative = jnp.sum(jnp.where(lane == head, gates, 0.0), axis=1, keepdims=True)
@@ -132,19 +143,22 @@
         cumulative_row, norm_row = across[0:1, :], across[1:2, :]
         ratio = jnp.where(row >= col, jnp.exp(jnp.minimum(cumulative - cumulative_row, 0.0)), 0.0) * norm_row
         attend = ratio * dot_nt(query, key)
-        system = jnp.where(row > col, ratio * dot_nt(key, key), 0.0) * (beta * norm)
+        systems.append(jnp.where(row > col, ratio * dot_nt(key, key), 0.0) * (beta * norm))
         growth = jnp.exp(cumulative)
-        right = jnp.concatenate([(beta * growth * norm) * key_wide, beta * value.astype(F32)], axis=1)
-        solved = inverse_times(system, right)
+        rights.append(jnp.concatenate([(beta * growth * norm) * key_wide, beta * value.astype(F32)], axis=1))
         last = cumulative[span - 1 : span, :]
-        high, low = halves(solved * (norm * jnp.exp(last - cumulative)))
+        kept.append((query, key, attend, growth, norm * jnp.exp(last - cumulative), jnp.exp(last)))
+    solutions = solve_lower(systems, rights)
+    for (local, part, rows), (query, key, attend, growth, tail, final), solved in zip(where, kept, solutions):
+        high, low = halves(solved * tail)
         pushed = dot_tn(key, high) + dot_tn(key, low)
         out = own_ref if part == 0 else send_ref
-        out[0, :, :dims] = jnp.exp(last) * eye - pushed[:, :dims]
-        out[0, :, dims:] = pushed[:, dims:]
+        out[local, :, :dims] = final * eye - pushed[:, :dims]
+        out[local, :, dims:] = pushed[:, dims:]
         seen = dot3(attend, solved)
-        query_ref[rows, :] = growth * query.astype(F32) - seen[:, :dims]
-        core_ref[rows, :] = seen[:, dims:]
+        lanes = slice(local * dims, (local + 1) * dims)
+        query_ref[rows, lanes] = growth * query.astype(F32) - seen[:, :dims]
+        core_ref[rows, lanes] = seen[:, dims:]
 
 
 def local_call(info, pin, ppool, rows, pool, gates, first_head, count_heads, heads, span):
@@ -152,14 +166,14 @@
     dims = pool.shape[1]
     maps = jax.ShapeDtypeStruct((count_heads, dims, 2 * dims), F32)
     wide = jax.ShapeDtypeStruct((count, count_heads * dims), F32)
-    map_spec = pl.BlockSpec((1, dims, 2 * dims), lambda i, *_: (i, 0, 0))
-    row_spec = pl.BlockSpec((count, dims), lambda i, *_: (0, i))
-    return pl.pallas_call(
-        functools.partial(local_kernel, first_head, heads, span),
+    map_spec = pl.BlockSpec((PER_STEP, dims, 2 * dims), lambda i, *_: (i, 0, 0))
+    row_spec = pl.BlockSpec((count, PER_STEP * dims), lambda i, *_: (0, i))
+    return pl.pallas_call(
+        functools.partial(local_kernel, first_head, heads, span, PER_STEP),
         out_shape=(maps, maps, wide, wide),
         grid_spec=pltpu.PrefetchScalarGridSpec(
             num_scalar_prefetch=3,
-            grid=(count_heads,),
+            grid=(count_heads // PER_STEP,),
             in_specs=[whole(rows.shape), whole(pool.shape), whole(gates.shape)],
             out_specs=(map_spec, map_spec, row_spec, row_spec),
         ),
@@ -385,7 +399,14 @@
         mixes.append(mix_call(info, locals_[g][2], locals_[g][3], keep, got, gain, cot, span))
     output, gain_part = finish_call([m[1] for m in mixes], [m[0] for m in mixes], out_weight, cot)
     scale = 1.0 / math.sqrt(count * n_shot * n_tm)
-    gain_grad = jnp.sum(lax.all_gather(gain_part, both, axis=0, tiled=True), axis=0) * scale
+    swaps = [(axis, 1 << bit) for axis, size in (("shot", n_shot), ("tm", n_tm)) for bit in range(size.bit_length() - 1)]
+    per_stage = -(-len(swaps) // 5)
+
+    def spread(value, part, stage):
+        for axis, reach in swaps[stage * per_stage : (stage + 1) * per_stage]:
+            size = lax.axis_size(axis)
+            part = part + lax.ppermute(part, axis, [(i, i ^ reach) for i in range(size)])
+        return lax.optimization_barrier((value, part))
 
     plane = [(dx, dy) for dx in range(n_x) for dy in range(PAIR)]
     n_plane = len(plane)
@@ -397,17 +418,21 @@
     def picked(array, index):
         return lax.dynamic_index_in_dim(array, index, 0, keepdims=False)
 
+    crossed = [moved(mixes[g][2], (0, 1, 0, 0)) for g in range(GROUPS)]
+    crossed[-1], gain_part, output = lax.optimization_barrier((crossed[-1], gain_part, output))
     grads = []
     for g in range(GROUPS):
-        _, _, w_send, w_keep = mixes[g]
-        summed = w_keep + moved(w_send, (0, 1, 0, 0))
-        summed = summed.reshape(n_plane, n_z, share, width)
+        summed = (mixes[g][3] + crossed[g]).reshape(n_plane, n_z, share, width)
         total = picked(summed, plane_index(0, 0))
         for dx, dy in plane[1:]:
             total = total + moved(picked(summed, plane_index(dx, dy)), (dx, 0, 0, dy))
+        if g == GROUPS - 1:
+            total, gain_part = spread(total, gain_part, 0)
         final = picked(total, z)
         for dz in range(1, n_z):
             final = final + moved(picked(total, (z + dz) % n_z), (0, 0, dz, 0))
+        if g == GROUPS - 1:
+            final, gain_part = spread(final, gain_part, 1)
         grads.append(final)
     pieces = []
     for g in range(GROUPS):
@@ -415,14 +440,21 @@
         for dz in range(n_z):
             piece = grads[g] if dz == 0 else moved(grads[g], (0, 0, dz, 0))
             along = lax.dynamic_update_index_in_dim(along, piece, (z - dz) % n_z, 0)
+        if g == GROUPS - 1:
+            along, gain_part = spread(along, gain_part, 2)
         wide = jnp.zeros((n_plane, n_z, share, width), F32)
         for dx, dy in plane:
             piece = along if (dx, dy) == (0, 0) else moved(along, (dx, 0, 0, dy))
             wide = lax.dynamic_update_index_in_dim(wide, piece, plane_index(-dx, -dy), 0)
+        if g == GROUPS - 1:
+            wide, gain_part = spread(wide, gain_part, 3)
         other = moved(wide, (0, 1, 0, 0))
+        if g == GROUPS - 1:
+            other, gain_part = spread(other, gain_part, 4)
         first = jnp.where(core == 0, wide, other)
         second = jnp.where(core == 0, other, wide)
         pieces += [first.reshape(-1, width), second.reshape(-1, width)]
+    gain_grad = jnp.sum(gain_part, axis=0) * scale
     weight_grad = (jnp.concatenate(pieces, axis=0) * scale).astype(BF16)
     return (output.reshape(seqs, span, width), weight_grad, gain_grad)
 

time: 331 us -> 191 us (0.58)
  blocking collectives: 71.7 us -> 0 us
  waiting for transfers between devices: 115 us -> 50.6 us
  starting transfers between devices: 37 us -> 69.4 us
  Pallas kernels: 71.9 us -> 44 us
  local copies, waits for them, and re-layouts: 24.5 us -> 17 us
    all_gather x1 -> x0, blocking collectives: 71.7 us -> none  [shards(): lax.all_gather(gain_part, both, axis=0, tiled=True)]
    ppermute x19 -> x38, waiting for transfers between devices: 115 us -> 44.4 us  [moved(): return lax.ppermute(array, both, route)]
    pallas_call x1 -> x2, Pallas kernels: 53.1 us -> 22.1 us  [local_call(): pl.pallas_call(functools.partial(local_kernel, first_head, heads, span, P...]
    ppermute x19 -> x38, starting transfers between devices: 37 us -> 63.7 us  [moved(): return lax.ppermute(array, both, route)]
    dynamic_update_slice x4 -> x8, local copies, waits for them, and re-layouts: 6.64 us -> 0.18 us  [shards(): lax.dynamic_update_index_in_dim(wide, piece, plane_index(-dx, -dy), 0)]
    ppermute x0 -> x5, waiting for transfers between devices: none -> 6.13 us  [spread(): lax.ppermute(part, axis, [(i, i ^ reach) for i in range(size)])]
    ppermute x0 -> x5, starting transfers between devices: none -> 5.66 us  [spread(): lax.ppermute(part, axis, [(i, i ^ reach) for i in range(size)])]
    unnamed x27 -> x35, local copies, waits for them, and re-layouts: 13 us -> 15.3 us
  transfers between devices with their start and end apart: 19 -> 43, of which waited for: 15 -> 20; matrix products, arithmetic and copies ran while one was open for 3% -> 3% of each run, Pallas kernels for 1% -> 17%
where the time goes in v2:
time: 191 us; the launch traced here: 190 us
  starting transfers between devices  69.4 us (36%)
  waiting for transfers between devices  50.6 us (26%)
  Pallas kernels  44 us (23%)
  local copies, waits for them, and re-layouts  17 us (9%)
  other arithmetic  8.09 us (4%)
    ppermute x38, starting transfers between devices, moved(): return lax.ppermute(array, both, route)  63.7 us
    ppermute x38, waiting for transfers between devices, moved(): return lax.ppermute(array, both, route)  44.4 us
    pallas_call x2, Pallas kernels, local_call(): pl.pallas_call(functools.partial(local_kernel, first_head, heads, span, P...  22.1 us
    unnamed x35, local copies, waits for them, and re-layouts  15.3 us
    pallas_call x2, Pallas kernels, mix_call(): pl.pallas_call(functools.partial(mix_kernel, span), out_shape=(jax.ShapeD...  10.4 us
    ppermute x5, waiting for transfers between devices, spread(): lax.ppermute(part, axis, [(i, i ^ reach) for i in range(size)])  6.13 us
    ppermute x5, starting transfers between devices, spread(): lax.ppermute(part, axis, [(i, i ^ reach) for i in range(size)])  5.66 us
    pallas_call x1, Pallas kernels, finish_call(): pl.pallas_call(functools.partial(finish_kernel, groups), out_shape=(jax.S...  4.72 us
  transfers between devices with their start and end apart: 43, of which 20 were waited for; matrix products, arithmetic and copies ran while one was open for 3% of the time, Pallas kernels for 17%

profile of v2, /device:TPU:0, one launch (start us, length us, event | category | flops | bytes accessed | tf_op | source)
XLA Modules:
  0.0 190.3 jit_solution(12201085472906613165)
XLA Ops:
  9.0 11.0 %local.2 = (f32[4,128,256]{2,1,0:T(8,128)S(1)}, f32[4,128,256]{2,1,0:T(8,128)S(1)}, f32[512,512]{1,0:T(8,128)S(1)}, f32[512,512]{1,0:T(8,128)S(1)}) custom-call(s32[2]{0:T(128)S(1)} %pad_add_fusion.info, s32[96]{0:T(128)S(1)} %reshape.48.pin, s32[96]{0:T(128)S(1)} %reshape.49.ppool, bf16[512,1024]{1,0:T(8,128)(2,1)S(1)} %bitcast.99, ...), custom_call_target="tpu_custom_call" | custom-call | flops 6442450944 | bytes 8388608 | tf_op jit(solution)/shard_map/local/pallas_call | solution.py:171
  20.1 3.0 %collective-permute-start = (f32[4,128,256]{2,1,0:T(8,128)S(1)}, f32[4,128,256]{2,1,0:T(8,128)S(1)}, u32[]{:S(2)}, u32[]{:S(2)}) collective-permute-start(f32[4,128,256]{2,1,0:T(8,128)S(1)} %get-tuple-element.45), channel_id=1, source_target_pairs={{0,1},{1,0},{2,3},{3,2},{4,5},{5,4},{6,7},{7,6},{8,9},{9,8},{10,11... | collective-permute-start | bytes 1572872 | tf_op jit(solution)/shard_map/ppermute | solution.py:377
  23.1 11.1 %local.3 = (f32[4,128,256]{2,1,0:T(8,128)S(1)}, f32[4,128,256]{2,1,0:T(8,128)S(1)}, f32[512,512]{1,0:T(8,128)S(1)}, f32[512,512]{1,0:T(8,128)S(1)}) custom-call(s32[2]{0:T(128)S(1)} %pad_add_fusion.info, s32[96]{0:T(128)S(1)} %reshape.48.pin, s32[96]{0:T(128)S(1)} %reshape.49.ppool, bf16[512,1024]{1,0:T(8,128)(2,1)S(1)} %bitcast.100, ...), custom_call_target="tpu_custom_call" | custom-call | flops 6442450944 | bytes 8388608 | tf_op jit(solution)/shard_map/local/pallas_call | solution.py:171
  36.3 3.7 %collective-permute-start.1 = (f32[4,128,128]{2,1,0:T(8,128)S(1)}, f32[4,128,128]{2,1,0:T(8,128)S(1)}, u32[]{:S(2)}, u32[]{:S(2)}) collective-permute-start(f32[4,128,128]{2,1,0:T(8,128)S(1)} %hop.6), channel_id=1, source_target_pairs={{0,2},{1,3},{2,4},{3,5},{4,6},{5,7},{8,10},{9,11},{10,12},{11,13},... | collective-permute-start | bytes 786440 | tf_op jit(solution)/shard_map/ppermute | solution.py:377
  40.1 7.6 %collective-permute-done.6.got_ref = f32[4,128,256]{2,1,0:T(8,128)S(1)} collective-permute-done((f32[4,128,256]{2,1,0:T(8,128)S(1)}, f32[4,128,256]{2,1,0:T(8,128)S(1)}, u32[]{:S(2)}, u32[]{:S(2)}) %collective-permute-start.6) | collective-permute-done | bytes 524320 | tf_op jit(solution)/shard_map/ppermute | solution.py:377
  48.9 3.5 %collective-permute-start.7 = (f32[4,128,128]{2,1,0:T(8,128)S(1)}, f32[4,128,128]{2,1,0:T(8,128)S(1)}, u32[]{:S(2)}, u32[]{:S(2)}) collective-permute-start(f32[4,128,128]{2,1,0:T(8,128)S(1)} %hop.9), channel_id=1, source_target_pairs={{0,2},{1,3},{2,4},{3,5},{4,6},{5,7},{8,10},{9,11},{10,12},{11,13},... | collective-permute-start | bytes 786440 | tf_op jit(solution)/shard_map/ppermute | solution.py:377
  52.7 3.7 %collective-permute-start.2 = (f32[4,128,128]{2,1,0:T(8,128)S(1)}, f32[4,128,128]{2,1,0:T(8,128)S(1)}, u32[]{:S(2)}, u32[]{:S(2)}) collective-permute-start(f32[4,128,128]{2,1,0:T(8,128)S(1)} %hop.7), channel_id=1, source_target_pairs={{0,2},{1,3},{2,4},{3,5},{4,6},{5,7},{8,10},{9,11},{10,12},{11,13},... | collective-permute-start | bytes 786440 | tf_op jit(solution)/shard_map/ppermute | solution.py:377
  56.4 2.5 %collective-permute-done.7.state_ref = f32[4,128,128]{2,1,0:T(8,128)S(1)} collective-permute-done((f32[4,128,128]{2,1,0:T(8,128)S(1)}, f32[4,128,128]{2,1,0:T(8,128)S(1)}, u32[]{:S(2)}, u32[]{:S(2)}) %collective-permute-start.7) | collective-permute-done | bytes 262176 | tf_op jit(solution)/shard_map/ppermute | solution.py:377
  59.1 4.5 %collective-permute-start.8 = (f32[4,128,128]{2,1,0:T(8,128)S(1)}, f32[4,128,128]{2,1,0:T(8,128)S(1)}, u32[]{:S(2)}, u32[]{:S(2)}) collective-permute-start(f32[4,128,128]{2,1,0:T(8,128)S(1)} %hop.10), channel_id=1, source_target_pairs={{0,2},{1,3},{2,4},{3,5},{4,6},{5,7},{8,10},{9,11},{10,12},{11,13},... | collective-permute-start | bytes 786440 | tf_op jit(solution)/shard_map/ppermute | solution.py:377
  64.7 4.4 %collective-permute-start.3 = (f32[4,128,128]{2,1,0:T(8,128)S(1)}, f32[4,128,128]{2,1,0:T(8,128)S(1)}, u32[]{:S(2)}, u32[]{:S(2)}) collective-permute-start(f32[4,128,128]{2,1,0:T(8,128)S(1)} %hop.8), channel_id=1, source_target_pairs={{0,2},{1,3},{2,4},{3,5},{4,6},{5,7},{8,10},{9,11},{10,12},{11,13},... | collective-permute-start | bytes 786440 | tf_op jit(solution)/shard_map/ppermute | solution.py:377
  70.7 4.4 %collective-permute-start.9 = (f32[4,128,128]{2,1,0:T(8,128)S(1)}, f32[4,128,128]{2,1,0:T(8,128)S(1)}, u32[]{:S(2)}, u32[]{:S(2)}) collective-permute-start(f32[4,128,128]{2,1,0:T(8,128)S(1)} %hop.11), channel_id=1, source_target_pairs={{0,2},{1,3},{2,4},{3,5},{4,6},{5,7},{8,10},{9,11},{10,12},{11,13},... | collective-permute-start | bytes 786440 | tf_op jit(solution)/shard_map/ppermute | solution.py:377
  80.6 5.0 %collective-permute-done.4.got_ref = f32[4,128,128]{2,1,0:T(8,128)S(1)} collective-permute-done((f32[4,128,128]{2,1,0:T(8,128)S(1)}, f32[4,128,128]{2,1,0:T(8,128)S(1)}, u32[]{:S(2)}, u32[]{:S(2)}) %collective-permute-start.4) | collective-permute-done | bytes 262176 | tf_op jit(solution)/shard_map/ppermute | solution.py:377
  85.6 5.2 %mix.2 = (f32[512,512]{1,0:T(8,128)S(1)}, bf16[512,512]{1,0:T(8,128)(2,1)S(1)}, f32[2,128,1024]{2,1,0:T(8,128)}, f32[2,128,1024]{2,1,0:T(8,128)S(1)}) custom-call(s32[2]{0:T(128)S(1)} %pad_add_fusion.info, f32[512,512]{1,0:T(8,128)S(1)} %get-tuple-element.42.core_ref, f32[512,512]{1,0:T(8,128)S(1)} %get-tuple-element.43.query_ref, ...), custom_call_target="tpu_custom_call" | custom-call | flops 536870912 | bytes 6291456 | tf_op jit(solution)/shard_map/mix/pallas_call | solution.py:291
  91.7 5.2 %mix.3 = (f32[512,512]{1,0:T(8,128)S(1)}, bf16[512,512]{1,0:T(8,128)(2,1)S(1)}, f32[2,128,1024]{2,1,0:T(8,128)}, f32[2,128,1024]{2,1,0:T(8,128)S(1)}) custom-call(s32[2]{0:T(128)S(1)} %pad_add_fusion.info, f32[512,512]{1,0:T(8,128)S(1)} %get-tuple-element.51.core_ref, f32[512,512]{1,0:T(8,128)S(1)} %get-tuple-element.52.query_ref, ...), custom_call_target="tpu_custom_call" | custom-call | flops 536870912 | bytes 6291456 | tf_op jit(solution)/shard_map/mix/pallas_call | solution.py:291
  105.3 4.7 %finish.1 = (bf16[512,1024]{1,0:T(8,128)(2,1)}, f32[8,128]{1,0:T(8,128)S(1)}) custom-call(bf16[512,512]{1,0:T(8,128)(2,1)S(1)} %copy-done.15, bf16[512,512]{1,0:T(8,128)(2,1)S(1)} %copy-done.13, f32[512,512]{1,0:T(8,128)S(1)} %copy-done.11, f32[512,512]{1,0:T(8,128)S(1)} %copy-done.9, bf16[1024,1024]{1,0:T(8,128)(2,1)S(1)} %copy-done.7, ...), custom_call_target="tpu_custom_call" | custom-call | flops 2147483648 | bytes 7340032 | tf_op jit(solution)/shard_map/finish/pallas_call | solution.py:340
  119.3 3.3 %collective-permute-done.27 = f32[4,16,1024]{2,1,0:T(8,128)S(1)} collective-permute-done((f32[4,16,1024]{2,1,0:T(8,128)}, f32[4,16,1024]{2,1,0:T(8,128)S(1)}, u32[]{:S(2)}, u32[]{:S(2)}) %collective-permute-start.27) | collective-permute-done | bytes 262176 | tf_op jit(solution)/shard_map/ppermute | solution.py:377
  123.1 4.3 %collective-permute-done.26 = f32[4,16,1024]{2,1,0:T(8,128)} collective-permute-done((f32[4,16,1024]{2,1,0:T(8,128)}, f32[4,16,1024]{2,1,0:T(8,128)}, u32[]{:S(2)}, u32[]{:S(2)}) %collective-permute-start.26) | collective-permute-done | bytes 262176 | tf_op jit(solution)/shard_map/ppermute | solution.py:377
  129.5 4.5 %collective-permute-start.31 = (f32[16,1024]{1,0:T(8,128)S(1)}, f32[16,1024]{1,0:T(8,128)S(1)}, u32[]{:S(2)}, u32[]{:S(2)}) collective-permute-start(f32[16,1024]{1,0:T(8,128)S(1)} %get-tuple-element.97), channel_id=1, source_target_pairs={{0,6},{1,7},{2,0},{3,1},{4,2},{5,3},{6,4},{7,5},{8,14},{9,15},{10,... | collective-permute-start | bytes 196616 | tf_op jit(solution)/shard_map/ppermute | solution.py:377
  134.0 2.5 %collective-permute-start.29 = (f32[16,1024]{1,0:T(8,128)S(1)}, f32[16,1024]{1,0:T(8,128)S(1)}, u32[]{:S(2)}, u32[]{:S(2)}) collective-permute-start(f32[16,1024]{1,0:T(8,128)S(1)} %get-tuple-element.96), channel_id=1, source_target_pairs={{0,2},{1,3},{2,4},{3,5},{4,6},{5,7},{6,0},{7,1},{8,10},{9,11},{10,... | collective-permute-start | bytes 196616 | tf_op jit(solution)/shard_map/ppermute | solution.py:377
  139.2 4.5 %collective-permute-start.17 = (f32[16,1024]{1,0:T(8,128)S(1)}, f32[16,1024]{1,0:T(8,128)S(1)}, u32[]{:S(2)}, u32[]{:S(2)}) collective-permute-start(f32[16,1024]{1,0:T(8,128)S(1)} %get-tuple-element.94), channel_id=1, source_target_pairs={{0,6},{1,7},{2,0},{3,1},{4,2},{5,3},{6,4},{7,5},{8,14},{9,15},{10,... | collective-permute-start | bytes 196616 | tf_op jit(solution)/shard_map/ppermute | solution.py:377
  150.4 3.8 %collective-permute-done.16 = f32[16,1024]{1,0:T(8,128)S(1)} collective-permute-done((f32[16,1024]{1,0:T(8,128)S(1)}, f32[16,1024]{1,0:T(8,128)S(1)}, u32[]{:S(2)}, u32[]{:S(2)}) %collective-permute-start.16) | collective-permute-done | bytes 65568 | tf_op jit(solution)/shard_map/ppermute | solution.py:377
  172.0 4.0 %collective-permute-done.39 = f32[4,16,1024]{2,1,0:T(8,128)S(1)} collective-permute-done((f32[4,16,1024]{2,1,0:T(8,128)S(1)}, f32[4,16,1024]{2,1,0:T(8,128)S(1)}, u32[]{:S(2)}, u32[]{:S(2)}) %collective-permute-start.39) | collective-permute-done | bytes 262176 | tf_op jit(solution)/shard_map/ppermute | solution.py:377
  178.2 3.3 %collective-permute-done.23 = f32[4,16,1024]{2,1,0:T(8,128)S(1)} collective-permute-done((f32[4,16,1024]{2,1,0:T(8,128)S(1)}, f32[4,16,1024]{2,1,0:T(8,128)S(1)}, u32[]{:S(2)}, u32[]{:S(2)}) %collective-permute-start.23) | collective-permute-done | bytes 262176 | tf_op jit(solution)/shard_map/ppermute | solution.py:377
  183.7 2.5 %collective-permute-done.42 = f32[8,128]{1,0:T(8,128)S(1)} collective-permute-done((f32[8,128]{1,0:T(8,128)S(1)}, f32[8,128]{1,0:T(8,128)S(1)}, u32[]{:S(2)}, u32[]{:S(2)}) %collective-permute-start.42) | collective-permute-done | bytes 4128 | tf_op jit(solution)/shard_map/ppermute | solution.py:408
  (156 shorter events, 76.9 us)
Async XLA Ops:
  20.1 15.0 %collective-permute-start = (f32[4,128,256]{2,1,0:T(8,128)S(1)}, f32[4,128,256]{2,1,0:T(8,128)S(1)}, u32[]{:S(2)}, u32[]{:S(2)}) collective-permute-start(f32[4,128,256]{2,1,0:T(8,128)S(1)} %get-tuple-element.45), channel_id=1, source_target_pairs={{0,1},{1,0},{2,3},{3,2},{4,5},{5,4},{6,7},{7,6},{8,9},{9,8},{10,11... | collective-permute-start | bytes 1572872 | tf_op jit(solution)/shard_map/ppermute | solution.py:377
  34.2 13.4 %collective-permute-start.6 = (f32[4,128,256]{2,1,0:T(8,128)S(1)}, f32[4,128,256]{2,1,0:T(8,128)S(1)}, u32[]{:S(2)}, u32[]{:S(2)}) collective-permute-start(f32[4,128,256]{2,1,0:T(8,128)S(1)} %get-tuple-element.54), channel_id=1, source_target_pairs={{0,1},{1,0},{2,3},{3,2},{4,5},{5,4},{6,7},{7,6},{8,9},{9,8},{10,11... | collective-permute-start | bytes 1572872 | tf_op jit(solution)/shard_map/ppermute | solution.py:377
  36.3 16.1 %collective-permute-start.1 = (f32[4,128,128]{2,1,0:T(8,128)S(1)}, f32[4,128,128]{2,1,0:T(8,128)S(1)}, u32[]{:S(2)}, u32[]{:S(2)}) collective-permute-start(f32[4,128,128]{2,1,0:T(8,128)S(1)} %hop.6), channel_id=1, source_target_pairs={{0,2},{1,3},{2,4},{3,5},{4,6},{5,7},{8,10},{9,11},{10,12},{11,13},... | collective-permute-start | bytes 786440 | tf_op jit(solution)/shard_map/ppermute | solution.py:377
  52.7 11.8 %collective-permute-start.2 = (f32[4,128,128]{2,1,0:T(8,128)S(1)}, f32[4,128,128]{2,1,0:T(8,128)S(1)}, u32[]{:S(2)}, u32[]{:S(2)}) collective-permute-start(f32[4,128,128]{2,1,0:T(8,128)S(1)} %hop.7), channel_id=1, source_target_pairs={{0,2},{1,3},{2,4},{3,5},{4,6},{5,7},{8,10},{9,11},{10,12},{11,13},... | collective-permute-start | bytes 786440 | tf_op jit(solution)/shard_map/ppermute | solution.py:377
  59.1 11.3 %collective-permute-start.8 = (f32[4,128,128]{2,1,0:T(8,128)S(1)}, f32[4,128,128]{2,1,0:T(8,128)S(1)}, u32[]{:S(2)}, u32[]{:S(2)}) collective-permute-start(f32[4,128,128]{2,1,0:T(8,128)S(1)} %hop.10), channel_id=1, source_target_pairs={{0,2},{1,3},{2,4},{3,5},{4,6},{5,7},{8,10},{9,11},{10,12},{11,13},... | collective-permute-start | bytes 786440 | tf_op jit(solution)/shard_map/ppermute | solution.py:377
  64.7 11.3 %collective-permute-start.3 = (f32[4,128,128]{2,1,0:T(8,128)S(1)}, f32[4,128,128]{2,1,0:T(8,128)S(1)}, u32[]{:S(2)}, u32[]{:S(2)}) collective-permute-start(f32[4,128,128]{2,1,0:T(8,128)S(1)} %hop.8), channel_id=1, source_target_pairs={{0,2},{1,3},{2,4},{3,5},{4,6},{5,7},{8,10},{9,11},{10,12},{11,13},... | collective-permute-start | bytes 786440 | tf_op jit(solution)/shard_map/ppermute | solution.py:377
  80.0 11.7 %collective-permute-start.10 = (f32[4,128,128]{2,1,0:T(8,128)S(1)}, f32[4,128,128]{2,1,0:T(8,128)S(1)}, u32[]{:S(2)}, u32[]{:S(2)}) collective-permute-start(f32[4,128,128]{2,1,0:T(8,128)S(1)} %get-tuple-element.58), channel_id=1, source_target_pairs={{0,1},{1,0},{2,3},{3,2},{4,5},{5,4},{6,7},{7,6},{8,9},{9,8},{10,11... | collective-permute-start | bytes 786440 | tf_op jit(solution)/shard_map/ppermute | solution.py:377
  91.7 18.3 %collective-permute-start.5 = (f32[2,128,1024]{2,1,0:T(8,128)}, f32[2,128,1024]{2,1,0:T(8,128)}, u32[]{:S(2)}, u32[]{:S(2)}) collective-permute-start(f32[2,128,1024]{2,1,0:T(8,128)} %get-tuple-element.50), channel_id=1, source_target_pairs={{0,8},{1,9},{2,10},{3,11},{4,12},{5,13},{6,14},{7,15},{8,0},{9,1},... | collective-permute-start | bytes 3145736 | tf_op jit(solution)/shard_map/ppermute | solution.py:377
  98.7 17.1 %collective-permute-start.11 = (f32[2,128,1024]{2,1,0:T(8,128)}, f32[2,128,1024]{2,1,0:T(8,128)}, u32[]{:S(2)}, u32[]{:S(2)}) collective-permute-start(f32[2,128,1024]{2,1,0:T(8,128)} %get-tuple-element.67), channel_id=1, source_target_pairs={{0,8},{1,9},{2,10},{3,11},{4,12},{5,13},{6,14},{7,15},{8,0},{9,1},... | collective-permute-start | bytes 3145736 | tf_op jit(solution)/shard_map/ppermute | solution.py:377
  113.7 13.7 %collective-permute-start.26 = (f32[4,16,1024]{2,1,0:T(8,128)}, f32[4,16,1024]{2,1,0:T(8,128)}, u32[]{:S(2)}, u32[]{:S(2)}) collective-permute-start(f32[4,16,1024]{2,1,0:T(8,128)} %get-tuple-element.92), channel_id=1, source_target_pairs={{0,16},{1,17},{2,18},{3,19},{4,20},{5,21},{6,22},{7,23},{8,24},{9,... | collective-permute-start | bytes 786440 | tf_op jit(solution)/shard_map/ppermute | solution.py:377
  114.3 14.1 %collective-permute-start.25 = (f32[4,16,1024]{2,1,0:T(8,128)}, f32[4,16,1024]{2,1,0:T(8,128)}, u32[]{:S(2)}, u32[]{:S(2)}) collective-permute-start(f32[4,16,1024]{2,1,0:T(8,128)} %get-tuple-element.90), channel_id=1, source_target_pairs={{0,1},{1,0},{2,3},{3,2},{4,5},{5,4},{6,7},{7,6},{8,9},{9,8},{10,11... | collective-permute-start | bytes 786440 | tf_op jit(solution)/shard_map/ppermute | solution.py:377
  117.2 16.8 %collective-permute-start.14 = (f32[4,16,1024]{2,1,0:T(8,128)S(1)}, f32[4,16,1024]{2,1,0:T(8,128)S(1)}, u32[]{:S(2)}, u32[]{:S(2)}) collective-permute-start(f32[4,16,1024]{2,1,0:T(8,128)S(1)} %get-tuple-element.88), channel_id=1, source_target_pairs={{0,17},{1,16},{2,19},{3,18},{4,21},{5,20},{6,23},{7,22},{8,25},{9,... | collective-permute-start | bytes 786440 | tf_op jit(solution)/shard_map/ppermute | solution.py:377
  118.8 18.9 %collective-permute-start.13 = (f32[4,16,1024]{2,1,0:T(8,128)S(1)}, f32[4,16,1024]{2,1,0:T(8,128)S(1)}, u32[]{:S(2)}, u32[]{:S(2)}) collective-permute-start(f32[4,16,1024]{2,1,0:T(8,128)S(1)} %get-tuple-element.89), channel_id=1, source_target_pairs={{0,16},{1,17},{2,18},{3,19},{4,20},{5,21},{6,22},{7,23},{8,24},{9,... | collective-permute-start | bytes 786440 | tf_op jit(solution)/shard_map/ppermute | solution.py:377
  122.6 16.5 %collective-permute-start.12 = (f32[4,16,1024]{2,1,0:T(8,128)S(1)}, f32[4,16,1024]{2,1,0:T(8,128)S(1)}, u32[]{:S(2)}, u32[]{:S(2)}) collective-permute-start(f32[4,16,1024]{2,1,0:T(8,128)S(1)} %get-tuple-element.87), channel_id=1, source_target_pairs={{0,1},{1,0},{2,3},{3,2},{4,5},{5,4},{6,7},{7,6},{8,9},{9,8},{10,11... | collective-permute-start | bytes 786440 | tf_op jit(solution)/shard_map/ppermute | solution.py:377
  129.5 15.4 %collective-permute-start.31 = (f32[16,1024]{1,0:T(8,128)S(1)}, f32[16,1024]{1,0:T(8,128)S(1)}, u32[]{:S(2)}, u32[]{:S(2)}) collective-permute-start(f32[16,1024]{1,0:T(8,128)S(1)} %get-tuple-element.97), channel_id=1, source_target_pairs={{0,6},{1,7},{2,0},{3,1},{4,2},{5,3},{6,4},{7,5},{8,14},{9,15},{10,... | collective-permute-start | bytes 196616 | tf_op jit(solution)/shard_map/ppermute | solution.py:377
  134.0 12.2 %collective-permute-start.30 = (f32[16,1024]{1,0:T(8,128)S(1)}, f32[16,1024]{1,0:T(8,128)S(1)}, u32[]{:S(2)}, u32[]{:S(2)}) collective-permute-start(f32[16,1024]{1,0:T(8,128)S(1)} %get-tuple-element.98), channel_id=1, source_target_pairs={{0,4},{1,5},{2,6},{3,7},{4,0},{5,1},{6,2},{7,3},{8,12},{9,13},{10,... | collective-permute-start | bytes 196616 | tf_op jit(solution)/shard_map/ppermute | solution.py:377
  134.0 12.2 %collective-permute-start.29 = (f32[16,1024]{1,0:T(8,128)S(1)}, f32[16,1024]{1,0:T(8,128)S(1)}, u32[]{:S(2)}, u32[]{:S(2)}) collective-permute-start(f32[16,1024]{1,0:T(8,128)S(1)} %get-tuple-element.96), channel_id=1, source_target_pairs={{0,2},{1,3},{2,4},{3,5},{4,6},{5,7},{6,0},{7,1},{8,10},{9,11},{10,... | collective-permute-start | bytes 196616 | tf_op jit(solution)/shard_map/ppermute | solution.py:377
  146.3 11.6 %collective-permute-start.33 = (f32[16,1024]{1,0:T(8,128)S(1)}, f32[16,1024]{1,0:T(8,128)S(1)}, u32[]{:S(2)}, u32[]{:S(2)}) collective-permute-start(f32[16,1024]{1,0:T(8,128)S(1)} %fusion.6), channel_id=1, source_target_pairs={{0,2},{1,3},{2,4},{3,5},{4,6},{5,7},{6,0},{7,1},{8,10},{9,11},{10,... | collective-permute-start | bytes 196616 | tf_op jit(solution)/shard_map/ppermute | solution.py:377
  147.3 12.5 %collective-permute-start.34 = (f32[16,1024]{1,0:T(8,128)S(1)}, f32[16,1024]{1,0:T(8,128)S(1)}, u32[]{:S(2)}, u32[]{:S(2)}) collective-permute-start(f32[16,1024]{1,0:T(8,128)S(1)} %fusion.6), channel_id=1, source_target_pairs={{0,4},{1,5},{2,6},{3,7},{4,0},{5,1},{6,2},{7,3},{8,12},{9,13},{10,... | collective-permute-start | bytes 196616 | tf_op jit(solution)/shard_map/ppermute | solution.py:377
  161.0 10.9 %collective-permute-start.38 = (f32[4,16,1024]{2,1,0:T(8,128)S(1)}, f32[4,16,1024]{2,1,0:T(8,128)S(1)}, u32[]{:S(2)}, u32[]{:S(2)}) collective-permute-start(f32[4,16,1024]{2,1,0:T(8,128)S(1)} %bitcast_dynamic-update-slice_fusion.8), channel_id=1, source_target_pairs={{0,16},{1,17},{2,18},{3,19},{4,20},{5,21},{6,22},{7,23},{8,24},{9,... | collective-permute-start | bytes 786440 | tf_op jit(solution)/shard_map/ppermute | solution.py:377
  162.7 13.3 %collective-permute-start.39 = (f32[4,16,1024]{2,1,0:T(8,128)S(1)}, f32[4,16,1024]{2,1,0:T(8,128)S(1)}, u32[]{:S(2)}, u32[]{:S(2)}) collective-permute-start(f32[4,16,1024]{2,1,0:T(8,128)S(1)} %bitcast_dynamic-update-slice_fusion.8), channel_id=1, source_target_pairs={{0,17},{1,16},{2,19},{3,18},{4,21},{5,20},{6,23},{7,22},{8,25},{9,... | collective-permute-start | bytes 786440 | tf_op jit(solution)/shard_map/ppermute | solution.py:377
  164.2 13.9 %collective-permute-start.21 = (f32[4,16,1024]{2,1,0:T(8,128)S(1)}, f32[4,16,1024]{2,1,0:T(8,128)S(1)}, u32[]{:S(2)}, u32[]{:S(2)}) collective-permute-start(f32[4,16,1024]{2,1,0:T(8,128)S(1)} %bitcast_dynamic-update-slice_fusion.12), channel_id=1, source_target_pairs={{0,1},{1,0},{2,3},{3,2},{4,5},{5,4},{6,7},{7,6},{8,9},{9,8},{10,11... | collective-permute-start | bytes 786440 | tf_op jit(solution)/shard_map/ppermute | solution.py:377
  167.3 10.9 %collective-permute-start.22 = (f32[4,16,1024]{2,1,0:T(8,128)S(1)}, f32[4,16,1024]{2,1,0:T(8,128)S(1)}, u32[]{:S(2)}, u32[]{:S(2)}) collective-permute-start(f32[4,16,1024]{2,1,0:T(8,128)S(1)} %bitcast_dynamic-update-slice_fusion.12), channel_id=1, source_target_pairs={{0,16},{1,17},{2,18},{3,19},{4,20},{5,21},{6,22},{7,23},{8,24},{9,... | collective-permute-start | bytes 786440 | tf_op jit(solution)/shard_map/ppermute | solution.py:377
  169.7 11.8 %collective-permute-start.23 = (f32[4,16,1024]{2,1,0:T(8,128)S(1)}, f32[4,16,1024]{2,1,0:T(8,128)S(1)}, u32[]{:S(2)}, u32[]{:S(2)}) collective-permute-start(f32[4,16,1024]{2,1,0:T(8,128)S(1)} %bitcast_dynamic-update-slice_fusion.12), channel_id=1, source_target_pairs={{0,17},{1,16},{2,19},{3,18},{4,21},{5,20},{6,23},{7,22},{8,25},{9,... | collective-permute-start | bytes 786440 | tf_op jit(solution)/shard_map/ppermute | solution.py:377
  (35 other events, 230.0 us)

commit v3 on v2

--- a/solution.py
+++ b/solution.py
@@ -14,7 +14,7 @@
 PER_STEP = 2
 F32 = jnp.float32
 BF16 = jnp.bfloat16
-VMEM_LIMIT = 40 * 1024 * 1024
+MIB = 1024 * 1024
 
 
 def dot(a, b):
@@ -40,8 +40,16 @@
     return dot(ah, bh) + (dot(ah, bl) + dot(al, bh))
 
 
-def params(**more):
-    return pltpu.CompilerParams(vmem_limit_bytes=VMEM_LIMIT, **more)
+def params(mib):
+    return pltpu.CompilerParams(vmem_limit_bytes=mib * MIB)
+
+
+def smem():
+    return pl.BlockSpec(memory_space=pltpu.SMEM)
+
+
+def vmem():
+    return pl.BlockSpec(memory_space=pltpu.VMEM)
 
 
 def whole(shape):
@@ -52,13 +60,18 @@
     return pl.CostEstimate(flops=flops, bytes_accessed=size, transcendentals=0)
 
 
-def gates_kernel(span, x_ref, w_ref, rate_ref, bias_ref, out_ref):
-    heads = rate_ref.shape[1]
-    gates = dot(x_ref[...], w_ref[...])
+def gates_kernel(span, heads, x_ref, w_ref, rate_ref, bias_ref, out_ref):
+    lane = lax.broadcasted_iota(jnp.int32, (1, heads), 1)
+    rate = jnp.zeros((1, heads), F32)
+    bias = jnp.zeros((1, heads), F32)
+    for h in range(heads):
+        rate = jnp.where(lane == h, rate_ref[h], rate)
+        bias = jnp.where(lane == h, bias_ref[h], bias)
+    gates = dot_nt(x_ref[...], w_ref[...])
     raw = gates[:, :heads]
     softplus = jnp.maximum(raw, 0.0) + jnp.log1p(jnp.exp(-jnp.abs(raw)))
-    logdecay = -rate_ref[...] * softplus
-    out_ref[:, heads : 2 * heads] = jax.nn.sigmoid(gates[:, heads:] + bias_ref[...])
+    logdecay = -rate * softplus
+    out_ref[:, heads : 2 * heads] = jax.nn.sigmoid(gates[:, heads:] + bias)
     row = lax.broadcasted_iota(jnp.int32, (span, span), 0)
     col = lax.broadcasted_iota(jnp.int32, (span, span), 1)
     lower = jnp.where(row >= col, 1.0, 0.0).astype(F32)
@@ -73,12 +86,13 @@
     count, width = rows.shape
     heads = decay_rate.shape[0]
     return pl.pallas_call(
-        functools.partial(gates_kernel, span),
+        functools.partial(gates_kernel, span, heads),
         out_shape=jax.ShapeDtypeStruct((count, 2 * heads), F32),
-        compiler_params=params(),
+        in_specs=[vmem(), vmem(), smem(), smem()],
+        compiler_params=params(12),
         cost_estimate=cost(2 * count * width * 128, count * width * 2),
         name="gates",
-    )(rows, gate_weight, decay_rate.reshape(1, heads), beta_bias.reshape(1, heads))
+    )(rows, gate_weight.T, decay_rate, beta_bias)
 
 
 def solve_lower(systems, rights):
@@ -103,7 +117,7 @@
 def local_kernel(
     first_head, heads, span, per_step, info, pin, ppool, x_ref, pool_ref, gate_ref, own_ref, send_ref, core_ref, query_ref
 ):
-    members = pin.shape[0] // (3 * heads)
+    members = pin.shape[0]
     dims = pool_ref.shape[1]
     lane = lax.broadcasted_iota(jnp.int32, (span, 2 * heads), 1)
     wide = lax.broadcasted_iota(jnp.int32, (span, dims), 1)
@@ -118,16 +132,16 @@
         head = first_head + pl.program_id(0) * per_step + local
         chosen = []
         for kind in range(3):
-            target = (kind * heads + head) * members
-            chosen.append(jnp.concatenate([pool_ref[ppool[target + j]] for j in range(members)], 0))
+            target = kind * heads + head
+            chosen.append(jnp.concatenate([pool_ref[ppool[j, target]] for j in range(members)], 0))
         for part in range(2):
             seq = info[0] if part == 0 else 1 - info[0]
             where.append((local, part, pl.ds(pl.multiple_of(seq * span, span), span)))
             projected = []
             for kind in range(3):
-                target = (kind * heads + head) * members
+                target = kind * heads + head
                 picked = [
-                    x_ref[where[-1][2], pl.ds(pl.multiple_of(pin[target + j] * dims, dims), dims)]
+                    x_ref[where[-1][2], pl.ds(pl.multiple_of(pin[j, target] * dims, dims), dims)]
                     for j in range(members)
                 ]
                 projected.append(dot(jnp.concatenate(picked, 1), chosen[kind]).astype(BF16))
@@ -177,7 +191,7 @@
             in_specs=[whole(rows.shape), whole(pool.shape), whole(gates.shape)],
             out_specs=(map_spec, map_spec, row_spec, row_spec),
         ),
-        compiler_params=params(),
+        compiler_params=params(28),
         cost_estimate=cost(count_heads * 2 * 2 * span * 256 * 256 * 24, 8 * 1024 * 1024),
         name="local",
     )(info, pin, ppool, rows, pool, gates)
@@ -188,7 +202,7 @@
     return dot3(maps[:, :dims], state)
 
 
-def combine_kernel(info, own_ref, got_ref, early_ref, both_ref):
+def combine_kernel(info, own_ref, got_ref, early_ref, both_ref, push_ref):
     later_is_own = info[0] == 1
     for h in range(own_ref.shape[0]):
         own, got = own_ref[h], got_ref[h]
@@ -197,72 +211,88 @@
         dims = own.shape[0]
         early_ref[h] = early
         both = apply_map(late, early)
+        push = both[:, dims:] + late[:, dims:]
         both_ref[h, :, :dims] = both[:, :dims]
-        both_ref[h, :, dims:] = both[:, dims:] + late[:, dims:]
+        both_ref[h, :, dims:] = push
+        push_ref[h] = push
 
 
 def combine_call(info, own, got):
     shape = jax.ShapeDtypeStruct(own.shape, F32)
+    push = jax.ShapeDtypeStruct(own.shape[:2] + (own.shape[1],), F32)
     return pl.pallas_call(
         combine_kernel,
-        out_shape=(shape, shape),
-        in_specs=[pl.BlockSpec(memory_space=pltpu.SMEM)] + [pl.BlockSpec(memory_space=pltpu.VMEM)] * 2,
-        compiler_params=params(),
+        out_shape=(shape, shape, push),
+        in_specs=[smem(), vmem(), vmem()],
+        compiler_params=params(12),
         cost_estimate=cost(own.shape[0] * 6 * 128 * 128 * 256, own.size * 16),
         name="combine",
     )(info, own, got)
 
 
-def hop_kernel(maps_ref, state_ref, out_ref):
+def hop_kernel(level, info, maps_ref, got_ref, state_ref, kept_ref, out_ref):
+    arrived = info[2] == level
     for h in range(maps_ref.shape[0]):
         maps = maps_ref[h]
         dims = maps.shape[0]
-        out_ref[h] = apply_map(maps, state_ref[h]) + maps[:, dims:]
-
-
-def hop_call(maps, state):
-    return pl.pallas_call(
-        hop_kernel,
-        out_shape=jax.ShapeDtypeStruct(state.shape, F32),
-        compiler_params=params(),
+        state = jnp.where(arrived, got_ref[h], state_ref[h])
+        kept_ref[h] = state
+        out_ref[h] = apply_map(maps, state) + maps[:, dims:]
+
+
+def hop_call(level, info, maps, got, state):
+    shape = jax.ShapeDtypeStruct(state.shape, F32)
+    return pl.pallas_call(
+        functools.partial(hop_kernel, level),
+        out_shape=(shape, shape),
+        in_specs=[smem(), vmem(), vmem(), vmem()],
+        compiler_params=params(12),
         cost_estimate=cost(maps.shape[0] * 6 * 128 * 128 * 128, maps.size * 8),
         name="hop",
-    )(maps, state)
-
-
-def split_kernel(info, maps_ref, state_ref, keep_ref, send_ref):
+    )(info, maps, got, state)
+
+
+def split_kernel(level, info, maps_ref, got_ref, state_ref, keep_ref, send_ref):
     second = info[0] == 1
+    arrived = info[2] == level
     for h in range(maps_ref.shape[0]):
         maps = maps_ref[h]
-        state = state_ref[h]
+        state = jnp.where(arrived, got_ref[h], state_ref[h])
         dims = maps.shape[0]
         middle = apply_map(maps, state) + maps[:, dims:]
         keep_ref[h] = jnp.where(second, middle, state)
         send_ref[h] = jnp.where(second, state, middle)
 
 
-def split_call(info, maps, state):
+def split_call(level, info, maps, got, state):
     shape = jax.ShapeDtypeStruct(state.shape, F32)
     return pl.pallas_call(
-        split_kernel,
+        functools.partial(split_kernel, level),
         out_shape=(shape, shape),
-        in_specs=[pl.BlockSpec(memory_space=pltpu.SMEM)] + [pl.BlockSpec(memory_space=pltpu.VMEM)] * 2,
-        compiler_params=params(),
+        in_specs=[smem(), vmem(), vmem(), vmem()],
+        compiler_params=params(12),
         cost_estimate=cost(maps.shape[0] * 6 * 128 * 128 * 128, maps.size * 8),
         name="split",
-    )(info, maps, state)
-
-
-def mix_kernel(span, info, core_ref, query_ref, keep_ref, got_ref, gain_ref, cot_ref, normal_ref, mixed_ref, wsend_ref, wkeep_ref):
+    )(info, maps, got, state)
+
+
+def mix_kernel(
+    span, info, core_ref, query_ref, keep_ref, got_ref, back_ref, gain_ref, cot_ref, mixed_ref, wsend_ref, wkeep_ref, part_ref
+):
     step = pl.program_id(0)
     half = wsend_ref.shape[0]
+
+    @pl.when(step == 0)
+    def _():
+        part_ref[...] = jnp.zeros_like(part_ref)
+
     for part in range(2):
         seq = info[0] if part == 0 else 1 - info[0]
         rows = pl.ds(pl.multiple_of(seq * span, span), span)
         state = (keep_ref if part == 0 else got_ref)[0]
         core = core_ref[rows, :] + dot3(query_ref[rows, :], state)
         normal = core * lax.rsqrt(jnp.mean(core * core, axis=1, keepdims=True) + 1e-05)
-        normal_ref[rows, :] = normal
+        part_ref[...] += jnp.sum((normal * back_ref[rows, :]).reshape(-1, 8, core.shape[1]), axis=0)
         mixed_ref[rows, :] = (normal * gain_ref[...]).astype(BF16)
     product = dot_tn(mixed_ref[...], cot_ref[...])
 
@@ -275,7 +305,7 @@
         wkeep_ref[step - half] = product
 
 
-def mix_call(info, core, query, keep, got, gain, cot, span):
+def mix_call(info, first_head, core, query, keep, got, back, gain, cot, span):
     count, width = cot.shape
     heads_here = keep.shape[0]
     dims = gain.shape[1]
@@ -286,67 +316,90 @@
         return first * half + lax.rem(i, half)
 
     row_spec = pl.BlockSpec((count, dims), lambda i, info: (0, order(i, info)))
+    back_spec = pl.BlockSpec((count, dims), lambda i, info: (0, first_head + order(i, info)))
     state_spec = pl.BlockSpec((1, dims, dims), lambda i, info: (order(i, info), 0, 0))
     weight = jax.ShapeDtypeStruct((half, dims, width), F32)
     return pl.pallas_call(
         functools.partial(mix_kernel, span),
         out_shape=(
-            jax.ShapeDtypeStruct((count, heads_here * dims), F32),
             jax.ShapeDtypeStruct((count, heads_here * dims), BF16),
             weight,
             weight,
+            jax.ShapeDtypeStruct((8, dims), F32),
         ),
         grid_spec=pltpu.PrefetchScalarGridSpec(
             num_scalar_prefetch=1,
             grid=(heads_here,),
-            in_specs=[row_spec, row_spec, state_spec, state_spec, whole(gain.shape), whole(cot.shape)],
-            out_specs=(row_spec, row_spec, whole(weight.shape), whole(weight.shape)),
+            in_specs=[row_spec, row_spec, state_spec, state_spec, back_spec, whole(gain.shape), whole(cot.shape)],
+            out_specs=(row_spec, whole(weight.shape), whole(weight.shape), whole((8, dims))),
         ),
-        compiler_params=params(),
-        cost_estimate=cost(heads_here * 2 * 512 * 1024 * 128, 6 * 1024 * 1024),
+        compiler_params=params(20),
+        cost_estimate=cost(heads_here * 2 * 512 * 1024 * 128, 6 * MIB),
         name="mix",
-    )(info, core, query, keep, got, gain, cot)
+    )(info, core, query, keep, got, back, gain, cot)
+
+
+def back_kernel(cot_ref, weight_ref, out_ref):
+    out_ref[...] = dot_nt(cot_ref[...], weight_ref[...])
+
+
+def back_call(cot, weight):
+    count, width = cot.shape
+    row_spec = pl.BlockSpec((128, width), lambda i: (i, 0))
+    return pl.pallas_call(
+        back_kernel,
+        out_shape=jax.ShapeDtypeStruct((count, width), F32),
+        grid=(count // 128,),
+        in_specs=[row_spec, whole(weight.shape)],
+        out_specs=row_spec,
+        compiler_params=params(12),
+        cost_estimate=cost(2 * count * width * width, 5 * MIB),
+        name="back",
+    )(cot, weight)
 
 
 def finish_kernel(groups, *refs):
-    mixed, normal = refs[:groups], refs[groups : 2 * groups]
-    weight_ref, cot_ref, out_ref, gain_ref = refs[2 * groups :]
-    dims = gain_ref.shape[1]
-
-    @pl.when(pl.program_id(0) == 0)
-    def _():
-        gain_ref[...] = jnp.zeros_like(gain_ref)
-
-    stacked = jnp.concatenate([ref[...] for ref in mixed], axis=1)
+    weight_ref, out_ref = refs[groups:]
+    stacked = jnp.concatenate([ref[...] for ref in refs[:groups]], axis=1)
     out_ref[...] = dot(stacked, weight_ref[...]).astype(BF16)
-    back = dot_nt(cot_ref[...], weight_ref[...])
-    total = jnp.zeros((out_ref.shape[0], dims), F32)
-    first = 0
-    for ref in normal:
-        for lane in range(0, ref.shape[1], dims):
-            total += back[:, first : first + dims] * ref[:, lane : lane + dims]
-            first += dims
-    gain_ref[...] += jnp.sum(total.reshape(-1, 8, dims), axis=0)
-
-
-def finish_call(mixed, normal, weight, cot):
-    count, width = cot.shape
-    block = 128
-    groups = len(mixed)
-    part = mixed[0].shape[1]
-    dims = 128
-    part_spec = pl.BlockSpec((block, part), lambda i: (i, 0))
-    row_spec = pl.BlockSpec((block, width), lambda i: (i, 0))
-    return pl.pallas_call(
-        functools.partial(finish_kernel, groups),
-        out_shape=(jax.ShapeDtypeStruct((count, width), BF16), jax.ShapeDtypeStruct((8, dims), F32)),
-        grid=(count // block,),
-        in_specs=[part_spec] * (2 * groups) + [whole(weight.shape), row_spec],
-        out_specs=(row_spec, whole((8, dims))),
-        compiler_params=params(),
-        cost_estimate=cost(4 * count * width * width, 7 * 1024 * 1024),
+
+
+def finish_call(mixed, weight):
+    count = mixed[0].shape[0]
+    width = weight.shape[1]
+    part_spec = pl.BlockSpec((128, mixed[0].shape[1]), lambda i: (i, 0))
+    row_spec = pl.BlockSpec((128, width), lambda i: (i, 0))
+    return pl.pallas_call(
+        functools.partial(finish_kernel, len(mixed)),
+        out_shape=jax.ShapeDtypeStruct((count, width), BF16),
+        grid=(count // 128,),
+        in_specs=[part_spec] * len(mixed) + [whole(weight.shape)],
+        out_specs=row_spec,
+        compiler_params=params(12),
+        cost_estimate=cost(2 * count * width * width, 4 * MIB),
         name="finish",
-    )(*mixed, *normal, weight, cot)
+    )(*mixed, weight)
+
+
+def join_kernel(groups, scale, info, *refs):
+    out_ref = refs[-1]
+    rows = refs[0].shape[0]
+    for g in range(groups):
+        for part, ref in enumerate(refs[2 * g : 2 * g + 2]):
+            side = info[1] if part == 0 else 1 - info[1]
+            first = pl.multiple_of((2 * g + side) * rows, rows)
+            out_ref[pl.ds(first, rows), :] = (ref[...] * scale).astype(BF16)
+
+
+def join_call(info, parts, scale):
+    rows, width = parts[0].shape
+    return pl.pallas_call(
+        functools.partial(join_kernel, len(parts) // 2, scale),
+        out_shape=jax.ShapeDtypeStruct((rows * len(parts), width), BF16),
+        in_specs=[smem()] + [vmem()] * len(parts),
+        compiler_params=params(16),
+        name="join",
+    )(info, *parts)
 
 
 def shards(mesh, features, weight_pool, pattern_in, pattern_pool, gate_weight, decay_rate, beta_bias, norm_gain, out_weight, cotangent):
@@ -363,24 +416,26 @@
     def place(xi, ci, zi, yi):
         return (xi * CORES + ci) * n_tm + zi * PAIR + yi
 
-    def moved(array, shift, wrap=True):
+    def moved(array, shift):
         dx, dc, dz, dy = shift
         route = []
         for xi in range(n_x):
             for ci in range(CORES):
                 for zi in range(n_z):
                     for yi in range(PAIR):
-                        if not wrap and zi + dz >= n_z:
-                            continue
-                        to = place((xi + dx) % n_x, (ci + dc) % CORES, (zi + dz) % n_z, (yi + dy) % PAIR)
-                        route.append((place(xi, ci, zi, yi), to))
+                        route.append((place(xi, ci, zi, yi), place(xi ^ dx, ci ^ dc, zi ^ dz, yi ^ dy)))
         return lax.ppermute(array, both, route)
 
-    info = jnp.stack([y, core]).astype(jnp.int32)
+    def lifted(array, level):
+        ends = ((level, level + 1), (level + 1, level))
+        route = [(a * PAIR + yi, b * PAIR + yi) for a, b in ends for yi in range(PAIR)]
+        return lax.ppermute(array, "tm", route)
+
+    info = jnp.stack([y, core, z]).astype(jnp.int32)
     rows = features.reshape(count, width)
     cot = cotangent.reshape(count, width)
     gain = norm_gain.reshape(1, dims)
-    pin, ppool = pattern_in.reshape(-1), pattern_pool.reshape(-1)
+    pin, ppool = pattern_in.T, pattern_pool.T
     gates = gates_call(rows, gate_weight, decay_rate, beta_bias, span)
     each = heads // GROUPS
 
@@ -389,15 +444,24 @@
     for own, send, _, _ in locals_:
         got = moved(send, (0, 0, 0, 1))
         maps.append(combine_call(info, own, got))
+    back = back_call(cot, out_weight)
     states = [jnp.zeros((each, dims, dims), F32)] * GROUPS
-    for _ in range(n_z - 1):
-        states = [moved(hop_call(maps[g][1], states[g]), (0, 0, 1, 0), wrap=False) for g in range(GROUPS)]
+    sends = [m[2] for m in maps]
+    for level in range(1, n_z):
+        gots = [lifted(send, level - 1) for send in sends]
+        if level == 1:
+            gots[0], back = lax.optimization_barrier((gots[0], back))
+        if level == n_z - 1:
+            break
+        for g in range(GROUPS):
+            states[g], sends[g] = hop_call(level, info, maps[g][1], gots[g], states[g])
     mixes = []
     for g in range(GROUPS):
-        keep, send = split_call(info, maps[g][0], states[g])
+        keep, send = split_call(n_z - 1, info, maps[g][0], gots[g], states[g])
         got = moved(send, (0, 0, 0, 1))
-        mixes.append(mix_call(info, locals_[g][2], locals_[g][3], keep, got, gain, cot, span))
-    output, gain_part = finish_call([m[1] for m in mixes], [m[0] for m in mixes], out_weight, cot)
+        mixes.append(mix_call(info, g * each, locals_[g][2], locals_[g][3], keep, got, back, gain, cot, span))
+    gain_part = sum(m[3] for m in mixes)
+    output = finish_call([m[0] for m in mixes], out_weight)
     scale = 1.0 / math.sqrt(count * n_shot * n_tm)
     swaps = [(axis, 1 << bit) for axis, size in (("shot", n_shot), ("tm", n_tm)) for bit in range(size.bit_length() - 1)]
     per_stage = -(-len(swaps) // 5)
@@ -413,24 +477,24 @@
     share = each * dims // (CORES * n_plane * n_z)
 
     def plane_index(dx, dy):
-        return ((x + dx) % n_x) * PAIR + (y + dy) % PAIR
+        return (x ^ dx) * PAIR + (y ^ dy)
 
     def picked(array, index):
         return lax.dynamic_index_in_dim(array, index, 0, keepdims=False)
 
-    crossed = [moved(mixes[g][2], (0, 1, 0, 0)) for g in range(GROUPS)]
-    crossed[-1], gain_part, output = lax.optimization_barrier((crossed[-1], gain_part, output))
+    crossed = [moved(mixes[g][1], (0, 1, 0, 0)) for g in range(GROUPS)]
     grads = []
     for g in range(GROUPS):
-        summed = (mixes[g][3] + crossed[g]).reshape(n_plane, n_z, share, width)
+        summed = (mixes[g][2] + crossed[g]).reshape(n_plane, n_z, share, width)
         total = picked(summed, plane_index(0, 0))
         for dx, dy in plane[1:]:
             total = total + moved(picked(summed, plane_index(dx, dy)), (dx, 0, 0, dy))
         if g == GROUPS - 1:
             total, gain_part = spread(total, gain_part, 0)
+            total, output = lax.optimization_barrier((total, output))
         final = picked(total, z)
         for dz in range(1, n_z):
-            final = final + moved(picked(total, (z + dz) % n_z), (0, 0, dz, 0))
+            final = final + moved(picked(total, z ^ dz), (0, 0, dz, 0))
         if g == GROUPS - 1:
             final, gain_part = spread(final, gain_part, 1)
         grads.append(final)
@@ -439,23 +503,21 @@
         along = jnp.zeros((n_z, share, width), F32)
         for dz in range(n_z):
             piece = grads[g] if dz == 0 else moved(grads[g], (0, 0, dz, 0))
-            along = lax.dynamic_update_index_in_dim(along, piece, (z - dz) % n_z, 0)
+            along = lax.dynamic_update_index_in_dim(along, piece, z ^ dz, 0)
         if g == GROUPS - 1:
             along, gain_part = spread(along, gain_part, 2)
         wide = jnp.zeros((n_plane, n_z, share, width), F32)
         for dx, dy in plane:
             piece = along if (dx, dy) == (0, 0) else moved(along, (dx, 0, 0, dy))
-            wide = lax.dynamic_update_index_in_dim(wide, piece, plane_index(-dx, -dy), 0)
+            wide = lax.dynamic_update_index_in_dim(wide, piece, plane_index(dx, dy), 0)
         if g == GROUPS - 1:
             wide, gain_part = spread(wide, gain_part, 3)
         other = moved(wide, (0, 1, 0, 0))
         if g == GROUPS - 1:
             other, gain_part = spread(other, gain_part, 4)
-        first = jnp.where(core == 0, wide, other)
-        second = jnp.where(core == 0, other, wide)
-        pieces += [first.reshape(-1, width), second.reshape(-1, width)]
+        pieces += [wide.reshape(-1, width), other.reshape(-1, width)]
     gain_grad = jnp.sum(gain_part, axis=0) * scale
-    weight_grad = (jnp.concatenate(pieces, axis=0) * scale).astype(BF16)
+    weight_grad = join_call(info, pieces, scale)
     return (output.reshape(seqs, span, width), weight_grad, gain_grad)
 
 

time: 191 us -> 175 us (0.916)
  waiting for transfers between devices: 50.6 us -> 33 us
  Pallas kernels: 44 us -> 50.4 us
  other arithmetic: 8.09 us -> 4.97 us
  local copies, waits for them, and re-layouts: 17 us -> 14.7 us
    ppermute x38 -> x32, waiting for transfers between devices: 44.4 us -> 29.7 us  [moved(): return lax.ppermute(array, both, route)]
    ppermute x38 -> x32, starting transfers between devices: 63.7 us -> 52.8 us  [moved(): return lax.ppermute(array, both, route)]
    ppermute x0 -> x6, starting transfers between devices: none -> 10.1 us  [lifted(): return lax.ppermute(array, 'tm', route)]
    pallas_call x12, Pallas kernels: 11.4 us -> 17.7 us  [the longest x1 3.31 us: back_call(): pl.pallas_call(back_kernel, out_shape=jax.ShapeDtypeStruct((count, width)...]
    ppermute x5, waiting for transfers between devices: 6.13 us -> 2.91 us  [spread(): lax.ppermute(part, axis, [(i, i ^ reach) for i in range(size)])]
    unnamed x35 -> x34, local copies, waits for them, and re-layouts: 15.3 us -> 13.2 us
  transfers between devices with their start and end apart: 43 -> 43, of which waited for: 20 -> 13; matrix products, arithmetic and copies ran while one was open for 3% -> 4% of each run, Pallas kernels for 17% -> 20%
where the time goes in v3:
time: 175 us; the launch traced here: 174 us
  starting transfers between devices  69.5 us (40%)
  Pallas kernels  50.4 us (29%)
  waiting for transfers between devices  33 us (19%)
  local copies, waits for them, and re-layouts  14.7 us (8%)
  other arithmetic  4.97 us (3%)
    ppermute x32, starting transfers between devices, moved(): return lax.ppermute(array, both, route)  52.8 us
    ppermute x32, waiting for transfers between devices, moved(): return lax.ppermute(array, both, route)  29.7 us
    pallas_call x2, Pallas kernels, local_call(): pl.pallas_call(functools.partial(local_kernel, first_head, heads, span, P...  22.2 us
    unnamed x34, local copies, waits for them, and re-layouts  13.2 us
    pallas_call x2, Pallas kernels, mix_call(): pl.pallas_call(functools.partial(mix_kernel, span), out_shape=(jax.ShapeD...  10.4 us
    ppermute x6, starting transfers between devices, lifted(): return lax.ppermute(array, 'tm', route)  10.1 us
    ppermute x5, starting transfers between devices, spread(): lax.ppermute(part, axis, [(i, i ^ reach) for i in range(size)])  6.6 us
  transfers between devices with their start and end apart: 43, of which 13 were waited for; matrix products, arithmetic and copies ran while one was open for 4% of the time, Pallas kernels for 20%

profile of v3, /device:TPU:0, one launch (start us, length us, event | category | flops | bytes accessed | tf_op | source)
XLA Modules:
  0.0 173.8 jit_solution(10310618230543765762)
XLA Ops:
  4.0 2.0 %gates.1.gate_ref = f32[512,16]{1,0:T(8,128)S(1)} custom-call(bf16[512,1024]{1,0:T(8,128)(2,1)S(1)} %bitcast.103, bf16[16,1024]{1,0:T(8,128)(2,1)S(1)} %bitcast.106, f32[8]{0:T(128)S(1)} %copy-done.11, f32[8]{0:T(128)S(1)} %copy-done.12), custom_call_target="tpu_custom_call" | custom-call | flops 134217728 | bytes 1048576 | tf_op jit(solution)/shard_map/gates/pallas_call | solution.py:88
  10.2 11.2 %local.2 = (f32[4,128,256]{2,1,0:T(8,128)S(1)}, f32[4,128,256]{2,1,0:T(8,128)S(1)}, f32[512,512]{1,0:T(8,128)S(1)}, f32[512,512]{1,0:T(8,128)S(1)}) custom-call(s32[3]{0:T(128)S(1)} %pad_add_fusion.info, s32[4,24]{1,0:T(4,128)S(1)} %bitcast.109, s32[4,24]{1,0:T(4,128)S(1)} %bitcast.111, bf16[512,1024]{1,0:T(8,128)(2,1)S(1)} %bitcast.104, ...), custom_call_target="tpu_custom_call" | custom-call | flops 6442450944 | bytes 8388608 | tf_op jit(solution)/shard_map/local/pallas_call | solution.py:185
  21.4 3.0 %collective-permute-start = (f32[4,128,256]{2,1,0:T(8,128)S(1)}, f32[4,128,256]{2,1,0:T(8,128)S(1)}, u32[]{:S(2)}, u32[]{:S(2)}) collective-permute-start(f32[4,128,256]{2,1,0:T(8,128)S(1)} %get-tuple-element.54), channel_id=1, source_target_pairs={{0,1},{1,0},{2,3},{3,2},{4,5},{5,4},{6,7},{7,6},{8,9},{9,8},{10,11... | collective-permute-start | bytes 1572872 | tf_op jit(solution)/shard_map/ppermute | solution.py:427
  24.4 11.1 %local.3 = (f32[4,128,256]{2,1,0:T(8,128)S(1)}, f32[4,128,256]{2,1,0:T(8,128)S(1)}, f32[512,512]{1,0:T(8,128)S(1)}, f32[512,512]{1,0:T(8,128)S(1)}) custom-call(s32[3]{0:T(128)S(1)} %pad_add_fusion.info, s32[4,24]{1,0:T(4,128)S(1)} %bitcast.110, s32[4,24]{1,0:T(4,128)S(1)} %bitcast.112, bf16[512,1024]{1,0:T(8,128)(2,1)S(1)} %bitcast.105, ...), custom_call_target="tpu_custom_call" | custom-call | flops 6442450944 | bytes 8388608 | tf_op jit(solution)/shard_map/local/pallas_call | solution.py:185
  37.4 3.9 %collective-permute-start.1 = (f32[4,128,128]{2,1,0:T(8,128)S(1)}, f32[4,128,128]{2,1,0:T(8,128)S(1)}, u32[]{:S(2)}, u32[]{:S(2)}) collective-permute-start(f32[4,128,128]{2,1,0:T(8,128)S(1)} %get-tuple-element.57), channel_id=1, source_target_pairs={{0,2},{1,3},{2,0},{3,1},{8,10},{9,11},{10,8},{11,9},{16,18},{17,19... | collective-permute-start | bytes 786440 | tf_op jit(solution)/shard_map/ppermute | solution.py:432
  41.2 7.8 %collective-permute-done.5.got_ref = f32[4,128,256]{2,1,0:T(8,128)S(1)} collective-permute-done((f32[4,128,256]{2,1,0:T(8,128)S(1)}, f32[4,128,256]{2,1,0:T(8,128)S(1)}, u32[]{:S(2)}, u32[]{:S(2)}) %collective-permute-start.5) | collective-permute-done | bytes 524320 | tf_op jit(solution)/shard_map/ppermute | solution.py:427
  50.0 3.5 %collective-permute-start.6 = (f32[4,128,128]{2,1,0:T(8,128)S(1)}, f32[4,128,128]{2,1,0:T(8,128)S(1)}, u32[]{:S(2)}, u32[]{:S(2)}) collective-permute-start(f32[4,128,128]{2,1,0:T(8,128)S(1)} %get-tuple-element.66), channel_id=1, source_target_pairs={{0,2},{1,3},{2,0},{3,1},{8,10},{9,11},{10,8},{11,9},{16,18},{17,19... | collective-permute-start | bytes 786440 | tf_op jit(solution)/shard_map/ppermute | solution.py:432
  55.1 3.3 %back.1.back_ref = f32[512,1024]{1,0:T(8,128)S(1)} custom-call(bf16[512,1024]{1,0:T(8,128)(2,1)S(1)} %bitcast.97, bf16[1024,1024]{1,0:T(8,128)(2,1)S(1)} %copy-done.1), custom_call_target="tpu_custom_call" | custom-call | flops 1073741824 | bytes 5242880 | tf_op jit(solution)/shard_map/back/pallas_call | solution.py:349
  67.1 6.1 %collective-permute-done.4.got_ref = f32[4,128,128]{2,1,0:T(8,128)S(1)} collective-permute-done((f32[4,128,128]{2,1,0:T(8,128)S(1)}, f32[4,128,128]{2,1,0:T(8,128)S(1)}, u32[]{:S(2)}, u32[]{:S(2)}) %collective-permute-start.4) | collective-permute-done | bytes 262176 | tf_op jit(solution)/shard_map/ppermute | solution.py:427
  73.2 5.2 %mix.2 = (bf16[512,512]{1,0:T(8,128)(2,1)S(1)}, f32[2,128,1024]{2,1,0:T(8,128)}, f32[2,128,1024]{2,1,0:T(8,128)S(1)}, f32[8,128]{1,0:T(8,128)S(1)}) custom-call(s32[3]{0:T(128)S(1)} %pad_add_fusion.info, f32[512,512]{1,0:T(8,128)S(1)} %get-tuple-element.51.core_ref, f32[512,512]{1,0:T(8,128)S(1)} %get-tuple-element.52.query_ref, ...), custom_call_target="tpu_custom_call" | custom-call | flops 536870912 | bytes 6291456 | tf_op jit(solution)/shard_map/mix/pallas_call | solution.py:322
  80.3 5.2 %mix.3 = (bf16[512,512]{1,0:T(8,128)(2,1)S(1)}, f32[2,128,1024]{2,1,0:T(8,128)}, f32[2,128,1024]{2,1,0:T(8,128)S(1)}, f32[8,128]{1,0:T(8,128)S(1)}) custom-call(s32[3]{0:T(128)S(1)} %pad_add_fusion.info, f32[512,512]{1,0:T(8,128)S(1)} %get-tuple-element.70.core_ref, f32[512,512]{1,0:T(8,128)S(1)} %get-tuple-element.71.query_ref, ...), custom_call_target="tpu_custom_call" | custom-call | flops 536870912 | bytes 6291456 | tf_op jit(solution)/shard_map/mix/pallas_call | solution.py:322
  96.0 2.8 %finish.1 = bf16[512,1024]{1,0:T(8,128)(2,1)} custom-call(bf16[512,512]{1,0:T(8,128)(2,1)S(1)} %copy-done.8, bf16[512,512]{1,0:T(8,128)(2,1)S(1)} %copy-done.6, bf16[1024,1024]{1,0:T(8,128)(2,1)S(1)} %copy-done.1), custom_call_target="tpu_custom_call" | custom-call | flops 1073741824 | bytes 4194304 | tf_op jit(solution)/shard_map/finish/pallas_call | solution.py:372
  108.4 6.6 %collective-permute-start.29 = (f32[16,1024]{1,0:T(8,128)S(1)}, f32[16,1024]{1,0:T(8,128)S(1)}, u32[]{:S(2)}, u32[]{:S(2)}) collective-permute-start(f32[16,1024]{1,0:T(8,128)S(1)} %get-tuple-element.107), channel_id=1, source_target_pairs={{0,2},{1,3},{2,0},{3,1},{4,6},{5,7},{6,4},{7,5},{8,10},{9,11},{10,... | collective-permute-start | bytes 196616 | tf_op jit(solution)/shard_map/ppermute | solution.py:427
  115.0 7.0 %collective-permute-start.30 = (f32[16,1024]{1,0:T(8,128)S(1)}, f32[16,1024]{1,0:T(8,128)S(1)}, u32[]{:S(2)}, u32[]{:S(2)}) collective-permute-start(f32[16,1024]{1,0:T(8,128)S(1)} %get-tuple-element.109), channel_id=1, source_target_pairs={{0,4},{1,5},{2,6},{3,7},{4,0},{5,1},{6,2},{7,3},{8,12},{9,13},{10,... | collective-permute-start | bytes 196616 | tf_op jit(solution)/shard_map/ppermute | solution.py:427
  124.1 5.0 %collective-permute-start.20 = (f32[16,1024]{1,0:T(8,128)S(1)}, f32[16,1024]{1,0:T(8,128)S(1)}, u32[]{:S(2)}, u32[]{:S(2)}) collective-permute-start(f32[16,1024]{1,0:T(8,128)S(1)} %get-tuple-element.112), channel_id=1, source_target_pairs={{0,4},{1,5},{2,6},{3,7},{4,0},{5,1},{6,2},{7,3},{8,12},{9,13},{10,... | collective-permute-start | bytes 196616 | tf_op jit(solution)/shard_map/ppermute | solution.py:427
  129.8 3.7 %collective-permute-start.34 = (f32[16,1024]{1,0:T(8,128)S(1)}, f32[16,1024]{1,0:T(8,128)S(1)}, u32[]{:S(2)}, u32[]{:S(2)}) collective-permute-start(f32[16,1024]{1,0:T(8,128)S(1)} %fusion.5), channel_id=1, source_target_pairs={{0,4},{1,5},{2,6},{3,7},{4,0},{5,1},{6,2},{7,3},{8,12},{9,13},{10,... | collective-permute-start | bytes 196616 | tf_op jit(solution)/shard_map/ppermute | solution.py:427
  135.2 2.9 %collective-permute-start.22 = (f32[16,1024]{1,0:T(8,128)S(1)}, f32[16,1024]{1,0:T(8,128)S(1)}, u32[]{:S(2)}, u32[]{:S(2)}) collective-permute-start(f32[16,1024]{1,0:T(8,128)S(1)} %get-tuple-element.100), channel_id=1, source_target_pairs={{0,2},{1,3},{2,0},{3,1},{4,6},{5,7},{6,4},{7,5},{8,10},{9,11},{10,... | collective-permute-start | bytes 196616 | tf_op jit(solution)/shard_map/ppermute | solution.py:427
  138.1 2.2 %collective-permute-start.23 = (f32[16,1024]{1,0:T(8,128)S(1)}, f32[16,1024]{1,0:T(8,128)S(1)}, u32[]{:S(2)}, u32[]{:S(2)}) collective-permute-start(f32[16,1024]{1,0:T(8,128)S(1)} %get-tuple-element.100), channel_id=1, source_target_pairs={{0,4},{1,5},{2,6},{3,7},{4,0},{5,1},{6,2},{7,3},{8,12},{9,13},{10,... | collective-permute-start | bytes 196616 | tf_op jit(solution)/shard_map/ppermute | solution.py:427
  151.1 3.5 %collective-permute-done.37 = f32[4,16,1024]{2,1,0:T(8,128)S(1)} collective-permute-done((f32[4,16,1024]{2,1,0:T(8,128)S(1)}, f32[4,16,1024]{2,1,0:T(8,128)S(1)}, u32[]{:S(2)}, u32[]{:S(2)}) %collective-permute-start.37) | collective-permute-done | bytes 262176 | tf_op jit(solution)/shard_map/ppermute | solution.py:427
  156.1 2.3 %collective-permute-done.39 = f32[4,16,1024]{2,1,0:T(8,128)S(1)} collective-permute-done((f32[4,16,1024]{2,1,0:T(8,128)S(1)}, f32[4,16,1024]{2,1,0:T(8,128)S(1)}, u32[]{:S(2)}, u32[]{:S(2)}) %collective-permute-start.39) | collective-permute-done | bytes 262176 | tf_op jit(solution)/shard_map/ppermute | solution.py:427
  158.6 3.6 %collective-permute-done.25 = f32[4,16,1024]{2,1,0:T(8,128)S(1)} collective-permute-done((f32[4,16,1024]{2,1,0:T(8,128)S(1)}, f32[4,16,1024]{2,1,0:T(8,128)S(1)}, u32[]{:S(2)}, u32[]{:S(2)}) %collective-permute-start.25) | collective-permute-done | bytes 262176 | tf_op jit(solution)/shard_map/ppermute | solution.py:427
  162.3 2.8 %collective-permute-done.27 = f32[4,16,1024]{2,1,0:T(8,128)S(1)} collective-permute-done((f32[4,16,1024]{2,1,0:T(8,128)S(1)}, f32[4,16,1024]{2,1,0:T(8,128)S(1)}, u32[]{:S(2)}, u32[]{:S(2)}) %collective-permute-start.27) | collective-permute-done | bytes 262176 | tf_op jit(solution)/shard_map/ppermute | solution.py:427
  165.2 3.7 %collective-permute-start.42 = (f32[8,128]{1,0:T(8,128)S(1)}, f32[8,128]{1,0:T(8,128)S(1)}, u32[]{:S(2)}, u32[]{:S(2)}) collective-permute-start(f32[8,128]{1,0:T(8,128)S(1)} %add.177), channel_id=1, source_target_pairs={{0,4},{1,5},{2,6},{3,7},{4,0},{5,1},{6,2},{7,3},{8,12},{9,13},{10,... | collective-permute-start | bytes 12296 | tf_op jit(solution)/shard_map/ppermute | solution.py:472
  171.0 2.8 %join.1 = bf16[1024,1024]{1,0:T(8,128)(2,1)} custom-call(s32[3]{0:T(128)S(1)} %pad_add_fusion.info, f32[256,1024]{1,0:T(8,128)S(1)} %bitcast.100, f32[256,1024]{1,0:T(8,128)} %bitcast.33.refs_1_, f32[256,1024]{1,0:T(8,128)S(1)} %bitcast.101, f32[256,1024]{1,0:T(8,128)S(1)} %bitcast.102), custom_call_target="tpu_custom_call" | custom-call | tf_op jit(solution)/shard_map/join/pallas_call | solution.py:396
  (151 shorter events, 61.3 us)
Async XLA Ops:
  21.4 15.0 %collective-permute-start = (f32[4,128,256]{2,1,0:T(8,128)S(1)}, f32[4,128,256]{2,1,0:T(8,128)S(1)}, u32[]{:S(2)}, u32[]{:S(2)}) collective-permute-start(f32[4,128,256]{2,1,0:T(8,128)S(1)} %get-tuple-element.54), channel_id=1, source_target_pairs={{0,1},{1,0},{2,3},{3,2},{4,5},{5,4},{6,7},{7,6},{8,9},{9,8},{10,11... | collective-permute-start | bytes 1572872 | tf_op jit(solution)/shard_map/ppermute | solution.py:427
  35.6 13.4 %collective-permute-start.5 = (f32[4,128,256]{2,1,0:T(8,128)S(1)}, f32[4,128,256]{2,1,0:T(8,128)S(1)}, u32[]{:S(2)}, u32[]{:S(2)}) collective-permute-start(f32[4,128,256]{2,1,0:T(8,128)S(1)} %get-tuple-element.65), channel_id=1, source_target_pairs={{0,1},{1,0},{2,3},{3,2},{4,5},{5,4},{6,7},{7,6},{8,9},{9,8},{10,11... | collective-permute-start | bytes 1572872 | tf_op jit(solution)/shard_map/ppermute | solution.py:427
  37.4 16.2 %collective-permute-start.1 = (f32[4,128,128]{2,1,0:T(8,128)S(1)}, f32[4,128,128]{2,1,0:T(8,128)S(1)}, u32[]{:S(2)}, u32[]{:S(2)}) collective-permute-start(f32[4,128,128]{2,1,0:T(8,128)S(1)} %get-tuple-element.57), channel_id=1, source_target_pairs={{0,2},{1,3},{2,0},{3,1},{8,10},{9,11},{10,8},{11,9},{16,18},{17,19... | collective-permute-start | bytes 786440 | tf_op jit(solution)/shard_map/ppermute | solution.py:432
  65.7 14.6 %collective-permute-start.13 = (f32[4,128,128]{2,1,0:T(8,128)S(1)}, f32[4,128,128]{2,1,0:T(8,128)S(1)}, u32[]{:S(2)}, u32[]{:S(2)}) collective-permute-start(f32[4,128,128]{2,1,0:T(8,128)S(1)} %get-tuple-element.80), channel_id=1, source_target_pairs={{0,1},{1,0},{2,3},{3,2},{4,5},{5,4},{6,7},{7,6},{8,9},{9,8},{10,11... | collective-permute-start | bytes 786440 | tf_op jit(solution)/shard_map/ppermute | solution.py:427
  86.3 12.5 %collective-permute-start.15 = (f32[2,128,1024]{2,1,0:T(8,128)}, f32[2,128,1024]{2,1,0:T(8,128)}, u32[]{:S(2)}, u32[]{:S(2)}) collective-permute-start(f32[2,128,1024]{2,1,0:T(8,128)} %get-tuple-element.88), channel_id=1, source_target_pairs={{0,8},{1,9},{2,10},{3,11},{4,12},{5,13},{6,14},{7,15},{8,0},{9,1},... | collective-permute-start | bytes 3145736 | tf_op jit(solution)/shard_map/ppermute | solution.py:427
  90.4 11.9 %collective-permute-start.10 = (f32[4,16,1024]{2,1,0:T(8,128)}, f32[4,16,1024]{2,1,0:T(8,128)S(1)}, u32[]{:S(2)}, u32[]{:S(2)}) collective-permute-start(f32[4,16,1024]{2,1,0:T(8,128)} %get-tuple-element.105), channel_id=1, source_target_pairs={{0,17},{1,16},{2,19},{3,18},{4,21},{5,20},{6,23},{7,22},{8,25},{9,... | collective-permute-start | bytes 786440 | tf_op jit(solution)/shard_map/ppermute | solution.py:427
  91.9 13.7 %collective-permute-start.8 = (f32[4,16,1024]{2,1,0:T(8,128)}, f32[4,16,1024]{2,1,0:T(8,128)}, u32[]{:S(2)}, u32[]{:S(2)}) collective-permute-start(f32[4,16,1024]{2,1,0:T(8,128)} %get-tuple-element.104), channel_id=1, source_target_pairs={{0,1},{1,0},{2,3},{3,2},{4,5},{5,4},{6,7},{7,6},{8,9},{9,8},{10,11... | collective-permute-start | bytes 786440 | tf_op jit(solution)/shard_map/ppermute | solution.py:427
  93.4 12.2 %collective-permute-start.9 = (f32[4,16,1024]{2,1,0:T(8,128)}, f32[4,16,1024]{2,1,0:T(8,128)}, u32[]{:S(2)}, u32[]{:S(2)}) collective-permute-start(f32[4,16,1024]{2,1,0:T(8,128)} %get-tuple-element.106), channel_id=1, source_target_pairs={{0,16},{1,17},{2,18},{3,19},{4,20},{5,21},{6,22},{7,23},{8,24},{9,... | collective-permute-start | bytes 786440 | tf_op jit(solution)/shard_map/ppermute | solution.py:427
  100.2 14.7 %collective-permute-start.16 = (f32[4,16,1024]{2,1,0:T(8,128)S(1)}, f32[4,16,1024]{2,1,0:T(8,128)S(1)}, u32[]{:S(2)}, u32[]{:S(2)}) collective-permute-start(f32[4,16,1024]{2,1,0:T(8,128)S(1)} %get-tuple-element.101), channel_id=1, source_target_pairs={{0,1},{1,0},{2,3},{3,2},{4,5},{5,4},{6,7},{7,6},{8,9},{9,8},{10,11... | collective-permute-start | bytes 786440 | tf_op jit(solution)/shard_map/ppermute | solution.py:427
  101.0 21.0 %collective-permute-start.17 = (f32[4,16,1024]{2,1,0:T(8,128)S(1)}, f32[4,16,1024]{2,1,0:T(8,128)S(1)}, u32[]{:S(2)}, u32[]{:S(2)}) collective-permute-start(f32[4,16,1024]{2,1,0:T(8,128)S(1)} %get-tuple-element.103), channel_id=1, source_target_pairs={{0,16},{1,17},{2,18},{3,19},{4,20},{5,21},{6,22},{7,23},{8,24},{9,... | collective-permute-start | bytes 786440 | tf_op jit(solution)/shard_map/ppermute | solution.py:427
  102.3 21.0 %collective-permute-start.18 = (f32[4,16,1024]{2,1,0:T(8,128)S(1)}, f32[4,16,1024]{2,1,0:T(8,128)S(1)}, u32[]{:S(2)}, u32[]{:S(2)}) collective-permute-start(f32[4,16,1024]{2,1,0:T(8,128)S(1)} %get-tuple-element.102), channel_id=1, source_target_pairs={{0,17},{1,16},{2,19},{3,18},{4,21},{5,20},{6,23},{7,22},{8,25},{9,... | collective-permute-start | bytes 786440 | tf_op jit(solution)/shard_map/ppermute | solution.py:427
  106.8 17.3 %collective-permute-start.32 = (f32[8,128]{1,0:T(8,128)S(1)}, f32[8,128]{1,0:T(8,128)S(1)}, u32[]{:S(2)}, u32[]{:S(2)}) collective-permute-start(f32[8,128]{1,0:T(8,128)S(1)} %add.160), channel_id=1, source_target_pairs={{0,16},{8,24},{16,0},{24,8},{1,17},{9,25},{17,1},{25,9},{2,18},{10... | collective-permute-start | bytes 12296 | tf_op jit(solution)/shard_map/ppermute | solution.py:472
  108.4 20.7 %collective-permute-start.29 = (f32[16,1024]{1,0:T(8,128)S(1)}, f32[16,1024]{1,0:T(8,128)S(1)}, u32[]{:S(2)}, u32[]{:S(2)}) collective-permute-start(f32[16,1024]{1,0:T(8,128)S(1)} %get-tuple-element.107), channel_id=1, source_target_pairs={{0,2},{1,3},{2,0},{3,1},{4,6},{5,7},{6,4},{7,5},{8,10},{9,11},{10,... | collective-permute-start | bytes 196616 | tf_op jit(solution)/shard_map/ppermute | solution.py:427
  115.0 14.1 %collective-permute-start.30 = (f32[16,1024]{1,0:T(8,128)S(1)}, f32[16,1024]{1,0:T(8,128)S(1)}, u32[]{:S(2)}, u32[]{:S(2)}) collective-permute-start(f32[16,1024]{1,0:T(8,128)S(1)} %get-tuple-element.109), channel_id=1, source_target_pairs={{0,4},{1,5},{2,6},{3,7},{4,0},{5,1},{6,2},{7,3},{8,12},{9,13},{10,... | collective-permute-start | bytes 196616 | tf_op jit(solution)/shard_map/ppermute | solution.py:427
  123.4 10.1 %collective-permute-start.19 = (f32[16,1024]{1,0:T(8,128)S(1)}, f32[16,1024]{1,0:T(8,128)S(1)}, u32[]{:S(2)}, u32[]{:S(2)}) collective-permute-start(f32[16,1024]{1,0:T(8,128)S(1)} %get-tuple-element.110), channel_id=1, source_target_pairs={{0,2},{1,3},{2,0},{3,1},{4,6},{5,7},{6,4},{7,5},{8,10},{9,11},{10,... | collective-permute-start | bytes 196616 | tf_op jit(solution)/shard_map/ppermute | solution.py:427
  129.1 11.3 %collective-permute-start.33 = (f32[16,1024]{1,0:T(8,128)S(1)}, f32[16,1024]{1,0:T(8,128)S(1)}, u32[]{:S(2)}, u32[]{:S(2)}) collective-permute-start(f32[16,1024]{1,0:T(8,128)S(1)} %fusion.5), channel_id=1, source_target_pairs={{0,2},{1,3},{2,0},{3,1},{4,6},{5,7},{6,4},{7,5},{8,10},{9,11},{10,... | collective-permute-start | bytes 196616 | tf_op jit(solution)/shard_map/ppermute | solution.py:427
  129.8 12.2 %collective-permute-start.34 = (f32[16,1024]{1,0:T(8,128)S(1)}, f32[16,1024]{1,0:T(8,128)S(1)}, u32[]{:S(2)}, u32[]{:S(2)}) collective-permute-start(f32[16,1024]{1,0:T(8,128)S(1)} %fusion.5), channel_id=1, source_target_pairs={{0,4},{1,5},{2,6},{3,7},{4,0},{5,1},{6,2},{7,3},{8,12},{9,13},{10,... | collective-permute-start | bytes 196616 | tf_op jit(solution)/shard_map/ppermute | solution.py:427
  142.0 12.7 %collective-permute-start.37 = (f32[4,16,1024]{2,1,0:T(8,128)S(1)}, f32[4,16,1024]{2,1,0:T(8,128)S(1)}, u32[]{:S(2)}, u32[]{:S(2)}) collective-permute-start(f32[4,16,1024]{2,1,0:T(8,128)S(1)} %bitcast_dynamic-update-slice_fusion.8), channel_id=1, source_target_pairs={{0,1},{1,0},{2,3},{3,2},{4,5},{5,4},{6,7},{7,6},{8,9},{9,8},{10,11... | collective-permute-start | bytes 786440 | tf_op jit(solution)/shard_map/ppermute | solution.py:427
  143.3 12.8 %collective-permute-start.38 = (f32[4,16,1024]{2,1,0:T(8,128)S(1)}, f32[4,16,1024]{2,1,0:T(8,128)S(1)}, u32[]{:S(2)}, u32[]{:S(2)}) collective-permute-start(f32[4,16,1024]{2,1,0:T(8,128)S(1)} %bitcast_dynamic-update-slice_fusion.8), channel_id=1, source_target_pairs={{0,16},{1,17},{2,18},{3,19},{4,20},{5,21},{6,22},{7,23},{8,24},{9,... | collective-permute-start | bytes 786440 | tf_op jit(solution)/shard_map/ppermute | solution.py:427
  144.2 14.3 %collective-permute-start.39 = (f32[4,16,1024]{2,1,0:T(8,128)S(1)}, f32[4,16,1024]{2,1,0:T(8,128)S(1)}, u32[]{:S(2)}, u32[]{:S(2)}) collective-permute-start(f32[4,16,1024]{2,1,0:T(8,128)S(1)} %bitcast_dynamic-update-slice_fusion.8), channel_id=1, source_target_pairs={{0,17},{1,16},{2,19},{3,18},{4,21},{5,20},{6,23},{7,22},{8,25},{9,... | collective-permute-start | bytes 786440 | tf_op jit(solution)/shard_map/ppermute | solution.py:427
  146.6 15.6 %collective-permute-start.25 = (f32[4,16,1024]{2,1,0:T(8,128)S(1)}, f32[4,16,1024]{2,1,0:T(8,128)S(1)}, u32[]{:S(2)}, u32[]{:S(2)}) collective-permute-start(f32[4,16,1024]{2,1,0:T(8,128)S(1)} %bitcast_dynamic-update-slice_fusion.12), channel_id=1, source_target_pairs={{0,1},{1,0},{2,3},{3,2},{4,5},{5,4},{6,7},{7,6},{8,9},{9,8},{10,11... | collective-permute-start | bytes 786440 | tf_op jit(solution)/shard_map/ppermute | solution.py:427
  149.5 12.8 %collective-permute-start.26 = (f32[4,16,1024]{2,1,0:T(8,128)S(1)}, f32[4,16,1024]{2,1,0:T(8,128)S(1)}, u32[]{:S(2)}, u32[]{:S(2)}) collective-permute-start(f32[4,16,1024]{2,1,0:T(8,128)S(1)} %bitcast_dynamic-update-slice_fusion.12), channel_id=1, source_target_pairs={{0,16},{1,17},{2,18},{3,19},{4,20},{5,21},{6,22},{7,23},{8,24},{9,... | collective-permute-start | bytes 786440 | tf_op jit(solution)/shard_map/ppermute | solution.py:427
  154.6 10.4 %collective-permute-start.27 = (f32[4,16,1024]{2,1,0:T(8,128)S(1)}, f32[4,16,1024]{2,1,0:T(8,128)S(1)}, u32[]{:S(2)}, u32[]{:S(2)}) collective-permute-start(f32[4,16,1024]{2,1,0:T(8,128)S(1)} %bitcast_dynamic-update-slice_fusion.12), channel_id=1, source_target_pairs={{0,17},{1,16},{2,19},{3,18},{4,21},{5,20},{6,23},{7,22},{8,25},{9,... | collective-permute-start | bytes 786440 | tf_op jit(solution)/shard_map/ppermute | solution.py:427
  158.5 12.0 %collective-permute-start.41 = (f32[4,4,16,1024]{3,2,1,0:T(8,128)S(1)}, f32[4,4,16,1024]{3,2,1,0:T(8,128)S(1)}, u32[]{:S(2)}, u32[]{:S(2)}) collective-permute-start(f32[4,4,16,1024]{3,2,1,0:T(8,128)S(1)} %bitcast_dynamic-update-slice_fusion), channel_id=1, source_target_pairs={{0,8},{1,9},{2,10},{3,11},{4,12},{5,13},{6,14},{7,15},{8,0},{9,1},... | collective-permute-start | bytes 3145736 | tf_op jit(solution)/shard_map/ppermute | solution.py:427
  (36 other events, 180.4 us)

commit v4 on v3

--- a/solution.py
+++ b/solution.py
@@ -8,10 +8,12 @@
 from jax.experimental.pallas import tpu as pltpu
 from jax.sharding import PartitionSpec as P
 
-GROUPS = 2
+GROUPS = 4
+SUMS = 2
 CORES = 2
 PAIR = 2
 PER_STEP = 2
+AHEAD = 3
 F32 = jnp.float32
 BF16 = jnp.bfloat16
 MIB = 1024 * 1024
@@ -60,13 +62,13 @@
     return pl.CostEstimate(flops=flops, bytes_accessed=size, transcendentals=0)
 
 
-def gates_kernel(span, heads, x_ref, w_ref, rate_ref, bias_ref, out_ref):
+def write_gates(span, heads, x_ref, w_ref, level_ref, out_ref):
     lane = lax.broadcasted_iota(jnp.int32, (1, heads), 1)
     rate = jnp.zeros((1, heads), F32)
     bias = jnp.zeros((1, heads), F32)
     for h in range(heads):
-        rate = jnp.where(lane == h, rate_ref[h], rate)
-        bias = jnp.where(lane == h, bias_ref[h], bias)
+        rate = jnp.where(lane == h, level_ref[0, h], rate)
+        bias = jnp.where(lane == h, level_ref[1, h], bias)
     gates = dot_nt(x_ref[...], w_ref[...])
     raw = gates[:, :heads]
     softplus = jnp.maximum(raw, 0.0) + jnp.log1p(jnp.exp(-jnp.abs(raw)))
@@ -80,19 +82,6 @@
         out_ref[first : first + span, :heads] = lax.dot_general(
             lower, piece, (((1,), (0,)), ((), ())), precision=lax.Precision.HIGHEST, preferred_element_type=F32
         )
-
-
-def gates_call(rows, gate_weight, decay_rate, beta_bias, span):
-    count, width = rows.shape
-    heads = decay_rate.shape[0]
-    return pl.pallas_call(
-        functools.partial(gates_kernel, span, heads),
-        out_shape=jax.ShapeDtypeStruct((count, 2 * heads), F32),
-        in_specs=[vmem(), vmem(), smem(), smem()],
-        compiler_params=params(12),
-        cost_estimate=cost(2 * count * width * 128, count * width * 2),
-        name="gates",
-    )(rows, gate_weight.T, decay_rate, beta_bias)
 
 
 def solve_lower(systems, rights):
@@ -114,10 +103,17 @@
     return [f + dot(i, r.astype(BF16)) for f, i, r in zip(firsts, invs, residuals)]
 
 
-def local_kernel(
-    first_head, heads, span, per_step, info, pin, ppool, x_ref, pool_ref, gate_ref, own_ref, send_ref, core_ref, query_ref
-):
-    members = pin.shape[0]
+def local_kernel(first_head, heads, span, per_step, opening, info, table, x_ref, pool_ref, *refs):
+    if opening:
+        w_ref, level_ref, own_ref, send_ref, core_ref, query_ref, gate_ref = refs
+
+        @pl.when(pl.program_id(0) == 0)
+        def _():
+            write_gates(span, heads, x_ref, w_ref, level_ref, gate_ref)
+
+    else:
+        gate_ref, own_ref, send_ref, core_ref, query_ref = refs
+    members = table.shape[1]
     dims = pool_ref.shape[1]
     lane = lax.broadcasted_iota(jnp.int32, (span, 2 * heads), 1)
     wide = lax.broadcasted_iota(jnp.int32, (span, dims), 1)
@@ -133,7 +129,7 @@
         chosen = []
         for kind in range(3):
             target = kind * heads + head
-            chosen.append(jnp.concatenate([pool_ref[ppool[j, target]] for j in range(members)], 0))
+            chosen.append(jnp.concatenate([pool_ref[table[1, j, target]] for j in range(members)], 0))
         for part in range(2):
             seq = info[0] if part == 0 else 1 - info[0]
             where.append((local, part, pl.ds(pl.multiple_of(seq * span, span), span)))
@@ -141,7 +137,7 @@
             for kind in range(3):
                 target = kind * heads + head
                 picked = [
-                    x_ref[where[-1][2], pl.ds(pl.multiple_of(pin[j, target] * dims, dims), dims)]
+                    x_ref[where[-1][2], pl.ds(pl.multiple_of(table[0, j, target] * dims, dims), dims)]
                     for j in range(members)
                 ]
                 projected.append(dot(jnp.concatenate(picked, 1), chosen[kind]).astype(BF16))
@@ -175,26 +171,33 @@
         core_ref[rows, lanes] = seen[:, dims:]
 
 
-def local_call(info, pin, ppool, rows, pool, gates, first_head, count_heads, heads, span):
+def local_call(info, table, rows, pool, extra, first_head, count_heads, heads, span):
     count, width = rows.shape
     dims = pool.shape[1]
+    opening = isinstance(extra, tuple)
     maps = jax.ShapeDtypeStruct((count_heads, dims, 2 * dims), F32)
     wide = jax.ShapeDtypeStruct((count, count_heads * dims), F32)
+    gates = jax.ShapeDtypeStruct((count, 2 * heads), F32)
     map_spec = pl.BlockSpec((PER_STEP, dims, 2 * dims), lambda i, *_: (i, 0, 0))
     row_spec = pl.BlockSpec((count, PER_STEP * dims), lambda i, *_: (0, i))
-    return pl.pallas_call(
-        functools.partial(local_kernel, first_head, heads, span, PER_STEP),
-        out_shape=(maps, maps, wide, wide),
+    if opening:
+        more_in = [whole(extra[0].shape), smem()]
+        more_out, more_out_specs = (gates,), (whole(gates.shape),)
+    else:
+        more_in, more_out, more_out_specs, extra = [whole(gates.shape)], (), (), (extra,)
+    return pl.pallas_call(
+        functools.partial(local_kernel, first_head, heads, span, PER_STEP, opening),
+        out_shape=(maps, maps, wide, wide) + more_out,
         grid_spec=pltpu.PrefetchScalarGridSpec(
-            num_scalar_prefetch=3,
+            num_scalar_prefetch=2,
             grid=(count_heads // PER_STEP,),
-            in_specs=[whole(rows.shape), whole(pool.shape), whole(gates.shape)],
-            out_specs=(map_spec, map_spec, row_spec, row_spec),
+            in_specs=[whole(rows.shape), whole(pool.shape)] + more_in,
+            out_specs=(map_spec, map_spec, row_spec, row_spec) + more_out_specs,
         ),
         compiler_params=params(28),
-        cost_estimate=cost(count_heads * 2 * 2 * span * 256 * 256 * 24, 8 * 1024 * 1024),
+        cost_estimate=cost(count_heads * 2 * 2 * span * 256 * 256 * 24, 8 * MIB),
         name="local",
-    )(info, pin, ppool, rows, pool, gates)
+    )(info, table, rows, pool, *extra)
 
 
 def apply_map(maps, state):
@@ -276,33 +279,48 @@
     )(info, maps, got, state)
 
 
-def mix_kernel(
-    span, info, core_ref, query_ref, keep_ref, got_ref, back_ref, gain_ref, cot_ref, mixed_ref, wsend_ref, wkeep_ref, part_ref
-):
+def mix_kernel(span, info, core_ref, query_ref, keep_ref, got_ref, back_ref, gain_ref, cot_ref, mixed_ref, wsend_ref, wkeep_ref):
     step = pl.program_id(0)
-    half = wsend_ref.shape[0]
-
-    @pl.when(step == 0)
-    def _():
-        part_ref[...] = jnp.zeros_like(part_ref)
-
+    half = pl.num_programs(0) // 2
+    dims = gain_ref.shape[1]
+    tiles = wsend_ref.shape[0] - 1
+    each = tiles // half
+    gain_part = jnp.zeros((8, dims), F32)
     for part in range(2):
         seq = info[0] if part == 0 else 1 - info[0]
         rows = pl.ds(pl.multiple_of(seq * span, span), span)
         state = (keep_ref if part == 0 else got_ref)[0]
         core = core_ref[rows, :] + dot3(query_ref[rows, :], state)
         normal = core * lax.rsqrt(jnp.mean(core * core, axis=1, keepdims=True) + 1e-05)
-        part_ref[...] += jnp.sum((normal * back_ref[rows, :]).reshape(-1, 8, core.shape[1]), axis=0)
+        gain_part += jnp.sum((normal * back_ref[rows, :]).reshape(-1, 8, dims), axis=0)
         mixed_ref[rows, :] = (normal * gain_ref[...]).astype(BF16)
     product = dot_tn(mixed_ref[...], cot_ref[...])
+    stripe = dims // 8
+    pieces = [
+        product[:, first : first + 128].reshape(stripe, 8, 128) for first in range(0, product.shape[1], 128)
+    ]
+
+    @pl.when(step == 0)
+    def _():
+        wkeep_ref[tiles] = gain_part
+
+    @pl.when(step > 0)
+    def _():
+        wkeep_ref[tiles] += gain_part
+
+    @pl.when(step == 2 * half - 1)
+    def _():
+        wsend_ref[tiles] = wkeep_ref[tiles]
 
     @pl.when(step < half)
     def _():
-        wsend_ref[step] = product
+        for i, piece in enumerate(pieces):
+            wsend_ref[pl.ds(step * each + i * stripe, stripe)] = piece
 
     @pl.when(step >= half)
     def _():
-        wkeep_ref[step - half] = product
+        for i, piece in enumerate(pieces):
+            wkeep_ref[pl.ds((step - half) * each + i * stripe, stripe)] = piece
 
 
 def mix_call(info, first_head, core, query, keep, got, back, gain, cot, span):
@@ -318,23 +336,18 @@
     row_spec = pl.BlockSpec((count, dims), lambda i, info: (0, order(i, info)))
     back_spec = pl.BlockSpec((count, dims), lambda i, info: (0, first_head + order(i, info)))
     state_spec = pl.BlockSpec((1, dims, dims), lambda i, info: (order(i, info), 0, 0))
-    weight = jax.ShapeDtypeStruct((half, dims, width), F32)
+    weight = jax.ShapeDtypeStruct((half * dims * width // 1024 + 1, 8, 128), F32)
     return pl.pallas_call(
         functools.partial(mix_kernel, span),
-        out_shape=(
-            jax.ShapeDtypeStruct((count, heads_here * dims), BF16),
-            weight,
-            weight,
-            jax.ShapeDtypeStruct((8, dims), F32),
-        ),
+        out_shape=(jax.ShapeDtypeStruct((count, heads_here * dims), BF16), weight, weight),
         grid_spec=pltpu.PrefetchScalarGridSpec(
             num_scalar_prefetch=1,
             grid=(heads_here,),
             in_specs=[row_spec, row_spec, state_spec, state_spec, back_spec, whole(gain.shape), whole(cot.shape)],
-            out_specs=(row_spec, whole(weight.shape), whole(weight.shape), whole((8, dims))),
+            out_specs=(row_spec, whole(weight.shape), whole(weight.shape)),
         ),
-        compiler_params=params(20),
-        cost_estimate=cost(heads_here * 2 * 512 * 1024 * 128, 6 * MIB),
+        compiler_params=params(16),
+        cost_estimate=cost(heads_here * 2 * 512 * 1024 * 128, 3 * MIB),
         name="mix",
     )(info, core, query, keep, got, back, gain, cot)
 
@@ -381,25 +394,107 @@
     )(*mixed, weight)
 
 
-def join_kernel(groups, scale, info, *refs):
-    out_ref = refs[-1]
-    rows = refs[0].shape[0]
-    for g in range(groups):
+def fold_kernel(parts, terms, where, flips, info, *refs):
+    ins, outs = refs[: parts * terms], refs[parts * terms :]
+    size = ins[0].shape[0] - 1
+    share = outs[0].shape[0] - 1
+    last = sum(ref[size] for ref in ins)
+    for flip, out in zip(flips, outs):
+        first = (info[where] ^ flip) * share
+        if parts == 1:
+            out[:share] = sum(ref[pl.ds(first, share)] for ref in ins)
+        else:
+            for part in range(parts):
+
+                @pl.when((first >= part * size) & (first < (part + 1) * size))
+                def _(part=part, out=out, first=first):
+                    out[:share] = sum(ref[pl.ds(first - part * size, share)] for ref in ins[part * terms : (part + 1) * terms])
+
+        out[share] = last
+
+
+def fold_call(info, where, flips, arrays, parts):
+    terms = len(arrays) // parts
+    size = arrays[0].shape[0] - 1
+    share = size * parts // len(flips)
+    shape = jax.ShapeDtypeStruct((share + 1, 8, 128), F32)
+    return pl.pallas_call(
+        functools.partial(fold_kernel, parts, terms, where, flips),
+        out_shape=[shape] * len(flips),
+        in_specs=[smem()] + [vmem()] * len(arrays),
+        compiler_params=params(12),
+        cost_estimate=cost(size * 1024 * len(arrays), size * 4096 * (len(arrays) + 1)),
+        name="fold",
+    )(info, *arrays)
+
+
+def total_kernel(*refs):
+    ins, (piece_ref, last_ref) = refs[:-2], refs[-2:]
+    size = piece_ref.shape[0]
+    piece_ref[...] = sum(ref[:size] for ref in ins)
+    last_ref[...] = sum(ref[size] for ref in ins)
+
+
+def total_call(arrays):
+    size = arrays[0].shape[0] - 1
+    return pl.pallas_call(
+        total_kernel,
+        out_shape=(jax.ShapeDtypeStruct((size, 8, 128), F32), jax.ShapeDtypeStruct((8, 128), F32)),
+        in_specs=[vmem()] * len(arrays),
+        out_specs=(vmem(), vmem()),
+        compiler_params=params(12),
+        cost_estimate=cost(size * 4096, size * 4096 * 5),
+        name="total",
+    )(*arrays)
+
+
+def lay_kernel(where, flips, info, *refs):
+    out = refs[-1]
+    share = refs[0].shape[0]
+    for flip, ref in zip(flips, refs):
+        out[pl.ds((info[where] ^ flip) * share, share)] = ref[...]
+
+
+def lay_call(info, where, flips, arrays):
+    share = arrays[0].shape[0]
+    return pl.pallas_call(
+        functools.partial(lay_kernel, where, flips),
+        out_shape=jax.ShapeDtypeStruct((share * len(flips), 8, 128), F32),
+        in_specs=[smem()] + [vmem()] * len(arrays),
+        compiler_params=params(12),
+        cost_estimate=cost(0, share * len(flips) * 8192),
+        name="lay",
+    )(info, *arrays)
+
+
+def join_kernel(scale, stripe, info, *refs):
+    sums = (len(refs) - 2) // 3
+    lasts, (out_ref, gain_ref) = refs[2 * sums : 3 * sums], refs[-2:]
+    columns = out_ref.shape[1] // 128
+    dims = stripe * 8
+    blocks = refs[0].shape[0] // (columns * stripe)
+    for g in range(sums):
         for part, ref in enumerate(refs[2 * g : 2 * g + 2]):
             side = info[1] if part == 0 else 1 - info[1]
-            first = pl.multiple_of((2 * g + side) * rows, rows)
-            out_ref[pl.ds(first, rows), :] = (ref[...] * scale).astype(BF16)
-
-
-def join_call(info, parts, scale):
-    rows, width = parts[0].shape
-    return pl.pallas_call(
-        functools.partial(join_kernel, len(parts) // 2, scale),
-        out_shape=jax.ShapeDtypeStruct((rows * len(parts), width), BF16),
-        in_specs=[smem()] + [vmem()] * len(parts),
+            for block in range(blocks):
+                head = (g * blocks + block) * 2 + side
+                for col in range(columns):
+                    first = (block * columns + col) * stripe
+                    values = ref[first : first + stripe].reshape(dims, 128) * scale
+                    out_ref[pl.ds(pl.multiple_of(head * dims, dims), dims), col * 128 : (col + 1) * 128] = values.astype(BF16)
+    gain_ref[...] = jnp.sum(sum(ref[...] for ref in lasts), axis=0, keepdims=True) * scale
+
+
+def join_call(info, parts, lasts, scale, dims, width):
+    total = sum(p.shape[0] for p in parts) * 1024 // width
+    return pl.pallas_call(
+        functools.partial(join_kernel, scale, dims // 8),
+        out_shape=(jax.ShapeDtypeStruct((total, width), BF16), jax.ShapeDtypeStruct((1, 128), F32)),
+        in_specs=[smem()] + [vmem()] * (len(parts) + len(lasts)),
+        out_specs=(vmem(), vmem()),
         compiler_params=params(16),
         name="join",
-    )(info, *parts)
+    )(info, *parts, *lasts)
 
 
 def shards(mesh, features, weight_pool, pattern_in, pattern_pool, gate_weight, decay_rate, beta_bias, norm_gain, out_weight, cotangent):
@@ -431,19 +526,28 @@
         route = [(a * PAIR + yi, b * PAIR + yi) for a, b in ends for yi in range(PAIR)]
         return lax.ppermute(array, "tm", route)
 
-    info = jnp.stack([y, core, z]).astype(jnp.int32)
+    plane = [(dx, dy) for dx in range(n_x) for dy in range(PAIR)]
+    info = jnp.stack([y, core, z, x * PAIR + y]).astype(jnp.int32)
+    table = jnp.stack([pattern_in.T, pattern_pool.T])
+    levels = jnp.stack([decay_rate, beta_bias])
     rows = features.reshape(count, width)
     cot = cotangent.reshape(count, width)
     gain = norm_gain.reshape(1, dims)
-    pin, ppool = pattern_in.T, pattern_pool.T
-    gates = gates_call(rows, gate_weight, decay_rate, beta_bias, span)
     each = heads // GROUPS
-
-    locals_ = [local_call(info, pin, ppool, rows, weight_pool, gates, g * each, each, heads, span) for g in range(GROUPS)]
-    maps = []
-    for own, send, _, _ in locals_:
-        got = moved(send, (0, 0, 0, 1))
-        maps.append(combine_call(info, own, got))
+    per_sum = GROUPS // SUMS
+
+    gates = None
+    locals_, maps = [], []
+    for g in range(GROUPS):
+        told = info
+        if g >= AHEAD:
+            told, maps[g - AHEAD] = lax.optimization_barrier((info, maps[g - AHEAD]))
+        extra = (gate_weight.T, levels) if g == 0 else gates
+        own, send, *rest = local_call(told, table, rows, weight_pool, extra, g * each, each, heads, span)
+        if g == 0:
+            gates = rest.pop()
+        locals_.append(rest)
+        maps.append(list(combine_call(info, own, moved(send, (0, 0, 0, 1)))))
     back = back_call(cot, out_weight)
     states = [jnp.zeros((each, dims, dims), F32)] * GROUPS
     sends = [m[2] for m in maps]
@@ -455,70 +559,37 @@
             break
         for g in range(GROUPS):
             states[g], sends[g] = hop_call(level, info, maps[g][1], gots[g], states[g])
-    mixes = []
+    mixed, halves_ = [], []
     for g in range(GROUPS):
         keep, send = split_call(n_z - 1, info, maps[g][0], gots[g], states[g])
         got = moved(send, (0, 0, 0, 1))
-        mixes.append(mix_call(info, g * each, locals_[g][2], locals_[g][3], keep, got, back, gain, cot, span))
-    gain_part = sum(m[3] for m in mixes)
-    output = finish_call([m[0] for m in mixes], out_weight)
+        flat, w_send, w_keep = mix_call(info, g * each, *locals_[g], keep, got, back, gain, cot, span)
+        mixed.append(flat)
+        halves_.append([w_keep, moved(w_send, (0, 1, 0, 0))])
+    output = finish_call(mixed, out_weight)
     scale = 1.0 / math.sqrt(count * n_shot * n_tm)
-    swaps = [(axis, 1 << bit) for axis, size in (("shot", n_shot), ("tm", n_tm)) for bit in range(size.bit_length() - 1)]
-    per_stage = -(-len(swaps) // 5)
-
-    def spread(value, part, stage):
-        for axis, reach in swaps[stage * per_stage : (stage + 1) * per_stage]:
-            size = lax.axis_size(axis)
-            part = part + lax.ppermute(part, axis, [(i, i ^ reach) for i in range(size)])
-        return lax.optimization_barrier((value, part))
-
-    plane = [(dx, dy) for dx in range(n_x) for dy in range(PAIR)]
-    n_plane = len(plane)
-    share = each * dims // (CORES * n_plane * n_z)
-
-    def plane_index(dx, dy):
-        return (x ^ dx) * PAIR + (y ^ dy)
-
-    def picked(array, index):
-        return lax.dynamic_index_in_dim(array, index, 0, keepdims=False)
-
-    crossed = [moved(mixes[g][1], (0, 1, 0, 0)) for g in range(GROUPS)]
-    grads = []
-    for g in range(GROUPS):
-        summed = (mixes[g][2] + crossed[g]).reshape(n_plane, n_z, share, width)
-        total = picked(summed, plane_index(0, 0))
-        for dx, dy in plane[1:]:
-            total = total + moved(picked(summed, plane_index(dx, dy)), (dx, 0, 0, dy))
-        if g == GROUPS - 1:
-            total, gain_part = spread(total, gain_part, 0)
-            total, output = lax.optimization_barrier((total, output))
-        final = picked(total, z)
-        for dz in range(1, n_z):
-            final = final + moved(picked(total, z ^ dz), (0, 0, dz, 0))
-        if g == GROUPS - 1:
-            final, gain_part = spread(final, gain_part, 1)
-        grads.append(final)
-    pieces = []
-    for g in range(GROUPS):
-        along = jnp.zeros((n_z, share, width), F32)
-        for dz in range(n_z):
-            piece = grads[g] if dz == 0 else moved(grads[g], (0, 0, dz, 0))
-            along = lax.dynamic_update_index_in_dim(along, piece, z ^ dz, 0)
-        if g == GROUPS - 1:
-            along, gain_part = spread(along, gain_part, 2)
-        wide = jnp.zeros((n_plane, n_z, share, width), F32)
-        for dx, dy in plane:
-            piece = along if (dx, dy) == (0, 0) else moved(along, (dx, 0, 0, dy))
-            wide = lax.dynamic_update_index_in_dim(wide, piece, plane_index(dx, dy), 0)
-        if g == GROUPS - 1:
-            wide, gain_part = spread(wide, gain_part, 3)
-        other = moved(wide, (0, 1, 0, 0))
-        if g == GROUPS - 1:
-            other, gain_part = spread(other, gain_part, 4)
-        pieces += [wide.reshape(-1, width), other.reshape(-1, width)]
-    gain_grad = jnp.sum(gain_part, axis=0) * scale
-    weight_grad = join_call(info, pieces, scale)
-    return (output.reshape(seqs, span, width), weight_grad, gain_grad)
+
+    flat_plane = tuple(dx * PAIR + dy for dx, dy in plane)
+    flat_z = tuple(range(n_z))
+    sums = range(SUMS)
+    spread = []
+    for g in sums:
+        arrays = [a for pair in halves_[g * per_sum : (g + 1) * per_sum] for a in pair]
+        spread.append(list(fold_call(info, 3, flat_plane, arrays, per_sum)))
+    spread[-1][0], output = lax.optimization_barrier((spread[-1][0], output))
+    met = [[p[0]] + [moved(a, (dx, 0, 0, dy)) for a, (dx, dy) in zip(p[1:], plane[1:])] for p in spread]
+    spread = [fold_call(info, 2, flat_z, m, 1) for m in met]
+    met = [[p[0]] + [moved(a, (0, 0, dz, 0)) for a, dz in zip(p[1:], flat_z[1:])] for p in spread]
+    totals = [total_call(m) for m in met]
+    along = []
+    for piece, _ in totals:
+        along.append(lay_call(info, 2, flat_z, [piece] + [moved(piece, (0, 0, dz, 0)) for dz in flat_z[1:]]))
+    parts = []
+    for piece in along:
+        laid = lay_call(info, 3, flat_plane, [piece] + [moved(piece, (dx, 0, 0, dy)) for dx, dy in plane[1:]])
+        parts += [laid, moved(laid, (0, 1, 0, 0))]
+    weight_grad, gain_grad = join_call(info, parts, [t[1] for t in totals], scale, dims, width)
+    return (output.reshape(seqs, span, width), weight_grad, gain_grad.reshape(dims))
 
 
 def solution(mesh):

time: 175 us -> 183 us (1.046)
  local copies, waits for them, and re-layouts: 14.7 us -> 3.6 us
  Pallas kernels: 50.4 us -> 60.4 us
  waiting for transfers between devices: 33 us -> 41 us
  starting transfers between devices: 69.5 us -> 74.4 us
  other arithmetic: 4.97 us -> 1.46 us
    ppermute x6 -> x12, starting transfers between devices: 10.1 us -> 23.5 us  [lifted(): return lax.ppermute(array, 'tm', route)]
    ppermute x32 -> x38, waiting for transfers between devices: 29.7 us -> 41 us  [moved(): return lax.ppermute(array, both, route)]
    unnamed x34 -> x12, local copies, waits for them, and re-layouts: 13.2 us -> 3.59 us
    ppermute x5 -> x0, starting transfers between devices: 6.6 us -> none  [spread(): lax.ppermute(part, axis, [(i, i ^ reach) for i in range(size)])]
    add x11 -> x0, other arithmetic: 4.34 us -> none  [the longest x2 3.04 us: shards(): summed = (mixes[g][2] + crossed[g]).reshape(n_plane, n_z, share, width)]
    ppermute x5 -> x0, waiting for transfers between devices: 2.91 us -> none  [spread(): lax.ppermute(part, axis, [(i, i ^ reach) for i in range(size)])]
    pallas_call x4 -> x8, Pallas kernels: 3.25 us -> 6 us  [hop_call(): pl.pallas_call(functools.partial(hop_kernel, level), out_shape=(shape, sh...]
    pallas_call x2 -> x11, Pallas kernels: 4.79 us -> 7.48 us  [the longest x4 2.72 us: fold_call(): pl.pallas_call(functools.partial(fold_kernel, parts, terms, where, flips)...]
  transfers between devices with their start and end apart: 43 -> 50, of which waited for: 13 -> 18; matrix products, arithmetic and copies ran while one was open for 4% -> 0% of each run, Pallas kernels for 20% -> 28%
where the time goes in v4:
time: 183 us; the launch traced here: 182 us
  starting transfers between devices  74.4 us (41%)
  Pallas kernels  60.4 us (33%)
  waiting for transfers between devices  41 us (22%)
  local copies, waits for them, and re-layouts  3.6 us (2%)
    ppermute x38, starting transfers between devices, moved(): return lax.ppermute(array, both, route)  50.9 us
    ppermute x38, waiting for transfers between devices, moved(): return lax.ppermute(array, both, route)  41 us
    pallas_call x4, Pallas kernels, local_call(): pl.pallas_call(functools.partial(local_kernel, first_head, heads, span, P...  24.9 us
    ppermute x12, starting transfers between devices, lifted(): return lax.ppermute(array, 'tm', route)  23.5 us
    pallas_call x4, Pallas kernels, mix_call(): pl.pallas_call(functools.partial(mix_kernel, span), out_shape=(jax.ShapeD...  9.66 us
    pallas_call x8, Pallas kernels, hop_call(): pl.pallas_call(functools.partial(hop_kernel, level), out_shape=(shape, sh...  6 us
  transfers between devices with their start and end apart: 50, of which 18 were waited for; matrix products, arithmetic and copies ran while one was open for 0% of the time, Pallas kernels for 28%

profile of v4, /device:TPU:0, one launch (start us, length us, event | category | flops | bytes accessed | tf_op | source)
XLA Modules:
  0.0 182.1 jit_solution(374744909861597553)
XLA Ops:
  5.7 7.5 %local.4 = (f32[2,128,256]{2,1,0:T(8,128)S(1)}, f32[2,128,256]{2,1,0:T(8,128)S(1)}, f32[512,256]{1,0:T(8,128)S(1)}, f32[512,256]{1,0:T(8,128)S(1)}, f32[512,16]{1,0:T(8,128)S(1)}) custom-call(s32[4]{0:T(128)S(1)} %pad_add_fusion.1.info, s32[2,4,24]{2,1,0:T(4,128)S(1)} %pad_add_fusion.table, bf16[512,1024]{1,0:T(8,128)(2,1)S(1)} %bitcast.27, ...), custom_call_target="tpu_custom_call" | custom-call | flops 3221225472 | bytes 8388608 | tf_op jit(solution)/shard_map/local/pallas_call | solution.py:188
  13.2 3.0 %collective-permute-start.5 = (f32[2,128,256]{2,1,0:T(8,128)S(1)}, f32[2,128,256]{2,1,0:T(8,128)S(1)}, u32[]{:S(2)}, u32[]{:S(2)}) collective-permute-start(f32[2,128,256]{2,1,0:T(8,128)S(1)} %get-tuple-element.113), channel_id=1, source_target_pairs={{0,1},{1,0},{2,3},{3,2},{4,5},{5,4},{6,7},{7,6},{8,9},{9,8},{10,11... | collective-permute-start | bytes 786440 | tf_op jit(solution)/shard_map/ppermute | solution.py:522
  16.2 5.7 %local.7 = (f32[2,128,256]{2,1,0:T(8,128)S(1)}, f32[2,128,256]{2,1,0:T(8,128)S(1)}, f32[512,256]{1,0:T(8,128)S(1)}, f32[512,256]{1,0:T(8,128)S(1)}) custom-call(s32[4]{0:T(128)S(1)} %pad_add_fusion.1.info, s32[2,4,24]{2,1,0:T(4,128)S(1)} %pad_add_fusion.table, bf16[512,1024]{1,0:T(8,128)(2,1)S(1)} %bitcast.28, bf16[64,128,128]{2,1,0:T(8,128)(2,1)S(1)} %copy-done.3, ...), custom_call_target="tpu_custom_call" | custom-call | flops 3221225472 | bytes 8388608 | tf_op jit(solution)/shard_map/local/pallas_call | solution.py:188
  22.1 5.9 %local.5 = (f32[2,128,256]{2,1,0:T(8,128)S(1)}, f32[2,128,256]{2,1,0:T(8,128)S(1)}, f32[512,256]{1,0:T(8,128)S(1)}, f32[512,256]{1,0:T(8,128)S(1)}) custom-call(s32[4]{0:T(128)S(1)} %pad_add_fusion.1.info, s32[2,4,24]{2,1,0:T(4,128)S(1)} %pad_add_fusion.table, bf16[512,1024]{1,0:T(8,128)(2,1)S(1)} %bitcast.29, bf16[64,128,128]{2,1,0:T(8,128)(2,1)S(1)} %copy-done.3, ...), custom_call_target="tpu_custom_call" | custom-call | flops 3221225472 | bytes 8388608 | tf_op jit(solution)/shard_map/local/pallas_call | solution.py:188
  30.9 3.5 %collective-permute-start.6 = (f32[2,128,128]{2,1,0:T(8,128)S(1)}, f32[2,128,128]{2,1,0:T(8,128)S(1)}, u32[]{:S(2)}, u32[]{:S(2)}) collective-permute-start(f32[2,128,128]{2,1,0:T(8,128)S(1)} %get-tuple-element.117), channel_id=1, source_target_pairs={{0,2},{1,3},{2,0},{3,1},{8,10},{9,11},{10,8},{11,9},{16,18},{17,19... | collective-permute-start | bytes 393224 | tf_op jit(solution)/shard_map/ppermute | solution.py:527
  35.3 2.6 %collective-permute-start.18 = (f32[2,128,128]{2,1,0:T(8,128)S(1)}, f32[2,128,128]{2,1,0:T(8,128)S(1)}, u32[]{:S(2)}, u32[]{:S(2)}) collective-permute-start(f32[2,128,128]{2,1,0:T(8,128)S(1)} %get-tuple-element.156), channel_id=1, source_target_pairs={{0,2},{1,3},{2,0},{3,1},{8,10},{9,11},{10,8},{11,9},{16,18},{17,19... | collective-permute-start | bytes 393224 | tf_op jit(solution)/shard_map/ppermute | solution.py:527
  37.9 5.7 %local.6 = (f32[2,128,256]{2,1,0:T(8,128)S(1)}, f32[2,128,256]{2,1,0:T(8,128)S(1)}, f32[512,256]{1,0:T(8,128)S(1)}, f32[512,256]{1,0:T(8,128)S(1)}) custom-call(s32[4]{0:T(128)S(1)} %pad_add_fusion.1.info, s32[2,4,24]{2,1,0:T(4,128)S(1)} %pad_add_fusion.table, bf16[512,1024]{1,0:T(8,128)(2,1)S(1)} %bitcast.30, bf16[64,128,128]{2,1,0:T(8,128)(2,1)S(1)} %copy-done.3, ...), custom_call_target="tpu_custom_call" | custom-call | flops 3221225472 | bytes 8388608 | tf_op jit(solution)/shard_map/local/pallas_call | solution.py:188
  43.8 3.3 %back.1.back_ref = f32[512,1024]{1,0:T(8,128)S(1)} custom-call(bf16[512,1024]{1,0:T(8,128)(2,1)S(1)} %bitcast.18, bf16[1024,1024]{1,0:T(8,128)(2,1)S(1)} %copy-done.1), custom_call_target="tpu_custom_call" | custom-call | flops 1073741824 | bytes 5242880 | tf_op jit(solution)/shard_map/back/pallas_call | solution.py:362
  53.7 9.9 %collective-permute-start.1 = (f32[2,128,128]{2,1,0:T(8,128)S(1)}, f32[2,128,128]{2,1,0:T(8,128)S(1)}, u32[]{:S(2)}, u32[]{:S(2)}) collective-permute-start(f32[2,128,128]{2,1,0:T(8,128)S(1)} %get-tuple-element.105), channel_id=1, source_target_pairs={{0,2},{1,3},{2,0},{3,1},{8,10},{9,11},{10,8},{11,9},{16,18},{17,19... | collective-permute-start | bytes 393224 | tf_op jit(solution)/shard_map/ppermute | solution.py:527
  75.8 2.4 %mix.7 = (bf16[512,256]{1,0:T(8,128)(2,1)S(1)}, f32[129,8,128]{2,1,0:T(8,128)S(1)}, f32[129,8,128]{2,1,0:T(8,128)S(1)}) custom-call(s32[4]{0:T(128)S(1)} %pad_add_fusion.1.info, f32[512,256]{1,0:T(8,128)S(1)} %get-tuple-element.150.core_ref, f32[512,256]{1,0:T(8,128)S(1)} %get-tuple-element.151.query_ref, f32[2,128,128]{2,1,0:T(8,128)S(1)} %get-tuple-element.161.keep_ref, ...), custom_call_target="tpu_custom_call" | custom-call | flops 268435456 | bytes 3145728 | tf_op jit(solution)/shard_map/mix/pallas_call | solution.py:340
  85.3 3.3 %collective-permute-done.4.got_ref = f32[2,128,128]{2,1,0:T(8,128)S(1)} collective-permute-done((f32[2,128,128]{2,1,0:T(8,128)S(1)}, f32[2,128,128]{2,1,0:T(8,128)S(1)}, u32[]{:S(2)}, u32[]{:S(2)}) %collective-permute-start.4) | collective-permute-done | bytes 131104 | tf_op jit(solution)/shard_map/ppermute | solution.py:522
  98.4 4.8 %collective-permute-done.24.refs_1_ = f32[65,8,128]{2,1,0:T(8,128)S(1)} collective-permute-done((f32[65,8,128]{2,1,0:T(8,128)S(1)}, f32[65,8,128]{2,1,0:T(8,128)S(1)}, u32[]{:S(2)}, u32[]{:S(2)}) %collective-permute-start.24) | collective-permute-done | bytes 266272 | tf_op jit(solution)/shard_map/ppermute | solution.py:522
  103.2 2.7 %collective-permute-done.25.refs_2_ = f32[65,8,128]{2,1,0:T(8,128)S(1)} collective-permute-done((f32[65,8,128]{2,1,0:T(8,128)S(1)}, f32[65,8,128]{2,1,0:T(8,128)S(1)}, u32[]{:S(2)}, u32[]{:S(2)}) %collective-permute-start.25) | collective-permute-done | bytes 266272 | tf_op jit(solution)/shard_map/ppermute | solution.py:522
  105.9 4.3 %collective-permute-done.26.refs_3_ = f32[65,8,128]{2,1,0:T(8,128)S(1)} collective-permute-done((f32[65,8,128]{2,1,0:T(8,128)S(1)}, f32[65,8,128]{2,1,0:T(8,128)S(1)}, u32[]{:S(2)}, u32[]{:S(2)}) %collective-permute-start.26) | collective-permute-done | bytes 266272 | tf_op jit(solution)/shard_map/ppermute | solution.py:522
  110.8 6.6 %collective-permute-start.27 = (f32[17,8,128]{2,1,0:T(8,128)S(1)}, f32[17,8,128]{2,1,0:T(8,128)S(1)}, u32[]{:S(2)}, u32[]{:S(2)}) collective-permute-start(f32[17,8,128]{2,1,0:T(8,128)S(1)} %get-tuple-element.176), channel_id=1, source_target_pairs={{0,2},{1,3},{2,0},{3,1},{4,6},{5,7},{6,4},{7,5},{8,10},{9,11},{10,... | collective-permute-start | bytes 208904 | tf_op jit(solution)/shard_map/ppermute | solution.py:522
  117.4 5.3 %collective-permute-start.28 = (f32[17,8,128]{2,1,0:T(8,128)S(1)}, f32[17,8,128]{2,1,0:T(8,128)S(1)}, u32[]{:S(2)}, u32[]{:S(2)}) collective-permute-start(f32[17,8,128]{2,1,0:T(8,128)S(1)} %get-tuple-element.177), channel_id=1, source_target_pairs={{0,4},{1,5},{2,6},{3,7},{4,0},{5,1},{6,2},{7,3},{8,12},{9,13},{10,... | collective-permute-start | bytes 208904 | tf_op jit(solution)/shard_map/ppermute | solution.py:522
  128.9 2.6 %collective-permute-start.31 = (f32[16,8,128]{2,1,0:T(8,128)S(1)}, f32[16,8,128]{2,1,0:T(8,128)S(1)}, u32[]{:S(2)}, u32[]{:S(2)}) collective-permute-start(f32[16,8,128]{2,1,0:T(8,128)S(1)} %get-tuple-element.179.refs_0_), channel_id=1, source_target_pairs={{0,4},{1,5},{2,6},{3,7},{4,0},{5,1},{6,2},{7,3},{8,12},{9,13},{10,... | collective-permute-start | bytes 196616 | tf_op jit(solution)/shard_map/ppermute | solution.py:522
  135.4 3.8 %collective-permute-done.32.refs_3_ = f32[16,8,128]{2,1,0:T(8,128)S(1)} collective-permute-done((f32[16,8,128]{2,1,0:T(8,128)S(1)}, f32[16,8,128]{2,1,0:T(8,128)S(1)}, u32[]{:S(2)}, u32[]{:S(2)}) %collective-permute-start.32) | collective-permute-done | bytes 65568 | tf_op jit(solution)/shard_map/ppermute | solution.py:522
  141.4 2.8 %finish.1 = bf16[512,1024]{1,0:T(8,128)(2,1)} custom-call(bf16[512,256]{1,0:T(8,128)(2,1)S(1)} %get-tuple-element.149.refs_0_, bf16[512,256]{1,0:T(8,128)(2,1)S(1)} %get-tuple-element.163.refs_1_, bf16[512,256]{1,0:T(8,128)(2,1)S(1)} %get-tuple-element.164.refs_2_, bf16[512,256]{1,0:T(8,128)(2,1)S(1)} %get-tuple-element.165.refs_3_, ...), custom_call_target="tpu_custom_call" | custom-call | flops 1073741824 | bytes 4194304 | tf_op jit(solution)/shard_map/finish/pallas_call | solution.py:385
  144.9 2.8 %collective-permute-start.41 = (f32[17,8,128]{2,1,0:T(8,128)S(1)}, f32[17,8,128]{2,1,0:T(8,128)S(1)}, u32[]{:S(2)}, u32[]{:S(2)}) collective-permute-start(f32[17,8,128]{2,1,0:T(8,128)S(1)} %get-tuple-element.186), channel_id=1, source_target_pairs={{0,4},{1,5},{2,6},{3,7},{4,0},{5,1},{6,2},{7,3},{8,12},{9,13},{10,... | collective-permute-start | bytes 208904 | tf_op jit(solution)/shard_map/ppermute | solution.py:522
  150.2 3.9 %collective-permute-done.42.refs_3_ = f32[17,8,128]{2,1,0:T(8,128)S(1)} collective-permute-done((f32[17,8,128]{2,1,0:T(8,128)S(1)}, f32[17,8,128]{2,1,0:T(8,128)S(1)}, u32[]{:S(2)}, u32[]{:S(2)}) %collective-permute-start.42) | collective-permute-done | bytes 69664 | tf_op jit(solution)/shard_map/ppermute | solution.py:522
  167.8 3.1 %collective-permute-done.35.refs_3_ = f32[64,8,128]{2,1,0:T(8,128)S(1)} collective-permute-done((f32[64,8,128]{2,1,0:T(8,128)S(1)}, f32[64,8,128]{2,1,0:T(8,128)S(1)}, u32[]{:S(2)}, u32[]{:S(2)}) %collective-permute-start.35) | collective-permute-done | bytes 262176 | tf_op jit(solution)/shard_map/ppermute | solution.py:522
  173.7 2.7 %collective-permute-done.48.refs_3_ = f32[64,8,128]{2,1,0:T(8,128)S(1)} collective-permute-done((f32[64,8,128]{2,1,0:T(8,128)S(1)}, f32[64,8,128]{2,1,0:T(8,128)S(1)}, u32[]{:S(2)}, u32[]{:S(2)}) %collective-permute-start.48) | collective-permute-done | bytes 262176 | tf_op jit(solution)/shard_map/ppermute | solution.py:522
  177.1 2.6 %collective-permute-done.49.refs_3_ = f32[256,8,128]{2,1,0:T(8,128)S(1)} collective-permute-done((f32[256,8,128]{2,1,0:T(8,128)S(1)}, f32[256,8,128]{2,1,0:T(8,128)S(1)}, u32[]{:S(2)}, u32[]{:S(2)}) %collective-permute-start.49) | collective-permute-done | bytes 1048608 | tf_op jit(solution)/shard_map/ppermute | solution.py:522
  (129 shorter events, 80.0 us)
Async XLA Ops:
  13.2 16.8 %collective-permute-start.5 = (f32[2,128,256]{2,1,0:T(8,128)S(1)}, f32[2,128,256]{2,1,0:T(8,128)S(1)}, u32[]{:S(2)}, u32[]{:S(2)}) collective-permute-start(f32[2,128,256]{2,1,0:T(8,128)S(1)} %get-tuple-element.113), channel_id=1, source_target_pairs={{0,1},{1,0},{2,3},{3,2},{4,5},{5,4},{6,7},{7,6},{8,9},{9,8},{10,11... | collective-permute-start | bytes 786440 | tf_op jit(solution)/shard_map/ppermute | solution.py:522
  22.0 12.4 %collective-permute-start.17 = (f32[2,128,256]{2,1,0:T(8,128)S(1)}, f32[2,128,256]{2,1,0:T(8,128)S(1)}, u32[]{:S(2)}, u32[]{:S(2)}) collective-permute-start(f32[2,128,256]{2,1,0:T(8,128)S(1)} %get-tuple-element.153), channel_id=1, source_target_pairs={{0,1},{1,0},{2,3},{3,2},{4,5},{5,4},{6,7},{7,6},{8,9},{9,8},{10,11... | collective-permute-start | bytes 786440 | tf_op jit(solution)/shard_map/ppermute | solution.py:522
  28.0 24.9 %collective-permute-start = (f32[2,128,256]{2,1,0:T(8,128)S(1)}, f32[2,128,256]{2,1,0:T(8,128)S(1)}, u32[]{:S(2)}, u32[]{:S(2)}) collective-permute-start(f32[2,128,256]{2,1,0:T(8,128)S(1)} %get-tuple-element.102), channel_id=1, source_target_pairs={{0,1},{1,0},{2,3},{3,2},{4,5},{5,4},{6,7},{7,6},{8,9},{9,8},{10,11... | collective-permute-start | bytes 786440 | tf_op jit(solution)/shard_map/ppermute | solution.py:522
  30.9 16.2 %collective-permute-start.6 = (f32[2,128,128]{2,1,0:T(8,128)S(1)}, f32[2,128,128]{2,1,0:T(8,128)S(1)}, u32[]{:S(2)}, u32[]{:S(2)}) collective-permute-start(f32[2,128,128]{2,1,0:T(8,128)S(1)} %get-tuple-element.117), channel_id=1, source_target_pairs={{0,2},{1,3},{2,0},{3,1},{8,10},{9,11},{10,8},{11,9},{16,18},{17,19... | collective-permute-start | bytes 393224 | tf_op jit(solution)/shard_map/ppermute | solution.py:527
  35.3 13.3 %collective-permute-start.18 = (f32[2,128,128]{2,1,0:T(8,128)S(1)}, f32[2,128,128]{2,1,0:T(8,128)S(1)}, u32[]{:S(2)}, u32[]{:S(2)}) collective-permute-start(f32[2,128,128]{2,1,0:T(8,128)S(1)} %get-tuple-element.156), channel_id=1, source_target_pairs={{0,2},{1,3},{2,0},{3,1},{8,10},{9,11},{10,8},{11,9},{16,18},{17,19... | collective-permute-start | bytes 393224 | tf_op jit(solution)/shard_map/ppermute | solution.py:527
  43.6 20.0 %collective-permute-start.8 = (f32[2,128,256]{2,1,0:T(8,128)S(1)}, f32[2,128,256]{2,1,0:T(8,128)S(1)}, u32[]{:S(2)}, u32[]{:S(2)}) collective-permute-start(f32[2,128,256]{2,1,0:T(8,128)S(1)} %get-tuple-element.125), channel_id=1, source_target_pairs={{0,1},{1,0},{2,3},{3,2},{4,5},{5,4},{6,7},{7,6},{8,9},{9,8},{10,11... | collective-permute-start | bytes 786440 | tf_op jit(solution)/shard_map/ppermute | solution.py:522
  50.8 15.9 %collective-permute-start.15 = (f32[2,128,128]{2,1,0:T(8,128)S(1)}, f32[2,128,128]{2,1,0:T(8,128)S(1)}, u32[]{:S(2)}, u32[]{:S(2)}) collective-permute-start(f32[2,128,128]{2,1,0:T(8,128)S(1)} %get-tuple-element.145), channel_id=1, source_target_pairs={{4,6},{5,7},{6,4},{7,5},{12,14},{13,15},{14,12},{15,13},{20,22},{2... | collective-permute-start | bytes 393224 | tf_op jit(solution)/shard_map/ppermute | solution.py:527
  52.2 16.8 %collective-permute-start.20 = (f32[2,128,128]{2,1,0:T(8,128)S(1)}, f32[2,128,128]{2,1,0:T(8,128)S(1)}, u32[]{:S(2)}, u32[]{:S(2)}) collective-permute-start(f32[2,128,128]{2,1,0:T(8,128)S(1)} %get-tuple-element.159), channel_id=1, source_target_pairs={{4,6},{5,7},{6,4},{7,5},{12,14},{13,15},{14,12},{15,13},{20,22},{2... | collective-permute-start | bytes 393224 | tf_op jit(solution)/shard_map/ppermute | solution.py:527
  53.7 16.6 %collective-permute-start.1 = (f32[2,128,128]{2,1,0:T(8,128)S(1)}, f32[2,128,128]{2,1,0:T(8,128)S(1)}, u32[]{:S(2)}, u32[]{:S(2)}) collective-permute-start(f32[2,128,128]{2,1,0:T(8,128)S(1)} %get-tuple-element.105), channel_id=1, source_target_pairs={{0,2},{1,3},{2,0},{3,1},{8,10},{9,11},{10,8},{11,9},{16,18},{17,19... | collective-permute-start | bytes 393224 | tf_op jit(solution)/shard_map/ppermute | solution.py:527
  75.7 18.4 %collective-permute-start.22 = (f32[129,8,128]{2,1,0:T(8,128)S(1)}, f32[129,8,128]{2,1,0:T(8,128)S(1)}, u32[]{:S(2)}, u32[]{:S(2)}) collective-permute-start(f32[129,8,128]{2,1,0:T(8,128)S(1)} %get-tuple-element.168), channel_id=1, source_target_pairs={{0,8},{1,9},{2,10},{3,11},{4,12},{5,13},{6,14},{7,15},{8,0},{9,1},... | collective-permute-start | bytes 1585160 | tf_op jit(solution)/shard_map/ppermute | solution.py:522
  78.2 15.9 %collective-permute-start.23 = (f32[129,8,128]{2,1,0:T(8,128)S(1)}, f32[129,8,128]{2,1,0:T(8,128)S(1)}, u32[]{:S(2)}, u32[]{:S(2)}) collective-permute-start(f32[129,8,128]{2,1,0:T(8,128)S(1)} %get-tuple-element.170), channel_id=1, source_target_pairs={{0,8},{1,9},{2,10},{3,11},{4,12},{5,13},{6,14},{7,15},{8,0},{9,1},... | collective-permute-start | bytes 1585160 | tf_op jit(solution)/shard_map/ppermute | solution.py:522
  91.1 31.6 %collective-permute-start.7 = (f32[129,8,128]{2,1,0:T(8,128)S(1)}, f32[129,8,128]{2,1,0:T(8,128)S(1)}, u32[]{:S(2)}, u32[]{:S(2)}) collective-permute-start(f32[129,8,128]{2,1,0:T(8,128)S(1)} %get-tuple-element.120), channel_id=1, source_target_pairs={{0,8},{1,9},{2,10},{3,11},{4,12},{5,13},{6,14},{7,15},{8,0},{9,1},... | collective-permute-start | bytes 1585160 | tf_op jit(solution)/shard_map/ppermute | solution.py:522
  93.6 29.1 %collective-permute-start.13 = (f32[129,8,128]{2,1,0:T(8,128)S(1)}, f32[129,8,128]{2,1,0:T(8,128)S(1)}, u32[]{:S(2)}, u32[]{:S(2)}) collective-permute-start(f32[129,8,128]{2,1,0:T(8,128)S(1)} %get-tuple-element.136), channel_id=1, source_target_pairs={{0,8},{1,9},{2,10},{3,11},{4,12},{5,13},{6,14},{7,15},{8,0},{9,1},... | collective-permute-start | bytes 1585160 | tf_op jit(solution)/shard_map/ppermute | solution.py:522
  98.1 12.1 %collective-permute-start.26 = (f32[65,8,128]{2,1,0:T(8,128)S(1)}, f32[65,8,128]{2,1,0:T(8,128)S(1)}, u32[]{:S(2)}, u32[]{:S(2)}) collective-permute-start(f32[65,8,128]{2,1,0:T(8,128)S(1)} %get-tuple-element.174), channel_id=1, source_target_pairs={{0,17},{1,16},{2,19},{3,18},{4,21},{5,20},{6,23},{7,22},{8,25},{9,... | collective-permute-start | bytes 798728 | tf_op jit(solution)/shard_map/ppermute | solution.py:522
  110.8 15.7 %collective-permute-start.27 = (f32[17,8,128]{2,1,0:T(8,128)S(1)}, f32[17,8,128]{2,1,0:T(8,128)S(1)}, u32[]{:S(2)}, u32[]{:S(2)}) collective-permute-start(f32[17,8,128]{2,1,0:T(8,128)S(1)} %get-tuple-element.176), channel_id=1, source_target_pairs={{0,2},{1,3},{2,0},{3,1},{4,6},{5,7},{6,4},{7,5},{8,10},{9,11},{10,... | collective-permute-start | bytes 208904 | tf_op jit(solution)/shard_map/ppermute | solution.py:522
  117.4 9.8 %collective-permute-start.28 = (f32[17,8,128]{2,1,0:T(8,128)S(1)}, f32[17,8,128]{2,1,0:T(8,128)S(1)}, u32[]{:S(2)}, u32[]{:S(2)}) collective-permute-start(f32[17,8,128]{2,1,0:T(8,128)S(1)} %get-tuple-element.177), channel_id=1, source_target_pairs={{0,4},{1,5},{2,6},{3,7},{4,0},{5,1},{6,2},{7,3},{8,12},{9,13},{10,... | collective-permute-start | bytes 208904 | tf_op jit(solution)/shard_map/ppermute | solution.py:522
  123.4 20.7 %collective-permute-start.37 = (f32[65,8,128]{2,1,0:T(8,128)S(1)}, f32[65,8,128]{2,1,0:T(8,128)S(1)}, u32[]{:S(2)}, u32[]{:S(2)}) collective-permute-start(f32[65,8,128]{2,1,0:T(8,128)S(1)} %get-tuple-element.181), channel_id=1, source_target_pairs={{0,1},{1,0},{2,3},{3,2},{4,5},{5,4},{6,7},{7,6},{8,9},{9,8},{10,11... | collective-permute-start | bytes 798728 | tf_op jit(solution)/shard_map/ppermute | solution.py:522
  125.0 19.2 %collective-permute-start.38 = (f32[65,8,128]{2,1,0:T(8,128)S(1)}, f32[65,8,128]{2,1,0:T(8,128)S(1)}, u32[]{:S(2)}, u32[]{:S(2)}) collective-permute-start(f32[65,8,128]{2,1,0:T(8,128)S(1)} %get-tuple-element.182), channel_id=1, source_target_pairs={{0,16},{1,17},{2,18},{3,19},{4,20},{5,21},{6,22},{7,23},{8,24},{9,... | collective-permute-start | bytes 798728 | tf_op jit(solution)/shard_map/ppermute | solution.py:522
  126.5 17.7 %collective-permute-start.39 = (f32[65,8,128]{2,1,0:T(8,128)S(1)}, f32[65,8,128]{2,1,0:T(8,128)S(1)}, u32[]{:S(2)}, u32[]{:S(2)}) collective-permute-start(f32[65,8,128]{2,1,0:T(8,128)S(1)} %get-tuple-element.183), channel_id=1, source_target_pairs={{0,17},{1,16},{2,19},{3,18},{4,21},{5,20},{6,23},{7,22},{8,25},{9,... | collective-permute-start | bytes 798728 | tf_op jit(solution)/shard_map/ppermute | solution.py:522
  139.8 25.5 %collective-permute-start.33 = (f32[64,8,128]{2,1,0:T(8,128)S(1)}, f32[64,8,128]{2,1,0:T(8,128)S(1)}, u32[]{:S(2)}, u32[]{:S(2)}) collective-permute-start(f32[64,8,128]{2,1,0:T(8,128)S(1)} %lay.4.refs_0_), channel_id=1, source_target_pairs={{0,1},{1,0},{2,3},{3,2},{4,5},{5,4},{6,7},{7,6},{8,9},{9,8},{10,11... | collective-permute-start | bytes 786440 | tf_op jit(solution)/shard_map/ppermute | solution.py:522
  160.0 10.9 %collective-permute-start.35 = (f32[64,8,128]{2,1,0:T(8,128)S(1)}, f32[64,8,128]{2,1,0:T(8,128)S(1)}, u32[]{:S(2)}, u32[]{:S(2)}) collective-permute-start(f32[64,8,128]{2,1,0:T(8,128)S(1)} %lay.4.refs_0_), channel_id=1, source_target_pairs={{0,17},{1,16},{2,19},{3,18},{4,21},{5,20},{6,23},{7,22},{8,25},{9,... | collective-permute-start | bytes 786440 | tf_op jit(solution)/shard_map/ppermute | solution.py:522
  163.2 9.9 %collective-permute-start.46 = (f32[64,8,128]{2,1,0:T(8,128)S(1)}, f32[64,8,128]{2,1,0:T(8,128)S(1)}, u32[]{:S(2)}, u32[]{:S(2)}) collective-permute-start(f32[64,8,128]{2,1,0:T(8,128)S(1)} %lay.6.refs_0_), channel_id=1, source_target_pairs={{0,1},{1,0},{2,3},{3,2},{4,5},{5,4},{6,7},{7,6},{8,9},{9,8},{10,11... | collective-permute-start | bytes 786440 | tf_op jit(solution)/shard_map/ppermute | solution.py:522
  163.8 9.9 %collective-permute-start.47 = (f32[64,8,128]{2,1,0:T(8,128)S(1)}, f32[64,8,128]{2,1,0:T(8,128)S(1)}, u32[]{:S(2)}, u32[]{:S(2)}) collective-permute-start(f32[64,8,128]{2,1,0:T(8,128)S(1)} %lay.6.refs_0_), channel_id=1, source_target_pairs={{0,16},{1,17},{2,18},{3,19},{4,20},{5,21},{6,22},{7,23},{8,24},{9,... | collective-permute-start | bytes 786440 | tf_op jit(solution)/shard_map/ppermute | solution.py:522
  165.3 11.2 %collective-permute-start.48 = (f32[64,8,128]{2,1,0:T(8,128)S(1)}, f32[64,8,128]{2,1,0:T(8,128)S(1)}, u32[]{:S(2)}, u32[]{:S(2)}) collective-permute-start(f32[64,8,128]{2,1,0:T(8,128)S(1)} %lay.6.refs_0_), channel_id=1, source_target_pairs={{0,17},{1,16},{2,19},{3,18},{4,21},{5,20},{6,23},{7,22},{8,25},{9,... | collective-permute-start | bytes 786440 | tf_op jit(solution)/shard_map/ppermute | solution.py:522
  (32 other events, 192.6 us)

commit v5 on v4

--- a/solution.py
+++ b/solution.py
@@ -8,7 +8,7 @@
 from jax.experimental.pallas import tpu as pltpu
 from jax.sharding import PartitionSpec as P
 
-GROUPS = 4
+GROUPS = 2
 SUMS = 2
 CORES = 2
 PAIR = 2
@@ -467,7 +467,7 @@
     )(info, *arrays)
 
 
-def join_kernel(scale, stripe, info, *refs):
+def join_kernel(scale, stripe, half, info, *refs):
     sums = (len(refs) - 2) // 3
     lasts, (out_ref, gain_ref) = refs[2 * sums : 3 * sums], refs[-2:]
     columns = out_ref.shape[1] // 128
@@ -477,7 +477,8 @@
         for part, ref in enumerate(refs[2 * g : 2 * g + 2]):
             side = info[1] if part == 0 else 1 - info[1]
             for block in range(blocks):
-                head = (g * blocks + block) * 2 + side
+                index = g * blocks + block
+                head = index // half * 2 * half + side * half + index % half
                 for col in range(columns):
                     first = (block * columns + col) * stripe
                     values = ref[first : first + stripe].reshape(dims, 128) * scale
@@ -485,10 +486,10 @@
     gain_ref[...] = jnp.sum(sum(ref[...] for ref in lasts), axis=0, keepdims=True) * scale
 
 
-def join_call(info, parts, lasts, scale, dims, width):
+def join_call(info, parts, lasts, scale, dims, width, half):
     total = sum(p.shape[0] for p in parts) * 1024 // width
     return pl.pallas_call(
-        functools.partial(join_kernel, scale, dims // 8),
+        functools.partial(join_kernel, scale, dims // 8, half),
         out_shape=(jax.ShapeDtypeStruct((total, width), BF16), jax.ShapeDtypeStruct((1, 128), F32)),
         in_specs=[smem()] + [vmem()] * (len(parts) + len(lasts)),
         out_specs=(vmem(), vmem()),
@@ -527,6 +528,7 @@
         return lax.ppermute(array, "tm", route)
 
     plane = [(dx, dy) for dx in range(n_x) for dy in range(PAIR)]
+    n_plane = len(plane)
     info = jnp.stack([y, core, z, x * PAIR + y]).astype(jnp.int32)
     table = jnp.stack([pattern_in.T, pattern_pool.T])
     levels = jnp.stack([decay_rate, beta_bias])
@@ -576,19 +578,25 @@
     for g in sums:
         arrays = [a for pair in halves_[g * per_sum : (g + 1) * per_sum] for a in pair]
         spread.append(list(fold_call(info, 3, flat_plane, arrays, per_sum)))
-    spread[-1][0], output = lax.optimization_barrier((spread[-1][0], output))
-    met = [[p[0]] + [moved(a, (dx, 0, 0, dy)) for a, (dx, dy) in zip(p[1:], plane[1:])] for p in spread]
-    spread = [fold_call(info, 2, flat_z, m, 1) for m in met]
-    met = [[p[0]] + [moved(a, (0, 0, dz, 0)) for a, dz in zip(p[1:], flat_z[1:])] for p in spread]
+
+    def exchanged(sends, shifts):
+        gots = [[moved(a, shift) for a, shift in zip(p[1:], shifts[1:])] for p in sends]
+        for g in range(SUMS - 1):
+            for later in range(g + 1, SUMS):
+                gots[g][0], sends[later][0] = lax.optimization_barrier((gots[g][0], sends[later][0]))
+        return [[p[0]] + got for p, got in zip(sends, gots)]
+
+    across = [(dx, 0, 0, dy) for dx, dy in plane]
+    upward = [(0, 0, dz, 0) for dz in flat_z]
+    met = exchanged(spread, across)
+    met[-1][0], output = lax.optimization_barrier((met[-1][0], output))
+    met = exchanged([list(fold_call(info, 2, flat_z, m, 1)) for m in met], upward)
     totals = [total_call(m) for m in met]
-    along = []
-    for piece, _ in totals:
-        along.append(lay_call(info, 2, flat_z, [piece] + [moved(piece, (0, 0, dz, 0)) for dz in flat_z[1:]]))
-    parts = []
-    for piece in along:
-        laid = lay_call(info, 3, flat_plane, [piece] + [moved(piece, (dx, 0, 0, dy)) for dx, dy in plane[1:]])
-        parts += [laid, moved(laid, (0, 1, 0, 0))]
-    weight_grad, gain_grad = join_call(info, parts, [t[1] for t in totals], scale, dims, width)
+    met = exchanged([[t[0]] * n_z for t in totals], upward)
+    met = exchanged([[lay_call(info, 2, flat_z, m)] * n_plane for m in met], across)
+    laid = [lay_call(info, 3, flat_plane, m) for m in met]
+    parts = [part for piece in laid for part in (piece, moved(piece, (0, 1, 0, 0)))]
+    weight_grad, gain_grad = join_call(info, parts, [t[1] for t in totals], scale, dims, width, each // 2)
     return (output.reshape(seqs, span, width), weight_grad, gain_grad.reshape(dims))
 
 

time: 183 us -> 174 us (0.951)
  starting transfers between devices: 74.4 us -> 59.4 us
  waiting for transfers between devices: 41 us -> 54.3 us
  Pallas kernels: 60.4 us -> 53.5 us
    ppermute x12 -> x6, starting transfers between devices: 23.5 us -> 10.1 us  [lifted(): return lax.ppermute(array, 'tm', route)]
    ppermute x38 -> x32, waiting for transfers between devices: 41 us -> 50.5 us  [moved(): return lax.ppermute(array, both, route)]
    ppermute x12 -> x6, waiting for transfers between devices: 0.03 us -> 3.72 us  [lifted(): return lax.ppermute(array, 'tm', route)]
    pallas_call x8 -> x4, Pallas kernels: 6 us -> 3.25 us  [hop_call(): pl.pallas_call(functools.partial(hop_kernel, level), out_shape=(shape, sh...]
    ppermute x38 -> x32, starting transfers between devices: 50.9 us -> 49.3 us  [moved(): return lax.ppermute(array, both, route)]
    pallas_call x4 -> x2, Pallas kernels: 9.66 us -> 8.75 us  [mix_call(): pl.pallas_call(functools.partial(mix_kernel, span), out_shape=(jax.ShapeD...]
    pallas_call x4 -> x2, Pallas kernels: 24.9 us -> 24.3 us  [local_call(): pl.pallas_call(functools.partial(local_kernel, first_head, heads, span, P...]
  transfers between devices with their start and end apart: 50 -> 38, of which waited for: 18 -> 16; matrix products, arithmetic and copies ran while one was open for 0% -> 0% of each run, Pallas kernels for 28% -> 22%
where the time goes in v5:
time: 174 us; the launch traced here: 173 us
  starting transfers between devices  59.4 us (34%)
  waiting for transfers between devices  54.3 us (31%)
  Pallas kernels  53.5 us (31%)
  local copies, waits for them, and re-layouts  3.61 us (2%)
    ppermute x32, waiting for transfers between devices, moved(): return lax.ppermute(array, both, route)  50.5 us
    ppermute x32, starting transfers between devices, moved(): return lax.ppermute(array, both, route)  49.3 us
    pallas_call x2, Pallas kernels, local_call(): pl.pallas_call(functools.partial(local_kernel, first_head, heads, span, P...  24.3 us
    ppermute x6, starting transfers between devices, lifted(): return lax.ppermute(array, 'tm', route)  10.1 us
    pallas_call x2, Pallas kernels, mix_call(): pl.pallas_call(functools.partial(mix_kernel, span), out_shape=(jax.ShapeD...  8.75 us
    ppermute x6, waiting for transfers between devices, lifted(): return lax.ppermute(array, 'tm', route)  3.72 us
    unnamed x12, local copies, waits for them, and re-layouts  3.59 us
  transfers between devices with their start and end apart: 38, of which 16 were waited for; matrix products, arithmetic and copies ran while one was open for 0% of the time, Pallas kernels for 22%

profile of v5, /device:TPU:0, one launch (start us, length us, event | category | flops | bytes accessed | tf_op | source)
XLA Modules:
  0.0 173.2 jit_solution(5319749059651588956)
XLA Ops:
  5.7 13.2 %local.2 = (f32[4,128,256]{2,1,0:T(8,128)S(1)}, f32[4,128,256]{2,1,0:T(8,128)S(1)}, f32[512,512]{1,0:T(8,128)S(1)}, f32[512,512]{1,0:T(8,128)S(1)}, f32[512,16]{1,0:T(8,128)S(1)}) custom-call(s32[4]{0:T(128)S(1)} %pad_add_fusion.1.info, s32[2,4,24]{2,1,0:T(4,128)S(1)} %pad_add_fusion.table, bf16[512,1024]{1,0:T(8,128)(2,1)S(1)} %bitcast.23, ...), custom_call_target="tpu_custom_call" | custom-call | flops 6442450944 | bytes 8388608 | tf_op jit(solution)/shard_map/local/pallas_call | solution.py:188
  18.9 3.0 %collective-permute-start = (f32[4,128,256]{2,1,0:T(8,128)S(1)}, f32[4,128,256]{2,1,0:T(8,128)S(1)}, u32[]{:S(2)}, u32[]{:S(2)}) collective-permute-start(f32[4,128,256]{2,1,0:T(8,128)S(1)} %get-tuple-element.73), channel_id=1, source_target_pairs={{0,1},{1,0},{2,3},{3,2},{4,5},{5,4},{6,7},{7,6},{8,9},{9,8},{10,11... | collective-permute-start | bytes 1572872 | tf_op jit(solution)/shard_map/ppermute | solution.py:523
  21.9 11.2 %local.3 = (f32[4,128,256]{2,1,0:T(8,128)S(1)}, f32[4,128,256]{2,1,0:T(8,128)S(1)}, f32[512,512]{1,0:T(8,128)S(1)}, f32[512,512]{1,0:T(8,128)S(1)}) custom-call(s32[4]{0:T(128)S(1)} %pad_add_fusion.1.info, s32[2,4,24]{2,1,0:T(4,128)S(1)} %pad_add_fusion.table, bf16[512,1024]{1,0:T(8,128)(2,1)S(1)} %bitcast.24, bf16[64,128,128]{2,1,0:T(8,128)(2,1)S(1)} %copy-done.3, ...), custom_call_target="tpu_custom_call" | custom-call | flops 6442450944 | bytes 8388608 | tf_op jit(solution)/shard_map/local/pallas_call | solution.py:188
  34.8 3.9 %collective-permute-start.1 = (f32[4,128,128]{2,1,0:T(8,128)S(1)}, f32[4,128,128]{2,1,0:T(8,128)S(1)}, u32[]{:S(2)}, u32[]{:S(2)}) collective-permute-start(f32[4,128,128]{2,1,0:T(8,128)S(1)} %get-tuple-element.76), channel_id=1, source_target_pairs={{0,2},{1,3},{2,0},{3,1},{8,10},{9,11},{10,8},{11,9},{16,18},{17,19... | collective-permute-start | bytes 786440 | tf_op jit(solution)/shard_map/ppermute | solution.py:528
  38.8 3.3 %back.1.back_ref = f32[512,1024]{1,0:T(8,128)S(1)} custom-call(bf16[512,1024]{1,0:T(8,128)(2,1)S(1)} %bitcast.18, bf16[1024,1024]{1,0:T(8,128)(2,1)S(1)} %copy-done.1), custom_call_target="tpu_custom_call" | custom-call | flops 1073741824 | bytes 5242880 | tf_op jit(solution)/shard_map/back/pallas_call | solution.py:362
  42.1 4.5 %collective-permute-done.7.got_ref = f32[4,128,256]{2,1,0:T(8,128)S(1)} collective-permute-done((f32[4,128,256]{2,1,0:T(8,128)S(1)}, f32[4,128,256]{2,1,0:T(8,128)S(1)}, u32[]{:S(2)}, u32[]{:S(2)}) %collective-permute-start.7) | collective-permute-done | bytes 524320 | tf_op jit(solution)/shard_map/ppermute | solution.py:523
  47.6 3.5 %collective-permute-start.8 = (f32[4,128,128]{2,1,0:T(8,128)S(1)}, f32[4,128,128]{2,1,0:T(8,128)S(1)}, u32[]{:S(2)}, u32[]{:S(2)}) collective-permute-start(f32[4,128,128]{2,1,0:T(8,128)S(1)} %get-tuple-element.95), channel_id=1, source_target_pairs={{0,2},{1,3},{2,0},{3,1},{8,10},{9,11},{10,8},{11,9},{16,18},{17,19... | collective-permute-start | bytes 786440 | tf_op jit(solution)/shard_map/ppermute | solution.py:528
  52.6 3.7 %collective-permute-done.8.got_ref = f32[4,128,128]{2,1,0:T(8,128)S(1)} collective-permute-done((f32[4,128,128]{2,1,0:T(8,128)S(1)}, f32[4,128,128]{2,1,0:T(8,128)S(1)}, u32[]{:S(2)}, u32[]{:S(2)}) %collective-permute-start.8) | collective-permute-done | bytes 262176 | tf_op jit(solution)/shard_map/ppermute | solution.py:528
  64.7 5.8 %collective-permute-done.4.got_ref = f32[4,128,128]{2,1,0:T(8,128)S(1)} collective-permute-done((f32[4,128,128]{2,1,0:T(8,128)S(1)}, f32[4,128,128]{2,1,0:T(8,128)S(1)}, u32[]{:S(2)}, u32[]{:S(2)}) %collective-permute-start.4) | collective-permute-done | bytes 262176 | tf_op jit(solution)/shard_map/ppermute | solution.py:523
  70.5 4.4 %mix.2 = (bf16[512,512]{1,0:T(8,128)(2,1)S(1)}, f32[257,8,128]{2,1,0:T(8,128)S(1)}, f32[257,8,128]{2,1,0:T(8,128)S(1)}) custom-call(s32[4]{0:T(128)S(1)} %pad_add_fusion.1.info, f32[512,512]{1,0:T(8,128)S(1)} %get-tuple-element.70.core_ref, f32[512,512]{1,0:T(8,128)S(1)} %get-tuple-element.71.query_ref, f32[4,128,128]{2,1,0:T(8,128)S(1)} %get-tuple-element.82.keep_ref, ...), custom_call_target="tpu_custom_call" | custom-call | flops 536870912 | bytes 3145728 | tf_op jit(solution)/shard_map/mix/pallas_call | solution.py:340
  75.0 4.4 %mix.3 = (bf16[512,512]{1,0:T(8,128)(2,1)S(1)}, f32[257,8,128]{2,1,0:T(8,128)S(1)}, f32[257,8,128]{2,1,0:T(8,128)S(1)}) custom-call(s32[4]{0:T(128)S(1)} %pad_add_fusion.1.info, f32[512,512]{1,0:T(8,128)S(1)} %get-tuple-element.89.core_ref, f32[512,512]{1,0:T(8,128)S(1)} %get-tuple-element.90.query_ref, f32[4,128,128]{2,1,0:T(8,128)S(1)} %get-tuple-element.100.keep_ref, ...), custom_call_target="tpu_custom_call" | custom-call | flops 536870912 | bytes 3145728 | tf_op jit(solution)/shard_map/mix/pallas_call | solution.py:340
  86.9 4.0 %collective-permute-done.6.refs_1_ = f32[65,8,128]{2,1,0:T(8,128)S(1)} collective-permute-done((f32[65,8,128]{2,1,0:T(8,128)S(1)}, f32[65,8,128]{2,1,0:T(8,128)S(1)}, u32[]{:S(2)}, u32[]{:S(2)}) %collective-permute-start.6) | collective-permute-done | bytes 266272 | tf_op jit(solution)/shard_map/ppermute | solution.py:523
  92.3 4.8 %collective-permute-done.14.refs_3_ = f32[65,8,128]{2,1,0:T(8,128)S(1)} collective-permute-done((f32[65,8,128]{2,1,0:T(8,128)S(1)}, f32[65,8,128]{2,1,0:T(8,128)S(1)}, u32[]{:S(2)}, u32[]{:S(2)}) %collective-permute-start.14) | collective-permute-done | bytes 266272 | tf_op jit(solution)/shard_map/ppermute | solution.py:523
  97.8 6.5 %collective-permute-start.15 = (f32[17,8,128]{2,1,0:T(8,128)S(1)}, f32[17,8,128]{2,1,0:T(8,128)S(1)}, u32[]{:S(2)}, u32[]{:S(2)}) collective-permute-start(f32[17,8,128]{2,1,0:T(8,128)S(1)} %get-tuple-element.114), channel_id=1, source_target_pairs={{0,2},{1,3},{2,0},{3,1},{4,6},{5,7},{6,4},{7,5},{8,10},{9,11},{10,... | collective-permute-start | bytes 208904 | tf_op jit(solution)/shard_map/ppermute | solution.py:523
  104.3 2.8 %finish.1 = bf16[512,1024]{1,0:T(8,128)(2,1)} custom-call(bf16[512,512]{1,0:T(8,128)(2,1)S(1)} %get-tuple-element.106.refs_0_, bf16[512,512]{1,0:T(8,128)(2,1)S(1)} %get-tuple-element.107.refs_1_, bf16[1024,1024]{1,0:T(8,128)(2,1)S(1)} %copy-done.1), custom_call_target="tpu_custom_call" | custom-call | flops 1073741824 | bytes 4194304 | tf_op jit(solution)/shard_map/finish/pallas_call | solution.py:385
  107.2 6.5 %collective-permute-start.19 = (f32[17,8,128]{2,1,0:T(8,128)S(1)}, f32[17,8,128]{2,1,0:T(8,128)S(1)}, u32[]{:S(2)}, u32[]{:S(2)}) collective-permute-start(f32[17,8,128]{2,1,0:T(8,128)S(1)} %get-tuple-element.121), channel_id=1, source_target_pairs={{0,4},{1,5},{2,6},{3,7},{4,0},{5,1},{6,2},{7,3},{8,12},{9,13},{10,... | collective-permute-start | bytes 208904 | tf_op jit(solution)/shard_map/ppermute | solution.py:523
  116.3 4.7 %collective-permute-start.23 = (f32[17,8,128]{2,1,0:T(8,128)S(1)}, f32[17,8,128]{2,1,0:T(8,128)S(1)}, u32[]{:S(2)}, u32[]{:S(2)}) collective-permute-start(f32[17,8,128]{2,1,0:T(8,128)S(1)} %get-tuple-element.126), channel_id=1, source_target_pairs={{0,4},{1,5},{2,6},{3,7},{4,0},{5,1},{6,2},{7,3},{8,12},{9,13},{10,... | collective-permute-start | bytes 208904 | tf_op jit(solution)/shard_map/ppermute | solution.py:523
  123.1 2.9 %collective-permute-start.26 = (f32[16,8,128]{2,1,0:T(8,128)S(1)}, f32[16,8,128]{2,1,0:T(8,128)S(1)}, u32[]{:S(2)}, u32[]{:S(2)}) collective-permute-start(f32[16,8,128]{2,1,0:T(8,128)S(1)} %get-tuple-element.123.refs_0_), channel_id=1, source_target_pairs={{0,6},{1,7},{2,4},{3,5},{4,2},{5,3},{6,0},{7,1},{8,14},{9,15},{10,... | collective-permute-start | bytes 196616 | tf_op jit(solution)/shard_map/ppermute | solution.py:523
  130.4 3.0 %collective-permute-done.25.refs_2_ = f32[16,8,128]{2,1,0:T(8,128)S(1)} collective-permute-done((f32[16,8,128]{2,1,0:T(8,128)S(1)}, f32[16,8,128]{2,1,0:T(8,128)S(1)}, u32[]{:S(2)}, u32[]{:S(2)}) %collective-permute-start.25) | collective-permute-done | bytes 65568 | tf_op jit(solution)/shard_map/ppermute | solution.py:523
  149.8 3.7 %collective-permute-done.36.refs_3_ = f32[64,8,128]{2,1,0:T(8,128)S(1)} collective-permute-done((f32[64,8,128]{2,1,0:T(8,128)S(1)}, f32[64,8,128]{2,1,0:T(8,128)S(1)}, u32[]{:S(2)}, u32[]{:S(2)}) %collective-permute-start.36) | collective-permute-done | bytes 262176 | tf_op jit(solution)/shard_map/ppermute | solution.py:523
  153.6 5.6 %collective-permute-done.35.refs_2_ = f32[64,8,128]{2,1,0:T(8,128)S(1)} collective-permute-done((f32[64,8,128]{2,1,0:T(8,128)S(1)}, f32[64,8,128]{2,1,0:T(8,128)S(1)}, u32[]{:S(2)}, u32[]{:S(2)}) %collective-permute-start.35) | collective-permute-done | bytes 262176 | tf_op jit(solution)/shard_map/ppermute | solution.py:523
  159.9 4.7 %collective-permute-done.32.refs_3_ = f32[64,8,128]{2,1,0:T(8,128)S(1)} collective-permute-done((f32[64,8,128]{2,1,0:T(8,128)S(1)}, f32[64,8,128]{2,1,0:T(8,128)S(1)}, u32[]{:S(2)}, u32[]{:S(2)}) %collective-permute-start.32) | collective-permute-done | bytes 262176 | tf_op jit(solution)/shard_map/ppermute | solution.py:523
  164.6 2.9 %collective-permute-done.31.refs_2_ = f32[64,8,128]{2,1,0:T(8,128)S(1)} collective-permute-done((f32[64,8,128]{2,1,0:T(8,128)S(1)}, f32[64,8,128]{2,1,0:T(8,128)S(1)}, u32[]{:S(2)}, u32[]{:S(2)}) %collective-permute-start.31) | collective-permute-done | bytes 262176 | tf_op jit(solution)/shard_map/ppermute | solution.py:523
  168.2 2.6 %collective-permute-done.33.refs_1_ = f32[256,8,128]{2,1,0:T(8,128)S(1)} collective-permute-done((f32[256,8,128]{2,1,0:T(8,128)S(1)}, f32[256,8,128]{2,1,0:T(8,128)S(1)}, u32[]{:S(2)}, u32[]{:S(2)}) %collective-permute-start.33) | collective-permute-done | bytes 1048608 | tf_op jit(solution)/shard_map/ppermute | solution.py:523
  (93 shorter events, 56.6 us)
Async XLA Ops:
  18.9 15.0 %collective-permute-start = (f32[4,128,256]{2,1,0:T(8,128)S(1)}, f32[4,128,256]{2,1,0:T(8,128)S(1)}, u32[]{:S(2)}, u32[]{:S(2)}) collective-permute-start(f32[4,128,256]{2,1,0:T(8,128)S(1)} %get-tuple-element.73), channel_id=1, source_target_pairs={{0,1},{1,0},{2,3},{3,2},{4,5},{5,4},{6,7},{7,6},{8,9},{9,8},{10,11... | collective-permute-start | bytes 1572872 | tf_op jit(solution)/shard_map/ppermute | solution.py:523
  33.1 13.5 %collective-permute-start.7 = (f32[4,128,256]{2,1,0:T(8,128)S(1)}, f32[4,128,256]{2,1,0:T(8,128)S(1)}, u32[]{:S(2)}, u32[]{:S(2)}) collective-permute-start(f32[4,128,256]{2,1,0:T(8,128)S(1)} %get-tuple-element.92), channel_id=1, source_target_pairs={{0,1},{1,0},{2,3},{3,2},{4,5},{5,4},{6,7},{7,6},{8,9},{9,8},{10,11... | collective-permute-start | bytes 1572872 | tf_op jit(solution)/shard_map/ppermute | solution.py:523
  34.8 16.2 %collective-permute-start.1 = (f32[4,128,128]{2,1,0:T(8,128)S(1)}, f32[4,128,128]{2,1,0:T(8,128)S(1)}, u32[]{:S(2)}, u32[]{:S(2)}) collective-permute-start(f32[4,128,128]{2,1,0:T(8,128)S(1)} %get-tuple-element.76), channel_id=1, source_target_pairs={{0,2},{1,3},{2,0},{3,1},{8,10},{9,11},{10,8},{11,9},{16,18},{17,19... | collective-permute-start | bytes 786440 | tf_op jit(solution)/shard_map/ppermute | solution.py:528
  47.6 8.7 %collective-permute-start.8 = (f32[4,128,128]{2,1,0:T(8,128)S(1)}, f32[4,128,128]{2,1,0:T(8,128)S(1)}, u32[]{:S(2)}, u32[]{:S(2)}) collective-permute-start(f32[4,128,128]{2,1,0:T(8,128)S(1)} %get-tuple-element.95), channel_id=1, source_target_pairs={{0,2},{1,3},{2,0},{3,1},{8,10},{9,11},{10,8},{11,9},{16,18},{17,19... | collective-permute-start | bytes 786440 | tf_op jit(solution)/shard_map/ppermute | solution.py:528
  61.7 8.8 %collective-permute-start.4 = (f32[4,128,128]{2,1,0:T(8,128)S(1)}, f32[4,128,128]{2,1,0:T(8,128)S(1)}, u32[]{:S(2)}, u32[]{:S(2)}) collective-permute-start(f32[4,128,128]{2,1,0:T(8,128)S(1)} %get-tuple-element.83), channel_id=1, source_target_pairs={{0,1},{1,0},{2,3},{3,2},{4,5},{5,4},{6,7},{7,6},{8,9},{9,8},{10,11... | collective-permute-start | bytes 786440 | tf_op jit(solution)/shard_map/ppermute | solution.py:523
  63.2 11.7 %collective-permute-start.11 = (f32[4,128,128]{2,1,0:T(8,128)S(1)}, f32[4,128,128]{2,1,0:T(8,128)S(1)}, u32[]{:S(2)}, u32[]{:S(2)}) collective-permute-start(f32[4,128,128]{2,1,0:T(8,128)S(1)} %get-tuple-element.101), channel_id=1, source_target_pairs={{0,1},{1,0},{2,3},{3,2},{4,5},{5,4},{6,7},{7,6},{8,9},{9,8},{10,11... | collective-permute-start | bytes 786440 | tf_op jit(solution)/shard_map/ppermute | solution.py:523
  80.6 10.3 %collective-permute-start.6 = (f32[65,8,128]{2,1,0:T(8,128)S(1)}, f32[65,8,128]{2,1,0:T(8,128)S(1)}, u32[]{:S(2)}, u32[]{:S(2)}) collective-permute-start(f32[65,8,128]{2,1,0:T(8,128)S(1)} %get-tuple-element.87), channel_id=1, source_target_pairs={{0,1},{1,0},{2,3},{3,2},{4,5},{5,4},{6,7},{7,6},{8,9},{9,8},{10,11... | collective-permute-start | bytes 798728 | tf_op jit(solution)/shard_map/ppermute | solution.py:523
  81.6 10.7 %collective-permute-start.13 = (f32[65,8,128]{2,1,0:T(8,128)S(1)}, f32[65,8,128]{2,1,0:T(8,128)S(1)}, u32[]{:S(2)}, u32[]{:S(2)}) collective-permute-start(f32[65,8,128]{2,1,0:T(8,128)S(1)} %get-tuple-element.111), channel_id=1, source_target_pairs={{0,16},{1,17},{2,18},{3,19},{4,20},{5,21},{6,22},{7,23},{8,24},{9,... | collective-permute-start | bytes 798728 | tf_op jit(solution)/shard_map/ppermute | solution.py:523
  82.7 14.5 %collective-permute-start.14 = (f32[65,8,128]{2,1,0:T(8,128)S(1)}, f32[65,8,128]{2,1,0:T(8,128)S(1)}, u32[]{:S(2)}, u32[]{:S(2)}) collective-permute-start(f32[65,8,128]{2,1,0:T(8,128)S(1)} %get-tuple-element.112), channel_id=1, source_target_pairs={{0,17},{1,16},{2,19},{3,18},{4,21},{5,20},{6,23},{7,22},{8,25},{9,... | collective-permute-start | bytes 798728 | tf_op jit(solution)/shard_map/ppermute | solution.py:523
  84.8 28.8 %collective-permute-start.16 = (f32[65,8,128]{2,1,0:T(8,128)S(1)}, f32[65,8,128]{2,1,0:T(8,128)S(1)}, u32[]{:S(2)}, u32[]{:S(2)}) collective-permute-start(f32[65,8,128]{2,1,0:T(8,128)S(1)} %get-tuple-element.116), channel_id=1, source_target_pairs={{0,1},{1,0},{2,3},{3,2},{4,5},{5,4},{6,7},{7,6},{8,9},{9,8},{10,11... | collective-permute-start | bytes 798728 | tf_op jit(solution)/shard_map/ppermute | solution.py:523
  85.9 29.2 %collective-permute-start.17 = (f32[65,8,128]{2,1,0:T(8,128)S(1)}, f32[65,8,128]{2,1,0:T(8,128)S(1)}, u32[]{:S(2)}, u32[]{:S(2)}) collective-permute-start(f32[65,8,128]{2,1,0:T(8,128)S(1)} %get-tuple-element.117), channel_id=1, source_target_pairs={{0,16},{1,17},{2,18},{3,19},{4,20},{5,21},{6,22},{7,23},{8,24},{9,... | collective-permute-start | bytes 798728 | tf_op jit(solution)/shard_map/ppermute | solution.py:523
  90.9 24.2 %collective-permute-start.18 = (f32[65,8,128]{2,1,0:T(8,128)S(1)}, f32[65,8,128]{2,1,0:T(8,128)S(1)}, u32[]{:S(2)}, u32[]{:S(2)}) collective-permute-start(f32[65,8,128]{2,1,0:T(8,128)S(1)} %get-tuple-element.118), channel_id=1, source_target_pairs={{0,17},{1,16},{2,19},{3,18},{4,21},{5,20},{6,23},{7,22},{8,25},{9,... | collective-permute-start | bytes 798728 | tf_op jit(solution)/shard_map/ppermute | solution.py:523
  97.8 23.2 %collective-permute-start.15 = (f32[17,8,128]{2,1,0:T(8,128)S(1)}, f32[17,8,128]{2,1,0:T(8,128)S(1)}, u32[]{:S(2)}, u32[]{:S(2)}) collective-permute-start(f32[17,8,128]{2,1,0:T(8,128)S(1)} %get-tuple-element.114), channel_id=1, source_target_pairs={{0,2},{1,3},{2,0},{3,1},{4,6},{5,7},{6,4},{7,5},{8,10},{9,11},{10,... | collective-permute-start | bytes 208904 | tf_op jit(solution)/shard_map/ppermute | solution.py:523
  107.2 15.3 %collective-permute-start.19 = (f32[17,8,128]{2,1,0:T(8,128)S(1)}, f32[17,8,128]{2,1,0:T(8,128)S(1)}, u32[]{:S(2)}, u32[]{:S(2)}) collective-permute-start(f32[17,8,128]{2,1,0:T(8,128)S(1)} %get-tuple-element.121), channel_id=1, source_target_pairs={{0,4},{1,5},{2,6},{3,7},{4,0},{5,1},{6,2},{7,3},{8,12},{9,13},{10,... | collective-permute-start | bytes 208904 | tf_op jit(solution)/shard_map/ppermute | solution.py:523
  113.6 8.8 %collective-permute-start.20 = (f32[17,8,128]{2,1,0:T(8,128)S(1)}, f32[17,8,128]{2,1,0:T(8,128)S(1)}, u32[]{:S(2)}, u32[]{:S(2)}) collective-permute-start(f32[17,8,128]{2,1,0:T(8,128)S(1)} %get-tuple-element.122), channel_id=1, source_target_pairs={{0,6},{1,7},{2,4},{3,5},{4,2},{5,3},{6,0},{7,1},{8,14},{9,15},{10,... | collective-permute-start | bytes 208904 | tf_op jit(solution)/shard_map/ppermute | solution.py:523
  115.7 10.3 %collective-permute-start.22 = (f32[17,8,128]{2,1,0:T(8,128)S(1)}, f32[17,8,128]{2,1,0:T(8,128)S(1)}, u32[]{:S(2)}, u32[]{:S(2)}) collective-permute-start(f32[17,8,128]{2,1,0:T(8,128)S(1)} %get-tuple-element.125), channel_id=1, source_target_pairs={{0,2},{1,3},{2,0},{3,1},{4,6},{5,7},{6,4},{7,5},{8,10},{9,11},{10,... | collective-permute-start | bytes 208904 | tf_op jit(solution)/shard_map/ppermute | solution.py:523
  116.3 9.7 %collective-permute-start.23 = (f32[17,8,128]{2,1,0:T(8,128)S(1)}, f32[17,8,128]{2,1,0:T(8,128)S(1)}, u32[]{:S(2)}, u32[]{:S(2)}) collective-permute-start(f32[17,8,128]{2,1,0:T(8,128)S(1)} %get-tuple-element.126), channel_id=1, source_target_pairs={{0,4},{1,5},{2,6},{3,7},{4,0},{5,1},{6,2},{7,3},{8,12},{9,13},{10,... | collective-permute-start | bytes 208904 | tf_op jit(solution)/shard_map/ppermute | solution.py:523
  134.0 15.3 %collective-permute-start.27 = (f32[64,8,128]{2,1,0:T(8,128)S(1)}, f32[64,8,128]{2,1,0:T(8,128)S(1)}, u32[]{:S(2)}, u32[]{:S(2)}) collective-permute-start(f32[64,8,128]{2,1,0:T(8,128)S(1)} %lay.4.refs_0_), channel_id=1, source_target_pairs={{0,1},{1,0},{2,3},{3,2},{4,5},{5,4},{6,7},{7,6},{8,9},{9,8},{10,11... | collective-permute-start | bytes 786440 | tf_op jit(solution)/shard_map/ppermute | solution.py:523
  143.3 10.2 %collective-permute-start.36 = (f32[64,8,128]{2,1,0:T(8,128)S(1)}, f32[64,8,128]{2,1,0:T(8,128)S(1)}, u32[]{:S(2)}, u32[]{:S(2)}) collective-permute-start(f32[64,8,128]{2,1,0:T(8,128)S(1)} %lay.5.refs_0_), channel_id=1, source_target_pairs={{0,17},{1,16},{2,19},{3,18},{4,21},{5,20},{6,23},{7,22},{8,25},{9,... | collective-permute-start | bytes 786440 | tf_op jit(solution)/shard_map/ppermute | solution.py:523
  145.8 13.4 %collective-permute-start.35 = (f32[64,8,128]{2,1,0:T(8,128)S(1)}, f32[64,8,128]{2,1,0:T(8,128)S(1)}, u32[]{:S(2)}, u32[]{:S(2)}) collective-permute-start(f32[64,8,128]{2,1,0:T(8,128)S(1)} %lay.5.refs_0_), channel_id=1, source_target_pairs={{0,16},{1,17},{2,18},{3,19},{4,20},{5,21},{6,22},{7,23},{8,24},{9,... | collective-permute-start | bytes 786440 | tf_op jit(solution)/shard_map/ppermute | solution.py:523
  146.3 12.8 %collective-permute-start.34 = (f32[64,8,128]{2,1,0:T(8,128)S(1)}, f32[64,8,128]{2,1,0:T(8,128)S(1)}, u32[]{:S(2)}, u32[]{:S(2)}) collective-permute-start(f32[64,8,128]{2,1,0:T(8,128)S(1)} %lay.5.refs_0_), channel_id=1, source_target_pairs={{0,1},{1,0},{2,3},{3,2},{4,5},{5,4},{6,7},{7,6},{8,9},{9,8},{10,11... | collective-permute-start | bytes 786440 | tf_op jit(solution)/shard_map/ppermute | solution.py:523
  146.9 17.7 %collective-permute-start.32 = (f32[64,8,128]{2,1,0:T(8,128)S(1)}, f32[64,8,128]{2,1,0:T(8,128)S(1)}, u32[]{:S(2)}, u32[]{:S(2)}) collective-permute-start(f32[64,8,128]{2,1,0:T(8,128)S(1)} %lay.4.refs_0_), channel_id=1, source_target_pairs={{0,17},{1,16},{2,19},{3,18},{4,21},{5,20},{6,23},{7,22},{8,25},{9,... | collective-permute-start | bytes 786440 | tf_op jit(solution)/shard_map/ppermute | solution.py:523
  149.3 18.2 %collective-permute-start.31 = (f32[64,8,128]{2,1,0:T(8,128)S(1)}, f32[64,8,128]{2,1,0:T(8,128)S(1)}, u32[]{:S(2)}, u32[]{:S(2)}) collective-permute-start(f32[64,8,128]{2,1,0:T(8,128)S(1)} %lay.4.refs_0_), channel_id=1, source_target_pairs={{0,16},{1,17},{2,18},{3,19},{4,20},{5,21},{6,22},{7,23},{8,24},{9,... | collective-permute-start | bytes 786440 | tf_op jit(solution)/shard_map/ppermute | solution.py:523
  159.8 8.4 %collective-permute-start.37 = (f32[256,8,128]{2,1,0:T(8,128)S(1)}, f32[256,8,128]{2,1,0:T(8,128)S(1)}, u32[]{:S(2)}, u32[]{:S(2)}) collective-permute-start(f32[256,8,128]{2,1,0:T(8,128)S(1)} %lay.7.refs_2_), channel_id=1, source_target_pairs={{0,8},{1,9},{2,10},{3,11},{4,12},{5,13},{6,14},{7,15},{8,0},{9,1},... | collective-permute-start | bytes 3145736 | tf_op jit(solution)/shard_map/ppermute | solution.py:523
  (20 other events, 107.0 us)

commit v6 on v4

--- a/solution.py
+++ b/solution.py
@@ -8,12 +8,11 @@
 from jax.experimental.pallas import tpu as pltpu
 from jax.sharding import PartitionSpec as P
 
-GROUPS = 4
-SUMS = 2
+RELAYS = (4, 2, 2)
+SUMS = ((0,), (1, 2))
 CORES = 2
 PAIR = 2
 PER_STEP = 2
-AHEAD = 3
 F32 = jnp.float32
 BF16 = jnp.bfloat16
 MIB = 1024 * 1024
@@ -56,6 +55,14 @@
 
 def whole(shape):
     return pl.BlockSpec(shape, lambda *_: (0,) * len(shape))
+
+
+def anywhere(after):
+    return [pl.BlockSpec(memory_space=pl.ANY)] * len(after)
+
+
+def skipping(kernel, first, after):
+    return lambda *refs: kernel(*refs[:first], *refs[first + len(after) :])
 
 
 def cost(flops, size):
@@ -171,7 +178,7 @@
         core_ref[rows, lanes] = seen[:, dims:]
 
 
-def local_call(info, table, rows, pool, extra, first_head, count_heads, heads, span):
+def local_call(info, table, rows, pool, extra, first_head, count_heads, heads, span, after=()):
     count, width = rows.shape
     dims = pool.shape[1]
     opening = isinstance(extra, tuple)
@@ -186,18 +193,18 @@
     else:
         more_in, more_out, more_out_specs, extra = [whole(gates.shape)], (), (), (extra,)
     return pl.pallas_call(
-        functools.partial(local_kernel, first_head, heads, span, PER_STEP, opening),
+        skipping(functools.partial(local_kernel, first_head, heads, span, PER_STEP, opening), 4 + len(extra), after),
         out_shape=(maps, maps, wide, wide) + more_out,
         grid_spec=pltpu.PrefetchScalarGridSpec(
             num_scalar_prefetch=2,
             grid=(count_heads // PER_STEP,),
-            in_specs=[whole(rows.shape), whole(pool.shape)] + more_in,
+            in_specs=[whole(rows.shape), whole(pool.shape)] + more_in + anywhere(after),
             out_specs=(map_spec, map_spec, row_spec, row_spec) + more_out_specs,
         ),
         compiler_params=params(28),
         cost_estimate=cost(count_heads * 2 * 2 * span * 256 * 256 * 24, 8 * MIB),
         name="local",
-    )(info, table, rows, pool, *extra)
+    )(info, table, rows, pool, *extra, *after)
 
 
 def apply_map(maps, state):
@@ -220,17 +227,17 @@
         push_ref[h] = push
 
 
-def combine_call(info, own, got):
+def combine_call(info, own, got, after=()):
     shape = jax.ShapeDtypeStruct(own.shape, F32)
     push = jax.ShapeDtypeStruct(own.shape[:2] + (own.shape[1],), F32)
     return pl.pallas_call(
-        combine_kernel,
+        skipping(combine_kernel, 3, after),
         out_shape=(shape, shape, push),
-        in_specs=[smem(), vmem(), vmem()],
+        in_specs=[smem(), vmem(), vmem()] + anywhere(after),
         compiler_params=params(12),
         cost_estimate=cost(own.shape[0] * 6 * 128 * 128 * 256, own.size * 16),
         name="combine",
-    )(info, own, got)
+    )(info, own, got, *after)
 
 
 def hop_kernel(level, info, maps_ref, got_ref, state_ref, kept_ref, out_ref):
@@ -243,16 +250,16 @@
         out_ref[h] = apply_map(maps, state) + maps[:, dims:]
 
 
-def hop_call(level, info, maps, got, state):
+def hop_call(level, info, maps, got, state, after=()):
     shape = jax.ShapeDtypeStruct(state.shape, F32)
     return pl.pallas_call(
-        functools.partial(hop_kernel, level),
+        skipping(functools.partial(hop_kernel, level), 4, after),
         out_shape=(shape, shape),
-        in_specs=[smem(), vmem(), vmem(), vmem()],
+        in_specs=[smem(), vmem(), vmem(), vmem()] + anywhere(after),
         compiler_params=params(12),
         cost_estimate=cost(maps.shape[0] * 6 * 128 * 128 * 128, maps.size * 8),
         name="hop",
-    )(info, maps, got, state)
+    )(info, maps, got, state, *after)
 
 
 def split_kernel(level, info, maps_ref, got_ref, state_ref, keep_ref, send_ref):
@@ -267,16 +274,16 @@
         send_ref[h] = jnp.where(second, state, middle)
 
 
-def split_call(level, info, maps, got, state):
+def split_call(level, info, maps, got, state, after=()):
     shape = jax.ShapeDtypeStruct(state.shape, F32)
     return pl.pallas_call(
-        functools.partial(split_kernel, level),
+        skipping(functools.partial(split_kernel, level), 4, after),
         out_shape=(shape, shape),
-        in_specs=[smem(), vmem(), vmem(), vmem()],
+        in_specs=[smem(), vmem(), vmem(), vmem()] + anywhere(after),
         compiler_params=params(12),
         cost_estimate=cost(maps.shape[0] * 6 * 128 * 128 * 128, maps.size * 8),
         name="split",
-    )(info, maps, got, state)
+    )(info, maps, got, state, *after)
 
 
 def mix_kernel(span, info, core_ref, query_ref, keep_ref, got_ref, back_ref, gain_ref, cot_ref, mixed_ref, wsend_ref, wkeep_ref):
@@ -323,7 +330,7 @@
             wkeep_ref[pl.ds((step - half) * each + i * stripe, stripe)] = piece
 
 
-def mix_call(info, first_head, core, query, keep, got, back, gain, cot, span):
+def mix_call(info, first_head, core, query, keep, got, back, gain, cot, span, after=()):
     count, width = cot.shape
     heads_here = keep.shape[0]
     dims = gain.shape[1]
@@ -338,18 +345,19 @@
     state_spec = pl.BlockSpec((1, dims, dims), lambda i, info: (order(i, info), 0, 0))
     weight = jax.ShapeDtypeStruct((half * dims * width // 1024 + 1, 8, 128), F32)
     return pl.pallas_call(
-        functools.partial(mix_kernel, span),
+        skipping(functools.partial(mix_kernel, span), 8, after),
         out_shape=(jax.ShapeDtypeStruct((count, heads_here * dims), BF16), weight, weight),
         grid_spec=pltpu.PrefetchScalarGridSpec(
             num_scalar_prefetch=1,
             grid=(heads_here,),
-            in_specs=[row_spec, row_spec, state_spec, state_spec, back_spec, whole(gain.shape), whole(cot.shape)],
+            in_specs=[row_spec, row_spec, state_spec, state_spec, back_spec, whole(gain.shape), whole(cot.shape)]
+            + anywhere(after),
             out_specs=(row_spec, whole(weight.shape), whole(weight.shape)),
         ),
         compiler_params=params(16),
         cost_estimate=cost(heads_here * 2 * 512 * 1024 * 128, 3 * MIB),
         name="mix",
-    )(info, core, query, keep, got, back, gain, cot)
+    )(info, core, query, keep, got, back, gain, cot, *after)
 
 
 def back_kernel(cot_ref, weight_ref, out_ref):
@@ -372,7 +380,8 @@
 
 
 def finish_kernel(groups, *refs):
-    weight_ref, out_ref = refs[groups:]
+    weight_ref, out_ref, done_ref = refs[groups:]
+    done_ref[...] = jnp.zeros_like(done_ref)
     stacked = jnp.concatenate([ref[...] for ref in refs[:groups]], axis=1)
     out_ref[...] = dot(stacked, weight_ref[...]).astype(BF16)
 
@@ -380,14 +389,13 @@
 def finish_call(mixed, weight):
     count = mixed[0].shape[0]
     width = weight.shape[1]
-    part_spec = pl.BlockSpec((128, mixed[0].shape[1]), lambda i: (i, 0))
     row_spec = pl.BlockSpec((128, width), lambda i: (i, 0))
     return pl.pallas_call(
         functools.partial(finish_kernel, len(mixed)),
-        out_shape=jax.ShapeDtypeStruct((count, width), BF16),
+        out_shape=(jax.ShapeDtypeStruct((count, width), BF16), jax.ShapeDtypeStruct((8, 128), F32)),
         grid=(count // 128,),
-        in_specs=[part_spec] * len(mixed) + [whole(weight.shape)],
-        out_specs=row_spec,
+        in_specs=[pl.BlockSpec((128, m.shape[1]), lambda i: (i, 0)) for m in mixed] + [whole(weight.shape)],
+        out_specs=(row_spec, whole((8, 128))),
         compiler_params=params(12),
         cost_estimate=cost(2 * count * width * width, 4 * MIB),
         name="finish",
@@ -413,19 +421,19 @@
         out[share] = last
 
 
-def fold_call(info, where, flips, arrays, parts):
+def fold_call(info, where, flips, arrays, parts, after=()):
     terms = len(arrays) // parts
     size = arrays[0].shape[0] - 1
     share = size * parts // len(flips)
     shape = jax.ShapeDtypeStruct((share + 1, 8, 128), F32)
     return pl.pallas_call(
-        functools.partial(fold_kernel, parts, terms, where, flips),
+        skipping(functools.partial(fold_kernel, parts, terms, where, flips), 1 + len(arrays), after),
         out_shape=[shape] * len(flips),
-        in_specs=[smem()] + [vmem()] * len(arrays),
+        in_specs=[smem()] + [vmem()] * len(arrays) + anywhere(after),
         compiler_params=params(12),
         cost_estimate=cost(size * 1024 * len(arrays), size * 4096 * (len(arrays) + 1)),
         name="fold",
-    )(info, *arrays)
+    )(info, *arrays, *after)
 
 
 def total_kernel(*refs):
@@ -448,47 +456,45 @@
     )(*arrays)
 
 
-def lay_kernel(where, flips, info, *refs):
-    out = refs[-1]
-    share = refs[0].shape[0]
-    for flip, ref in zip(flips, refs):
-        out[pl.ds((info[where] ^ flip) * share, share)] = ref[...]
-
-
-def lay_call(info, where, flips, arrays):
-    share = arrays[0].shape[0]
-    return pl.pallas_call(
-        functools.partial(lay_kernel, where, flips),
-        out_shape=jax.ShapeDtypeStruct((share * len(flips), 8, 128), F32),
-        in_specs=[smem()] + [vmem()] * len(arrays),
-        compiler_params=params(12),
-        cost_estimate=cost(0, share * len(flips) * 8192),
+def lay_kernel(where, info, own_ref, got_ref, out_ref):
+    share = own_ref.shape[0]
+    out_ref[pl.ds(info[where] * share, share)] = own_ref[...]
+    out_ref[pl.ds((1 - info[where]) * share, share)] = got_ref[...]
+
+
+def lay_call(info, where, own, got, after=()):
+    share = own.shape[0]
+    return pl.pallas_call(
+        skipping(functools.partial(lay_kernel, where), 3, after),
+        out_shape=jax.ShapeDtypeStruct((share * 2, 8, 128), F32),
+        in_specs=[smem(), vmem(), vmem()] + anywhere(after),
+        compiler_params=params(12),
+        cost_estimate=cost(0, share * 16384),
         name="lay",
-    )(info, *arrays)
-
-
-def join_kernel(scale, stripe, info, *refs):
+    )(info, own, got, *after)
+
+
+def join_kernel(scale, stripe, blocks, info, *refs):
     sums = (len(refs) - 2) // 3
     lasts, (out_ref, gain_ref) = refs[2 * sums : 3 * sums], refs[-2:]
     columns = out_ref.shape[1] // 128
     dims = stripe * 8
-    blocks = refs[0].shape[0] // (columns * stripe)
     for g in range(sums):
         for part, ref in enumerate(refs[2 * g : 2 * g + 2]):
             side = info[1] if part == 0 else 1 - info[1]
-            for block in range(blocks):
-                head = (g * blocks + block) * 2 + side
+            for index, (base, half) in enumerate(blocks[g]):
+                rows = pl.ds(pl.multiple_of((base + side * half) * dims, dims), dims)
                 for col in range(columns):
-                    first = (block * columns + col) * stripe
+                    first = (index * columns + col) * stripe
                     values = ref[first : first + stripe].reshape(dims, 128) * scale
-                    out_ref[pl.ds(pl.multiple_of(head * dims, dims), dims), col * 128 : (col + 1) * 128] = values.astype(BF16)
+                    out_ref[rows, col * 128 : (col + 1) * 128] = values.astype(BF16)
     gain_ref[...] = jnp.sum(sum(ref[...] for ref in lasts), axis=0, keepdims=True) * scale
 
 
-def join_call(info, parts, lasts, scale, dims, width):
+def join_call(info, parts, lasts, blocks, scale, dims, width):
     total = sum(p.shape[0] for p in parts) * 1024 // width
     return pl.pallas_call(
-        functools.partial(join_kernel, scale, dims // 8),
+        functools.partial(join_kernel, scale, dims // 8, blocks),
         out_shape=(jax.ShapeDtypeStruct((total, width), BF16), jax.ShapeDtypeStruct((1, 128), F32)),
         in_specs=[smem()] + [vmem()] * (len(parts) + len(lasts)),
         out_specs=(vmem(), vmem()),
@@ -526,69 +532,89 @@
         route = [(a * PAIR + yi, b * PAIR + yi) for a, b in ends for yi in range(PAIR)]
         return lax.ppermute(array, "tm", route)
 
-    plane = [(dx, dy) for dx in range(n_x) for dy in range(PAIR)]
-    info = jnp.stack([y, core, z, x * PAIR + y]).astype(jnp.int32)
+    def bits(size):
+        return [1 << bit for bit in range(size.bit_length() - 1)]
+
+    steps_x = [((reach, 0, 0, 0), (x // reach) % 2) for reach in bits(n_x)]
+    steps_y = [((0, 0, 0, reach), (y // reach) % 2) for reach in bits(PAIR)]
+    steps_z = [((0, 0, reach, 0), (z // reach) % 2) for reach in bits(n_z)]
+    labelled = [(shift, 3 + i) for i, (shift, _) in enumerate(steps_x + steps_y + steps_z)]
+    on_x, on_y = labelled[: len(steps_x)], labelled[len(steps_x) : len(steps_x) + len(steps_y)]
+    on_z = labelled[len(steps_x) + len(steps_y) :]
+    info = jnp.stack([y, core, z] + [bit for _, bit in steps_x + steps_y + steps_z]).astype(jnp.int32)
     table = jnp.stack([pattern_in.T, pattern_pool.T])
     levels = jnp.stack([decay_rate, beta_bias])
     rows = features.reshape(count, width)
     cot = cotangent.reshape(count, width)
     gain = norm_gain.reshape(1, dims)
-    each = heads // GROUPS
-    per_sum = GROUPS // SUMS
-
-    gates = None
-    locals_, maps = [], []
-    for g in range(GROUPS):
-        told = info
-        if g >= AHEAD:
-            told, maps[g - AHEAD] = lax.optimization_barrier((info, maps[g - AHEAD]))
-        extra = (gate_weight.T, levels) if g == 0 else gates
-        own, send, *rest = local_call(told, table, rows, weight_pool, extra, g * each, each, heads, span)
+    relays = range(len(RELAYS))
+    last = len(RELAYS) - 1
+    first_of = [sum(RELAYS[:g]) for g in relays]
+
+    extra = (gate_weight.T, levels)
+    locals_ = []
+    for g in relays:
+        after = [locals_[-1][0]] if g else []
+        out = list(local_call(info, table, rows, weight_pool, extra, first_of[g], RELAYS[g], heads, span, after))
         if g == 0:
-            gates = rest.pop()
-        locals_.append(rest)
-        maps.append(list(combine_call(info, own, moved(send, (0, 0, 0, 1)))))
+            extra = out.pop()
+        locals_.append(out)
     back = back_call(cot, out_weight)
-    states = [jnp.zeros((each, dims, dims), F32)] * GROUPS
+    maps = []
+    for g in relays:
+        after = [locals_[last][0]] if g == 0 else [maps[-1][2]]
+        if g == last:
+            after.append(back)
+        maps.append(combine_call(info, locals_[g][0], moved(locals_[g][1], (0, 0, 0, 1)), after))
+    states = [jnp.zeros((size, dims, dims), F32) for size in RELAYS]
     sends = [m[2] for m in maps]
     for level in range(1, n_z):
         gots = [lifted(send, level - 1) for send in sends]
-        if level == 1:
-            gots[0], back = lax.optimization_barrier((gots[0], back))
+        after = [sends[last]]
         if level == n_z - 1:
             break
-        for g in range(GROUPS):
-            states[g], sends[g] = hop_call(level, info, maps[g][1], gots[g], states[g])
-    mixed, halves_ = [], []
-    for g in range(GROUPS):
-        keep, send = split_call(n_z - 1, info, maps[g][0], gots[g], states[g])
-        got = moved(send, (0, 0, 0, 1))
-        flat, w_send, w_keep = mix_call(info, g * each, *locals_[g], keep, got, back, gain, cot, span)
+        for g in relays:
+            states[g], sends[g] = hop_call(level, info, maps[g][1], gots[g], states[g], after)
+            after = [sends[g]]
+    mixed, kept, got, ready = [], [], [], []
+    for g in relays:
+        keep, send = split_call(n_z - 1, info, maps[g][0], gots[g], states[g], after)
+        after = [send]
+        ready.append((keep, moved(send, (0, 0, 0, 1))))
+    for g in relays:
+        states_g = *locals_[g][2:], *ready[g]
+        flat, w_send, w_keep = mix_call(info, first_of[g], *states_g, back, gain, cot, span, after)
+        after = [w_keep]
         mixed.append(flat)
-        halves_.append([w_keep, moved(w_send, (0, 1, 0, 0))])
-    output = finish_call(mixed, out_weight)
+        kept.append(w_keep)
+        got.append(moved(w_send, (0, 1, 0, 0)))
+    output, done = finish_call(mixed, out_weight)
     scale = 1.0 / math.sqrt(count * n_shot * n_tm)
 
-    flat_plane = tuple(dx * PAIR + dy for dx, dy in plane)
-    flat_z = tuple(range(n_z))
-    sums = range(SUMS)
-    spread = []
-    for g in sums:
-        arrays = [a for pair in halves_[g * per_sum : (g + 1) * per_sum] for a in pair]
-        spread.append(list(fold_call(info, 3, flat_plane, arrays, per_sum)))
-    spread[-1][0], output = lax.optimization_barrier((spread[-1][0], output))
-    met = [[p[0]] + [moved(a, (dx, 0, 0, dy)) for a, (dx, dy) in zip(p[1:], plane[1:])] for p in spread]
-    spread = [fold_call(info, 2, flat_z, m, 1) for m in met]
-    met = [[p[0]] + [moved(a, (0, 0, dz, 0)) for a, dz in zip(p[1:], flat_z[1:])] for p in spread]
-    totals = [total_call(m) for m in met]
-    along = []
-    for piece, _ in totals:
-        along.append(lay_call(info, 2, flat_z, [piece] + [moved(piece, (0, 0, dz, 0)) for dz in flat_z[1:]]))
-    parts = []
-    for piece in along:
-        laid = lay_call(info, 3, flat_plane, [piece] + [moved(piece, (dx, 0, 0, dy)) for dx, dy in plane[1:]])
-        parts += [laid, moved(laid, (0, 1, 0, 0))]
-    weight_grad, gain_grad = join_call(info, parts, [t[1] for t in totals], scale, dims, width)
+    sums = range(len(SUMS))
+    orders = [(on_x + on_y if g % 2 == 0 else on_y + on_x) + on_z for g in sums]
+    arrays = [[a for r in SUMS[g] for a in (kept[r], got[r])] for g in sums]
+    parts = [len(SUMS[g]) for g in sums]
+    previous = None
+    for step in range(len(orders[0])):
+        for g in sums:
+            shift, where = orders[g][step]
+            after = [previous] if g or step else []
+            if g == sums[-1] and step == 1:
+                after.append(done)
+            own, send = fold_call(info, where, (0, 1), arrays[g], parts[g], after)
+            arrays[g], parts[g] = [own, moved(send, shift)], 1
+            previous = own
+    totals = [total_call(a) for a in arrays]
+    pieces = [t[0] for t in totals]
+    for step in reversed(range(len(orders[0]))):
+        arrived = [moved(pieces[g], orders[g][step][0]) for g in sums]
+        previous = pieces[-1]
+        for g in sums:
+            pieces[g] = previous = lay_call(info, orders[g][step][1], pieces[g], arrived[g], [previous])
+    ends = [part for piece in pieces for part in (piece, moved(piece, (0, 1, 0, 0)))]
+    blocks = [[(first_of[r] + i, RELAYS[r] // 2) for r in SUMS[g] for i in range(RELAYS[r] // 2)] for g in sums]
+    weight_grad, gain_grad = join_call(info, ends, [t[1] for t in totals], blocks, scale, dims, width)
     return (output.reshape(seqs, span, width), weight_grad, gain_grad.reshape(dims))
 
 

time: 183 us -> 180 us (0.984)
  starting transfers between devices: 74.4 us -> 62.3 us
  waiting for transfers between devices: 41 us -> 49.3 us
    ppermute x12 -> x9, starting transfers between devices: 23.5 us -> 16.1 us  [lifted(): return lax.ppermute(array, 'tm', route)]
    ppermute x38 -> x27, starting transfers between devices: 50.9 us -> 46.2 us  [moved(): return lax.ppermute(array, both, route)]
    ppermute x38 -> x27, waiting for transfers between devices: 41 us -> 45.2 us  [moved(): return lax.ppermute(array, both, route)]
    ppermute x12 -> x9, waiting for transfers between devices: 0.03 us -> 4.18 us  [lifted(): return lax.ppermute(array, 'tm', route)]
    pallas_call x34 -> x36, Pallas kernels: 57.1 us -> 58.3 us  [the longest x3 24.8 us: local_call(): pl.pallas_call(skipping(functools.partial(local_kernel, first_head, heads...]
  transfers between devices with their start and end apart: 50 -> 36, of which waited for: 18 -> 19; matrix products, arithmetic and copies ran while one was open for 0% -> 0% of each run, Pallas kernels for 28% -> 21%
where the time goes in v6:
time: 180 us
  starting transfers between devices  62.3 us (35%)
  Pallas kernels  61.6 us (34%)
  waiting for transfers between devices  49.3 us (27%)
  local copies, waits for them, and re-layouts  3.7 us (2%)
    ppermute x27, starting transfers between devices, moved(): return lax.ppermute(array, both, route)  46.2 us
    ppermute x27, waiting for transfers between devices, moved(): return lax.ppermute(array, both, route)  45.2 us
    pallas_call x3, Pallas kernels, local_call(): pl.pallas_call(skipping(functools.partial(local_kernel, first_head, heads...  24.8 us
    ppermute x9, starting transfers between devices, lifted(): return lax.ppermute(array, 'tm', route)  16.1 us
    pallas_call x3, Pallas kernels, mix_call(): pl.pallas_call(skipping(functools.partial(mix_kernel, span), 8, after), o...  9.21 us
    pallas_call x8, Pallas kernels, fold_call(): pl.pallas_call(skipping(functools.partial(fold_kernel, parts, terms, wher...  4.88 us
    pallas_call x6, Pallas kernels, hop_call(): pl.pallas_call(skipping(functools.partial(hop_kernel, level), 4, after),...  4.62 us
    pallas_call x8, Pallas kernels, lay_call(): pl.pallas_call(skipping(functools.partial(lay_kernel, where), 3, after),...  4.61 us
  transfers between devices with their start and end apart: 36, of which 19 were waited for; matrix products, arithmetic and copies ran while one was open for 0% of the time, Pallas kernels for 21%

profile of v6, /device:TPU:0, one launch (start us, length us, event | category | flops | bytes accessed | tf_op | source)
XLA Modules:
  0.0 179.6 jit_solution(16450750695214645593)
XLA Ops:
  5.8 13.3 %local.3 = (f32[4,128,256]{2,1,0:T(8,128)S(1)}, f32[4,128,256]{2,1,0:T(8,128)S(1)}, f32[512,512]{1,0:T(8,128)S(1)}, f32[512,512]{1,0:T(8,128)S(1)}, f32[512,16]{1,0:T(8,128)S(1)}) custom-call(s32[7]{0:T(128)S(1)} %stack.49.refs_0_.info, s32[2,4,24]{2,1,0:T(4,128)S(1)} %pad_add_fusion.refs_1_, bf16[512,1024]{1,0:T(8,128)(2,1)S(1)} %bitcast.28, ...), custom_call_target="tpu_custom_call" | custom-call | flops 6442450944 | bytes 8388608 | tf_op jit(solution)/shard_map/local/pallas_call | solution.py:195
  19.1 3.0 %collective-permute-start = (f32[4,128,256]{2,1,0:T(8,128)S(1)}, f32[4,128,256]{2,1,0:T(8,128)S(1)}, u32[]{:S(2)}, u32[]{:S(2)}) collective-permute-start(f32[4,128,256]{2,1,0:T(8,128)S(1)} %get-tuple-element.79), channel_id=1, source_target_pairs={{0,1},{1,0},{2,3},{3,2},{4,5},{5,4},{6,7},{7,6},{8,9},{9,8},{10,11... | collective-permute-start | bytes 1572872 | tf_op jit(solution)/shard_map/ppermute | solution.py:528
  22.2 5.7 %local.4 = (f32[2,128,256]{2,1,0:T(8,128)S(1)}, f32[2,128,256]{2,1,0:T(8,128)S(1)}, f32[512,256]{1,0:T(8,128)S(1)}, f32[512,256]{1,0:T(8,128)S(1)}) custom-call(s32[7]{0:T(128)S(1)} %stack.49.refs_0_.info, s32[2,4,24]{2,1,0:T(4,128)S(1)} %pad_add_fusion.refs_1_, bf16[512,1024]{1,0:T(8,128)(2,1)S(1)} %bitcast.29, bf16[64,128,128]{2,1,0:T(8,128)(2,1)S(1)} %copy-done.3, ...), custom_call_target="tpu_custom_call" | custom-call | flops 3221225472 | bytes 8388608 | tf_op jit(solution)/shard_map/local/pallas_call | solution.py:195
  28.0 5.7 %local.5 = (f32[2,128,256]{2,1,0:T(8,128)S(1)}, f32[2,128,256]{2,1,0:T(8,128)S(1)}, f32[512,256]{1,0:T(8,128)S(1)}, f32[512,256]{1,0:T(8,128)S(1)}) custom-call(s32[7]{0:T(128)S(1)} %stack.49.refs_0_.info, s32[2,4,24]{2,1,0:T(4,128)S(1)} %pad_add_fusion.refs_1_, bf16[512,1024]{1,0:T(8,128)(2,1)S(1)} %bitcast.30, bf16[64,128,128]{2,1,0:T(8,128)(2,1)S(1)} %copy-done.3, ...), custom_call_target="tpu_custom_call" | custom-call | flops 3221225472 | bytes 8388608 | tf_op jit(solution)/shard_map/local/pallas_call | solution.py:195
  36.8 3.5 %collective-permute-start.1 = (f32[4,128,128]{2,1,0:T(8,128)S(1)}, f32[4,128,128]{2,1,0:T(8,128)S(1)}, u32[]{:S(2)}, u32[]{:S(2)}) collective-permute-start(f32[4,128,128]{2,1,0:T(8,128)S(1)} %get-tuple-element.85.refs_3_), channel_id=1, source_target_pairs={{0,2},{1,3},{2,0},{3,1},{8,10},{9,11},{10,8},{11,9},{16,18},{17,19... | collective-permute-start | bytes 786440 | tf_op jit(solution)/shard_map/ppermute | solution.py:533
  40.3 3.3 %back.1.refs_4_.refs_5_ = f32[512,1024]{1,0:T(8,128)S(1)} custom-call(bf16[512,1024]{1,0:T(8,128)(2,1)S(1)} %bitcast.21, bf16[1024,1024]{1,0:T(8,128)(2,1)S(1)} %copy-done.1), custom_call_target="tpu_custom_call" | custom-call | flops 1073741824 | bytes 5242880 | tf_op jit(solution)/shard_map/back/pallas_call | solution.py:370
  47.7 6.5 %collective-permute-start.6 = (f32[2,128,128]{2,1,0:T(8,128)S(1)}, f32[2,128,128]{2,1,0:T(8,128)S(1)}, u32[]{:S(2)}, u32[]{:S(2)}) collective-permute-start(f32[2,128,128]{2,1,0:T(8,128)S(1)} %get-tuple-element.88.refs_3_), channel_id=1, source_target_pairs={{0,2},{1,3},{2,0},{3,1},{8,10},{9,11},{10,8},{11,9},{16,18},{17,19... | collective-permute-start | bytes 393224 | tf_op jit(solution)/shard_map/ppermute | solution.py:533
  58.7 2.6 %collective-permute-done.5.refs_2_ = f32[2,128,128]{2,1,0:T(8,128)S(1)} collective-permute-done((f32[2,128,128]{2,1,0:T(8,128)S(1)}, f32[2,128,128]{2,1,0:T(8,128)S(1)}, u32[]{:S(2)}, u32[]{:S(2)}) %collective-permute-start.5) | collective-permute-done | bytes 131104 | tf_op jit(solution)/shard_map/ppermute | solution.py:533
  73.7 4.4 %mix.3 = (bf16[512,512]{1,0:T(8,128)(2,1)S(1)}, f32[257,8,128]{2,1,0:T(8,128)S(1)}, f32[257,8,128]{2,1,0:T(8,128)S(1)}) custom-call(s32[7]{0:T(128)S(1)} %stack.49.refs_0_.info, f32[512,512]{1,0:T(8,128)S(1)} %get-tuple-element.76.refs_1_, f32[512,512]{1,0:T(8,128)S(1)} %get-tuple-element.77.refs_2_, f32[4,128,128]{2,1,0:T(8,128)S(1)} %get-tuple-element.102.refs_3_, ...), custom_call_target="tpu_custom_call" | custom-call | flops 536870912 | bytes 3145728 | tf_op jit(solution)/shard_map/mix/pallas_call | solution.py:347
  80.3 4.3 %collective-permute-done.13.refs_4_ = f32[2,128,128]{2,1,0:T(8,128)S(1)} collective-permute-done((f32[2,128,128]{2,1,0:T(8,128)S(1)}, f32[2,128,128]{2,1,0:T(8,128)S(1)}, u32[]{:S(2)}, u32[]{:S(2)}) %collective-permute-start.13) | collective-permute-done | bytes 131104 | tf_op jit(solution)/shard_map/ppermute | solution.py:528
  84.6 2.4 %mix.4 = (bf16[512,256]{1,0:T(8,128)(2,1)S(1)}, f32[129,8,128]{2,1,0:T(8,128)S(1)}, f32[129,8,128]{2,1,0:T(8,128)S(1)}) custom-call(s32[7]{0:T(128)S(1)} %stack.49.refs_0_.info, f32[512,256]{1,0:T(8,128)S(1)} %get-tuple-element.111.refs_1_, f32[512,256]{1,0:T(8,128)S(1)} %get-tuple-element.112.refs_2_, f32[2,128,128]{2,1,0:T(8,128)S(1)} %get-tuple-element.113.refs_3_, ...), custom_call_target="tpu_custom_call" | custom-call | flops 268435456 | bytes 3145728 | tf_op jit(solution)/shard_map/mix/pallas_call | solution.py:347
  87.0 2.4 %mix.5 = (bf16[512,256]{1,0:T(8,128)(2,1)S(1)}, f32[129,8,128]{2,1,0:T(8,128)S(1)}, f32[129,8,128]{2,1,0:T(8,128)S(1)}) custom-call(s32[7]{0:T(128)S(1)} %stack.49.refs_0_.info, f32[512,256]{1,0:T(8,128)S(1)} %get-tuple-element.116.refs_1_, f32[512,256]{1,0:T(8,128)S(1)} %get-tuple-element.117.refs_2_, f32[2,128,128]{2,1,0:T(8,128)S(1)} %get-tuple-element.118.refs_3_, ...), custom_call_target="tpu_custom_call" | custom-call | flops 268435456 | bytes 3145728 | tf_op jit(solution)/shard_map/mix/pallas_call | solution.py:347
  94.5 2.8 %finish.1 = (bf16[512,1024]{1,0:T(8,128)(2,1)}, f32[8,128]{1,0:T(8,128)S(1)}) custom-call(bf16[512,512]{1,0:T(8,128)(2,1)S(1)} %get-tuple-element.110.refs_0_, bf16[512,256]{1,0:T(8,128)(2,1)S(1)} %get-tuple-element.115.refs_1_, bf16[512,256]{1,0:T(8,128)(2,1)S(1)} %get-tuple-element.120.refs_2_, bf16[1024,1024]{1,0:T(8,128)(2,1)S(1)} %copy-done.1), custom_call_target="tpu_custom_call" | custom-call | flops 1073741824 | bytes 4194304 | tf_op jit(solution)/shard_map/finish/pallas_call | solution.py:393
  97.4 7.4 %collective-permute-done.16.refs_2_ = f32[129,8,128]{2,1,0:T(8,128)S(1)} collective-permute-done((f32[129,8,128]{2,1,0:T(8,128)S(1)}, f32[129,8,128]{2,1,0:T(8,128)S(1)}, u32[]{:S(2)}, u32[]{:S(2)}) %collective-permute-start.16) | collective-permute-done | bytes 528416 | tf_op jit(solution)/shard_map/ppermute | solution.py:528
  109.2 3.8 %collective-permute-done.19.refs_2_ = f32[65,8,128]{2,1,0:T(8,128)S(1)} collective-permute-done((f32[65,8,128]{2,1,0:T(8,128)S(1)}, f32[65,8,128]{2,1,0:T(8,128)S(1)}, u32[]{:S(2)}, u32[]{:S(2)}) %collective-permute-start.19) | collective-permute-done | bytes 266272 | tf_op jit(solution)/shard_map/ppermute | solution.py:528
  113.6 7.8 %collective-permute-start.21 = (f32[33,8,128]{2,1,0:T(8,128)S(1)}, f32[33,8,128]{2,1,0:T(8,128)S(1)}, u32[]{:S(2)}, u32[]{:S(2)}) collective-permute-start(f32[33,8,128]{2,1,0:T(8,128)S(1)} %get-tuple-element.135), channel_id=1, source_target_pairs={{0,2},{1,3},{2,0},{3,1},{4,6},{5,7},{6,4},{7,5},{8,10},{9,11},{10,... | collective-permute-start | bytes 405512 | tf_op jit(solution)/shard_map/ppermute | solution.py:528
  126.1 8.0 %collective-permute-start.23 = (f32[17,8,128]{2,1,0:T(8,128)S(1)}, f32[17,8,128]{2,1,0:T(8,128)S(1)}, u32[]{:S(2)}, u32[]{:S(2)}) collective-permute-start(f32[17,8,128]{2,1,0:T(8,128)S(1)} %get-tuple-element.139), channel_id=1, source_target_pairs={{0,4},{1,5},{2,6},{3,7},{4,0},{5,1},{6,2},{7,3},{8,12},{9,13},{10,... | collective-permute-start | bytes 208904 | tf_op jit(solution)/shard_map/ppermute | solution.py:528
  136.0 2.9 %collective-permute-done.23.refs_1_ = f32[17,8,128]{2,1,0:T(8,128)S(1)} collective-permute-done((f32[17,8,128]{2,1,0:T(8,128)S(1)}, f32[17,8,128]{2,1,0:T(8,128)S(1)}, u32[]{:S(2)}, u32[]{:S(2)}) %collective-permute-start.23) | collective-permute-done | bytes 69664 | tf_op jit(solution)/shard_map/ppermute | solution.py:528
  142.0 2.2 %collective-permute-done.24.refs_2_ = f32[16,8,128]{2,1,0:T(8,128)S(1)} collective-permute-done((f32[16,8,128]{2,1,0:T(8,128)S(1)}, f32[16,8,128]{2,1,0:T(8,128)S(1)}, u32[]{:S(2)}, u32[]{:S(2)}) %collective-permute-start.24) | collective-permute-done | bytes 65568 | tf_op jit(solution)/shard_map/ppermute | solution.py:528
  147.4 2.4 %collective-permute-start.30 = (f32[32,8,128]{2,1,0:T(8,128)S(1)}, f32[32,8,128]{2,1,0:T(8,128)S(1)}, u32[]{:S(2)}, u32[]{:S(2)}) collective-permute-start(f32[32,8,128]{2,1,0:T(8,128)S(1)} %lay.9.refs_3_.refs_1_), channel_id=1, source_target_pairs={{0,2},{1,3},{2,0},{3,1},{4,6},{5,7},{6,4},{7,5},{8,10},{9,11},{10,... | collective-permute-start | bytes 393224 | tf_op jit(solution)/shard_map/ppermute | solution.py:528
  159.6 2.9 %collective-permute-done.32.refs_2_ = f32[64,8,128]{2,1,0:T(8,128)S(1)} collective-permute-done((f32[64,8,128]{2,1,0:T(8,128)S(1)}, f32[64,8,128]{2,1,0:T(8,128)S(1)}, u32[]{:S(2)}, u32[]{:S(2)}) %collective-permute-start.32) | collective-permute-done | bytes 262176 | tf_op jit(solution)/shard_map/ppermute | solution.py:528
  163.7 6.6 %collective-permute-done.31.refs_2_ = f32[128,8,128]{2,1,0:T(8,128)S(1)} collective-permute-done((f32[128,8,128]{2,1,0:T(8,128)S(1)}, f32[128,8,128]{2,1,0:T(8,128)S(1)}, u32[]{:S(2)}, u32[]{:S(2)}) %collective-permute-start.31) | collective-permute-done | bytes 524320 | tf_op jit(solution)/shard_map/ppermute | solution.py:528
  173.5 2.1 %collective-permute-done.35.refs_3_ = f32[256,8,128]{2,1,0:T(8,128)S(1)} collective-permute-done((f32[256,8,128]{2,1,0:T(8,128)S(1)}, f32[256,8,128]{2,1,0:T(8,128)S(1)}, u32[]{:S(2)}, u32[]{:S(2)}) %collective-permute-start.35) | collective-permute-done | bytes 1048608 | tf_op jit(solution)/shard_map/ppermute | solution.py:528
  177.2 2.4 %join.1 = (bf16[1024,1024]{1,0:T(8,128)(2,1)}, f32[1,128]{1,0:T(1,128)}) custom-call(s32[7]{0:T(128)S(1)} %stack.49.refs_0_.info, f32[256,8,128]{2,1,0:T(8,128)S(1)} %lay.14.refs_3_.refs_0_, f32[256,8,128]{2,1,0:T(8,128)S(1)} %collective-permute-done.33.refs_1_, f32[256,8,128]{2,1,0:T(8,128)S(1)} %lay.15.refs_2_, ...), custom_call_target="tpu_custom_call" | custom-call | tf_op jit(solution)/shard_map/join/pallas_call | solution.py:496
  (104 shorter events, 69.8 us)
Async XLA Ops:
  19.1 16.7 %collective-permute-start = (f32[4,128,256]{2,1,0:T(8,128)S(1)}, f32[4,128,256]{2,1,0:T(8,128)S(1)}, u32[]{:S(2)}, u32[]{:S(2)}) collective-permute-start(f32[4,128,256]{2,1,0:T(8,128)S(1)} %get-tuple-element.79), channel_id=1, source_target_pairs={{0,1},{1,0},{2,3},{3,2},{4,5},{5,4},{6,7},{7,6},{8,9},{9,8},{10,11... | collective-permute-start | bytes 1572872 | tf_op jit(solution)/shard_map/ppermute | solution.py:528
  27.9 15.7 %collective-permute-start.3 = (f32[2,128,256]{2,1,0:T(8,128)S(1)}, f32[2,128,256]{2,1,0:T(8,128)S(1)}, u32[]{:S(2)}, u32[]{:S(2)}) collective-permute-start(f32[2,128,256]{2,1,0:T(8,128)S(1)} %get-tuple-element.87), channel_id=1, source_target_pairs={{0,1},{1,0},{2,3},{3,2},{4,5},{5,4},{6,7},{7,6},{8,9},{9,8},{10,11... | collective-permute-start | bytes 786440 | tf_op jit(solution)/shard_map/ppermute | solution.py:528
  33.7 11.6 %collective-permute-start.2 = (f32[2,128,256]{2,1,0:T(8,128)S(1)}, f32[2,128,256]{2,1,0:T(8,128)S(1)}, u32[]{:S(2)}, u32[]{:S(2)}) collective-permute-start(f32[2,128,256]{2,1,0:T(8,128)S(1)} %get-tuple-element.86), channel_id=1, source_target_pairs={{0,1},{1,0},{2,3},{3,2},{4,5},{5,4},{6,7},{7,6},{8,9},{9,8},{10,11... | collective-permute-start | bytes 786440 | tf_op jit(solution)/shard_map/ppermute | solution.py:528
  36.8 9.4 %collective-permute-start.1 = (f32[4,128,128]{2,1,0:T(8,128)S(1)}, f32[4,128,128]{2,1,0:T(8,128)S(1)}, u32[]{:S(2)}, u32[]{:S(2)}) collective-permute-start(f32[4,128,128]{2,1,0:T(8,128)S(1)} %get-tuple-element.85.refs_3_), channel_id=1, source_target_pairs={{0,2},{1,3},{2,0},{3,1},{8,10},{9,11},{10,8},{11,9},{16,18},{17,19... | collective-permute-start | bytes 786440 | tf_op jit(solution)/shard_map/ppermute | solution.py:533
  47.0 15.0 %collective-permute-start.4 = (f32[4,128,128]{2,1,0:T(8,128)S(1)}, f32[4,128,128]{2,1,0:T(8,128)S(1)}, u32[]{:S(2)}, u32[]{:S(2)}) collective-permute-start(f32[4,128,128]{2,1,0:T(8,128)S(1)} %get-tuple-element.90.refs_4_), channel_id=1, source_target_pairs={{2,4},{3,5},{4,2},{5,3},{10,12},{11,13},{12,10},{13,11},{18,20},{1... | collective-permute-start | bytes 786440 | tf_op jit(solution)/shard_map/ppermute | solution.py:533
  47.7 10.2 %collective-permute-start.6 = (f32[2,128,128]{2,1,0:T(8,128)S(1)}, f32[2,128,128]{2,1,0:T(8,128)S(1)}, u32[]{:S(2)}, u32[]{:S(2)}) collective-permute-start(f32[2,128,128]{2,1,0:T(8,128)S(1)} %get-tuple-element.88.refs_3_), channel_id=1, source_target_pairs={{0,2},{1,3},{2,0},{3,1},{8,10},{9,11},{10,8},{11,9},{16,18},{17,19... | collective-permute-start | bytes 393224 | tf_op jit(solution)/shard_map/ppermute | solution.py:533
  54.2 7.1 %collective-permute-start.5 = (f32[2,128,128]{2,1,0:T(8,128)S(1)}, f32[2,128,128]{2,1,0:T(8,128)S(1)}, u32[]{:S(2)}, u32[]{:S(2)}) collective-permute-start(f32[2,128,128]{2,1,0:T(8,128)S(1)} %get-tuple-element.89.refs_4_), channel_id=1, source_target_pairs={{0,2},{1,3},{2,0},{3,1},{8,10},{9,11},{10,8},{11,9},{16,18},{17,19... | collective-permute-start | bytes 393224 | tf_op jit(solution)/shard_map/ppermute | solution.py:533
  67.3 6.4 %collective-permute-start.10 = (f32[4,128,128]{2,1,0:T(8,128)S(1)}, f32[4,128,128]{2,1,0:T(8,128)S(1)}, u32[]{:S(2)}, u32[]{:S(2)}) collective-permute-start(f32[4,128,128]{2,1,0:T(8,128)S(1)} %get-tuple-element.103.refs_4_), channel_id=1, source_target_pairs={{0,1},{1,0},{2,3},{3,2},{4,5},{5,4},{6,7},{7,6},{8,9},{9,8},{10,11... | collective-permute-start | bytes 786440 | tf_op jit(solution)/shard_map/ppermute | solution.py:528
  78.1 11.9 %collective-permute-start.15 = (f32[257,8,128]{2,1,0:T(8,128)S(1)}, f32[257,8,128]{2,1,0:T(8,128)S(1)}, u32[]{:S(2)}, u32[]{:S(2)}) collective-permute-start(f32[257,8,128]{2,1,0:T(8,128)S(1)} %get-tuple-element.122), channel_id=1, source_target_pairs={{0,8},{1,9},{2,10},{3,11},{4,12},{5,13},{6,14},{7,15},{8,0},{9,1},... | collective-permute-start | bytes 3158024 | tf_op jit(solution)/shard_map/ppermute | solution.py:528
  78.2 6.4 %collective-permute-start.13 = (f32[2,128,128]{2,1,0:T(8,128)S(1)}, f32[2,128,128]{2,1,0:T(8,128)S(1)}, u32[]{:S(2)}, u32[]{:S(2)}) collective-permute-start(f32[2,128,128]{2,1,0:T(8,128)S(1)} %get-tuple-element.108.refs_4_), channel_id=1, source_target_pairs={{0,1},{1,0},{2,3},{3,2},{4,5},{5,4},{6,7},{7,6},{8,9},{9,8},{10,11... | collective-permute-start | bytes 393224 | tf_op jit(solution)/shard_map/ppermute | solution.py:528
  79.8 7.2 %collective-permute-start.14 = (f32[2,128,128]{2,1,0:T(8,128)S(1)}, f32[2,128,128]{2,1,0:T(8,128)S(1)}, u32[]{:S(2)}, u32[]{:S(2)}) collective-permute-start(f32[2,128,128]{2,1,0:T(8,128)S(1)} %get-tuple-element.109.refs_8_), channel_id=1, source_target_pairs={{0,1},{1,0},{2,3},{3,2},{4,5},{5,4},{6,7},{7,6},{8,9},{9,8},{10,11... | collective-permute-start | bytes 393224 | tf_op jit(solution)/shard_map/ppermute | solution.py:528
  90.7 14.1 %collective-permute-start.16 = (f32[129,8,128]{2,1,0:T(8,128)S(1)}, f32[129,8,128]{2,1,0:T(8,128)S(1)}, u32[]{:S(2)}, u32[]{:S(2)}) collective-permute-start(f32[129,8,128]{2,1,0:T(8,128)S(1)} %get-tuple-element.124), channel_id=1, source_target_pairs={{0,16},{1,17},{2,18},{3,19},{4,20},{5,21},{6,22},{7,23},{8,24},{9,... | collective-permute-start | bytes 1585160 | tf_op jit(solution)/shard_map/ppermute | solution.py:528
  93.0 14.0 %collective-permute-start.20 = (f32[129,8,128]{2,1,0:T(8,128)S(1)}, f32[129,8,128]{2,1,0:T(8,128)S(1)}, u32[]{:S(2)}, u32[]{:S(2)}) collective-permute-start(f32[129,8,128]{2,1,0:T(8,128)S(1)} %get-tuple-element.131), channel_id=1, source_target_pairs={{0,1},{1,0},{2,3},{3,2},{4,5},{5,4},{6,7},{7,6},{8,9},{9,8},{10,11... | collective-permute-start | bytes 1585160 | tf_op jit(solution)/shard_map/ppermute | solution.py:528
  105.4 7.6 %collective-permute-start.19 = (f32[65,8,128]{2,1,0:T(8,128)S(1)}, f32[65,8,128]{2,1,0:T(8,128)S(1)}, u32[]{:S(2)}, u32[]{:S(2)}) collective-permute-start(f32[65,8,128]{2,1,0:T(8,128)S(1)} %get-tuple-element.130), channel_id=1, source_target_pairs={{0,1},{1,0},{2,3},{3,2},{4,5},{5,4},{6,7},{7,6},{8,9},{9,8},{10,11... | collective-permute-start | bytes 798728 | tf_op jit(solution)/shard_map/ppermute | solution.py:528
  107.6 13.8 %collective-permute-start.22 = (f32[65,8,128]{2,1,0:T(8,128)S(1)}, f32[65,8,128]{2,1,0:T(8,128)S(1)}, u32[]{:S(2)}, u32[]{:S(2)}) collective-permute-start(f32[65,8,128]{2,1,0:T(8,128)S(1)} %get-tuple-element.136), channel_id=1, source_target_pairs={{0,16},{1,17},{2,18},{3,19},{4,20},{5,21},{6,22},{7,23},{8,24},{9,... | collective-permute-start | bytes 798728 | tf_op jit(solution)/shard_map/ppermute | solution.py:528
  113.6 12.0 %collective-permute-start.21 = (f32[33,8,128]{2,1,0:T(8,128)S(1)}, f32[33,8,128]{2,1,0:T(8,128)S(1)}, u32[]{:S(2)}, u32[]{:S(2)}) collective-permute-start(f32[33,8,128]{2,1,0:T(8,128)S(1)} %get-tuple-element.135), channel_id=1, source_target_pairs={{0,2},{1,3},{2,0},{3,1},{4,6},{5,7},{6,4},{7,5},{8,10},{9,11},{10,... | collective-permute-start | bytes 405512 | tf_op jit(solution)/shard_map/ppermute | solution.py:528
  121.9 12.1 %collective-permute-start.25 = (f32[33,8,128]{2,1,0:T(8,128)S(1)}, f32[33,8,128]{2,1,0:T(8,128)S(1)}, u32[]{:S(2)}, u32[]{:S(2)}) collective-permute-start(f32[33,8,128]{2,1,0:T(8,128)S(1)} %get-tuple-element.141), channel_id=1, source_target_pairs={{0,2},{1,3},{2,0},{3,1},{4,6},{5,7},{6,4},{7,5},{8,10},{9,11},{10,... | collective-permute-start | bytes 405512 | tf_op jit(solution)/shard_map/ppermute | solution.py:528
  126.1 12.8 %collective-permute-start.23 = (f32[17,8,128]{2,1,0:T(8,128)S(1)}, f32[17,8,128]{2,1,0:T(8,128)S(1)}, u32[]{:S(2)}, u32[]{:S(2)}) collective-permute-start(f32[17,8,128]{2,1,0:T(8,128)S(1)} %get-tuple-element.139), channel_id=1, source_target_pairs={{0,4},{1,5},{2,6},{3,7},{4,0},{5,1},{6,2},{7,3},{8,12},{9,13},{10,... | collective-permute-start | bytes 208904 | tf_op jit(solution)/shard_map/ppermute | solution.py:528
  134.6 6.7 %collective-permute-start.26 = (f32[17,8,128]{2,1,0:T(8,128)S(1)}, f32[17,8,128]{2,1,0:T(8,128)S(1)}, u32[]{:S(2)}, u32[]{:S(2)}) collective-permute-start(f32[17,8,128]{2,1,0:T(8,128)S(1)} %get-tuple-element.143), channel_id=1, source_target_pairs={{0,4},{1,5},{2,6},{3,7},{4,0},{5,1},{6,2},{7,3},{8,12},{9,13},{10,... | collective-permute-start | bytes 208904 | tf_op jit(solution)/shard_map/ppermute | solution.py:528
  141.4 5.5 %collective-permute-start.28 = (f32[16,8,128]{2,1,0:T(8,128)S(1)}, f32[16,8,128]{2,1,0:T(8,128)S(1)}, u32[]{:S(2)}, u32[]{:S(2)}) collective-permute-start(f32[16,8,128]{2,1,0:T(8,128)S(1)} %get-tuple-element.144.refs_3_.refs_1_), channel_id=1, source_target_pairs={{0,4},{1,5},{2,6},{3,7},{4,0},{5,1},{6,2},{7,3},{8,12},{9,13},{10,... | collective-permute-start | bytes 196616 | tf_op jit(solution)/shard_map/ppermute | solution.py:528
  150.6 6.4 %collective-permute-start.29 = (f32[64,8,128]{2,1,0:T(8,128)S(1)}, f32[64,8,128]{2,1,0:T(8,128)S(1)}, u32[]{:S(2)}, u32[]{:S(2)}) collective-permute-start(f32[64,8,128]{2,1,0:T(8,128)S(1)} %lay.10.refs_3_.refs_1_), channel_id=1, source_target_pairs={{0,1},{1,0},{2,3},{3,2},{4,5},{5,4},{6,7},{7,6},{8,9},{9,8},{10,11... | collective-permute-start | bytes 786440 | tf_op jit(solution)/shard_map/ppermute | solution.py:528
  153.3 9.2 %collective-permute-start.32 = (f32[64,8,128]{2,1,0:T(8,128)S(1)}, f32[64,8,128]{2,1,0:T(8,128)S(1)}, u32[]{:S(2)}, u32[]{:S(2)}) collective-permute-start(f32[64,8,128]{2,1,0:T(8,128)S(1)} %lay.11.refs_3_.refs_1_), channel_id=1, source_target_pairs={{0,16},{1,17},{2,18},{3,19},{4,20},{5,21},{6,22},{7,23},{8,24},{9,... | collective-permute-start | bytes 786440 | tf_op jit(solution)/shard_map/ppermute | solution.py:528
  157.6 12.8 %collective-permute-start.31 = (f32[128,8,128]{2,1,0:T(8,128)S(1)}, f32[128,8,128]{2,1,0:T(8,128)S(1)}, u32[]{:S(2)}, u32[]{:S(2)}) collective-permute-start(f32[128,8,128]{2,1,0:T(8,128)S(1)} %lay.12.refs_3_.refs_1_), channel_id=1, source_target_pairs={{0,16},{1,17},{2,18},{3,19},{4,20},{5,21},{6,22},{7,23},{8,24},{9,... | collective-permute-start | bytes 1572872 | tf_op jit(solution)/shard_map/ppermute | solution.py:528
  163.1 9.2 %collective-permute-start.34 = (f32[128,8,128]{2,1,0:T(8,128)S(1)}, f32[128,8,128]{2,1,0:T(8,128)S(1)}, u32[]{:S(2)}, u32[]{:S(2)}) collective-permute-start(f32[128,8,128]{2,1,0:T(8,128)S(1)} %lay.13.refs_3_.refs_1_), channel_id=1, source_target_pairs={{0,1},{1,0},{2,3},{3,2},{4,5},{5,4},{6,7},{7,6},{8,9},{9,8},{10,11... | collective-permute-start | bytes 1572872 | tf_op jit(solution)/shard_map/ppermute | solution.py:528
  (18 other events, 76.6 us)

commit v7 on v6

--- a/solution.py
+++ b/solution.py
@@ -8,8 +8,8 @@
 from jax.experimental.pallas import tpu as pltpu
 from jax.sharding import PartitionSpec as P
 
-RELAYS = (4, 2, 2)
-SUMS = ((0,), (1, 2))
+RELAYS = (4, 4)
+SUMS = ((0,), (1,))
 CORES = 2
 PAIR = 2
 PER_STEP = 2

time: 180 us -> 170 us (0.944)
  starting transfers between devices: 62.3 us -> 48.1 us
  waiting for transfers between devices: 49.3 us -> 57.1 us
  Pallas kernels: 61.6 us -> 58 us
    ppermute x27 -> x24, waiting for transfers between devices: 45.2 us -> 53.4 us  [moved(): return lax.ppermute(array, both, route)]
    ppermute x27 -> x24, starting transfers between devices: 46.2 us -> 38 us  [moved(): return lax.ppermute(array, both, route)]
    ppermute x9 -> x6, starting transfers between devices: 16.1 us -> 10.1 us  [lifted(): return lax.ppermute(array, 'tm', route)]
    pallas_call x6 -> x4, Pallas kernels: 4.62 us -> 3.25 us  [hop_call(): pl.pallas_call(skipping(functools.partial(hop_kernel, level), 4, after),...]
    pallas_call x3 -> x2, Pallas kernels: 24.8 us -> 24.3 us  [local_call(): pl.pallas_call(skipping(functools.partial(local_kernel, first_head, heads...]
    ppermute x9 -> x6, waiting for transfers between devices: 4.18 us -> 3.73 us  [lifted(): return lax.ppermute(array, 'tm', route)]
    pallas_call x3 -> x2, Pallas kernels: 9.21 us -> 8.78 us  [mix_call(): pl.pallas_call(skipping(functools.partial(mix_kernel, span), 8, after), o...]
  transfers between devices with their start and end apart: 36 -> 30, of which waited for: 19 -> 20; matrix products, arithmetic and copies ran while one was open for 0% -> 0% of each run, Pallas kernels for 21% -> 25%
where the time goes in v7:
time: 170 us; the launch traced here: 169 us
  Pallas kernels  58 us (34%)
  waiting for transfers between devices  57.1 us (34%)
  starting transfers between devices  48.1 us (28%)
  local copies, waits for them, and re-layouts  3.69 us (2%)
    ppermute x24, waiting for transfers between devices, moved(): return lax.ppermute(array, both, route)  53.4 us
    ppermute x24, starting transfers between devices, moved(): return lax.ppermute(array, both, route)  38 us
    pallas_call x2, Pallas kernels, local_call(): pl.pallas_call(skipping(functools.partial(local_kernel, first_head, heads...  24.3 us
    ppermute x6, starting transfers between devices, lifted(): return lax.ppermute(array, 'tm', route)  10.1 us
    pallas_call x2, Pallas kernels, mix_call(): pl.pallas_call(skipping(functools.partial(mix_kernel, span), 8, after), o...  8.78 us
    pallas_call x8, Pallas kernels, fold_call(): pl.pallas_call(skipping(functools.partial(fold_kernel, parts, terms, wher...  4.87 us
    pallas_call x8, Pallas kernels, lay_call(): pl.pallas_call(skipping(functools.partial(lay_kernel, where), 3, after),...  4.61 us
    ppermute x6, waiting for transfers between devices, lifted(): return lax.ppermute(array, 'tm', route)  3.73 us
  transfers between devices with their start and end apart: 30, of which 20 were waited for; matrix products, arithmetic and copies ran while one was open for 0% of the time, Pallas kernels for 25%

profile of v7, /device:TPU:0, one launch (start us, length us, event | category | flops | bytes accessed | tf_op | source)
XLA Modules:
  0.0 169.4 jit_solution(7134070822522140826)
XLA Ops:
  5.8 13.2 %local.2 = (f32[4,128,256]{2,1,0:T(8,128)S(1)}, f32[4,128,256]{2,1,0:T(8,128)S(1)}, f32[512,512]{1,0:T(8,128)S(1)}, f32[512,512]{1,0:T(8,128)S(1)}, f32[512,16]{1,0:T(8,128)S(1)}) custom-call(s32[7]{0:T(128)S(1)} %stack.49.refs_0_.info, s32[2,4,24]{2,1,0:T(4,128)S(1)} %pad_add_fusion.refs_1_, bf16[512,1024]{1,0:T(8,128)(2,1)S(1)} %bitcast.26, ...), custom_call_target="tpu_custom_call" | custom-call | flops 6442450944 | bytes 8388608 | tf_op jit(solution)/shard_map/local/pallas_call | solution.py:195
  18.9 3.0 %collective-permute-start = (f32[4,128,256]{2,1,0:T(8,128)S(1)}, f32[4,128,256]{2,1,0:T(8,128)S(1)}, u32[]{:S(2)}, u32[]{:S(2)}) collective-permute-start(f32[4,128,256]{2,1,0:T(8,128)S(1)} %get-tuple-element.63), channel_id=1, source_target_pairs={{0,1},{1,0},{2,3},{3,2},{4,5},{5,4},{6,7},{7,6},{8,9},{9,8},{10,11... | collective-permute-start | bytes 1572872 | tf_op jit(solution)/shard_map/ppermute | solution.py:528
  22.0 11.2 %local.3 = (f32[4,128,256]{2,1,0:T(8,128)S(1)}, f32[4,128,256]{2,1,0:T(8,128)S(1)}, f32[512,512]{1,0:T(8,128)S(1)}, f32[512,512]{1,0:T(8,128)S(1)}) custom-call(s32[7]{0:T(128)S(1)} %stack.49.refs_0_.info, s32[2,4,24]{2,1,0:T(4,128)S(1)} %pad_add_fusion.refs_1_, bf16[512,1024]{1,0:T(8,128)(2,1)S(1)} %bitcast.27, bf16[64,128,128]{2,1,0:T(8,128)(2,1)S(1)} %copy-done.3, ...), custom_call_target="tpu_custom_call" | custom-call | flops 6442450944 | bytes 8388608 | tf_op jit(solution)/shard_map/local/pallas_call | solution.py:195
  34.9 3.9 %collective-permute-start.1 = (f32[4,128,128]{2,1,0:T(8,128)S(1)}, f32[4,128,128]{2,1,0:T(8,128)S(1)}, u32[]{:S(2)}, u32[]{:S(2)}) collective-permute-start(f32[4,128,128]{2,1,0:T(8,128)S(1)} %get-tuple-element.68.refs_3_), channel_id=1, source_target_pairs={{0,2},{1,3},{2,0},{3,1},{8,10},{9,11},{10,8},{11,9},{16,18},{17,19... | collective-permute-start | bytes 786440 | tf_op jit(solution)/shard_map/ppermute | solution.py:533
  38.8 3.3 %back.1.refs_4_.refs_5_ = f32[512,1024]{1,0:T(8,128)S(1)} custom-call(bf16[512,1024]{1,0:T(8,128)(2,1)S(1)} %bitcast.21, bf16[1024,1024]{1,0:T(8,128)(2,1)S(1)} %copy-done.1), custom_call_target="tpu_custom_call" | custom-call | flops 1073741824 | bytes 5242880 | tf_op jit(solution)/shard_map/back/pallas_call | solution.py:370
  42.1 4.5 %collective-permute-done.2.refs_2_ = f32[4,128,256]{2,1,0:T(8,128)S(1)} collective-permute-done((f32[4,128,256]{2,1,0:T(8,128)S(1)}, f32[4,128,256]{2,1,0:T(8,128)S(1)}, u32[]{:S(2)}, u32[]{:S(2)}) %collective-permute-start.2) | collective-permute-done | bytes 524320 | tf_op jit(solution)/shard_map/ppermute | solution.py:528
  47.6 3.5 %collective-permute-start.4 = (f32[4,128,128]{2,1,0:T(8,128)S(1)}, f32[4,128,128]{2,1,0:T(8,128)S(1)}, u32[]{:S(2)}, u32[]{:S(2)}) collective-permute-start(f32[4,128,128]{2,1,0:T(8,128)S(1)} %get-tuple-element.70.refs_4_), channel_id=1, source_target_pairs={{0,2},{1,3},{2,0},{3,1},{8,10},{9,11},{10,8},{11,9},{16,18},{17,19... | collective-permute-start | bytes 786440 | tf_op jit(solution)/shard_map/ppermute | solution.py:533
  52.6 3.7 %collective-permute-done.4.refs_2_ = f32[4,128,128]{2,1,0:T(8,128)S(1)} collective-permute-done((f32[4,128,128]{2,1,0:T(8,128)S(1)}, f32[4,128,128]{2,1,0:T(8,128)S(1)}, u32[]{:S(2)}, u32[]{:S(2)}) %collective-permute-start.4) | collective-permute-done | bytes 262176 | tf_op jit(solution)/shard_map/ppermute | solution.py:533
  64.7 5.8 %collective-permute-done.7.refs_4_ = f32[4,128,128]{2,1,0:T(8,128)S(1)} collective-permute-done((f32[4,128,128]{2,1,0:T(8,128)S(1)}, f32[4,128,128]{2,1,0:T(8,128)S(1)}, u32[]{:S(2)}, u32[]{:S(2)}) %collective-permute-start.7) | collective-permute-done | bytes 262176 | tf_op jit(solution)/shard_map/ppermute | solution.py:528
  70.6 4.4 %mix.2 = (bf16[512,512]{1,0:T(8,128)(2,1)S(1)}, f32[257,8,128]{2,1,0:T(8,128)S(1)}, f32[257,8,128]{2,1,0:T(8,128)S(1)}) custom-call(s32[7]{0:T(128)S(1)} %stack.49.refs_0_.info, f32[512,512]{1,0:T(8,128)S(1)} %get-tuple-element.60.refs_1_, f32[512,512]{1,0:T(8,128)S(1)} %get-tuple-element.61.refs_2_, f32[4,128,128]{2,1,0:T(8,128)S(1)} %get-tuple-element.79.refs_3_, ...), custom_call_target="tpu_custom_call" | custom-call | flops 536870912 | bytes 3145728 | tf_op jit(solution)/shard_map/mix/pallas_call | solution.py:347
  75.0 4.4 %mix.3 = (bf16[512,512]{1,0:T(8,128)(2,1)S(1)}, f32[257,8,128]{2,1,0:T(8,128)S(1)}, f32[257,8,128]{2,1,0:T(8,128)S(1)}) custom-call(s32[7]{0:T(128)S(1)} %stack.49.refs_0_.info, f32[512,512]{1,0:T(8,128)S(1)} %get-tuple-element.85.refs_1_, f32[512,512]{1,0:T(8,128)S(1)} %get-tuple-element.86.refs_2_, f32[4,128,128]{2,1,0:T(8,128)S(1)} %get-tuple-element.87.refs_3_, ...), custom_call_target="tpu_custom_call" | custom-call | flops 536870912 | bytes 3145728 | tf_op jit(solution)/shard_map/mix/pallas_call | solution.py:347
  84.0 2.8 %finish.1 = (bf16[512,1024]{1,0:T(8,128)(2,1)}, f32[8,128]{1,0:T(8,128)S(1)}) custom-call(bf16[512,512]{1,0:T(8,128)(2,1)S(1)} %get-tuple-element.84.refs_0_, bf16[512,512]{1,0:T(8,128)(2,1)S(1)} %get-tuple-element.89.refs_1_, bf16[1024,1024]{1,0:T(8,128)(2,1)S(1)} %copy-done.1), custom_call_target="tpu_custom_call" | custom-call | flops 1073741824 | bytes 4194304 | tf_op jit(solution)/shard_map/finish/pallas_call | solution.py:393
  86.8 7.9 %collective-permute-done.11.refs_2_ = f32[129,8,128]{2,1,0:T(8,128)S(1)} collective-permute-done((f32[129,8,128]{2,1,0:T(8,128)S(1)}, f32[129,8,128]{2,1,0:T(8,128)S(1)}, u32[]{:S(2)}, u32[]{:S(2)}) %collective-permute-start.11) | collective-permute-done | bytes 528416 | tf_op jit(solution)/shard_map/ppermute | solution.py:528
  99.6 3.4 %collective-permute-done.13.refs_2_ = f32[65,8,128]{2,1,0:T(8,128)S(1)} collective-permute-done((f32[65,8,128]{2,1,0:T(8,128)S(1)}, f32[65,8,128]{2,1,0:T(8,128)S(1)}, u32[]{:S(2)}, u32[]{:S(2)}) %collective-permute-start.13) | collective-permute-done | bytes 266272 | tf_op jit(solution)/shard_map/ppermute | solution.py:528
  103.6 6.5 %collective-permute-start.15 = (f32[33,8,128]{2,1,0:T(8,128)S(1)}, f32[33,8,128]{2,1,0:T(8,128)S(1)}, u32[]{:S(2)}, u32[]{:S(2)}) collective-permute-start(f32[33,8,128]{2,1,0:T(8,128)S(1)} %get-tuple-element.103), channel_id=1, source_target_pairs={{0,2},{1,3},{2,0},{3,1},{4,6},{5,7},{6,4},{7,5},{8,10},{9,11},{10,... | collective-permute-start | bytes 405512 | tf_op jit(solution)/shard_map/ppermute | solution.py:528
  110.8 2.2 %collective-permute-start.19 = (f32[33,8,128]{2,1,0:T(8,128)S(1)}, f32[33,8,128]{2,1,0:T(8,128)S(1)}, u32[]{:S(2)}, u32[]{:S(2)}) collective-permute-start(f32[33,8,128]{2,1,0:T(8,128)S(1)} %get-tuple-element.109), channel_id=1, source_target_pairs={{0,2},{1,3},{2,0},{3,1},{4,6},{5,7},{6,4},{7,5},{8,10},{9,11},{10,... | collective-permute-start | bytes 405512 | tf_op jit(solution)/shard_map/ppermute | solution.py:528
  114.6 8.8 %collective-permute-start.17 = (f32[17,8,128]{2,1,0:T(8,128)S(1)}, f32[17,8,128]{2,1,0:T(8,128)S(1)}, u32[]{:S(2)}, u32[]{:S(2)}) collective-permute-start(f32[17,8,128]{2,1,0:T(8,128)S(1)} %get-tuple-element.107), channel_id=1, source_target_pairs={{0,4},{1,5},{2,6},{3,7},{4,0},{5,1},{6,2},{7,3},{8,12},{9,13},{10,... | collective-permute-start | bytes 208904 | tf_op jit(solution)/shard_map/ppermute | solution.py:528
  124.0 2.4 %collective-permute-start.20 = (f32[17,8,128]{2,1,0:T(8,128)S(1)}, f32[17,8,128]{2,1,0:T(8,128)S(1)}, u32[]{:S(2)}, u32[]{:S(2)}) collective-permute-start(f32[17,8,128]{2,1,0:T(8,128)S(1)} %get-tuple-element.111), channel_id=1, source_target_pairs={{0,4},{1,5},{2,6},{3,7},{4,0},{5,1},{6,2},{7,3},{8,12},{9,13},{10,... | collective-permute-start | bytes 208904 | tf_op jit(solution)/shard_map/ppermute | solution.py:528
  126.4 2.6 %collective-permute-done.17.refs_1_ = f32[17,8,128]{2,1,0:T(8,128)S(1)} collective-permute-done((f32[17,8,128]{2,1,0:T(8,128)S(1)}, f32[17,8,128]{2,1,0:T(8,128)S(1)}, u32[]{:S(2)}, u32[]{:S(2)}) %collective-permute-start.17) | collective-permute-done | bytes 69664 | tf_op jit(solution)/shard_map/ppermute | solution.py:528
  144.6 2.2 %collective-permute-done.23.refs_2_ = f32[64,8,128]{2,1,0:T(8,128)S(1)} collective-permute-done((f32[64,8,128]{2,1,0:T(8,128)S(1)}, f32[64,8,128]{2,1,0:T(8,128)S(1)}, u32[]{:S(2)}, u32[]{:S(2)}) %collective-permute-start.23) | collective-permute-done | bytes 262176 | tf_op jit(solution)/shard_map/ppermute | solution.py:528
  149.1 3.3 %collective-permute-done.26.refs_2_ = f32[64,8,128]{2,1,0:T(8,128)S(1)} collective-permute-done((f32[64,8,128]{2,1,0:T(8,128)S(1)}, f32[64,8,128]{2,1,0:T(8,128)S(1)}, u32[]{:S(2)}, u32[]{:S(2)}) %collective-permute-start.26) | collective-permute-done | bytes 262176 | tf_op jit(solution)/shard_map/ppermute | solution.py:528
  153.6 5.7 %collective-permute-done.25.refs_2_ = f32[128,8,128]{2,1,0:T(8,128)S(1)} collective-permute-done((f32[128,8,128]{2,1,0:T(8,128)S(1)}, f32[128,8,128]{2,1,0:T(8,128)S(1)}, u32[]{:S(2)}, u32[]{:S(2)}) %collective-permute-start.25) | collective-permute-done | bytes 524320 | tf_op jit(solution)/shard_map/ppermute | solution.py:528
  159.9 2.3 %collective-permute-done.28.refs_2_ = f32[128,8,128]{2,1,0:T(8,128)S(1)} collective-permute-done((f32[128,8,128]{2,1,0:T(8,128)S(1)}, f32[128,8,128]{2,1,0:T(8,128)S(1)}, u32[]{:S(2)}, u32[]{:S(2)}) %collective-permute-start.28) | collective-permute-done | bytes 524320 | tf_op jit(solution)/shard_map/ppermute | solution.py:528
  167.1 2.4 %join.1 = (bf16[1024,1024]{1,0:T(8,128)(2,1)}, f32[1,128]{1,0:T(1,128)}) custom-call(s32[7]{0:T(128)S(1)} %stack.49.refs_0_.info, f32[256,8,128]{2,1,0:T(8,128)S(1)} %lay.14.refs_3_.refs_0_, f32[256,8,128]{2,1,0:T(8,128)S(1)} %collective-permute-done.27.refs_1_, f32[256,8,128]{2,1,0:T(8,128)S(1)} %lay.15.refs_2_, ...), custom_call_target="tpu_custom_call" | custom-call | tf_op jit(solution)/shard_map/join/pallas_call | solution.py:496
  (85 shorter events, 54.8 us)
Async XLA Ops:
  18.9 15.0 %collective-permute-start = (f32[4,128,256]{2,1,0:T(8,128)S(1)}, f32[4,128,256]{2,1,0:T(8,128)S(1)}, u32[]{:S(2)}, u32[]{:S(2)}) collective-permute-start(f32[4,128,256]{2,1,0:T(8,128)S(1)} %get-tuple-element.63), channel_id=1, source_target_pairs={{0,1},{1,0},{2,3},{3,2},{4,5},{5,4},{6,7},{7,6},{8,9},{9,8},{10,11... | collective-permute-start | bytes 1572872 | tf_op jit(solution)/shard_map/ppermute | solution.py:528
  33.1 13.5 %collective-permute-start.2 = (f32[4,128,256]{2,1,0:T(8,128)S(1)}, f32[4,128,256]{2,1,0:T(8,128)S(1)}, u32[]{:S(2)}, u32[]{:S(2)}) collective-permute-start(f32[4,128,256]{2,1,0:T(8,128)S(1)} %get-tuple-element.69), channel_id=1, source_target_pairs={{0,1},{1,0},{2,3},{3,2},{4,5},{5,4},{6,7},{7,6},{8,9},{9,8},{10,11... | collective-permute-start | bytes 1572872 | tf_op jit(solution)/shard_map/ppermute | solution.py:528
  34.9 16.2 %collective-permute-start.1 = (f32[4,128,128]{2,1,0:T(8,128)S(1)}, f32[4,128,128]{2,1,0:T(8,128)S(1)}, u32[]{:S(2)}, u32[]{:S(2)}) collective-permute-start(f32[4,128,128]{2,1,0:T(8,128)S(1)} %get-tuple-element.68.refs_3_), channel_id=1, source_target_pairs={{0,2},{1,3},{2,0},{3,1},{8,10},{9,11},{10,8},{11,9},{16,18},{17,19... | collective-permute-start | bytes 786440 | tf_op jit(solution)/shard_map/ppermute | solution.py:533
  47.6 8.8 %collective-permute-start.4 = (f32[4,128,128]{2,1,0:T(8,128)S(1)}, f32[4,128,128]{2,1,0:T(8,128)S(1)}, u32[]{:S(2)}, u32[]{:S(2)}) collective-permute-start(f32[4,128,128]{2,1,0:T(8,128)S(1)} %get-tuple-element.70.refs_4_), channel_id=1, source_target_pairs={{0,2},{1,3},{2,0},{3,1},{8,10},{9,11},{10,8},{11,9},{16,18},{17,19... | collective-permute-start | bytes 786440 | tf_op jit(solution)/shard_map/ppermute | solution.py:533
  52.0 5.9 %collective-permute-start.3 = (f32[4,128,128]{2,1,0:T(8,128)S(1)}, f32[4,128,128]{2,1,0:T(8,128)S(1)}, u32[]{:S(2)}, u32[]{:S(2)}) collective-permute-start(f32[4,128,128]{2,1,0:T(8,128)S(1)} %get-tuple-element.71.refs_4_), channel_id=1, source_target_pairs={{2,4},{3,5},{4,2},{5,3},{10,12},{11,13},{12,10},{13,11},{18,20},{1... | collective-permute-start | bytes 786440 | tf_op jit(solution)/shard_map/ppermute | solution.py:533
  61.8 8.8 %collective-permute-start.7 = (f32[4,128,128]{2,1,0:T(8,128)S(1)}, f32[4,128,128]{2,1,0:T(8,128)S(1)}, u32[]{:S(2)}, u32[]{:S(2)}) collective-permute-start(f32[4,128,128]{2,1,0:T(8,128)S(1)} %get-tuple-element.80.refs_4_), channel_id=1, source_target_pairs={{0,1},{1,0},{2,3},{3,2},{4,5},{5,4},{6,7},{7,6},{8,9},{9,8},{10,11... | collective-permute-start | bytes 786440 | tf_op jit(solution)/shard_map/ppermute | solution.py:528
  63.3 11.8 %collective-permute-start.9 = (f32[4,128,128]{2,1,0:T(8,128)S(1)}, f32[4,128,128]{2,1,0:T(8,128)S(1)}, u32[]{:S(2)}, u32[]{:S(2)}) collective-permute-start(f32[4,128,128]{2,1,0:T(8,128)S(1)} %get-tuple-element.83.refs_8_), channel_id=1, source_target_pairs={{0,1},{1,0},{2,3},{3,2},{4,5},{5,4},{6,7},{7,6},{8,9},{9,8},{10,11... | collective-permute-start | bytes 786440 | tf_op jit(solution)/shard_map/ppermute | solution.py:528
  74.9 5.1 %collective-permute-start.10 = (f32[257,8,128]{2,1,0:T(8,128)S(1)}, f32[257,8,128]{2,1,0:T(8,128)S(1)}, u32[]{:S(2)}, u32[]{:S(2)}) collective-permute-start(f32[257,8,128]{2,1,0:T(8,128)S(1)} %get-tuple-element.91), channel_id=1, source_target_pairs={{0,8},{1,9},{2,10},{3,11},{4,12},{5,13},{6,14},{7,15},{8,0},{9,1},... | collective-permute-start | bytes 3158024 | tf_op jit(solution)/shard_map/ppermute | solution.py:528
  80.7 14.0 %collective-permute-start.11 = (f32[129,8,128]{2,1,0:T(8,128)S(1)}, f32[129,8,128]{2,1,0:T(8,128)S(1)}, u32[]{:S(2)}, u32[]{:S(2)}) collective-permute-start(f32[129,8,128]{2,1,0:T(8,128)S(1)} %get-tuple-element.93), channel_id=1, source_target_pairs={{0,16},{1,17},{2,18},{3,19},{4,20},{5,21},{6,22},{7,23},{8,24},{9,... | collective-permute-start | bytes 1585160 | tf_op jit(solution)/shard_map/ppermute | solution.py:528
  83.0 14.5 %collective-permute-start.14 = (f32[129,8,128]{2,1,0:T(8,128)S(1)}, f32[129,8,128]{2,1,0:T(8,128)S(1)}, u32[]{:S(2)}, u32[]{:S(2)}) collective-permute-start(f32[129,8,128]{2,1,0:T(8,128)S(1)} %get-tuple-element.99), channel_id=1, source_target_pairs={{0,1},{1,0},{2,3},{3,2},{4,5},{5,4},{6,7},{7,6},{8,9},{9,8},{10,11... | collective-permute-start | bytes 1585160 | tf_op jit(solution)/shard_map/ppermute | solution.py:528
  95.3 7.7 %collective-permute-start.13 = (f32[65,8,128]{2,1,0:T(8,128)S(1)}, f32[65,8,128]{2,1,0:T(8,128)S(1)}, u32[]{:S(2)}, u32[]{:S(2)}) collective-permute-start(f32[65,8,128]{2,1,0:T(8,128)S(1)} %get-tuple-element.98), channel_id=1, source_target_pairs={{0,1},{1,0},{2,3},{3,2},{4,5},{5,4},{6,7},{7,6},{8,9},{9,8},{10,11... | collective-permute-start | bytes 798728 | tf_op jit(solution)/shard_map/ppermute | solution.py:528
  98.1 12.1 %collective-permute-start.16 = (f32[65,8,128]{2,1,0:T(8,128)S(1)}, f32[65,8,128]{2,1,0:T(8,128)S(1)}, u32[]{:S(2)}, u32[]{:S(2)}) collective-permute-start(f32[65,8,128]{2,1,0:T(8,128)S(1)} %get-tuple-element.104), channel_id=1, source_target_pairs={{0,16},{1,17},{2,18},{3,19},{4,20},{5,21},{6,22},{7,23},{8,24},{9,... | collective-permute-start | bytes 798728 | tf_op jit(solution)/shard_map/ppermute | solution.py:528
  103.6 10.4 %collective-permute-start.15 = (f32[33,8,128]{2,1,0:T(8,128)S(1)}, f32[33,8,128]{2,1,0:T(8,128)S(1)}, u32[]{:S(2)}, u32[]{:S(2)}) collective-permute-start(f32[33,8,128]{2,1,0:T(8,128)S(1)} %get-tuple-element.103), channel_id=1, source_target_pairs={{0,2},{1,3},{2,0},{3,1},{4,6},{5,7},{6,4},{7,5},{8,10},{9,11},{10,... | collective-permute-start | bytes 405512 | tf_op jit(solution)/shard_map/ppermute | solution.py:528
  110.8 12.6 %collective-permute-start.19 = (f32[33,8,128]{2,1,0:T(8,128)S(1)}, f32[33,8,128]{2,1,0:T(8,128)S(1)}, u32[]{:S(2)}, u32[]{:S(2)}) collective-permute-start(f32[33,8,128]{2,1,0:T(8,128)S(1)} %get-tuple-element.109), channel_id=1, source_target_pairs={{0,2},{1,3},{2,0},{3,1},{4,6},{5,7},{6,4},{7,5},{8,10},{9,11},{10,... | collective-permute-start | bytes 405512 | tf_op jit(solution)/shard_map/ppermute | solution.py:528
  114.6 14.4 %collective-permute-start.17 = (f32[17,8,128]{2,1,0:T(8,128)S(1)}, f32[17,8,128]{2,1,0:T(8,128)S(1)}, u32[]{:S(2)}, u32[]{:S(2)}) collective-permute-start(f32[17,8,128]{2,1,0:T(8,128)S(1)} %get-tuple-element.107), channel_id=1, source_target_pairs={{0,4},{1,5},{2,6},{3,7},{4,0},{5,1},{6,2},{7,3},{8,12},{9,13},{10,... | collective-permute-start | bytes 208904 | tf_op jit(solution)/shard_map/ppermute | solution.py:528
  124.0 7.0 %collective-permute-start.20 = (f32[17,8,128]{2,1,0:T(8,128)S(1)}, f32[17,8,128]{2,1,0:T(8,128)S(1)}, u32[]{:S(2)}, u32[]{:S(2)}) collective-permute-start(f32[17,8,128]{2,1,0:T(8,128)S(1)} %get-tuple-element.111), channel_id=1, source_target_pairs={{0,4},{1,5},{2,6},{3,7},{4,0},{5,1},{6,2},{7,3},{8,12},{9,13},{10,... | collective-permute-start | bytes 208904 | tf_op jit(solution)/shard_map/ppermute | solution.py:528
  129.0 5.2 %collective-permute-start.18 = (f32[16,8,128]{2,1,0:T(8,128)S(1)}, f32[16,8,128]{2,1,0:T(8,128)S(1)}, u32[]{:S(2)}, u32[]{:S(2)}) collective-permute-start(f32[16,8,128]{2,1,0:T(8,128)S(1)} %get-tuple-element.108.refs_1_), channel_id=1, source_target_pairs={{0,4},{1,5},{2,6},{3,7},{4,0},{5,1},{6,2},{7,3},{8,12},{9,13},{10,... | collective-permute-start | bytes 196616 | tf_op jit(solution)/shard_map/ppermute | solution.py:528
  131.0 5.9 %collective-permute-start.22 = (f32[16,8,128]{2,1,0:T(8,128)S(1)}, f32[16,8,128]{2,1,0:T(8,128)S(1)}, u32[]{:S(2)}, u32[]{:S(2)}) collective-permute-start(f32[16,8,128]{2,1,0:T(8,128)S(1)} %get-tuple-element.112.refs_3_.refs_1_), channel_id=1, source_target_pairs={{0,4},{1,5},{2,6},{3,7},{4,0},{5,1},{6,2},{7,3},{8,12},{9,13},{10,... | collective-permute-start | bytes 196616 | tf_op jit(solution)/shard_map/ppermute | solution.py:528
  134.8 5.0 %collective-permute-start.21 = (f32[32,8,128]{2,1,0:T(8,128)S(1)}, f32[32,8,128]{2,1,0:T(8,128)S(1)}, u32[]{:S(2)}, u32[]{:S(2)}) collective-permute-start(f32[32,8,128]{2,1,0:T(8,128)S(1)} %lay.8.refs_3_.refs_1_), channel_id=1, source_target_pairs={{0,2},{1,3},{2,0},{3,1},{4,6},{5,7},{6,4},{7,5},{8,10},{9,11},{10,... | collective-permute-start | bytes 393224 | tf_op jit(solution)/shard_map/ppermute | solution.py:528
  137.5 5.0 %collective-permute-start.24 = (f32[32,8,128]{2,1,0:T(8,128)S(1)}, f32[32,8,128]{2,1,0:T(8,128)S(1)}, u32[]{:S(2)}, u32[]{:S(2)}) collective-permute-start(f32[32,8,128]{2,1,0:T(8,128)S(1)} %lay.9.refs_3_.refs_1_), channel_id=1, source_target_pairs={{0,2},{1,3},{2,0},{3,1},{4,6},{5,7},{6,4},{7,5},{8,10},{9,11},{10,... | collective-permute-start | bytes 393224 | tf_op jit(solution)/shard_map/ppermute | solution.py:528
  140.4 6.4 %collective-permute-start.23 = (f32[64,8,128]{2,1,0:T(8,128)S(1)}, f32[64,8,128]{2,1,0:T(8,128)S(1)}, u32[]{:S(2)}, u32[]{:S(2)}) collective-permute-start(f32[64,8,128]{2,1,0:T(8,128)S(1)} %lay.10.refs_3_.refs_1_), channel_id=1, source_target_pairs={{0,1},{1,0},{2,3},{3,2},{4,5},{5,4},{6,7},{7,6},{8,9},{9,8},{10,11... | collective-permute-start | bytes 786440 | tf_op jit(solution)/shard_map/ppermute | solution.py:528
  143.1 9.3 %collective-permute-start.26 = (f32[64,8,128]{2,1,0:T(8,128)S(1)}, f32[64,8,128]{2,1,0:T(8,128)S(1)}, u32[]{:S(2)}, u32[]{:S(2)}) collective-permute-start(f32[64,8,128]{2,1,0:T(8,128)S(1)} %lay.11.refs_3_.refs_1_), channel_id=1, source_target_pairs={{0,16},{1,17},{2,18},{3,19},{4,20},{5,21},{6,22},{7,23},{8,24},{9,... | collective-permute-start | bytes 786440 | tf_op jit(solution)/shard_map/ppermute | solution.py:528
  147.4 11.9 %collective-permute-start.25 = (f32[128,8,128]{2,1,0:T(8,128)S(1)}, f32[128,8,128]{2,1,0:T(8,128)S(1)}, u32[]{:S(2)}, u32[]{:S(2)}) collective-permute-start(f32[128,8,128]{2,1,0:T(8,128)S(1)} %lay.12.refs_3_.refs_1_), channel_id=1, source_target_pairs={{0,16},{1,17},{2,18},{3,19},{4,20},{5,21},{6,22},{7,23},{8,24},{9,... | collective-permute-start | bytes 1572872 | tf_op jit(solution)/shard_map/ppermute | solution.py:528
  153.0 9.2 %collective-permute-start.28 = (f32[128,8,128]{2,1,0:T(8,128)S(1)}, f32[128,8,128]{2,1,0:T(8,128)S(1)}, u32[]{:S(2)}, u32[]{:S(2)}) collective-permute-start(f32[128,8,128]{2,1,0:T(8,128)S(1)} %lay.13.refs_3_.refs_1_), channel_id=1, source_target_pairs={{0,1},{1,0},{2,3},{3,2},{4,5},{5,4},{6,7},{7,6},{8,9},{9,8},{10,11... | collective-permute-start | bytes 1572872 | tf_op jit(solution)/shard_map/ppermute | solution.py:528
  (12 other events, 52.0 us)

commit v8 on v7

--- a/solution.py
+++ b/solution.py
@@ -98,12 +98,36 @@
     apart = row ^ col
     invs = [jnp.where(row == col, 1.0, jnp.where(apart == 1, -s, 0.0)).astype(BF16) for s in systems]
     step = 2
-    while step < span:
+    while 2 * step < span:
         keep = (apart >= step) & (apart < 2 * step)
         bands = [jnp.where(keep, s, 0.0).astype(BF16) for s in systems]
-        inners = [dot(i, b).astype(BF16) for i, b in zip(invs, bands)]
-        invs = [i - dot(n, i).astype(BF16) for n, i in zip(inners, invs)]
+        if step < 16:
+            inners = [dot(i, b).astype(BF16) for i, b in zip(invs, bands)]
+            invs = [i - dot(n, i).astype(BF16) for n, i in zip(inners, invs)]
+        else:
+            odds = [jnp.concatenate([i[r : r + step] for r in range(step, span, 2 * step)], 0) for i in invs]
+            inners = [dot(o, b).astype(BF16) for o, b in zip(odds, bands)]
+            news = [o - dot(n, i).astype(BF16) for o, n, i in zip(odds, inners, invs)]
+            invs = [
+                jnp.concatenate(
+                    [
+                        piece
+                        for k in range(span // (2 * step))
+                        for piece in (i[2 * k * step : (2 * k + 1) * step], n[k * step : (k + 1) * step])
+                    ],
+                    0,
+                )
+                for i, n in zip(invs, news)
+            ]
         step *= 2
+    lows = [dot(dot(i[step:, step:], s[step:, :step].astype(BF16)).astype(BF16), i[:step, :step]) for i, s in zip(invs, systems)]
+    blank = jnp.zeros((step, step), BF16)
+    invs = [
+        jnp.concatenate(
+            [jnp.concatenate([i[:step, :step], blank], 1), jnp.concatenate([-low.astype(BF16), i[step:, step:]], 1)], 0
+        )
+        for i, low in zip(invs, lows)
+    ]
     rounded = [r.astype(BF16) for r in rights]
     firsts = [dot(i, b) + (r - b.astype(F32)) for i, b, r in zip(invs, rounded, rights)]
     residuals = [(r - f) - dot3(s, f) for r, f, s in zip(rights, firsts, systems)]
@@ -286,75 +310,53 @@
     )(info, maps, got, state, *after)
 
 
-def mix_kernel(span, info, core_ref, query_ref, keep_ref, got_ref, back_ref, gain_ref, cot_ref, mixed_ref, wsend_ref, wkeep_ref):
-    step = pl.program_id(0)
-    half = pl.num_programs(0) // 2
+def mix_kernel(span, first_head, info, core_ref, query_ref, keep_ref, got_ref, back_ref, gain_ref, cot_ref, mixed_ref, wsend_ref, wkeep_ref):
+    count = keep_ref.shape[0]
+    half = count // 2
     dims = gain_ref.shape[1]
     tiles = wsend_ref.shape[0] - 1
     each = tiles // half
+    stripe = dims // 8
     gain_part = jnp.zeros((8, dims), F32)
     for part in range(2):
         seq = info[0] if part == 0 else 1 - info[0]
         rows = pl.ds(pl.multiple_of(seq * span, span), span)
-        state = (keep_ref if part == 0 else got_ref)[0]
-        core = core_ref[rows, :] + dot3(query_ref[rows, :], state)
-        normal = core * lax.rsqrt(jnp.mean(core * core, axis=1, keepdims=True) + 1e-05)
-        gain_part += jnp.sum((normal * back_ref[rows, :]).reshape(-1, 8, dims), axis=0)
-        mixed_ref[rows, :] = (normal * gain_ref[...]).astype(BF16)
+        for h in range(count):
+            lanes = slice(h * dims, (h + 1) * dims)
+            state = (keep_ref if part == 0 else got_ref)[h]
+            core = core_ref[rows, lanes] + dot3(query_ref[rows, lanes], state)
+            normal = core * lax.rsqrt(jnp.mean(core * core, axis=1, keepdims=True) + 1e-05)
+            back = back_ref[rows, (first_head + h) * dims : (first_head + h + 1) * dims]
+            gain_part += jnp.sum((normal * back).reshape(-1, 8, dims), axis=0)
+            mixed_ref[rows, lanes] = (normal * gain_ref[...]).astype(BF16)
+    wkeep_ref[tiles] = gain_part
+    wsend_ref[tiles] = gain_part
     product = dot_tn(mixed_ref[...], cot_ref[...])
-    stripe = dims // 8
-    pieces = [
-        product[:, first : first + 128].reshape(stripe, 8, 128) for first in range(0, product.shape[1], 128)
-    ]
-
-    @pl.when(step == 0)
-    def _():
-        wkeep_ref[tiles] = gain_part
-
-    @pl.when(step > 0)
-    def _():
-        wkeep_ref[tiles] += gain_part
-
-    @pl.when(step == 2 * half - 1)
-    def _():
-        wsend_ref[tiles] = wkeep_ref[tiles]
-
-    @pl.when(step < half)
-    def _():
-        for i, piece in enumerate(pieces):
-            wsend_ref[pl.ds(step * each + i * stripe, stripe)] = piece
-
-    @pl.when(step >= half)
-    def _():
-        for i, piece in enumerate(pieces):
-            wkeep_ref[pl.ds((step - half) * each + i * stripe, stripe)] = piece
+    for h in range(count):
+        first = (h % half) * each
+        pieces = [
+            (first + i * stripe, product[h * dims : (h + 1) * dims, i * 128 : (i + 1) * 128].reshape(stripe, 8, 128))
+            for i in range(product.shape[1] // 128)
+        ]
+        for side, ref in ((0, wkeep_ref), (1, wsend_ref)):
+
+            @pl.when((info[1] ^ side) == h // half)
+            def _(ref=ref, pieces=pieces):
+                for at, piece in pieces:
+                    ref[at : at + stripe] = piece
 
 
 def mix_call(info, first_head, core, query, keep, got, back, gain, cot, span, after=()):
     count, width = cot.shape
     heads_here = keep.shape[0]
     dims = gain.shape[1]
-    half = heads_here // 2
-
-    def order(i, info):
-        first = jnp.where(i < half, 1 - info[1], info[1])
-        return first * half + lax.rem(i, half)
-
-    row_spec = pl.BlockSpec((count, dims), lambda i, info: (0, order(i, info)))
-    back_spec = pl.BlockSpec((count, dims), lambda i, info: (0, first_head + order(i, info)))
-    state_spec = pl.BlockSpec((1, dims, dims), lambda i, info: (order(i, info), 0, 0))
-    weight = jax.ShapeDtypeStruct((half * dims * width // 1024 + 1, 8, 128), F32)
-    return pl.pallas_call(
-        skipping(functools.partial(mix_kernel, span), 8, after),
+    weight = jax.ShapeDtypeStruct((heads_here // 2 * dims * width // 1024 + 1, 8, 128), F32)
+    return pl.pallas_call(
+        skipping(functools.partial(mix_kernel, span, first_head), 8, after),
         out_shape=(jax.ShapeDtypeStruct((count, heads_here * dims), BF16), weight, weight),
-        grid_spec=pltpu.PrefetchScalarGridSpec(
-            num_scalar_prefetch=1,
-            grid=(heads_here,),
-            in_specs=[row_spec, row_spec, state_spec, state_spec, back_spec, whole(gain.shape), whole(cot.shape)]
-            + anywhere(after),
-            out_specs=(row_spec, whole(weight.shape), whole(weight.shape)),
-        ),
-        compiler_params=params(16),
+        in_specs=[smem()] + [vmem()] * 7 + anywhere(after),
+        out_specs=(vmem(), vmem(), vmem()),
+        compiler_params=params(20),
         cost_estimate=cost(heads_here * 2 * 512 * 1024 * 128, 3 * MIB),
         name="mix",
     )(info, core, query, keep, got, back, gain, cot, *after)
@@ -474,27 +476,37 @@
     )(info, own, got, *after)
 
 
-def join_kernel(scale, stripe, blocks, info, *refs):
-    sums = (len(refs) - 2) // 3
-    lasts, (out_ref, gain_ref) = refs[2 * sums : 3 * sums], refs[-2:]
+def join_kernel(scale, stripe, blocks, flags, info, *refs):
+    sums = len(blocks)
+    lasts, (out_ref, gain_ref) = refs[4 * sums : 5 * sums], refs[-2:]
     columns = out_ref.shape[1] // 128
     dims = stripe * 8
+    size = refs[0].shape[0]
+    per_half = size // stripe
     for g in range(sums):
-        for part, ref in enumerate(refs[2 * g : 2 * g + 2]):
+        for part in range(2):
             side = info[1] if part == 0 else 1 - info[1]
-            for index, (base, half) in enumerate(blocks[g]):
-                rows = pl.ds(pl.multiple_of((base + side * half) * dims, dims), dims)
-                for col in range(columns):
-                    first = (index * columns + col) * stripe
-                    values = ref[first : first + stripe].reshape(dims, 128) * scale
-                    out_ref[rows, col * 128 : (col + 1) * 128] = values.astype(BF16)
+            for flip in range(2):
+                ref = refs[4 * g + 2 * part + flip]
+                low = info[flags[g]] == flip
+                for at in range(2):
+
+                    @pl.when(low if at == 0 else jnp.logical_not(low))
+                    def _(ref=ref, at=at, side=side, g=g):
+                        for index in range(per_half):
+                            block, col = divmod(at * per_half + index, columns)
+                            base, half = blocks[g][block]
+                            rows = pl.ds(pl.multiple_of((base + side * half) * dims, dims), dims)
+                            values = ref[index * stripe : (index + 1) * stripe].reshape(dims, 128) * scale
+                            out_ref[rows, col * 128 : (col + 1) * 128] = values.astype(BF16)
+
     gain_ref[...] = jnp.sum(sum(ref[...] for ref in lasts), axis=0, keepdims=True) * scale
 
 
-def join_call(info, parts, lasts, blocks, scale, dims, width):
+def join_call(info, parts, lasts, blocks, flags, scale, dims, width):
     total = sum(p.shape[0] for p in parts) * 1024 // width
     return pl.pallas_call(
-        functools.partial(join_kernel, scale, dims // 8, blocks),
+        functools.partial(join_kernel, scale, dims // 8, blocks, flags),
         out_shape=(jax.ShapeDtypeStruct((total, width), BF16), jax.ShapeDtypeStruct((1, 128), F32)),
         in_specs=[smem()] + [vmem()] * (len(parts) + len(lasts)),
         out_specs=(vmem(), vmem()),
@@ -607,14 +619,18 @@
             previous = own
     totals = [total_call(a) for a in arrays]
     pieces = [t[0] for t in totals]
-    for step in reversed(range(len(orders[0]))):
+    for step in reversed(range(1, len(orders[0]))):
         arrived = [moved(pieces[g], orders[g][step][0]) for g in sums]
         previous = pieces[-1]
         for g in sums:
             pieces[g] = previous = lay_call(info, orders[g][step][1], pieces[g], arrived[g], [previous])
-    ends = [part for piece in pieces for part in (piece, moved(piece, (0, 1, 0, 0)))]
+    ends = []
+    for g in sums:
+        arrived = moved(pieces[g], orders[g][0][0])
+        ends += [pieces[g], arrived, moved(pieces[g], (0, 1, 0, 0)), moved(arrived, (0, 1, 0, 0))]
+    flags = [orders[g][0][1] for g in sums]
     blocks = [[(first_of[r] + i, RELAYS[r] // 2) for r in SUMS[g] for i in range(RELAYS[r] // 2)] for g in sums]
-    weight_grad, gain_grad = join_call(info, ends, [t[1] for t in totals], blocks, scale, dims, width)
+    weight_grad, gain_grad = join_call(info, ends, [t[1] for t in totals], blocks, flags, scale, dims, width)
     return (output.reshape(seqs, span, width), weight_grad, gain_grad.reshape(dims))
 
 

time: 170 us -> 162 us (0.953)
  Pallas kernels: 58 us -> 51.6 us
  waiting for transfers between devices: 57.1 us -> 54 us
    pallas_call x3, Pallas kernels: 11.1 us -> 6.85 us  [the longest x2 4.44 us: mix_call(): pl.pallas_call(skipping(functools.partial(mix_kernel, span, first_head),...]
    ppermute x24 -> x26, waiting for transfers between devices: 53.4 us -> 50.3 us  [moved(): return lax.ppermute(array, both, route)]
    ppermute x24 -> x26, starting transfers between devices: 38 us -> 39.3 us  [moved(): return lax.ppermute(array, both, route)]
    pallas_call x8 -> x6, Pallas kernels: 4.61 us -> 3.38 us  [lay_call(): pl.pallas_call(skipping(functools.partial(lay_kernel, where), 3, after),...]
  transfers between devices with their start and end apart: 30 -> 32, of which waited for: 20 -> 20; matrix products, arithmetic and copies ran while one was open for 0% -> 0% of each run, Pallas kernels for 25% -> 22%
where the time goes in v8:
time: 162 us; the launch traced here: 161 us
  waiting for transfers between devices  54 us (33%)
  Pallas kernels  51.6 us (32%)
  starting transfers between devices  49.4 us (30%)
  local copies, waits for them, and re-layouts  3.69 us (2%)
    ppermute x26, waiting for transfers between devices, moved(): return lax.ppermute(array, both, route)  50.3 us
    ppermute x26, starting transfers between devices, moved(): return lax.ppermute(array, both, route)  39.3 us
    pallas_call x2, Pallas kernels, local_call(): pl.pallas_call(skipping(functools.partial(local_kernel, first_head, heads...  23.5 us
    ppermute x6, starting transfers between devices, lifted(): return lax.ppermute(array, 'tm', route)  10.1 us
    pallas_call x8, Pallas kernels, fold_call(): pl.pallas_call(skipping(functools.partial(fold_kernel, parts, terms, wher...  4.87 us
    pallas_call x2, Pallas kernels, mix_call(): pl.pallas_call(skipping(functools.partial(mix_kernel, span, first_head),...  4.44 us
    ppermute x6, waiting for transfers between devices, lifted(): return lax.ppermute(array, 'tm', route)  3.72 us
    unnamed x12, local copies, waits for them, and re-layouts  3.59 us
  transfers between devices with their start and end apart: 32, of which 20 were waited for; matrix products, arithmetic and copies ran while one was open for 0% of the time, Pallas kernels for 22%

profile of v8, /device:TPU:0, one launch (start us, length us, event | category | flops | bytes accessed | tf_op | source)
XLA Modules:
  0.0 161.3 jit_solution(6480624072653168178)
XLA Ops:
  5.8 12.8 %local.2 = (f32[4,128,256]{2,1,0:T(8,128)S(1)}, f32[4,128,256]{2,1,0:T(8,128)S(1)}, f32[512,512]{1,0:T(8,128)S(1)}, f32[512,512]{1,0:T(8,128)S(1)}, f32[512,16]{1,0:T(8,128)S(1)}) custom-call(s32[7]{0:T(128)S(1)} %stack.49.refs_0_.info, s32[2,4,24]{2,1,0:T(4,128)S(1)} %pad_add_fusion.refs_1_, bf16[512,1024]{1,0:T(8,128)(2,1)S(1)} %bitcast.26, ...), custom_call_target="tpu_custom_call" | custom-call | flops 6442450944 | bytes 8388608 | tf_op jit(solution)/shard_map/local/pallas_call | solution.py:219
  18.6 3.0 %collective-permute-start = (f32[4,128,256]{2,1,0:T(8,128)S(1)}, f32[4,128,256]{2,1,0:T(8,128)S(1)}, u32[]{:S(2)}, u32[]{:S(2)}) collective-permute-start(f32[4,128,256]{2,1,0:T(8,128)S(1)} %get-tuple-element.63), channel_id=1, source_target_pairs={{0,1},{1,0},{2,3},{3,2},{4,5},{5,4},{6,7},{7,6},{8,9},{9,8},{10,11... | collective-permute-start | bytes 1572872 | tf_op jit(solution)/shard_map/ppermute | solution.py:540
  21.6 10.7 %local.3 = (f32[4,128,256]{2,1,0:T(8,128)S(1)}, f32[4,128,256]{2,1,0:T(8,128)S(1)}, f32[512,512]{1,0:T(8,128)S(1)}, f32[512,512]{1,0:T(8,128)S(1)}) custom-call(s32[7]{0:T(128)S(1)} %stack.49.refs_0_.info, s32[2,4,24]{2,1,0:T(4,128)S(1)} %pad_add_fusion.refs_1_, bf16[512,1024]{1,0:T(8,128)(2,1)S(1)} %bitcast.27, bf16[64,128,128]{2,1,0:T(8,128)(2,1)S(1)} %copy-done.3, ...), custom_call_target="tpu_custom_call" | custom-call | flops 6442450944 | bytes 8388608 | tf_op jit(solution)/shard_map/local/pallas_call | solution.py:219
  34.5 3.9 %collective-permute-start.1 = (f32[4,128,128]{2,1,0:T(8,128)S(1)}, f32[4,128,128]{2,1,0:T(8,128)S(1)}, u32[]{:S(2)}, u32[]{:S(2)}) collective-permute-start(f32[4,128,128]{2,1,0:T(8,128)S(1)} %get-tuple-element.68.refs_3_), channel_id=1, source_target_pairs={{0,2},{1,3},{2,0},{3,1},{8,10},{9,11},{10,8},{11,9},{16,18},{17,19... | collective-permute-start | bytes 786440 | tf_op jit(solution)/shard_map/ppermute | solution.py:545
  38.4 3.3 %back.1.refs_4_.refs_5_ = f32[512,1024]{1,0:T(8,128)S(1)} custom-call(bf16[512,1024]{1,0:T(8,128)(2,1)S(1)} %bitcast.21, bf16[1024,1024]{1,0:T(8,128)(2,1)S(1)} %copy-done.1), custom_call_target="tpu_custom_call" | custom-call | flops 1073741824 | bytes 5242880 | tf_op jit(solution)/shard_map/back/pallas_call | solution.py:372
  41.8 4.0 %collective-permute-done.2.refs_2_ = f32[4,128,256]{2,1,0:T(8,128)S(1)} collective-permute-done((f32[4,128,256]{2,1,0:T(8,128)S(1)}, f32[4,128,256]{2,1,0:T(8,128)S(1)}, u32[]{:S(2)}, u32[]{:S(2)}) %collective-permute-start.2) | collective-permute-done | bytes 524320 | tf_op jit(solution)/shard_map/ppermute | solution.py:540
  46.8 3.5 %collective-permute-start.4 = (f32[4,128,128]{2,1,0:T(8,128)S(1)}, f32[4,128,128]{2,1,0:T(8,128)S(1)}, u32[]{:S(2)}, u32[]{:S(2)}) collective-permute-start(f32[4,128,128]{2,1,0:T(8,128)S(1)} %get-tuple-element.70.refs_4_), channel_id=1, source_target_pairs={{0,2},{1,3},{2,0},{3,1},{8,10},{9,11},{10,8},{11,9},{16,18},{17,19... | collective-permute-start | bytes 786440 | tf_op jit(solution)/shard_map/ppermute | solution.py:545
  51.8 3.7 %collective-permute-done.4.refs_2_ = f32[4,128,128]{2,1,0:T(8,128)S(1)} collective-permute-done((f32[4,128,128]{2,1,0:T(8,128)S(1)}, f32[4,128,128]{2,1,0:T(8,128)S(1)}, u32[]{:S(2)}, u32[]{:S(2)}) %collective-permute-start.4) | collective-permute-done | bytes 262176 | tf_op jit(solution)/shard_map/ppermute | solution.py:545
  63.9 6.2 %collective-permute-done.7.refs_4_ = f32[4,128,128]{2,1,0:T(8,128)S(1)} collective-permute-done((f32[4,128,128]{2,1,0:T(8,128)S(1)}, f32[4,128,128]{2,1,0:T(8,128)S(1)}, u32[]{:S(2)}, u32[]{:S(2)}) %collective-permute-start.7) | collective-permute-done | bytes 262176 | tf_op jit(solution)/shard_map/ppermute | solution.py:540
  70.2 2.2 %mix.2 = (bf16[512,512]{1,0:T(8,128)(2,1)S(1)}, f32[257,8,128]{2,1,0:T(8,128)S(1)}, f32[257,8,128]{2,1,0:T(8,128)S(1)}) custom-call(s32[7]{0:T(128)S(1)} %stack.49.refs_0_.info, f32[512,512]{1,0:T(8,128)S(1)} %get-tuple-element.60.refs_1_, f32[512,512]{1,0:T(8,128)S(1)} %get-tuple-element.61.refs_2_, f32[4,128,128]{2,1,0:T(8,128)S(1)} %get-tuple-element.79.refs_3_, ...), custom_call_target="tpu_custom_call" | custom-call | flops 536870912 | bytes 3145728 | tf_op jit(solution)/shard_map/mix/pallas_call | solution.py:354
  73.0 2.2 %mix.3 = (bf16[512,512]{1,0:T(8,128)(2,1)S(1)}, f32[257,8,128]{2,1,0:T(8,128)S(1)}, f32[257,8,128]{2,1,0:T(8,128)S(1)}) custom-call(s32[7]{0:T(128)S(1)} %stack.49.refs_0_.info, f32[512,512]{1,0:T(8,128)S(1)} %get-tuple-element.85.refs_1_, f32[512,512]{1,0:T(8,128)S(1)} %get-tuple-element.86.refs_2_, f32[4,128,128]{2,1,0:T(8,128)S(1)} %get-tuple-element.87.refs_3_, ...), custom_call_target="tpu_custom_call" | custom-call | flops 536870912 | bytes 3145728 | tf_op jit(solution)/shard_map/mix/pallas_call | solution.py:354
  80.4 2.8 %finish.1 = (bf16[512,1024]{1,0:T(8,128)(2,1)}, f32[8,128]{1,0:T(8,128)S(1)}) custom-call(bf16[512,512]{1,0:T(8,128)(2,1)S(1)} %get-tuple-element.84.refs_0_, bf16[512,512]{1,0:T(8,128)(2,1)S(1)} %get-tuple-element.89.refs_1_, bf16[1024,1024]{1,0:T(8,128)(2,1)S(1)} %copy-done.1), custom_call_target="tpu_custom_call" | custom-call | flops 1073741824 | bytes 4194304 | tf_op jit(solution)/shard_map/finish/pallas_call | solution.py:395
  83.2 7.2 %collective-permute-done.11.refs_2_ = f32[129,8,128]{2,1,0:T(8,128)S(1)} collective-permute-done((f32[129,8,128]{2,1,0:T(8,128)S(1)}, f32[129,8,128]{2,1,0:T(8,128)S(1)}, u32[]{:S(2)}, u32[]{:S(2)}) %collective-permute-start.11) | collective-permute-done | bytes 528416 | tf_op jit(solution)/shard_map/ppermute | solution.py:540
  94.5 4.6 %collective-permute-done.13.refs_2_ = f32[65,8,128]{2,1,0:T(8,128)S(1)} collective-permute-done((f32[65,8,128]{2,1,0:T(8,128)S(1)}, f32[65,8,128]{2,1,0:T(8,128)S(1)}, u32[]{:S(2)}, u32[]{:S(2)}) %collective-permute-start.13) | collective-permute-done | bytes 266272 | tf_op jit(solution)/shard_map/ppermute | solution.py:540
  99.7 6.1 %collective-permute-start.15 = (f32[33,8,128]{2,1,0:T(8,128)S(1)}, f32[33,8,128]{2,1,0:T(8,128)S(1)}, u32[]{:S(2)}, u32[]{:S(2)}) collective-permute-start(f32[33,8,128]{2,1,0:T(8,128)S(1)} %get-tuple-element.103), channel_id=1, source_target_pairs={{0,2},{1,3},{2,0},{3,1},{4,6},{5,7},{6,4},{7,5},{8,10},{9,11},{10,... | collective-permute-start | bytes 405512 | tf_op jit(solution)/shard_map/ppermute | solution.py:540
  107.7 2.3 %collective-permute-done.15.refs_2_ = f32[33,8,128]{2,1,0:T(8,128)S(1)} collective-permute-done((f32[33,8,128]{2,1,0:T(8,128)S(1)}, f32[33,8,128]{2,1,0:T(8,128)S(1)}, u32[]{:S(2)}, u32[]{:S(2)}) %collective-permute-start.15) | collective-permute-done | bytes 135200 | tf_op jit(solution)/shard_map/ppermute | solution.py:540
  110.6 8.8 %collective-permute-start.17 = (f32[17,8,128]{2,1,0:T(8,128)S(1)}, f32[17,8,128]{2,1,0:T(8,128)S(1)}, u32[]{:S(2)}, u32[]{:S(2)}) collective-permute-start(f32[17,8,128]{2,1,0:T(8,128)S(1)} %get-tuple-element.107), channel_id=1, source_target_pairs={{0,4},{1,5},{2,6},{3,7},{4,0},{5,1},{6,2},{7,3},{8,12},{9,13},{10,... | collective-permute-start | bytes 208904 | tf_op jit(solution)/shard_map/ppermute | solution.py:540
  120.9 3.7 %collective-permute-done.17.refs_1_ = f32[17,8,128]{2,1,0:T(8,128)S(1)} collective-permute-done((f32[17,8,128]{2,1,0:T(8,128)S(1)}, f32[17,8,128]{2,1,0:T(8,128)S(1)}, u32[]{:S(2)}, u32[]{:S(2)}) %collective-permute-start.17) | collective-permute-done | bytes 69664 | tf_op jit(solution)/shard_map/ppermute | solution.py:540
  125.3 2.3 %collective-permute-start.22 = (f32[16,8,128]{2,1,0:T(8,128)S(1)}, f32[16,8,128]{2,1,0:T(8,128)S(1)}, u32[]{:S(2)}, u32[]{:S(2)}) collective-permute-start(f32[16,8,128]{2,1,0:T(8,128)S(1)} %get-tuple-element.112.refs_3_.refs_1_), channel_id=1, source_target_pairs={{0,4},{1,5},{2,6},{3,7},{4,0},{5,1},{6,2},{7,3},{8,12},{9,13},{10,... | collective-permute-start | bytes 196616 | tf_op jit(solution)/shard_map/ppermute | solution.py:540
  127.6 2.3 %collective-permute-done.18.refs_2_ = f32[16,8,128]{2,1,0:T(8,128)S(1)} collective-permute-done((f32[16,8,128]{2,1,0:T(8,128)S(1)}, f32[16,8,128]{2,1,0:T(8,128)S(1)}, u32[]{:S(2)}, u32[]{:S(2)}) %collective-permute-start.18) | collective-permute-done | bytes 65568 | tf_op jit(solution)/shard_map/ppermute | solution.py:540
  131.2 2.2 %collective-permute-start.24 = (f32[32,8,128]{2,1,0:T(8,128)S(1)}, f32[32,8,128]{2,1,0:T(8,128)S(1)}, u32[]{:S(2)}, u32[]{:S(2)}) collective-permute-start(f32[32,8,128]{2,1,0:T(8,128)S(1)} %lay.7.refs_3_.refs_1_), channel_id=1, source_target_pairs={{0,2},{1,3},{2,0},{3,1},{4,6},{5,7},{6,4},{7,5},{8,10},{9,11},{10,... | collective-permute-start | bytes 393224 | tf_op jit(solution)/shard_map/ppermute | solution.py:540
  139.3 4.2 %collective-permute-done.23.refs_2_ = f32[64,8,128]{2,1,0:T(8,128)S(1)} collective-permute-done((f32[64,8,128]{2,1,0:T(8,128)S(1)}, f32[64,8,128]{2,1,0:T(8,128)S(1)}, u32[]{:S(2)}, u32[]{:S(2)}) %collective-permute-start.23) | collective-permute-done | bytes 262176 | tf_op jit(solution)/shard_map/ppermute | solution.py:540
  150.1 5.7 %collective-permute-done.29.refs_5_ = f32[128,8,128]{2,1,0:T(8,128)S(1)} collective-permute-done((f32[128,8,128]{2,1,0:T(8,128)S(1)}, f32[128,8,128]{2,1,0:T(8,128)S(1)}, u32[]{:S(2)}, u32[]{:S(2)}) %collective-permute-start.29) | collective-permute-done | bytes 524320 | tf_op jit(solution)/shard_map/ppermute | solution.py:540
  158.9 2.4 %join.1 = (bf16[1024,1024]{1,0:T(8,128)(2,1)}, f32[1,128]{1,0:T(1,128)}) custom-call(s32[7]{0:T(128)S(1)} %stack.49.refs_0_.info, f32[128,8,128]{2,1,0:T(8,128)S(1)} %lay.10.refs_3_.refs_0_, f32[128,8,128]{2,1,0:T(8,128)S(1)} %collective-permute-done.25.refs_1_, f32[128,8,128]{2,1,0:T(8,128)S(1)} %collective-permute-done.26.refs_2_, ...), custom_call_target="tpu_custom_call" | custom-call | tf_op jit(solution)/shard_map/join/pallas_call | solution.py:508
  (87 shorter events, 49.9 us)
Async XLA Ops:
  18.6 14.9 %collective-permute-start = (f32[4,128,256]{2,1,0:T(8,128)S(1)}, f32[4,128,256]{2,1,0:T(8,128)S(1)}, u32[]{:S(2)}, u32[]{:S(2)}) collective-permute-start(f32[4,128,256]{2,1,0:T(8,128)S(1)} %get-tuple-element.63), channel_id=1, source_target_pairs={{0,1},{1,0},{2,3},{3,2},{4,5},{5,4},{6,7},{7,6},{8,9},{9,8},{10,11... | collective-permute-start | bytes 1572872 | tf_op jit(solution)/shard_map/ppermute | solution.py:540
  32.3 13.4 %collective-permute-start.2 = (f32[4,128,256]{2,1,0:T(8,128)S(1)}, f32[4,128,256]{2,1,0:T(8,128)S(1)}, u32[]{:S(2)}, u32[]{:S(2)}) collective-permute-start(f32[4,128,256]{2,1,0:T(8,128)S(1)} %get-tuple-element.69), channel_id=1, source_target_pairs={{0,1},{1,0},{2,3},{3,2},{4,5},{5,4},{6,7},{7,6},{8,9},{9,8},{10,11... | collective-permute-start | bytes 1572872 | tf_op jit(solution)/shard_map/ppermute | solution.py:540
  34.5 15.8 %collective-permute-start.1 = (f32[4,128,128]{2,1,0:T(8,128)S(1)}, f32[4,128,128]{2,1,0:T(8,128)S(1)}, u32[]{:S(2)}, u32[]{:S(2)}) collective-permute-start(f32[4,128,128]{2,1,0:T(8,128)S(1)} %get-tuple-element.68.refs_3_), channel_id=1, source_target_pairs={{0,2},{1,3},{2,0},{3,1},{8,10},{9,11},{10,8},{11,9},{16,18},{17,19... | collective-permute-start | bytes 786440 | tf_op jit(solution)/shard_map/ppermute | solution.py:545
  46.8 8.7 %collective-permute-start.4 = (f32[4,128,128]{2,1,0:T(8,128)S(1)}, f32[4,128,128]{2,1,0:T(8,128)S(1)}, u32[]{:S(2)}, u32[]{:S(2)}) collective-permute-start(f32[4,128,128]{2,1,0:T(8,128)S(1)} %get-tuple-element.70.refs_4_), channel_id=1, source_target_pairs={{0,2},{1,3},{2,0},{3,1},{8,10},{9,11},{10,8},{11,9},{16,18},{17,19... | collective-permute-start | bytes 786440 | tf_op jit(solution)/shard_map/ppermute | solution.py:545
  51.1 5.9 %collective-permute-start.3 = (f32[4,128,128]{2,1,0:T(8,128)S(1)}, f32[4,128,128]{2,1,0:T(8,128)S(1)}, u32[]{:S(2)}, u32[]{:S(2)}) collective-permute-start(f32[4,128,128]{2,1,0:T(8,128)S(1)} %get-tuple-element.71.refs_4_), channel_id=1, source_target_pairs={{2,4},{3,5},{4,2},{5,3},{10,12},{11,13},{12,10},{13,11},{18,20},{1... | collective-permute-start | bytes 786440 | tf_op jit(solution)/shard_map/ppermute | solution.py:545
  60.9 9.2 %collective-permute-start.7 = (f32[4,128,128]{2,1,0:T(8,128)S(1)}, f32[4,128,128]{2,1,0:T(8,128)S(1)}, u32[]{:S(2)}, u32[]{:S(2)}) collective-permute-start(f32[4,128,128]{2,1,0:T(8,128)S(1)} %get-tuple-element.80.refs_4_), channel_id=1, source_target_pairs={{0,1},{1,0},{2,3},{3,2},{4,5},{5,4},{6,7},{7,6},{8,9},{9,8},{10,11... | collective-permute-start | bytes 786440 | tf_op jit(solution)/shard_map/ppermute | solution.py:540
  63.3 9.7 %collective-permute-start.9 = (f32[4,128,128]{2,1,0:T(8,128)S(1)}, f32[4,128,128]{2,1,0:T(8,128)S(1)}, u32[]{:S(2)}, u32[]{:S(2)}) collective-permute-start(f32[4,128,128]{2,1,0:T(8,128)S(1)} %get-tuple-element.83.refs_8_), channel_id=1, source_target_pairs={{0,1},{1,0},{2,3},{3,2},{4,5},{5,4},{6,7},{7,6},{8,9},{9,8},{10,11... | collective-permute-start | bytes 786440 | tf_op jit(solution)/shard_map/ppermute | solution.py:540
  76.0 14.5 %collective-permute-start.11 = (f32[129,8,128]{2,1,0:T(8,128)S(1)}, f32[129,8,128]{2,1,0:T(8,128)S(1)}, u32[]{:S(2)}, u32[]{:S(2)}) collective-permute-start(f32[129,8,128]{2,1,0:T(8,128)S(1)} %get-tuple-element.93), channel_id=1, source_target_pairs={{0,16},{1,17},{2,18},{3,19},{4,20},{5,21},{6,22},{7,23},{8,24},{9,... | collective-permute-start | bytes 1585160 | tf_op jit(solution)/shard_map/ppermute | solution.py:540
  78.6 14.3 %collective-permute-start.14 = (f32[129,8,128]{2,1,0:T(8,128)S(1)}, f32[129,8,128]{2,1,0:T(8,128)S(1)}, u32[]{:S(2)}, u32[]{:S(2)}) collective-permute-start(f32[129,8,128]{2,1,0:T(8,128)S(1)} %get-tuple-element.99), channel_id=1, source_target_pairs={{0,1},{1,0},{2,3},{3,2},{4,5},{5,4},{6,7},{7,6},{8,9},{9,8},{10,11... | collective-permute-start | bytes 1585160 | tf_op jit(solution)/shard_map/ppermute | solution.py:540
  91.1 8.1 %collective-permute-start.13 = (f32[65,8,128]{2,1,0:T(8,128)S(1)}, f32[65,8,128]{2,1,0:T(8,128)S(1)}, u32[]{:S(2)}, u32[]{:S(2)}) collective-permute-start(f32[65,8,128]{2,1,0:T(8,128)S(1)} %get-tuple-element.98), channel_id=1, source_target_pairs={{0,1},{1,0},{2,3},{3,2},{4,5},{5,4},{6,7},{7,6},{8,9},{9,8},{10,11... | collective-permute-start | bytes 798728 | tf_op jit(solution)/shard_map/ppermute | solution.py:540
  93.5 12.4 %collective-permute-start.16 = (f32[65,8,128]{2,1,0:T(8,128)S(1)}, f32[65,8,128]{2,1,0:T(8,128)S(1)}, u32[]{:S(2)}, u32[]{:S(2)}) collective-permute-start(f32[65,8,128]{2,1,0:T(8,128)S(1)} %get-tuple-element.104), channel_id=1, source_target_pairs={{0,16},{1,17},{2,18},{3,19},{4,20},{5,21},{6,22},{7,23},{8,24},{9,... | collective-permute-start | bytes 798728 | tf_op jit(solution)/shard_map/ppermute | solution.py:540
  99.7 10.3 %collective-permute-start.15 = (f32[33,8,128]{2,1,0:T(8,128)S(1)}, f32[33,8,128]{2,1,0:T(8,128)S(1)}, u32[]{:S(2)}, u32[]{:S(2)}) collective-permute-start(f32[33,8,128]{2,1,0:T(8,128)S(1)} %get-tuple-element.103), channel_id=1, source_target_pairs={{0,2},{1,3},{2,0},{3,1},{4,6},{5,7},{6,4},{7,5},{8,10},{9,11},{10,... | collective-permute-start | bytes 405512 | tf_op jit(solution)/shard_map/ppermute | solution.py:540
  106.4 13.0 %collective-permute-start.19 = (f32[33,8,128]{2,1,0:T(8,128)S(1)}, f32[33,8,128]{2,1,0:T(8,128)S(1)}, u32[]{:S(2)}, u32[]{:S(2)}) collective-permute-start(f32[33,8,128]{2,1,0:T(8,128)S(1)} %get-tuple-element.109), channel_id=1, source_target_pairs={{0,2},{1,3},{2,0},{3,1},{4,6},{5,7},{6,4},{7,5},{8,10},{9,11},{10,... | collective-permute-start | bytes 405512 | tf_op jit(solution)/shard_map/ppermute | solution.py:540
  110.6 13.9 %collective-permute-start.17 = (f32[17,8,128]{2,1,0:T(8,128)S(1)}, f32[17,8,128]{2,1,0:T(8,128)S(1)}, u32[]{:S(2)}, u32[]{:S(2)}) collective-permute-start(f32[17,8,128]{2,1,0:T(8,128)S(1)} %get-tuple-element.107), channel_id=1, source_target_pairs={{0,4},{1,5},{2,6},{3,7},{4,0},{5,1},{6,2},{7,3},{8,12},{9,13},{10,... | collective-permute-start | bytes 208904 | tf_op jit(solution)/shard_map/ppermute | solution.py:540
  120.0 5.3 %collective-permute-start.20 = (f32[17,8,128]{2,1,0:T(8,128)S(1)}, f32[17,8,128]{2,1,0:T(8,128)S(1)}, u32[]{:S(2)}, u32[]{:S(2)}) collective-permute-start(f32[17,8,128]{2,1,0:T(8,128)S(1)} %get-tuple-element.111), channel_id=1, source_target_pairs={{0,4},{1,5},{2,6},{3,7},{4,0},{5,1},{6,2},{7,3},{8,12},{9,13},{10,... | collective-permute-start | bytes 208904 | tf_op jit(solution)/shard_map/ppermute | solution.py:540
  124.5 5.3 %collective-permute-start.18 = (f32[16,8,128]{2,1,0:T(8,128)S(1)}, f32[16,8,128]{2,1,0:T(8,128)S(1)}, u32[]{:S(2)}, u32[]{:S(2)}) collective-permute-start(f32[16,8,128]{2,1,0:T(8,128)S(1)} %get-tuple-element.108.refs_1_), channel_id=1, source_target_pairs={{0,4},{1,5},{2,6},{3,7},{4,0},{5,1},{6,2},{7,3},{8,12},{9,13},{10,... | collective-permute-start | bytes 196616 | tf_op jit(solution)/shard_map/ppermute | solution.py:540
  125.3 5.3 %collective-permute-start.22 = (f32[16,8,128]{2,1,0:T(8,128)S(1)}, f32[16,8,128]{2,1,0:T(8,128)S(1)}, u32[]{:S(2)}, u32[]{:S(2)}) collective-permute-start(f32[16,8,128]{2,1,0:T(8,128)S(1)} %get-tuple-element.112.refs_3_.refs_1_), channel_id=1, source_target_pairs={{0,4},{1,5},{2,6},{3,7},{4,0},{5,1},{6,2},{7,3},{8,12},{9,13},{10,... | collective-permute-start | bytes 196616 | tf_op jit(solution)/shard_map/ppermute | solution.py:540
  131.2 5.9 %collective-permute-start.24 = (f32[32,8,128]{2,1,0:T(8,128)S(1)}, f32[32,8,128]{2,1,0:T(8,128)S(1)}, u32[]{:S(2)}, u32[]{:S(2)}) collective-permute-start(f32[32,8,128]{2,1,0:T(8,128)S(1)} %lay.7.refs_3_.refs_1_), channel_id=1, source_target_pairs={{0,2},{1,3},{2,0},{3,1},{4,6},{5,7},{6,4},{7,5},{8,10},{9,11},{10,... | collective-permute-start | bytes 393224 | tf_op jit(solution)/shard_map/ppermute | solution.py:540
  136.0 7.4 %collective-permute-start.23 = (f32[64,8,128]{2,1,0:T(8,128)S(1)}, f32[64,8,128]{2,1,0:T(8,128)S(1)}, u32[]{:S(2)}, u32[]{:S(2)}) collective-permute-start(f32[64,8,128]{2,1,0:T(8,128)S(1)} %lay.8.refs_3_.refs_1_), channel_id=1, source_target_pairs={{0,1},{1,0},{2,3},{3,2},{4,5},{5,4},{6,7},{7,6},{8,9},{9,8},{10,11... | collective-permute-start | bytes 786440 | tf_op jit(solution)/shard_map/ppermute | solution.py:540
  137.7 8.3 %collective-permute-start.28 = (f32[64,8,128]{2,1,0:T(8,128)S(1)}, f32[64,8,128]{2,1,0:T(8,128)S(1)}, u32[]{:S(2)}, u32[]{:S(2)}) collective-permute-start(f32[64,8,128]{2,1,0:T(8,128)S(1)} %lay.9.refs_3_.refs_1_), channel_id=1, source_target_pairs={{0,16},{1,17},{2,18},{3,19},{4,20},{5,21},{6,22},{7,23},{8,24},{9,... | collective-permute-start | bytes 786440 | tf_op jit(solution)/shard_map/ppermute | solution.py:540
  146.6 9.2 %collective-permute-start.29 = (f32[128,8,128]{2,1,0:T(8,128)S(1)}, f32[128,8,128]{2,1,0:T(8,128)S(1)}, u32[]{:S(2)}, u32[]{:S(2)}) collective-permute-start(f32[128,8,128]{2,1,0:T(8,128)S(1)} %lay.11.refs_4_), channel_id=1, source_target_pairs={{0,1},{1,0},{2,3},{3,2},{4,5},{5,4},{6,7},{7,6},{8,9},{9,8},{10,11... | collective-permute-start | bytes 1572872 | tf_op jit(solution)/shard_map/ppermute | solution.py:540
  147.8 9.2 %collective-permute-start.25 = (f32[128,8,128]{2,1,0:T(8,128)S(1)}, f32[128,8,128]{2,1,0:T(8,128)S(1)}, u32[]{:S(2)}, u32[]{:S(2)}) collective-permute-start(f32[128,8,128]{2,1,0:T(8,128)S(1)} %lay.10.refs_3_.refs_0_), channel_id=1, source_target_pairs={{0,16},{1,17},{2,18},{3,19},{4,20},{5,21},{6,22},{7,23},{8,24},{9,... | collective-permute-start | bytes 1572872 | tf_op jit(solution)/shard_map/ppermute | solution.py:540
  149.6 7.4 %collective-permute-start.30 = (f32[128,8,128]{2,1,0:T(8,128)S(1)}, f32[128,8,128]{2,1,0:T(8,128)S(1)}, u32[]{:S(2)}, u32[]{:S(2)}) collective-permute-start(f32[128,8,128]{2,1,0:T(8,128)S(1)} %lay.11.refs_4_), channel_id=1, source_target_pairs={{0,8},{1,9},{2,10},{3,11},{4,12},{5,13},{6,14},{7,15},{8,0},{9,1},... | collective-permute-start | bytes 1572872 | tf_op jit(solution)/shard_map/ppermute | solution.py:540
  149.6 7.4 %collective-permute-start.26 = (f32[128,8,128]{2,1,0:T(8,128)S(1)}, f32[128,8,128]{2,1,0:T(8,128)S(1)}, u32[]{:S(2)}, u32[]{:S(2)}) collective-permute-start(f32[128,8,128]{2,1,0:T(8,128)S(1)} %lay.10.refs_3_.refs_0_), channel_id=1, source_target_pairs={{0,8},{1,9},{2,10},{3,11},{4,12},{5,13},{6,14},{7,15},{8,0},{9,1},... | collective-permute-start | bytes 1572872 | tf_op jit(solution)/shard_map/ppermute | solution.py:540
  (14 other events, 58.5 us)

commit v9 on v8

--- a/solution.py
+++ b/solution.py
@@ -13,6 +13,8 @@
 CORES = 2
 PAIR = 2
 PER_STEP = 2
+DELAYS = (0, 1)
+LIGHT = False
 F32 = jnp.float32
 BF16 = jnp.bfloat16
 MIB = 1024 * 1024
@@ -63,6 +65,10 @@
 
 def skipping(kernel, first, after):
     return lambda *refs: kernel(*refs[:first], *refs[first + len(after) :])
+
+
+def light(flops, size):
+    return cost(1, 1) if LIGHT else cost(flops, size)
 
 
 def cost(flops, size):
@@ -259,7 +265,7 @@
         out_shape=(shape, shape, push),
         in_specs=[smem(), vmem(), vmem()] + anywhere(after),
         compiler_params=params(12),
-        cost_estimate=cost(own.shape[0] * 6 * 128 * 128 * 256, own.size * 16),
+        cost_estimate=light(own.shape[0] * 6 * 128 * 128 * 256, own.size * 16),
         name="combine",
     )(info, own, got, *after)
 
@@ -281,7 +287,7 @@
         out_shape=(shape, shape),
         in_specs=[smem(), vmem(), vmem(), vmem()] + anywhere(after),
         compiler_params=params(12),
-        cost_estimate=cost(maps.shape[0] * 6 * 128 * 128 * 128, maps.size * 8),
+        cost_estimate=light(maps.shape[0] * 6 * 128 * 128 * 128, maps.size * 8),
         name="hop",
     )(info, maps, got, state, *after)
 
@@ -305,7 +311,7 @@
         out_shape=(shape, shape),
         in_specs=[smem(), vmem(), vmem(), vmem()] + anywhere(after),
         compiler_params=params(12),
-        cost_estimate=cost(maps.shape[0] * 6 * 128 * 128 * 128, maps.size * 8),
+        cost_estimate=light(maps.shape[0] * 6 * 128 * 128 * 128, maps.size * 8),
         name="split",
     )(info, maps, got, state, *after)
 
@@ -433,7 +439,7 @@
         out_shape=[shape] * len(flips),
         in_specs=[smem()] + [vmem()] * len(arrays) + anywhere(after),
         compiler_params=params(12),
-        cost_estimate=cost(size * 1024 * len(arrays), size * 4096 * (len(arrays) + 1)),
+        cost_estimate=light(size * 1024 * len(arrays), size * 4096 * (len(arrays) + 1)),
         name="fold",
     )(info, *arrays, *after)
 
@@ -453,7 +459,7 @@
         in_specs=[vmem()] * len(arrays),
         out_specs=(vmem(), vmem()),
         compiler_params=params(12),
-        cost_estimate=cost(size * 4096, size * 4096 * 5),
+        cost_estimate=light(size * 4096, size * 4096 * 5),
         name="total",
     )(*arrays)
 
@@ -471,7 +477,7 @@
         out_shape=jax.ShapeDtypeStruct((share * 2, 8, 128), F32),
         in_specs=[smem(), vmem(), vmem()] + anywhere(after),
         compiler_params=params(12),
-        cost_estimate=cost(0, share * 16384),
+        cost_estimate=light(0, share * 16384),
         name="lay",
     )(info, own, got, *after)
 
@@ -572,50 +578,55 @@
             extra = out.pop()
         locals_.append(out)
     back = back_call(cot, out_weight)
-    maps = []
-    for g in relays:
-        after = [locals_[last][0]] if g == 0 else [maps[-1][2]]
-        if g == last:
-            after.append(back)
-        maps.append(combine_call(info, locals_[g][0], moved(locals_[g][1], (0, 0, 0, 1)), after))
+    maps = [None] * len(RELAYS)
     states = [jnp.zeros((size, dims, dims), F32) for size in RELAYS]
-    sends = [m[2] for m in maps]
-    for level in range(1, n_z):
-        gots = [lifted(send, level - 1) for send in sends]
-        after = [sends[last]]
-        if level == n_z - 1:
-            break
-        for g in relays:
-            states[g], sends[g] = hop_call(level, info, maps[g][1], gots[g], states[g], after)
-            after = [sends[g]]
-    mixed, kept, got, ready = [], [], [], []
-    for g in relays:
-        keep, send = split_call(n_z - 1, info, maps[g][0], gots[g], states[g], after)
-        after = [send]
-        ready.append((keep, moved(send, (0, 0, 0, 1))))
-    for g in relays:
-        states_g = *locals_[g][2:], *ready[g]
-        flat, w_send, w_keep = mix_call(info, first_of[g], *states_g, back, gain, cot, span, after)
-        after = [w_keep]
-        mixed.append(flat)
-        kept.append(w_keep)
-        got.append(moved(w_send, (0, 1, 0, 0)))
+    sends = [None] * len(RELAYS)
+    ready = [None] * len(RELAYS)
+    turns = sorted((stage + DELAYS[g], g, stage) for g in relays for stage in range(n_z))
+    after = [locals_[last][0]]
+    for _, g, stage in turns:
+        if stage == 0:
+            if g == last:
+                after.append(back)
+            maps[g] = combine_call(info, locals_[g][0], moved(locals_[g][1], (0, 0, 0, 1)), after)
+            sends[g] = maps[g][2]
+        else:
+            came = lifted(sends[g], stage - 1)
+            if stage < n_z - 1:
+                states[g], sends[g] = hop_call(stage, info, maps[g][1], came, states[g], after)
+            else:
+                keep, sends[g] = split_call(stage, info, maps[g][0], came, states[g], after)
+                ready[g] = (keep, moved(sends[g], (0, 0, 0, 1)))
+        after = [sends[g]]
+    sums = range(len(SUMS))
+    orders = [(on_x + on_y if g % 2 == 0 else on_y + on_x) + on_z for g in sums]
+    mixed, arrays, parts = [], [], []
+    for group in SUMS:
+        terms = []
+        for g in group:
+            states_g = *locals_[g][2:], *ready[g]
+            flat, w_send, w_keep = mix_call(info, first_of[g], *states_g, back, gain, cot, span, after)
+            after = [w_keep]
+            mixed.append(flat)
+            terms += [w_keep, moved(w_send, (0, 1, 0, 0))]
+        arrays.append(terms)
+    for g in sums:
+        shift, where = orders[g][0]
+        own, send = fold_call(info, where, (0, 1), arrays[g], len(SUMS[g]), after)
+        after = [own]
+        arrays[g] = [own, moved(send, shift)]
     output, done = finish_call(mixed, out_weight)
     scale = 1.0 / math.sqrt(count * n_shot * n_tm)
 
-    sums = range(len(SUMS))
-    orders = [(on_x + on_y if g % 2 == 0 else on_y + on_x) + on_z for g in sums]
-    arrays = [[a for r in SUMS[g] for a in (kept[r], got[r])] for g in sums]
-    parts = [len(SUMS[g]) for g in sums]
-    previous = None
-    for step in range(len(orders[0])):
+    previous = after[0]
+    for step in range(1, len(orders[0])):
         for g in sums:
             shift, where = orders[g][step]
-            after = [previous] if g or step else []
+            after = [previous]
             if g == sums[-1] and step == 1:
                 after.append(done)
-            own, send = fold_call(info, where, (0, 1), arrays[g], parts[g], after)
-            arrays[g], parts[g] = [own, moved(send, shift)], 1
+            own, send = fold_call(info, where, (0, 1), arrays[g], 1, after)
+            arrays[g] = [own, moved(send, shift)]
             previous = own
     totals = [total_call(a) for a in arrays]
     pieces = [t[0] for t in totals]

time: 162 us -> 159 us (0.981)
  waiting for transfers between devices: 54 us -> 49.1 us
  starting transfers between devices: 49.4 us -> 51.5 us
    ppermute x26, waiting for transfers between devices: 50.3 us -> 44 us  [moved(): return lax.ppermute(array, both, route)]
where the time goes in v9:
time: 159 us; the launch traced here: 158 us
  Pallas kernels  51.6 us (32%)
  starting transfers between devices  51.5 us (32%)
  waiting for transfers between devices  49.1 us (31%)
  local copies, waits for them, and re-layouts  3.69 us (2%)
    ppermute x26, waiting for transfers between devices, moved(): return lax.ppermute(array, both, route)  44 us
    ppermute x26, starting transfers between devices, moved(): return lax.ppermute(array, both, route)  40.6 us
    pallas_call x2, Pallas kernels, local_call(): pl.pallas_call(skipping(functools.partial(local_kernel, first_head, heads...  23.5 us
    ppermute x6, starting transfers between devices, lifted(): return lax.ppermute(array, 'tm', route)  10.8 us
    ppermute x6, waiting for transfers between devices, lifted(): return lax.ppermute(array, 'tm', route)  5.14 us
    pallas_call x8, Pallas kernels, fold_call(): pl.pallas_call(skipping(functools.partial(fold_kernel, parts, terms, wher...  4.79 us
    pallas_call x2, Pallas kernels, mix_call(): pl.pallas_call(skipping(functools.partial(mix_kernel, span, first_head),...  4.44 us
    unnamed x12, local copies, waits for them, and re-layouts  3.59 us
  transfers between devices with their start and end apart: 32, of which 20 were waited for; matrix products, arithmetic and copies ran while one was open for 0% of the time, Pallas kernels for 22%

profile of v9, /device:TPU:0, one launch (start us, length us, event | category | flops | bytes accessed | tf_op | source)
XLA Modules:
  0.0 158.3 jit_solution(12510947998580797248)
XLA Ops:
  5.8 12.8 %local.2 = (f32[4,128,256]{2,1,0:T(8,128)S(1)}, f32[4,128,256]{2,1,0:T(8,128)S(1)}, f32[512,512]{1,0:T(8,128)S(1)}, f32[512,512]{1,0:T(8,128)S(1)}, f32[512,16]{1,0:T(8,128)S(1)}) custom-call(s32[7]{0:T(128)S(1)} %stack.49.refs_0_.info, s32[2,4,24]{2,1,0:T(4,128)S(1)} %pad_add_fusion.refs_1_, bf16[512,1024]{1,0:T(8,128)(2,1)S(1)} %bitcast.26, ...), custom_call_target="tpu_custom_call" | custom-call | flops 6442450944 | bytes 8388608 | tf_op jit(solution)/shard_map/local/pallas_call | solution.py:225
  18.6 3.0 %collective-permute-start = (f32[4,128,256]{2,1,0:T(8,128)S(1)}, f32[4,128,256]{2,1,0:T(8,128)S(1)}, u32[]{:S(2)}, u32[]{:S(2)}) collective-permute-start(f32[4,128,256]{2,1,0:T(8,128)S(1)} %get-tuple-element.63), channel_id=1, source_target_pairs={{0,1},{1,0},{2,3},{3,2},{4,5},{5,4},{6,7},{7,6},{8,9},{9,8},{10,11... | collective-permute-start | bytes 1572872 | tf_op jit(solution)/shard_map/ppermute | solution.py:546
  21.6 10.7 %local.3 = (f32[4,128,256]{2,1,0:T(8,128)S(1)}, f32[4,128,256]{2,1,0:T(8,128)S(1)}, f32[512,512]{1,0:T(8,128)S(1)}, f32[512,512]{1,0:T(8,128)S(1)}) custom-call(s32[7]{0:T(128)S(1)} %stack.49.refs_0_.info, s32[2,4,24]{2,1,0:T(4,128)S(1)} %pad_add_fusion.refs_1_, bf16[512,1024]{1,0:T(8,128)(2,1)S(1)} %bitcast.27, bf16[64,128,128]{2,1,0:T(8,128)(2,1)S(1)} %copy-done.3, ...), custom_call_target="tpu_custom_call" | custom-call | flops 6442450944 | bytes 8388608 | tf_op jit(solution)/shard_map/local/pallas_call | solution.py:225
  34.5 3.9 %collective-permute-start.1 = (f32[4,128,128]{2,1,0:T(8,128)S(1)}, f32[4,128,128]{2,1,0:T(8,128)S(1)}, u32[]{:S(2)}, u32[]{:S(2)}) collective-permute-start(f32[4,128,128]{2,1,0:T(8,128)S(1)} %get-tuple-element.68.refs_4_), channel_id=1, source_target_pairs={{0,2},{1,3},{2,0},{3,1},{8,10},{9,11},{10,8},{11,9},{16,18},{17,19... | collective-permute-start | bytes 786440 | tf_op jit(solution)/shard_map/ppermute | solution.py:551
  38.4 3.3 %back.1.refs_4_.refs_5_ = f32[512,1024]{1,0:T(8,128)S(1)} custom-call(bf16[512,1024]{1,0:T(8,128)(2,1)S(1)} %bitcast.21, bf16[1024,1024]{1,0:T(8,128)(2,1)S(1)} %copy-done.1), custom_call_target="tpu_custom_call" | custom-call | flops 1073741824 | bytes 5242880 | tf_op jit(solution)/shard_map/back/pallas_call | solution.py:378
  46.8 4.2 %collective-permute-start.5 = (f32[4,128,128]{2,1,0:T(8,128)S(1)}, f32[4,128,128]{2,1,0:T(8,128)S(1)}, u32[]{:S(2)}, u32[]{:S(2)}) collective-permute-start(f32[4,128,128]{2,1,0:T(8,128)S(1)} %get-tuple-element.72.refs_4_), channel_id=1, source_target_pairs={{0,2},{1,3},{2,0},{3,1},{8,10},{9,11},{10,8},{11,9},{16,18},{17,19... | collective-permute-start | bytes 786440 | tf_op jit(solution)/shard_map/ppermute | solution.py:551
  52.6 3.0 %collective-permute-done.5.refs_2_ = f32[4,128,128]{2,1,0:T(8,128)S(1)} collective-permute-done((f32[4,128,128]{2,1,0:T(8,128)S(1)}, f32[4,128,128]{2,1,0:T(8,128)S(1)}, u32[]{:S(2)}, u32[]{:S(2)}) %collective-permute-start.5) | collective-permute-done | bytes 262176 | tf_op jit(solution)/shard_map/ppermute | solution.py:551
  62.4 5.5 %collective-permute-done.6.refs_4_ = f32[4,128,128]{2,1,0:T(8,128)S(1)} collective-permute-done((f32[4,128,128]{2,1,0:T(8,128)S(1)}, f32[4,128,128]{2,1,0:T(8,128)S(1)}, u32[]{:S(2)}, u32[]{:S(2)}) %collective-permute-start.6) | collective-permute-done | bytes 262176 | tf_op jit(solution)/shard_map/ppermute | solution.py:546
  67.9 2.2 %mix.2 = (bf16[512,512]{1,0:T(8,128)(2,1)S(1)}, f32[257,8,128]{2,1,0:T(8,128)S(1)}, f32[257,8,128]{2,1,0:T(8,128)S(1)}) custom-call(s32[7]{0:T(128)S(1)} %stack.49.refs_0_.info, f32[512,512]{1,0:T(8,128)S(1)} %get-tuple-element.60.refs_1_, f32[512,512]{1,0:T(8,128)S(1)} %get-tuple-element.61.refs_2_, f32[4,128,128]{2,1,0:T(8,128)S(1)} %get-tuple-element.77.refs_3_, ...), custom_call_target="tpu_custom_call" | custom-call | flops 536870912 | bytes 3145728 | tf_op jit(solution)/shard_map/mix/pallas_call | solution.py:360
  70.7 2.2 %mix.3 = (bf16[512,512]{1,0:T(8,128)(2,1)S(1)}, f32[257,8,128]{2,1,0:T(8,128)S(1)}, f32[257,8,128]{2,1,0:T(8,128)S(1)}) custom-call(s32[7]{0:T(128)S(1)} %stack.49.refs_0_.info, f32[512,512]{1,0:T(8,128)S(1)} %get-tuple-element.85.refs_1_, f32[512,512]{1,0:T(8,128)S(1)} %get-tuple-element.86.refs_2_, f32[4,128,128]{2,1,0:T(8,128)S(1)} %get-tuple-element.87.refs_3_, ...), custom_call_target="tpu_custom_call" | custom-call | flops 536870912 | bytes 3145728 | tf_op jit(solution)/shard_map/mix/pallas_call | solution.py:360
  77.4 2.8 %finish.1 = (bf16[512,1024]{1,0:T(8,128)(2,1)}, f32[8,128]{1,0:T(8,128)S(1)}) custom-call(bf16[512,512]{1,0:T(8,128)(2,1)S(1)} %get-tuple-element.84.refs_0_, bf16[512,512]{1,0:T(8,128)(2,1)S(1)} %get-tuple-element.89.refs_1_, bf16[1024,1024]{1,0:T(8,128)(2,1)S(1)} %copy-done.1), custom_call_target="tpu_custom_call" | custom-call | flops 1073741824 | bytes 4194304 | tf_op jit(solution)/shard_map/finish/pallas_call | solution.py:401
  80.3 7.9 %collective-permute-done.11.refs_2_ = f32[129,8,128]{2,1,0:T(8,128)S(1)} collective-permute-done((f32[129,8,128]{2,1,0:T(8,128)S(1)}, f32[129,8,128]{2,1,0:T(8,128)S(1)}, u32[]{:S(2)}, u32[]{:S(2)}) %collective-permute-start.11) | collective-permute-done | bytes 528416 | tf_op jit(solution)/shard_map/ppermute | solution.py:546
  92.7 4.2 %collective-permute-done.13.refs_2_ = f32[65,8,128]{2,1,0:T(8,128)S(1)} collective-permute-done((f32[65,8,128]{2,1,0:T(8,128)S(1)}, f32[65,8,128]{2,1,0:T(8,128)S(1)}, u32[]{:S(2)}, u32[]{:S(2)}) %collective-permute-start.13) | collective-permute-done | bytes 266272 | tf_op jit(solution)/shard_map/ppermute | solution.py:546
  97.4 7.3 %collective-permute-start.15 = (f32[33,8,128]{2,1,0:T(8,128)S(1)}, f32[33,8,128]{2,1,0:T(8,128)S(1)}, u32[]{:S(2)}, u32[]{:S(2)}) collective-permute-start(f32[33,8,128]{2,1,0:T(8,128)S(1)} %get-tuple-element.103), channel_id=1, source_target_pairs={{0,2},{1,3},{2,0},{3,1},{4,6},{5,7},{6,4},{7,5},{8,10},{9,11},{10,... | collective-permute-start | bytes 405512 | tf_op jit(solution)/shard_map/ppermute | solution.py:546
  106.6 2.3 %collective-permute-done.15.refs_2_ = f32[33,8,128]{2,1,0:T(8,128)S(1)} collective-permute-done((f32[33,8,128]{2,1,0:T(8,128)S(1)}, f32[33,8,128]{2,1,0:T(8,128)S(1)}, u32[]{:S(2)}, u32[]{:S(2)}) %collective-permute-start.15) | collective-permute-done | bytes 135200 | tf_op jit(solution)/shard_map/ppermute | solution.py:546
  109.5 6.7 %collective-permute-start.17 = (f32[17,8,128]{2,1,0:T(8,128)S(1)}, f32[17,8,128]{2,1,0:T(8,128)S(1)}, u32[]{:S(2)}, u32[]{:S(2)}) collective-permute-start(f32[17,8,128]{2,1,0:T(8,128)S(1)} %get-tuple-element.107), channel_id=1, source_target_pairs={{0,4},{1,5},{2,6},{3,7},{4,0},{5,1},{6,2},{7,3},{8,12},{9,13},{10,... | collective-permute-start | bytes 208904 | tf_op jit(solution)/shard_map/ppermute | solution.py:546
  117.8 2.8 %collective-permute-done.17.refs_1_ = f32[17,8,128]{2,1,0:T(8,128)S(1)} collective-permute-done((f32[17,8,128]{2,1,0:T(8,128)S(1)}, f32[17,8,128]{2,1,0:T(8,128)S(1)}, u32[]{:S(2)}, u32[]{:S(2)}) %collective-permute-start.17) | collective-permute-done | bytes 69664 | tf_op jit(solution)/shard_map/ppermute | solution.py:546
  123.6 2.3 %collective-permute-done.18.refs_2_ = f32[16,8,128]{2,1,0:T(8,128)S(1)} collective-permute-done((f32[16,8,128]{2,1,0:T(8,128)S(1)}, f32[16,8,128]{2,1,0:T(8,128)S(1)}, u32[]{:S(2)}, u32[]{:S(2)}) %collective-permute-start.18) | collective-permute-done | bytes 65568 | tf_op jit(solution)/shard_map/ppermute | solution.py:546
  128.9 3.0 %collective-permute-start.24 = (f32[32,8,128]{2,1,0:T(8,128)S(1)}, f32[32,8,128]{2,1,0:T(8,128)S(1)}, u32[]{:S(2)}, u32[]{:S(2)}) collective-permute-start(f32[32,8,128]{2,1,0:T(8,128)S(1)} %lay.7.refs_3_.refs_1_), channel_id=1, source_target_pairs={{0,2},{1,3},{2,0},{3,1},{4,6},{5,7},{6,4},{7,5},{8,10},{9,11},{10,... | collective-permute-start | bytes 393224 | tf_op jit(solution)/shard_map/ppermute | solution.py:546
  137.0 2.7 %collective-permute-done.23.refs_2_ = f32[64,8,128]{2,1,0:T(8,128)S(1)} collective-permute-done((f32[64,8,128]{2,1,0:T(8,128)S(1)}, f32[64,8,128]{2,1,0:T(8,128)S(1)}, u32[]{:S(2)}, u32[]{:S(2)}) %collective-permute-start.23) | collective-permute-done | bytes 262176 | tf_op jit(solution)/shard_map/ppermute | solution.py:546
  141.8 2.4 %collective-permute-done.28.refs_2_ = f32[64,8,128]{2,1,0:T(8,128)S(1)} collective-permute-done((f32[64,8,128]{2,1,0:T(8,128)S(1)}, f32[64,8,128]{2,1,0:T(8,128)S(1)}, u32[]{:S(2)}, u32[]{:S(2)}) %collective-permute-start.28) | collective-permute-done | bytes 262176 | tf_op jit(solution)/shard_map/ppermute | solution.py:546
  146.7 3.1 %collective-permute-done.25.refs_1_ = f32[128,8,128]{2,1,0:T(8,128)S(1)} collective-permute-done((f32[128,8,128]{2,1,0:T(8,128)S(1)}, f32[128,8,128]{2,1,0:T(8,128)S(1)}, u32[]{:S(2)}, u32[]{:S(2)}) %collective-permute-start.25) | collective-permute-done | bytes 524320 | tf_op jit(solution)/shard_map/ppermute | solution.py:546
  149.8 4.2 %collective-permute-done.29.refs_5_ = f32[128,8,128]{2,1,0:T(8,128)S(1)} collective-permute-done((f32[128,8,128]{2,1,0:T(8,128)S(1)}, f32[128,8,128]{2,1,0:T(8,128)S(1)}, u32[]{:S(2)}, u32[]{:S(2)}) %collective-permute-start.29) | collective-permute-done | bytes 524320 | tf_op jit(solution)/shard_map/ppermute | solution.py:546
  155.9 2.4 %join.1 = (bf16[1024,1024]{1,0:T(8,128)(2,1)}, f32[1,128]{1,0:T(1,128)}) custom-call(s32[7]{0:T(128)S(1)} %stack.49.refs_0_.info, f32[128,8,128]{2,1,0:T(8,128)S(1)} %lay.10.refs_3_.refs_0_, f32[128,8,128]{2,1,0:T(8,128)S(1)} %collective-permute-done.25.refs_1_, f32[128,8,128]{2,1,0:T(8,128)S(1)} %collective-permute-done.26.refs_2_, ...), custom_call_target="tpu_custom_call" | custom-call | tf_op jit(solution)/shard_map/join/pallas_call | solution.py:514
  (87 shorter events, 52.2 us)
Async XLA Ops:
  18.6 15.0 %collective-permute-start = (f32[4,128,256]{2,1,0:T(8,128)S(1)}, f32[4,128,256]{2,1,0:T(8,128)S(1)}, u32[]{:S(2)}, u32[]{:S(2)}) collective-permute-start(f32[4,128,256]{2,1,0:T(8,128)S(1)} %get-tuple-element.63), channel_id=1, source_target_pairs={{0,1},{1,0},{2,3},{3,2},{4,5},{5,4},{6,7},{7,6},{8,9},{9,8},{10,11... | collective-permute-start | bytes 1572872 | tf_op jit(solution)/shard_map/ppermute | solution.py:546
  32.4 13.5 %collective-permute-start.3 = (f32[4,128,256]{2,1,0:T(8,128)S(1)}, f32[4,128,256]{2,1,0:T(8,128)S(1)}, u32[]{:S(2)}, u32[]{:S(2)}) collective-permute-start(f32[4,128,256]{2,1,0:T(8,128)S(1)} %get-tuple-element.71), channel_id=1, source_target_pairs={{0,1},{1,0},{2,3},{3,2},{4,5},{5,4},{6,7},{7,6},{8,9},{9,8},{10,11... | collective-permute-start | bytes 1572872 | tf_op jit(solution)/shard_map/ppermute | solution.py:546
  34.5 9.4 %collective-permute-start.1 = (f32[4,128,128]{2,1,0:T(8,128)S(1)}, f32[4,128,128]{2,1,0:T(8,128)S(1)}, u32[]{:S(2)}, u32[]{:S(2)}) collective-permute-start(f32[4,128,128]{2,1,0:T(8,128)S(1)} %get-tuple-element.68.refs_4_), channel_id=1, source_target_pairs={{0,2},{1,3},{2,0},{3,1},{8,10},{9,11},{10,8},{11,9},{16,18},{17,19... | collective-permute-start | bytes 786440 | tf_op jit(solution)/shard_map/ppermute | solution.py:551
  44.7 6.3 %collective-permute-start.2 = (f32[4,128,128]{2,1,0:T(8,128)S(1)}, f32[4,128,128]{2,1,0:T(8,128)S(1)}, u32[]{:S(2)}, u32[]{:S(2)}) collective-permute-start(f32[4,128,128]{2,1,0:T(8,128)S(1)} %get-tuple-element.69.refs_3_), channel_id=1, source_target_pairs={{2,4},{3,5},{4,2},{5,3},{10,12},{11,13},{12,10},{13,11},{18,20},{1... | collective-permute-start | bytes 786440 | tf_op jit(solution)/shard_map/ppermute | solution.py:551
  46.8 8.7 %collective-permute-start.5 = (f32[4,128,128]{2,1,0:T(8,128)S(1)}, f32[4,128,128]{2,1,0:T(8,128)S(1)}, u32[]{:S(2)}, u32[]{:S(2)}) collective-permute-start(f32[4,128,128]{2,1,0:T(8,128)S(1)} %get-tuple-element.72.refs_4_), channel_id=1, source_target_pairs={{0,2},{1,3},{2,0},{3,1},{8,10},{9,11},{10,8},{11,9},{16,18},{17,19... | collective-permute-start | bytes 786440 | tf_op jit(solution)/shard_map/ppermute | solution.py:551
  59.4 8.5 %collective-permute-start.6 = (f32[4,128,128]{2,1,0:T(8,128)S(1)}, f32[4,128,128]{2,1,0:T(8,128)S(1)}, u32[]{:S(2)}, u32[]{:S(2)}) collective-permute-start(f32[4,128,128]{2,1,0:T(8,128)S(1)} %get-tuple-element.78.refs_4_), channel_id=1, source_target_pairs={{0,1},{1,0},{2,3},{3,2},{4,5},{5,4},{6,7},{7,6},{8,9},{9,8},{10,11... | collective-permute-start | bytes 786440 | tf_op jit(solution)/shard_map/ppermute | solution.py:546
  61.7 9.0 %collective-permute-start.9 = (f32[4,128,128]{2,1,0:T(8,128)S(1)}, f32[4,128,128]{2,1,0:T(8,128)S(1)}, u32[]{:S(2)}, u32[]{:S(2)}) collective-permute-start(f32[4,128,128]{2,1,0:T(8,128)S(1)} %get-tuple-element.83.refs_8_), channel_id=1, source_target_pairs={{0,1},{1,0},{2,3},{3,2},{4,5},{5,4},{6,7},{7,6},{8,9},{9,8},{10,11... | collective-permute-start | bytes 786440 | tf_op jit(solution)/shard_map/ppermute | solution.py:546
  73.7 14.5 %collective-permute-start.11 = (f32[129,8,128]{2,1,0:T(8,128)S(1)}, f32[129,8,128]{2,1,0:T(8,128)S(1)}, u32[]{:S(2)}, u32[]{:S(2)}) collective-permute-start(f32[129,8,128]{2,1,0:T(8,128)S(1)} %get-tuple-element.94), channel_id=1, source_target_pairs={{0,16},{1,17},{2,18},{3,19},{4,20},{5,21},{6,22},{7,23},{8,24},{9,... | collective-permute-start | bytes 1585160 | tf_op jit(solution)/shard_map/ppermute | solution.py:546
  76.3 14.1 %collective-permute-start.14 = (f32[129,8,128]{2,1,0:T(8,128)S(1)}, f32[129,8,128]{2,1,0:T(8,128)S(1)}, u32[]{:S(2)}, u32[]{:S(2)}) collective-permute-start(f32[129,8,128]{2,1,0:T(8,128)S(1)} %get-tuple-element.99), channel_id=1, source_target_pairs={{0,1},{1,0},{2,3},{3,2},{4,5},{5,4},{6,7},{7,6},{8,9},{9,8},{10,11... | collective-permute-start | bytes 1585160 | tf_op jit(solution)/shard_map/ppermute | solution.py:546
  88.8 8.1 %collective-permute-start.13 = (f32[65,8,128]{2,1,0:T(8,128)S(1)}, f32[65,8,128]{2,1,0:T(8,128)S(1)}, u32[]{:S(2)}, u32[]{:S(2)}) collective-permute-start(f32[65,8,128]{2,1,0:T(8,128)S(1)} %get-tuple-element.98), channel_id=1, source_target_pairs={{0,1},{1,0},{2,3},{3,2},{4,5},{5,4},{6,7},{7,6},{8,9},{9,8},{10,11... | collective-permute-start | bytes 798728 | tf_op jit(solution)/shard_map/ppermute | solution.py:546
  91.1 13.6 %collective-permute-start.16 = (f32[65,8,128]{2,1,0:T(8,128)S(1)}, f32[65,8,128]{2,1,0:T(8,128)S(1)}, u32[]{:S(2)}, u32[]{:S(2)}) collective-permute-start(f32[65,8,128]{2,1,0:T(8,128)S(1)} %get-tuple-element.104), channel_id=1, source_target_pairs={{0,16},{1,17},{2,18},{3,19},{4,20},{5,21},{6,22},{7,23},{8,24},{9,... | collective-permute-start | bytes 798728 | tf_op jit(solution)/shard_map/ppermute | solution.py:546
  97.4 11.4 %collective-permute-start.15 = (f32[33,8,128]{2,1,0:T(8,128)S(1)}, f32[33,8,128]{2,1,0:T(8,128)S(1)}, u32[]{:S(2)}, u32[]{:S(2)}) collective-permute-start(f32[33,8,128]{2,1,0:T(8,128)S(1)} %get-tuple-element.103), channel_id=1, source_target_pairs={{0,2},{1,3},{2,0},{3,1},{4,6},{5,7},{6,4},{7,5},{8,10},{9,11},{10,... | collective-permute-start | bytes 405512 | tf_op jit(solution)/shard_map/ppermute | solution.py:546
  105.3 10.9 %collective-permute-start.19 = (f32[33,8,128]{2,1,0:T(8,128)S(1)}, f32[33,8,128]{2,1,0:T(8,128)S(1)}, u32[]{:S(2)}, u32[]{:S(2)}) collective-permute-start(f32[33,8,128]{2,1,0:T(8,128)S(1)} %get-tuple-element.109), channel_id=1, source_target_pairs={{0,2},{1,3},{2,0},{3,1},{4,6},{5,7},{6,4},{7,5},{8,10},{9,11},{10,... | collective-permute-start | bytes 405512 | tf_op jit(solution)/shard_map/ppermute | solution.py:546
  109.5 11.1 %collective-permute-start.17 = (f32[17,8,128]{2,1,0:T(8,128)S(1)}, f32[17,8,128]{2,1,0:T(8,128)S(1)}, u32[]{:S(2)}, u32[]{:S(2)}) collective-permute-start(f32[17,8,128]{2,1,0:T(8,128)S(1)} %get-tuple-element.107), channel_id=1, source_target_pairs={{0,4},{1,5},{2,6},{3,7},{4,0},{5,1},{6,2},{7,3},{8,12},{9,13},{10,... | collective-permute-start | bytes 208904 | tf_op jit(solution)/shard_map/ppermute | solution.py:546
  116.7 5.9 %collective-permute-start.20 = (f32[17,8,128]{2,1,0:T(8,128)S(1)}, f32[17,8,128]{2,1,0:T(8,128)S(1)}, u32[]{:S(2)}, u32[]{:S(2)}) collective-permute-start(f32[17,8,128]{2,1,0:T(8,128)S(1)} %get-tuple-element.111), channel_id=1, source_target_pairs={{0,4},{1,5},{2,6},{3,7},{4,0},{5,1},{6,2},{7,3},{8,12},{9,13},{10,... | collective-permute-start | bytes 208904 | tf_op jit(solution)/shard_map/ppermute | solution.py:546
  122.6 5.8 %collective-permute-start.22 = (f32[16,8,128]{2,1,0:T(8,128)S(1)}, f32[16,8,128]{2,1,0:T(8,128)S(1)}, u32[]{:S(2)}, u32[]{:S(2)}) collective-permute-start(f32[16,8,128]{2,1,0:T(8,128)S(1)} %get-tuple-element.112.refs_3_.refs_1_), channel_id=1, source_target_pairs={{0,4},{1,5},{2,6},{3,7},{4,0},{5,1},{6,2},{7,3},{8,12},{9,13},{10,... | collective-permute-start | bytes 196616 | tf_op jit(solution)/shard_map/ppermute | solution.py:546
  126.5 5.5 %collective-permute-start.21 = (f32[32,8,128]{2,1,0:T(8,128)S(1)}, f32[32,8,128]{2,1,0:T(8,128)S(1)}, u32[]{:S(2)}, u32[]{:S(2)}) collective-permute-start(f32[32,8,128]{2,1,0:T(8,128)S(1)} %lay.6.refs_3_.refs_1_), channel_id=1, source_target_pairs={{0,2},{1,3},{2,0},{3,1},{4,6},{5,7},{6,4},{7,5},{8,10},{9,11},{10,... | collective-permute-start | bytes 393224 | tf_op jit(solution)/shard_map/ppermute | solution.py:546
  128.9 6.0 %collective-permute-start.24 = (f32[32,8,128]{2,1,0:T(8,128)S(1)}, f32[32,8,128]{2,1,0:T(8,128)S(1)}, u32[]{:S(2)}, u32[]{:S(2)}) collective-permute-start(f32[32,8,128]{2,1,0:T(8,128)S(1)} %lay.7.refs_3_.refs_1_), channel_id=1, source_target_pairs={{0,2},{1,3},{2,0},{3,1},{4,6},{5,7},{6,4},{7,5},{8,10},{9,11},{10,... | collective-permute-start | bytes 393224 | tf_op jit(solution)/shard_map/ppermute | solution.py:546
  132.5 7.2 %collective-permute-start.23 = (f32[64,8,128]{2,1,0:T(8,128)S(1)}, f32[64,8,128]{2,1,0:T(8,128)S(1)}, u32[]{:S(2)}, u32[]{:S(2)}) collective-permute-start(f32[64,8,128]{2,1,0:T(8,128)S(1)} %lay.8.refs_3_.refs_1_), channel_id=1, source_target_pairs={{0,1},{1,0},{2,3},{3,2},{4,5},{5,4},{6,7},{7,6},{8,9},{9,8},{10,11... | collective-permute-start | bytes 786440 | tf_op jit(solution)/shard_map/ppermute | solution.py:546
  135.5 8.7 %collective-permute-start.28 = (f32[64,8,128]{2,1,0:T(8,128)S(1)}, f32[64,8,128]{2,1,0:T(8,128)S(1)}, u32[]{:S(2)}, u32[]{:S(2)}) collective-permute-start(f32[64,8,128]{2,1,0:T(8,128)S(1)} %lay.9.refs_3_.refs_1_), channel_id=1, source_target_pairs={{0,16},{1,17},{2,18},{3,19},{4,20},{5,21},{6,22},{7,23},{8,24},{9,... | collective-permute-start | bytes 786440 | tf_op jit(solution)/shard_map/ppermute | solution.py:546
  140.3 9.5 %collective-permute-start.25 = (f32[128,8,128]{2,1,0:T(8,128)S(1)}, f32[128,8,128]{2,1,0:T(8,128)S(1)}, u32[]{:S(2)}, u32[]{:S(2)}) collective-permute-start(f32[128,8,128]{2,1,0:T(8,128)S(1)} %lay.10.refs_3_.refs_0_), channel_id=1, source_target_pairs={{0,16},{1,17},{2,18},{3,19},{4,20},{5,21},{6,22},{7,23},{8,24},{9,... | collective-permute-start | bytes 1572872 | tf_op jit(solution)/shard_map/ppermute | solution.py:546
  144.8 9.2 %collective-permute-start.29 = (f32[128,8,128]{2,1,0:T(8,128)S(1)}, f32[128,8,128]{2,1,0:T(8,128)S(1)}, u32[]{:S(2)}, u32[]{:S(2)}) collective-permute-start(f32[128,8,128]{2,1,0:T(8,128)S(1)} %lay.11.refs_4_), channel_id=1, source_target_pairs={{0,1},{1,0},{2,3},{3,2},{4,5},{5,4},{6,7},{7,6},{8,9},{9,8},{10,11... | collective-permute-start | bytes 1572872 | tf_op jit(solution)/shard_map/ppermute | solution.py:546
  146.2 7.8 %collective-permute-start.26 = (f32[128,8,128]{2,1,0:T(8,128)S(1)}, f32[128,8,128]{2,1,0:T(8,128)S(1)}, u32[]{:S(2)}, u32[]{:S(2)}) collective-permute-start(f32[128,8,128]{2,1,0:T(8,128)S(1)} %lay.10.refs_3_.refs_0_), channel_id=1, source_target_pairs={{0,8},{1,9},{2,10},{3,11},{4,12},{5,13},{6,14},{7,15},{8,0},{9,1},... | collective-permute-start | bytes 1572872 | tf_op jit(solution)/shard_map/ppermute | solution.py:546
  146.2 7.8 %collective-permute-start.30 = (f32[128,8,128]{2,1,0:T(8,128)S(1)}, f32[128,8,128]{2,1,0:T(8,128)S(1)}, u32[]{:S(2)}, u32[]{:S(2)}) collective-permute-start(f32[128,8,128]{2,1,0:T(8,128)S(1)} %lay.11.refs_4_), channel_id=1, source_target_pairs={{0,8},{1,9},{2,10},{3,11},{4,12},{5,13},{6,14},{7,15},{8,0},{9,1},... | collective-permute-start | bytes 1572872 | tf_op jit(solution)/shard_map/ppermute | solution.py:546
  (14 other events, 62.4 us)

commit v10 on v9

--- a/solution.py
+++ b/solution.py
@@ -89,12 +89,12 @@
     out_ref[:, heads : 2 * heads] = jax.nn.sigmoid(gates[:, heads:] + bias)
     row = lax.broadcasted_iota(jnp.int32, (span, span), 0)
     col = lax.broadcasted_iota(jnp.int32, (span, span), 1)
-    lower = jnp.where(row >= col, 1.0, 0.0).astype(F32)
+    lower = jnp.where(row >= col, 1.0, 0.0).astype(BF16)
+    high, rest = halves(logdecay)
+    low = (logdecay - high.astype(F32) - rest.astype(F32)).astype(BF16)
     for first in range(0, x_ref.shape[0], span):
-        piece = logdecay[first : first + span]
-        out_ref[first : first + span, :heads] = lax.dot_general(
-            lower, piece, (((1,), (0,)), ((), ())), precision=lax.Precision.HIGHEST, preferred_element_type=F32
-        )
+        here = slice(first, first + span)
+        out_ref[here, :heads] = dot(lower, high[here]) + (dot(lower, rest[here]) + dot(lower, low[here]))
 
 
 def solve_lower(systems, rights):
@@ -599,7 +599,7 @@
                 ready[g] = (keep, moved(sends[g], (0, 0, 0, 1)))
         after = [sends[g]]
     sums = range(len(SUMS))
-    orders = [(on_x + on_y if g % 2 == 0 else on_y + on_x) + on_z for g in sums]
+    orders = [on_x + on_y + on_z if g % 2 == 0 else on_y + on_z + on_x for g in sums]
     mixed, arrays, parts = [], [], []
     for group in SUMS:
         terms = []

time: 159 us -> 157 us (0.987)
  waiting for transfers between devices: 49.1 us -> 45.5 us
  starting transfers between devices: 51.5 us -> 53.6 us
    ppermute x26, waiting for transfers between devices: 44 us -> 40.3 us  [moved(): return lax.ppermute(array, both, route)]
    ppermute x26, starting transfers between devices: 40.6 us -> 42.7 us  [moved(): return lax.ppermute(array, both, route)]
  transfers between devices with their start and end apart: 32 -> 32, of which waited for: 20 -> 20; matrix products, arithmetic and copies ran while one was open for 0% -> 0% of each run, Pallas kernels for 22% -> 23%
where the time goes in v10:
time: 157 us; the launch traced here: 156 us
  starting transfers between devices  53.6 us (34%)
  Pallas kernels  51.2 us (33%)
  waiting for transfers between devices  45.5 us (29%)
  local copies, waits for them, and re-layouts  3.69 us (2%)
    ppermute x26, starting transfers between devices, moved(): return lax.ppermute(array, both, route)  42.7 us
    ppermute x26, waiting for transfers between devices, moved(): return lax.ppermute(array, both, route)  40.3 us
    pallas_call x2, Pallas kernels, local_call(): pl.pallas_call(skipping(functools.partial(local_kernel, first_head, heads...  23.1 us
    ppermute x6, starting transfers between devices, lifted(): return lax.ppermute(array, 'tm', route)  10.9 us
    ppermute x6, waiting for transfers between devices, lifted(): return lax.ppermute(array, 'tm', route)  5.13 us
    pallas_call x8, Pallas kernels, fold_call(): pl.pallas_call(skipping(functools.partial(fold_kernel, parts, terms, wher...  4.79 us
    pallas_call x2, Pallas kernels, mix_call(): pl.pallas_call(skipping(functools.partial(mix_kernel, span, first_head),...  4.44 us
    unnamed x12, local copies, waits for them, and re-layouts  3.59 us
  transfers between devices with their start and end apart: 32, of which 20 were waited for; matrix products, arithmetic and copies ran while one was open for 0% of the time, Pallas kernels for 23%

profile of v10, /device:TPU:0, one launch (start us, length us, event | category | flops | bytes accessed | tf_op | source)
XLA Modules:
  0.0 156.4 jit_solution(7475850438436585524)
XLA Ops:
  5.8 12.4 %local.2 = (f32[4,128,256]{2,1,0:T(8,128)S(1)}, f32[4,128,256]{2,1,0:T(8,128)S(1)}, f32[512,512]{1,0:T(8,128)S(1)}, f32[512,512]{1,0:T(8,128)S(1)}, f32[512,16]{1,0:T(8,128)S(1)}) custom-call(s32[7]{0:T(128)S(1)} %stack.49.refs_0_.info, s32[2,4,24]{2,1,0:T(4,128)S(1)} %pad_add_fusion.refs_1_, bf16[512,1024]{1,0:T(8,128)(2,1)S(1)} %bitcast.26, ...), custom_call_target="tpu_custom_call" | custom-call | flops 6442450944 | bytes 8388608 | tf_op jit(solution)/shard_map/local/pallas_call | solution.py:225
  18.2 3.0 %collective-permute-start = (f32[4,128,256]{2,1,0:T(8,128)S(1)}, f32[4,128,256]{2,1,0:T(8,128)S(1)}, u32[]{:S(2)}, u32[]{:S(2)}) collective-permute-start(f32[4,128,256]{2,1,0:T(8,128)S(1)} %get-tuple-element.63), channel_id=1, source_target_pairs={{0,1},{1,0},{2,3},{3,2},{4,5},{5,4},{6,7},{7,6},{8,9},{9,8},{10,11... | collective-permute-start | bytes 1572872 | tf_op jit(solution)/shard_map/ppermute | solution.py:546
  21.2 10.7 %local.3 = (f32[4,128,256]{2,1,0:T(8,128)S(1)}, f32[4,128,256]{2,1,0:T(8,128)S(1)}, f32[512,512]{1,0:T(8,128)S(1)}, f32[512,512]{1,0:T(8,128)S(1)}) custom-call(s32[7]{0:T(128)S(1)} %stack.49.refs_0_.info, s32[2,4,24]{2,1,0:T(4,128)S(1)} %pad_add_fusion.refs_1_, bf16[512,1024]{1,0:T(8,128)(2,1)S(1)} %bitcast.27, bf16[64,128,128]{2,1,0:T(8,128)(2,1)S(1)} %copy-done.3, ...), custom_call_target="tpu_custom_call" | custom-call | flops 6442450944 | bytes 8388608 | tf_op jit(solution)/shard_map/local/pallas_call | solution.py:225
  34.1 3.9 %collective-permute-start.1 = (f32[4,128,128]{2,1,0:T(8,128)S(1)}, f32[4,128,128]{2,1,0:T(8,128)S(1)}, u32[]{:S(2)}, u32[]{:S(2)}) collective-permute-start(f32[4,128,128]{2,1,0:T(8,128)S(1)} %get-tuple-element.68.refs_4_), channel_id=1, source_target_pairs={{0,2},{1,3},{2,0},{3,1},{8,10},{9,11},{10,8},{11,9},{16,18},{17,19... | collective-permute-start | bytes 786440 | tf_op jit(solution)/shard_map/ppermute | solution.py:551
  38.1 3.3 %back.1.refs_4_.refs_5_ = f32[512,1024]{1,0:T(8,128)S(1)} custom-call(bf16[512,1024]{1,0:T(8,128)(2,1)S(1)} %bitcast.21, bf16[1024,1024]{1,0:T(8,128)(2,1)S(1)} %copy-done.1), custom_call_target="tpu_custom_call" | custom-call | flops 1073741824 | bytes 5242880 | tf_op jit(solution)/shard_map/back/pallas_call | solution.py:378
  41.4 2.1 %collective-permute-done.1.refs_2_ = f32[4,128,128]{2,1,0:T(8,128)S(1)} collective-permute-done((f32[4,128,128]{2,1,0:T(8,128)S(1)}, f32[4,128,128]{2,1,0:T(8,128)S(1)}, u32[]{:S(2)}, u32[]{:S(2)}) %collective-permute-start.1) | collective-permute-done | bytes 262176 | tf_op jit(solution)/shard_map/ppermute | solution.py:551
  46.4 4.3 %collective-permute-start.5 = (f32[4,128,128]{2,1,0:T(8,128)S(1)}, f32[4,128,128]{2,1,0:T(8,128)S(1)}, u32[]{:S(2)}, u32[]{:S(2)}) collective-permute-start(f32[4,128,128]{2,1,0:T(8,128)S(1)} %get-tuple-element.72.refs_4_), channel_id=1, source_target_pairs={{0,2},{1,3},{2,0},{3,1},{8,10},{9,11},{10,8},{11,9},{16,18},{17,19... | collective-permute-start | bytes 786440 | tf_op jit(solution)/shard_map/ppermute | solution.py:551
  52.2 3.0 %collective-permute-done.5.refs_2_ = f32[4,128,128]{2,1,0:T(8,128)S(1)} collective-permute-done((f32[4,128,128]{2,1,0:T(8,128)S(1)}, f32[4,128,128]{2,1,0:T(8,128)S(1)}, u32[]{:S(2)}, u32[]{:S(2)}) %collective-permute-start.5) | collective-permute-done | bytes 262176 | tf_op jit(solution)/shard_map/ppermute | solution.py:551
  62.1 5.5 %collective-permute-done.6.refs_4_ = f32[4,128,128]{2,1,0:T(8,128)S(1)} collective-permute-done((f32[4,128,128]{2,1,0:T(8,128)S(1)}, f32[4,128,128]{2,1,0:T(8,128)S(1)}, u32[]{:S(2)}, u32[]{:S(2)}) %collective-permute-start.6) | collective-permute-done | bytes 262176 | tf_op jit(solution)/shard_map/ppermute | solution.py:546
  67.6 2.2 %mix.2 = (bf16[512,512]{1,0:T(8,128)(2,1)S(1)}, f32[257,8,128]{2,1,0:T(8,128)S(1)}, f32[257,8,128]{2,1,0:T(8,128)S(1)}) custom-call(s32[7]{0:T(128)S(1)} %stack.49.refs_0_.info, f32[512,512]{1,0:T(8,128)S(1)} %get-tuple-element.60.refs_1_, f32[512,512]{1,0:T(8,128)S(1)} %get-tuple-element.61.refs_2_, f32[4,128,128]{2,1,0:T(8,128)S(1)} %get-tuple-element.77.refs_3_, ...), custom_call_target="tpu_custom_call" | custom-call | flops 536870912 | bytes 3145728 | tf_op jit(solution)/shard_map/mix/pallas_call | solution.py:360
  70.4 2.2 %mix.3 = (bf16[512,512]{1,0:T(8,128)(2,1)S(1)}, f32[257,8,128]{2,1,0:T(8,128)S(1)}, f32[257,8,128]{2,1,0:T(8,128)S(1)}) custom-call(s32[7]{0:T(128)S(1)} %stack.49.refs_0_.info, f32[512,512]{1,0:T(8,128)S(1)} %get-tuple-element.85.refs_1_, f32[512,512]{1,0:T(8,128)S(1)} %get-tuple-element.86.refs_2_, f32[4,128,128]{2,1,0:T(8,128)S(1)} %get-tuple-element.87.refs_3_, ...), custom_call_target="tpu_custom_call" | custom-call | flops 536870912 | bytes 3145728 | tf_op jit(solution)/shard_map/mix/pallas_call | solution.py:360
  77.1 2.8 %finish.1 = (bf16[512,1024]{1,0:T(8,128)(2,1)}, f32[8,128]{1,0:T(8,128)S(1)}) custom-call(bf16[512,512]{1,0:T(8,128)(2,1)S(1)} %get-tuple-element.84.refs_0_, bf16[512,512]{1,0:T(8,128)(2,1)S(1)} %get-tuple-element.89.refs_1_, bf16[1024,1024]{1,0:T(8,128)(2,1)S(1)} %copy-done.1), custom_call_target="tpu_custom_call" | custom-call | flops 1073741824 | bytes 4194304 | tf_op jit(solution)/shard_map/finish/pallas_call | solution.py:401
  79.9 7.9 %collective-permute-done.11.refs_2_ = f32[129,8,128]{2,1,0:T(8,128)S(1)} collective-permute-done((f32[129,8,128]{2,1,0:T(8,128)S(1)}, f32[129,8,128]{2,1,0:T(8,128)S(1)}, u32[]{:S(2)}, u32[]{:S(2)}) %collective-permute-start.11) | collective-permute-done | bytes 528416 | tf_op jit(solution)/shard_map/ppermute | solution.py:546
  90.7 7.2 %collective-permute-start.16 = (f32[65,8,128]{2,1,0:T(8,128)S(1)}, f32[65,8,128]{2,1,0:T(8,128)S(1)}, u32[]{:S(2)}, u32[]{:S(2)}) collective-permute-start(f32[65,8,128]{2,1,0:T(8,128)S(1)} %get-tuple-element.104), channel_id=1, source_target_pairs={{0,2},{1,3},{2,0},{3,1},{4,6},{5,7},{6,4},{7,5},{8,10},{9,11},{10,... | collective-permute-start | bytes 798728 | tf_op jit(solution)/shard_map/ppermute | solution.py:546
  98.6 5.8 %collective-permute-start.15 = (f32[33,8,128]{2,1,0:T(8,128)S(1)}, f32[33,8,128]{2,1,0:T(8,128)S(1)}, u32[]{:S(2)}, u32[]{:S(2)}) collective-permute-start(f32[33,8,128]{2,1,0:T(8,128)S(1)} %get-tuple-element.103), channel_id=1, source_target_pairs={{0,2},{1,3},{2,0},{3,1},{4,6},{5,7},{6,4},{7,5},{8,10},{9,11},{10,... | collective-permute-start | bytes 405512 | tf_op jit(solution)/shard_map/ppermute | solution.py:546
  104.9 5.7 %collective-permute-start.19 = (f32[33,8,128]{2,1,0:T(8,128)S(1)}, f32[33,8,128]{2,1,0:T(8,128)S(1)}, u32[]{:S(2)}, u32[]{:S(2)}) collective-permute-start(f32[33,8,128]{2,1,0:T(8,128)S(1)} %get-tuple-element.109), channel_id=1, source_target_pairs={{0,4},{1,5},{2,6},{3,7},{4,0},{5,1},{6,2},{7,3},{8,12},{9,13},{10,... | collective-permute-start | bytes 405512 | tf_op jit(solution)/shard_map/ppermute | solution.py:546
  111.2 4.5 %collective-permute-start.17 = (f32[17,8,128]{2,1,0:T(8,128)S(1)}, f32[17,8,128]{2,1,0:T(8,128)S(1)}, u32[]{:S(2)}, u32[]{:S(2)}) collective-permute-start(f32[17,8,128]{2,1,0:T(8,128)S(1)} %get-tuple-element.107), channel_id=1, source_target_pairs={{0,4},{1,5},{2,6},{3,7},{4,0},{5,1},{6,2},{7,3},{8,12},{9,13},{10,... | collective-permute-start | bytes 208904 | tf_op jit(solution)/shard_map/ppermute | solution.py:546
  115.8 2.2 %collective-permute-done.19.refs_2_ = f32[33,8,128]{2,1,0:T(8,128)S(1)} collective-permute-done((f32[33,8,128]{2,1,0:T(8,128)S(1)}, f32[33,8,128]{2,1,0:T(8,128)S(1)}, u32[]{:S(2)}, u32[]{:S(2)}) %collective-permute-start.19) | collective-permute-done | bytes 135200 | tf_op jit(solution)/shard_map/ppermute | solution.py:546
  133.2 2.0 %collective-permute-done.24.refs_2_ = f32[32,8,128]{2,1,0:T(8,128)S(1)} collective-permute-done((f32[32,8,128]{2,1,0:T(8,128)S(1)}, f32[32,8,128]{2,1,0:T(8,128)S(1)}, u32[]{:S(2)}, u32[]{:S(2)}) %collective-permute-start.24) | collective-permute-done | bytes 131104 | tf_op jit(solution)/shard_map/ppermute | solution.py:546
  135.9 2.2 %collective-permute-done.23.refs_2_ = f32[64,8,128]{2,1,0:T(8,128)S(1)} collective-permute-done((f32[64,8,128]{2,1,0:T(8,128)S(1)}, f32[64,8,128]{2,1,0:T(8,128)S(1)}, u32[]{:S(2)}, u32[]{:S(2)}) %collective-permute-start.23) | collective-permute-done | bytes 262176 | tf_op jit(solution)/shard_map/ppermute | solution.py:546
  139.3 3.0 %collective-permute-done.28.refs_2_ = f32[64,8,128]{2,1,0:T(8,128)S(1)} collective-permute-done((f32[64,8,128]{2,1,0:T(8,128)S(1)}, f32[64,8,128]{2,1,0:T(8,128)S(1)}, u32[]{:S(2)}, u32[]{:S(2)}) %collective-permute-start.28) | collective-permute-done | bytes 262176 | tf_op jit(solution)/shard_map/ppermute | solution.py:546
  144.9 3.0 %collective-permute-done.25.refs_1_ = f32[128,8,128]{2,1,0:T(8,128)S(1)} collective-permute-done((f32[128,8,128]{2,1,0:T(8,128)S(1)}, f32[128,8,128]{2,1,0:T(8,128)S(1)}, u32[]{:S(2)}, u32[]{:S(2)}) %collective-permute-start.25) | collective-permute-done | bytes 524320 | tf_op jit(solution)/shard_map/ppermute | solution.py:546
  147.9 4.2 %collective-permute-done.29.refs_5_ = f32[128,8,128]{2,1,0:T(8,128)S(1)} collective-permute-done((f32[128,8,128]{2,1,0:T(8,128)S(1)}, f32[128,8,128]{2,1,0:T(8,128)S(1)}, u32[]{:S(2)}, u32[]{:S(2)}) %collective-permute-start.29) | collective-permute-done | bytes 524320 | tf_op jit(solution)/shard_map/ppermute | solution.py:546
  154.0 2.4 %join.1 = (bf16[1024,1024]{1,0:T(8,128)(2,1)}, f32[1,128]{1,0:T(1,128)}) custom-call(s32[7]{0:T(128)S(1)} %stack.49.refs_0_.info, f32[128,8,128]{2,1,0:T(8,128)S(1)} %lay.10.refs_3_.refs_0_, f32[128,8,128]{2,1,0:T(8,128)S(1)} %collective-permute-done.25.refs_1_, f32[128,8,128]{2,1,0:T(8,128)S(1)} %collective-permute-done.26.refs_2_, ...), custom_call_target="tpu_custom_call" | custom-call | tf_op jit(solution)/shard_map/join/pallas_call | solution.py:514
  (87 shorter events, 49.5 us)
Async XLA Ops:
  18.2 15.0 %collective-permute-start = (f32[4,128,256]{2,1,0:T(8,128)S(1)}, f32[4,128,256]{2,1,0:T(8,128)S(1)}, u32[]{:S(2)}, u32[]{:S(2)}) collective-permute-start(f32[4,128,256]{2,1,0:T(8,128)S(1)} %get-tuple-element.63), channel_id=1, source_target_pairs={{0,1},{1,0},{2,3},{3,2},{4,5},{5,4},{6,7},{7,6},{8,9},{9,8},{10,11... | collective-permute-start | bytes 1572872 | tf_op jit(solution)/shard_map/ppermute | solution.py:546
  32.0 13.4 %collective-permute-start.3 = (f32[4,128,256]{2,1,0:T(8,128)S(1)}, f32[4,128,256]{2,1,0:T(8,128)S(1)}, u32[]{:S(2)}, u32[]{:S(2)}) collective-permute-start(f32[4,128,256]{2,1,0:T(8,128)S(1)} %get-tuple-element.71), channel_id=1, source_target_pairs={{0,1},{1,0},{2,3},{3,2},{4,5},{5,4},{6,7},{7,6},{8,9},{9,8},{10,11... | collective-permute-start | bytes 1572872 | tf_op jit(solution)/shard_map/ppermute | solution.py:546
  34.1 9.4 %collective-permute-start.1 = (f32[4,128,128]{2,1,0:T(8,128)S(1)}, f32[4,128,128]{2,1,0:T(8,128)S(1)}, u32[]{:S(2)}, u32[]{:S(2)}) collective-permute-start(f32[4,128,128]{2,1,0:T(8,128)S(1)} %get-tuple-element.68.refs_4_), channel_id=1, source_target_pairs={{0,2},{1,3},{2,0},{3,1},{8,10},{9,11},{10,8},{11,9},{16,18},{17,19... | collective-permute-start | bytes 786440 | tf_op jit(solution)/shard_map/ppermute | solution.py:551
  44.4 6.4 %collective-permute-start.2 = (f32[4,128,128]{2,1,0:T(8,128)S(1)}, f32[4,128,128]{2,1,0:T(8,128)S(1)}, u32[]{:S(2)}, u32[]{:S(2)}) collective-permute-start(f32[4,128,128]{2,1,0:T(8,128)S(1)} %get-tuple-element.69.refs_3_), channel_id=1, source_target_pairs={{2,4},{3,5},{4,2},{5,3},{10,12},{11,13},{12,10},{13,11},{18,20},{1... | collective-permute-start | bytes 786440 | tf_op jit(solution)/shard_map/ppermute | solution.py:551
  46.4 8.8 %collective-permute-start.5 = (f32[4,128,128]{2,1,0:T(8,128)S(1)}, f32[4,128,128]{2,1,0:T(8,128)S(1)}, u32[]{:S(2)}, u32[]{:S(2)}) collective-permute-start(f32[4,128,128]{2,1,0:T(8,128)S(1)} %get-tuple-element.72.refs_4_), channel_id=1, source_target_pairs={{0,2},{1,3},{2,0},{3,1},{8,10},{9,11},{10,8},{11,9},{16,18},{17,19... | collective-permute-start | bytes 786440 | tf_op jit(solution)/shard_map/ppermute | solution.py:551
  51.6 5.2 %collective-permute-start.4 = (f32[4,128,128]{2,1,0:T(8,128)S(1)}, f32[4,128,128]{2,1,0:T(8,128)S(1)}, u32[]{:S(2)}, u32[]{:S(2)}) collective-permute-start(f32[4,128,128]{2,1,0:T(8,128)S(1)} %get-tuple-element.73.refs_4_), channel_id=1, source_target_pairs={{4,6},{5,7},{6,4},{7,5},{12,14},{13,15},{14,12},{15,13},{20,22},{2... | collective-permute-start | bytes 786440 | tf_op jit(solution)/shard_map/ppermute | solution.py:551
  59.1 8.5 %collective-permute-start.6 = (f32[4,128,128]{2,1,0:T(8,128)S(1)}, f32[4,128,128]{2,1,0:T(8,128)S(1)}, u32[]{:S(2)}, u32[]{:S(2)}) collective-permute-start(f32[4,128,128]{2,1,0:T(8,128)S(1)} %get-tuple-element.78.refs_4_), channel_id=1, source_target_pairs={{0,1},{1,0},{2,3},{3,2},{4,5},{5,4},{6,7},{7,6},{8,9},{9,8},{10,11... | collective-permute-start | bytes 786440 | tf_op jit(solution)/shard_map/ppermute | solution.py:546
  61.4 9.0 %collective-permute-start.9 = (f32[4,128,128]{2,1,0:T(8,128)S(1)}, f32[4,128,128]{2,1,0:T(8,128)S(1)}, u32[]{:S(2)}, u32[]{:S(2)}) collective-permute-start(f32[4,128,128]{2,1,0:T(8,128)S(1)} %get-tuple-element.83.refs_8_), channel_id=1, source_target_pairs={{0,1},{1,0},{2,3},{3,2},{4,5},{5,4},{6,7},{7,6},{8,9},{9,8},{10,11... | collective-permute-start | bytes 786440 | tf_op jit(solution)/shard_map/ppermute | solution.py:546
  73.4 14.5 %collective-permute-start.11 = (f32[129,8,128]{2,1,0:T(8,128)S(1)}, f32[129,8,128]{2,1,0:T(8,128)S(1)}, u32[]{:S(2)}, u32[]{:S(2)}) collective-permute-start(f32[129,8,128]{2,1,0:T(8,128)S(1)} %get-tuple-element.94), channel_id=1, source_target_pairs={{0,16},{1,17},{2,18},{3,19},{4,20},{5,21},{6,22},{7,23},{8,24},{9,... | collective-permute-start | bytes 1585160 | tf_op jit(solution)/shard_map/ppermute | solution.py:546
  76.0 14.1 %collective-permute-start.14 = (f32[129,8,128]{2,1,0:T(8,128)S(1)}, f32[129,8,128]{2,1,0:T(8,128)S(1)}, u32[]{:S(2)}, u32[]{:S(2)}) collective-permute-start(f32[129,8,128]{2,1,0:T(8,128)S(1)} %get-tuple-element.99), channel_id=1, source_target_pairs={{0,1},{1,0},{2,3},{3,2},{4,5},{5,4},{6,7},{7,6},{8,9},{9,8},{10,11... | collective-permute-start | bytes 1585160 | tf_op jit(solution)/shard_map/ppermute | solution.py:546
  88.5 9.5 %collective-permute-start.13 = (f32[65,8,128]{2,1,0:T(8,128)S(1)}, f32[65,8,128]{2,1,0:T(8,128)S(1)}, u32[]{:S(2)}, u32[]{:S(2)}) collective-permute-start(f32[65,8,128]{2,1,0:T(8,128)S(1)} %get-tuple-element.98), channel_id=1, source_target_pairs={{0,1},{1,0},{2,3},{3,2},{4,5},{5,4},{6,7},{7,6},{8,9},{9,8},{10,11... | collective-permute-start | bytes 798728 | tf_op jit(solution)/shard_map/ppermute | solution.py:546
  90.7 13.6 %collective-permute-start.16 = (f32[65,8,128]{2,1,0:T(8,128)S(1)}, f32[65,8,128]{2,1,0:T(8,128)S(1)}, u32[]{:S(2)}, u32[]{:S(2)}) collective-permute-start(f32[65,8,128]{2,1,0:T(8,128)S(1)} %get-tuple-element.104), channel_id=1, source_target_pairs={{0,2},{1,3},{2,0},{3,1},{4,6},{5,7},{6,4},{7,5},{8,10},{9,11},{10,... | collective-permute-start | bytes 798728 | tf_op jit(solution)/shard_map/ppermute | solution.py:546
  98.6 12.1 %collective-permute-start.15 = (f32[33,8,128]{2,1,0:T(8,128)S(1)}, f32[33,8,128]{2,1,0:T(8,128)S(1)}, u32[]{:S(2)}, u32[]{:S(2)}) collective-permute-start(f32[33,8,128]{2,1,0:T(8,128)S(1)} %get-tuple-element.103), channel_id=1, source_target_pairs={{0,2},{1,3},{2,0},{3,1},{4,6},{5,7},{6,4},{7,5},{8,10},{9,11},{10,... | collective-permute-start | bytes 405512 | tf_op jit(solution)/shard_map/ppermute | solution.py:546
  104.9 13.0 %collective-permute-start.19 = (f32[33,8,128]{2,1,0:T(8,128)S(1)}, f32[33,8,128]{2,1,0:T(8,128)S(1)}, u32[]{:S(2)}, u32[]{:S(2)}) collective-permute-start(f32[33,8,128]{2,1,0:T(8,128)S(1)} %get-tuple-element.109), channel_id=1, source_target_pairs={{0,4},{1,5},{2,6},{3,7},{4,0},{5,1},{6,2},{7,3},{8,12},{9,13},{10,... | collective-permute-start | bytes 405512 | tf_op jit(solution)/shard_map/ppermute | solution.py:546
  111.2 8.9 %collective-permute-start.17 = (f32[17,8,128]{2,1,0:T(8,128)S(1)}, f32[17,8,128]{2,1,0:T(8,128)S(1)}, u32[]{:S(2)}, u32[]{:S(2)}) collective-permute-start(f32[17,8,128]{2,1,0:T(8,128)S(1)} %get-tuple-element.107), channel_id=1, source_target_pairs={{0,4},{1,5},{2,6},{3,7},{4,0},{5,1},{6,2},{7,3},{8,12},{9,13},{10,... | collective-permute-start | bytes 208904 | tf_op jit(solution)/shard_map/ppermute | solution.py:546
  120.1 5.2 %collective-permute-start.18 = (f32[16,8,128]{2,1,0:T(8,128)S(1)}, f32[16,8,128]{2,1,0:T(8,128)S(1)}, u32[]{:S(2)}, u32[]{:S(2)}) collective-permute-start(f32[16,8,128]{2,1,0:T(8,128)S(1)} %get-tuple-element.108.refs_1_), channel_id=1, source_target_pairs={{0,4},{1,5},{2,6},{3,7},{4,0},{5,1},{6,2},{7,3},{8,12},{9,13},{10,... | collective-permute-start | bytes 196616 | tf_op jit(solution)/shard_map/ppermute | solution.py:546
  125.9 5.2 %collective-permute-start.21 = (f32[32,8,128]{2,1,0:T(8,128)S(1)}, f32[32,8,128]{2,1,0:T(8,128)S(1)}, u32[]{:S(2)}, u32[]{:S(2)}) collective-permute-start(f32[32,8,128]{2,1,0:T(8,128)S(1)} %lay.6.refs_3_.refs_1_), channel_id=1, source_target_pairs={{0,2},{1,3},{2,0},{3,1},{4,6},{5,7},{6,4},{7,5},{8,10},{9,11},{10,... | collective-permute-start | bytes 393224 | tf_op jit(solution)/shard_map/ppermute | solution.py:546
  127.8 7.4 %collective-permute-start.24 = (f32[32,8,128]{2,1,0:T(8,128)S(1)}, f32[32,8,128]{2,1,0:T(8,128)S(1)}, u32[]{:S(2)}, u32[]{:S(2)}) collective-permute-start(f32[32,8,128]{2,1,0:T(8,128)S(1)} %lay.7.refs_3_.refs_1_), channel_id=1, source_target_pairs={{0,4},{1,5},{2,6},{3,7},{4,0},{5,1},{6,2},{7,3},{8,12},{9,13},{10,... | collective-permute-start | bytes 393224 | tf_op jit(solution)/shard_map/ppermute | solution.py:546
  131.6 6.4 %collective-permute-start.23 = (f32[64,8,128]{2,1,0:T(8,128)S(1)}, f32[64,8,128]{2,1,0:T(8,128)S(1)}, u32[]{:S(2)}, u32[]{:S(2)}) collective-permute-start(f32[64,8,128]{2,1,0:T(8,128)S(1)} %lay.8.refs_3_.refs_1_), channel_id=1, source_target_pairs={{0,1},{1,0},{2,3},{3,2},{4,5},{5,4},{6,7},{7,6},{8,9},{9,8},{10,11... | collective-permute-start | bytes 786440 | tf_op jit(solution)/shard_map/ppermute | solution.py:546
  135.8 6.4 %collective-permute-start.28 = (f32[64,8,128]{2,1,0:T(8,128)S(1)}, f32[64,8,128]{2,1,0:T(8,128)S(1)}, u32[]{:S(2)}, u32[]{:S(2)}) collective-permute-start(f32[64,8,128]{2,1,0:T(8,128)S(1)} %lay.9.refs_3_.refs_1_), channel_id=1, source_target_pairs={{0,2},{1,3},{2,0},{3,1},{4,6},{5,7},{6,4},{7,5},{8,10},{9,11},{10,... | collective-permute-start | bytes 786440 | tf_op jit(solution)/shard_map/ppermute | solution.py:546
  138.7 9.2 %collective-permute-start.25 = (f32[128,8,128]{2,1,0:T(8,128)S(1)}, f32[128,8,128]{2,1,0:T(8,128)S(1)}, u32[]{:S(2)}, u32[]{:S(2)}) collective-permute-start(f32[128,8,128]{2,1,0:T(8,128)S(1)} %lay.10.refs_3_.refs_0_), channel_id=1, source_target_pairs={{0,16},{1,17},{2,18},{3,19},{4,20},{5,21},{6,22},{7,23},{8,24},{9,... | collective-permute-start | bytes 1572872 | tf_op jit(solution)/shard_map/ppermute | solution.py:546
  142.8 9.2 %collective-permute-start.29 = (f32[128,8,128]{2,1,0:T(8,128)S(1)}, f32[128,8,128]{2,1,0:T(8,128)S(1)}, u32[]{:S(2)}, u32[]{:S(2)}) collective-permute-start(f32[128,8,128]{2,1,0:T(8,128)S(1)} %lay.11.refs_4_), channel_id=1, source_target_pairs={{0,1},{1,0},{2,3},{3,2},{4,5},{5,4},{6,7},{7,6},{8,9},{9,8},{10,11... | collective-permute-start | bytes 1572872 | tf_op jit(solution)/shard_map/ppermute | solution.py:546
  144.3 7.7 %collective-permute-start.26 = (f32[128,8,128]{2,1,0:T(8,128)S(1)}, f32[128,8,128]{2,1,0:T(8,128)S(1)}, u32[]{:S(2)}, u32[]{:S(2)}) collective-permute-start(f32[128,8,128]{2,1,0:T(8,128)S(1)} %lay.10.refs_3_.refs_0_), channel_id=1, source_target_pairs={{0,8},{1,9},{2,10},{3,11},{4,12},{5,13},{6,14},{7,15},{8,0},{9,1},... | collective-permute-start | bytes 1572872 | tf_op jit(solution)/shard_map/ppermute | solution.py:546
  144.3 7.7 %collective-permute-start.30 = (f32[128,8,128]{2,1,0:T(8,128)S(1)}, f32[128,8,128]{2,1,0:T(8,128)S(1)}, u32[]{:S(2)}, u32[]{:S(2)}) collective-permute-start(f32[128,8,128]{2,1,0:T(8,128)S(1)} %lay.11.refs_4_), channel_id=1, source_target_pairs={{0,8},{1,9},{2,10},{3,11},{4,12},{5,13},{6,14},{7,15},{8,0},{9,1},... | collective-permute-start | bytes 1572872 | tf_op jit(solution)/shard_map/ppermute | solution.py:546
  (14 other events, 60.6 us)
